TPU v7x, 128 devices: a whole 4x4x4 slice. The times are simulated.
128 devices in a mesh: ctx: 32 (over y, x, core), tp: 4 (over z).
Axes of the slice: x: 4, y: 4, z: 4, core: 2. Of those that a mesh axis runs over, the one named last changes fastest.
Arguments:
- hidden: bfloat16 [8192, 5120], P('ctx', 'tp'), may hold values from -6 to 6
- queries: bfloat16 [8192, 5120], P('ctx', 'tp'), may hold values from -28 to 28
- key_weight: bfloat16 [5120, 1024], P(None, 'tp'), may hold values from -0.078125 to 0.078125
- value_weight: bfloat16 [5120, 1024], P(None, 'tp'), may hold values from -0.078125 to 0.078125
- parents: int32 [64], replicated, may hold values from -1 to 62, as said below
- upstream: bfloat16 [8192, 5120], P('ctx', 'tp'), may hold values from -6 to 6
Outputs:
- attention: bfloat16 [8192, 5120], P('ctx', 'tp')
- query_grad: bfloat16 [8192, 5120], P('ctx', 'tp')
- hidden_grad: bfloat16 [8192, 5120], P('ctx', 'tp')
- key_weight_grad: float32 [5120, 1024], P('ctx', 'tp')
- value_weight_grad: float32 [5120, 1024], P('ctx', 'tp')
Inputs may be any that keep to these rules, and one draw needn't show every extreme that they name: Node blocks lie in depth-first order: parents[b] < b is the parent of block b for b > 0, parents[0] = -1 and block 0 is the only root; no root-to-leaf path holds more than 8 blocks; the last 7 blocks form one chain below block 0, so that the last block's path holds exactly 8 blocks.
All inputs are finite; a program needn't handle non-finite values.
Results may differ from a plain program's by a relative error of at most 0.023.
The roundings to bfloat16 on the way count: a program that leaves them out, or rounds other values in their place, can miss the bound.
Values may be sent and summed in bfloat16 or wider, within the bound.
No kernel may reach another device: no remote copies, remote signals or barrier semaphores. Data moves between devices by JAX's collectives and lax.ppermute only.
A program may use at most 128 MiB of HBM per device.

v0:
```python
import math

import jax
import jax.numpy as jnp
from jax import lax
from jax.experimental import pallas as pl
from jax.experimental.pallas import tpu as pltpu
from jax.sharding import PartitionSpec as P

HD = 128
BLOCK = 128
DEPTH = 8
THETA = 1000000.0
NEGATIVE = -1e30
BF = jnp.bfloat16
F32 = jnp.float32
SCALE = 1.0 / math.sqrt(HD)
STACK = DEPTH - 1
SLOTS = STACK + 4
OFFSETS = (0, 3, 1, 2)


def side(delta):
    return jnp.where(delta == 0, 0, jnp.where(delta == 3, 1, jnp.where(delta == 1, 2, 3)))


def device_tables(parents, position):
    block_total = parents.shape[0]

    def body(links, where, table, place, depths, level):
        y, x, core, tp = where[0], where[1], where[2], where[3]
        first = 16 * y + 4 * x
        level[0] = 0

        def descend(b, carry):
            level[b] = level[links[b]] + 1
            return carry

        lax.fori_loop(1, block_total, descend, 0)
        place[0] = tp
        place[1] = (tp + 3) % 4
        place[2] = (tp + 1) % 4
        place[3] = (tp + 2) % 4
        place[4] = core
        for k, o in enumerate(OFFSETS):
            place[5 + k] = (tp + o) % 4
            place[9 + k] = side((tp + o - y + 4) % 4)
            place[13 + k] = (x + o) % 4
        table[AT_CORE] = core

        def blank(i, carry):
            table[AT_DENSE + i] = SLOTS
            return carry

        lax.fori_loop(0, 64, blank, 0)
        for r in range(4):
            table[AT_DENSE + r] = STACK + r
            block = first + (2 * core + r) % 4
            own_depth = level[block]
            depths[r] = own_depth
            table[AT_DEPTH + r] = own_depth
            node = block
            for d in range(DEPTH - 1, -1, -1):
                live = d <= own_depth
                slot = jnp.where(node >= first, STACK + (node - first + 4 - 2 * core) % 4, d)
                table[AT_SLOT + r * DEPTH + d] = jnp.where(live, slot, STACK + r)
                node = jnp.where(live, jnp.maximum(links[node], 0), node)
        lead_depth = level[first]
        node = first
        for d in range(STACK - 1, -1, -1):
            live = d < lead_depth
            node = jnp.where(live, jnp.maximum(links[node], 0), node)
            column = side((node // 4 + 4 - x) % 4)
            line = side((node // 16 + 4 - y) % 4)
            same = (node // 2) % 2 == core
            parity = node % 2
            outer = jnp.where(same, line, column)
            inner = jnp.where(same, column, line)
            piece = jnp.where(same, 0, 8) + outer * 2 + parity
            table[d] = jnp.where(live, piece, -1)
            table[AT_PLACE + d] = jnp.where(live, inner, 0)
            spot = AT_DENSE + (column * 4 + line) * 4 + (node + 4 - 2 * core) % 4

            @pl.when(live)
            def _(spot=spot, d=d):
                table[spot] = d

    smem = pl.BlockSpec(memory_space=pltpu.SMEM)
    return pl.pallas_call(
        body,
        in_specs=[smem, smem],
        out_specs=[smem] * 3,
        out_shape=[
            jax.ShapeDtypeStruct((AT_CORE + 1,), jnp.int32),
            jax.ShapeDtypeStruct((17,), jnp.int32),
            jax.ShapeDtypeStruct((4,), jnp.int32),
        ],
        scratch_shapes=[pltpu.SMEM((block_total,), jnp.int32)],
        name="device_tables",
    )(parents, position)


AT_PLACE = STACK
AT_DEPTH = 2 * STACK
AT_SLOT = AT_DEPTH + 4
AT_DENSE = AT_SLOT + 4 * DEPTH
AT_CORE = AT_DENSE + 64


def rope_tables(depths):
    offset = jnp.arange(BLOCK, dtype=jnp.int32)
    position = (depths[:, None] * BLOCK + offset[None, :]).astype(F32)
    frequency = jnp.exp(jnp.arange(HD // 2, dtype=F32) * (-2.0 * math.log(THETA) / HD))
    angles = (position[:, :, None] * frequency[None, None, :]).reshape(4 * BLOCK, HD // 2)
    cosine, sine = jnp.cos(angles), jnp.sin(angles)
    return (
        jnp.concatenate([cosine, cosine], axis=-1),
        jnp.concatenate([-sine, sine], axis=-1),
    )


def nn(a, b):
    return jnp.dot(a, b, preferred_element_type=F32)


def nt(a, b):
    return lax.dot_general(a, b, (((1,), (1,)), ((), ())), preferred_element_type=F32)


def tn(a, b):
    return lax.dot_general(a, b, (((0,), (0,)), ((), ())), preferred_element_type=F32)


def params(mib):
    return pltpu.CompilerParams(vmem_limit_bytes=mib * 1024 * 1024)


def project_near(place, own, left_top, left_low, right_top, right_low, key_weight, value_weight):
    rows, width = own.shape
    cols = key_weight.shape[1]

    def body(place_ref, a, bt, bl, ct, cl, ka, kb, kc, va, vb, vc, key_out, value_out):
        b = jnp.concatenate([bt[...], bl[...]], axis=0)
        c = jnp.concatenate([ct[...], cl[...]], axis=0)
        key_out[...] = nn(a[...], ka[...]) + nn(b, kb[...]) + nn(c, kc[...])
        value_out[...] = nn(a[...], va[...]) + nn(b, vb[...]) + nn(c, vc[...])

    whole = pl.BlockSpec((rows, width), lambda i, p: (0, 0))
    half = pl.BlockSpec((rows // 2, width), lambda i, p: (0, 0))
    weights = [pl.BlockSpec((width, cols), lambda i, p, k=k: (p[k], 0)) for k in range(3)]
    out = pl.BlockSpec((rows, cols), lambda i, p: (0, 0))
    return pl.pallas_call(
        body,
        grid_spec=pltpu.PrefetchScalarGridSpec(
            num_scalar_prefetch=1,
            grid=(1,),
            in_specs=[whole] + [half] * 4 + weights + weights,
            out_specs=[out, out],
        ),
        out_shape=[jax.ShapeDtypeStruct((rows, cols), F32)] * 2,
        compiler_params=params(18),
        name="project_near",
    )(
        place,
        own,
        left_top,
        left_low,
        right_top,
        right_low,
        *([key_weight] * 3),
        *([value_weight] * 3),
    )


def pack(own, back, forth, far):
    def body(a, b, c, d, first, second):
        for k, ref in enumerate((a, b, c, d)):
            first[k] = ref[:BLOCK]
            second[k] = ref[BLOCK:]

    return pl.pallas_call(
        body,
        in_specs=[pl.BlockSpec(memory_space=pltpu.VMEM)] * 4,
        out_specs=[pl.BlockSpec(memory_space=pltpu.VMEM)] * 2,
        out_shape=[jax.ShapeDtypeStruct((4, BLOCK, 2 * HD), BF)] * 2,
        compiler_params=params(6),
        name="pack",
    )(own, back, forth, far)


def join_weights(place, mine, other):
    share = mine.shape[0]

    def body(p, a, b, key, value):
        swap = p[4] == 1
        first = jnp.where(swap, b[...], a[...])
        second = jnp.where(swap, a[...], b[...])
        key[:, :HD] = first[:, :HD]
        key[:, HD:] = second[:, :HD]
        value[:, :HD] = first[:, HD:]
        value[:, HD:] = second[:, HD:]

    return pl.pallas_call(
        body,
        in_specs=[pl.BlockSpec(memory_space=pltpu.SMEM)]
        + [pl.BlockSpec(memory_space=pltpu.VMEM)] * 2,
        out_specs=[pl.BlockSpec(memory_space=pltpu.VMEM)] * 2,
        out_shape=[jax.ShapeDtypeStruct((share, 2 * HD), F32)] * 2,
        compiler_params=params(6),
        name="join_weights",
    )(place, mine, other)


def project_far(place, top, bottom, key_weight, value_weight, key_sum, value_sum, cosine, sine):
    rows, cols = key_sum.shape
    width = top.shape[1]
    half = rows // 2

    def body(p, a, b, kw, vw, ks, vs, cs, sn, keep, send):
        far = jnp.concatenate([a[...], b[...]], axis=0)
        key = ks[...] + nn(far, kw[...])
        value = vs[...] + nn(far, vw[...])
        heads = []
        for h in range(2):
            part = key[:, h * HD : (h + 1) * HD]
            turned = part * cs[...] + pltpu.roll(part, HD // 2, 1) * sn[...]
            heads.append(
                jnp.concatenate([turned, value[:, h * HD : (h + 1) * HD]], axis=1).astype(BF)
            )
        swap = p[4] == 1
        keep[...] = jnp.where(swap, heads[1], heads[0])
        send[...] = jnp.where(swap, heads[0], heads[1])

    weight = pl.BlockSpec((width, cols), lambda i, p: (p[3], 0))
    part = pl.BlockSpec((half, width), lambda i, p: (0, 0))
    sums = pl.BlockSpec((rows, cols), lambda i, p: (0, 0))
    angle = pl.BlockSpec((rows, HD), lambda i, p: (0, 0))
    return pl.pallas_call(
        body,
        grid_spec=pltpu.PrefetchScalarGridSpec(
            num_scalar_prefetch=1,
            grid=(1,),
            in_specs=[part, part, weight, weight, sums, sums, angle, angle],
            out_specs=[sums, sums],
        ),
        out_shape=[jax.ShapeDtypeStruct((rows, cols), BF)] * 2,
        compiler_params=params(10),
        name="project_far",
    )(place, top, bottom, key_weight, value_weight, key_sum, value_sum, cosine, sine)


def attend(table, queries, query_peer, upstream, upstream_peer, pieces):
    groups = queries.shape[1] // (2 * HD)
    width = groups * HD
    lanes = groups * BLOCK

    def body(t, q_own, q_far, u_own, u_far, *refs):
        parts = refs[:16]
        k_outs = refs[17:21]
        v_outs = refs[21:25]
        out = refs[16]
        kv, total, q_rows, u_rows = refs[25:]
        step = pl.program_id(0)

        @pl.when(step == 0)
        def _():
            for s in range(STACK):
                for index in range(16):

                    @pl.when(t[s] == index)
                    def _(s=s, index=index):
                        kv[s] = parts[index][t[AT_PLACE + s]]

            for r in range(4):
                kv[STACK + r] = parts[r if r < 2 else 6 + r][0]
            total[...] = jnp.zeros(total.shape, F32)

        own = step < 2
        q = jnp.where(own, q_own[...], q_far[...])
        u = jnp.where(own, u_own[...], u_far[...])
        for h in range(groups):
            q_rows[h * BLOCK : (h + 1) * BLOCK] = q[:, h * HD : (h + 1) * HD]
            u_rows[h * BLOCK : (h + 1) * BLOCK] = u[:, h * HD : (h + 1) * HD]
        q = q_rows[...]
        u = u_rows[...]
        depth = t[AT_DEPTH + step]
        slots = [t[AT_SLOT + step * DEPTH + d] for d in range(DEPTH)]
        keys = jnp.concatenate([kv[s, :, :HD] for s in slots], axis=0)
        values = jnp.concatenate([kv[s, :, HD:] for s in slots], axis=0)
        ahead = lax.broadcasted_iota(jnp.int32, (BLOCK, lanes), 0) - (
            lax.broadcasted_iota(jnp.int32, (BLOCK, lanes), 1) % BLOCK
        )
        raw = nt(keys, q)
        scores = []
        peak = None
        for d in range(DEPTH):
            reach = jnp.where(d < depth, BLOCK, jnp.where(d == depth, 0, -BLOCK))
            tile = jnp.where(
                ahead <= reach, raw[d * BLOCK : (d + 1) * BLOCK] * SCALE, NEGATIVE
            )
            scores.append(tile)
            top = jnp.max(tile, axis=0, keepdims=True)
            peak = top if peak is None else jnp.maximum(peak, top)
        weights = [jnp.exp(tile - peak) for tile in scores]
        mass = None
        for w in weights:
            part = jnp.sum(w, axis=0, keepdims=True)
            mass = part if mass is None else mass + part
        rounded = jnp.concatenate([w.astype(BF) for w in weights], axis=0)
        mixed = (tn(values, rounded) / mass).astype(BF).astype(F32)
        delta = jnp.sum(u.astype(F32).T * mixed, axis=0, keepdims=True)
        for h in range(groups):
            out[:, h * HD : (h + 1) * HD] = mixed[:, h * BLOCK : (h + 1) * BLOCK].T.astype(BF)
        inverse = 1.0 / mass
        slopes = nt(values, u)
        chances = []
        pulls = []
        for d in range(DEPTH):
            p = weights[d] * inverse
            chances.append(p.astype(BF))
            pulls.append((p * (slopes[d * BLOCK : (d + 1) * BLOCK] - delta)).astype(BF))
        chances = jnp.concatenate(chances, axis=0)
        pulls = jnp.concatenate(pulls, axis=0)
        turned = tn(keys, pulls) * SCALE
        for h in range(groups):
            out[:, width + h * HD : width + (h + 1) * HD] = (
                turned[:, h * BLOCK : (h + 1) * BLOCK].T.astype(BF)
            )
        v_part = nn(chances, u)
        k_part = nn(pulls, q) * SCALE
        for d in range(DEPTH):
            low = d * BLOCK
            total[slots[d], :, :HD] += k_part[low : low + BLOCK]
            total[slots[d], :, HD:] += v_part[low : low + BLOCK]

        @pl.when(step == 3)
        def _():
            for outer in range(4):

                def fill(i, carry, outer=outer):
                    k_slot = t[AT_DENSE + outer * 16 + i]
                    v_slot = t[AT_DENSE + (i // 4) * 16 + outer * 4 + i % 4]
                    k = total[k_slot, :, :HD]
                    v = total[v_slot, :, HD:]
                    k_outs[outer][i] = k.astype(k_outs[outer].dtype)
                    v_outs[outer][i] = v.astype(v_outs[outer].dtype)
                    return carry

                lax.fori_loop(0, 16, fill, 0)

    mine = pl.BlockSpec((BLOCK, width), lambda i, t: (jnp.minimum(i, 1), t[AT_CORE]))
    peer = pl.BlockSpec((BLOCK, width), lambda i, t: (jnp.maximum(i - 2, 0), 0))
    rows = pl.BlockSpec((BLOCK, 2 * width), lambda i, t: (i, 0))

    def full(shape):
        return pl.BlockSpec(
            shape, lambda i, t: (0,) * len(shape), pipeline_mode=pl.Buffered(1)
        )

    def held(shape):
        return pl.BlockSpec(shape, lambda i, t: (0,) * len(shape))

    wide = (16, BLOCK, HD)
    grads = [(wide, F32)] + [(wide, BF)] * 3
    return pl.pallas_call(
        body,
        grid_spec=pltpu.PrefetchScalarGridSpec(
            num_scalar_prefetch=1,
            grid=(4,),
            in_specs=[mine, peer, mine, peer] + [full(p.shape) for p in pieces],
            out_specs=[rows] + [held(s) for s, _ in grads + grads],
            scratch_shapes=[
                pltpu.VMEM((SLOTS, BLOCK, 2 * HD), BF),
                pltpu.VMEM((SLOTS + 1, BLOCK, 2 * HD), F32),
                pltpu.VMEM((lanes, HD), BF),
                pltpu.VMEM((lanes, HD), BF),
            ],
        ),
        out_shape=[jax.ShapeDtypeStruct((4 * BLOCK, 2 * width), BF)]
        + [jax.ShapeDtypeStruct(s, d) for s, d in grads + grads],
        compiler_params=params(36),
        name="attend",
    )(table, queries, query_peer, upstream, upstream_peer, *pieces)


def combine(sums):
    def body(*refs):
        for side_of in range(2):
            home, a, b, c = refs[4 * side_of : 4 * side_of + 4]
            outs = refs[8 + 4 * side_of : 12 + 4 * side_of]
            rows = outs[0].shape[0]
            for k in range(4):
                at = slice(k * rows, (k + 1) * rows)
                outs[k][...] = (
                    home[at] + a[at].astype(F32) + b[at].astype(F32) + c[at].astype(F32)
                )

    shape = sums[0].shape
    part = (shape[0] // 4,) + shape[1:]
    return pl.pallas_call(
        body,
        in_specs=[pl.BlockSpec(memory_space=pltpu.VMEM)] * 8,
        out_specs=[pl.BlockSpec(memory_space=pltpu.VMEM)] * 8,
        out_shape=[jax.ShapeDtypeStruct(part, F32)] * 8,
        compiler_params=params(12),
        name="combine",
    )(*sums)


def finish_grads(sums, cosine, sine):
    rows = 4 * BLOCK

    def body(*refs):
        ks, vs = refs[:4], refs[4:8]
        cs, sn, every, away = refs[8:]
        key = (ks[0][...] + ks[1][...] + ks[2][...] + ks[3][...]).reshape(rows, HD)
        value = (vs[0][...] + vs[1][...] + vs[2][...] + vs[3][...]).reshape(rows, HD)
        key = key * cs[...] - pltpu.roll(key, HD // 2, 1) * sn[...]
        both = jnp.concatenate([key.astype(BF), value.astype(BF)], axis=1)
        every[...] = both
        away[...] = both[rows // 2 :]

    return pl.pallas_call(
        body,
        in_specs=[pl.BlockSpec(memory_space=pltpu.VMEM)] * 10,
        out_specs=[pl.BlockSpec(memory_space=pltpu.VMEM)] * 2,
        out_shape=[
            jax.ShapeDtypeStruct((rows, 2 * HD), BF),
            jax.ShapeDtypeStruct((rows // 2, 2 * HD), BF),
        ],
        compiler_params=params(8),
        name="finish_grads",
    )(*sums, cosine, sine)


def finish_weights(sums):
    share = sums[0].shape[1]

    def body(*refs):
        ks, vs = refs[:4], refs[4:8]
        for row, out in enumerate(refs[8:]):
            out[:, :HD] = ks[0][row] + ks[1][row] + ks[2][row] + ks[3][row]
            out[:, HD:] = vs[0][row] + vs[1][row] + vs[2][row] + vs[3][row]

    return pl.pallas_call(
        body,
        in_specs=[pl.BlockSpec(memory_space=pltpu.VMEM)] * 8,
        out_specs=[pl.BlockSpec(memory_space=pltpu.VMEM)] * 2,
        out_shape=[jax.ShapeDtypeStruct((share, 2 * HD), F32)] * 2,
        compiler_params=params(6),
        name="finish_weights",
    )(*sums)


def input_partials(place, mine, other, key_weight, value_weight):
    rows = other.shape[0]
    cols = key_weight.shape[1]
    width = key_weight.shape[0] // 4

    def body(p, a, b, kw, vw, *outs):
        swap = p[4] == 1
        first = jnp.where(swap, b[...], a[...])
        second = jnp.where(swap, a[...], b[...])
        key = jnp.concatenate([first[:, :HD], second[:, :HD]], axis=1)
        value = jnp.concatenate([first[:, HD:], second[:, HD:]], axis=1)
        result = (nt(key, kw[...]) + nt(value, vw[...])).astype(BF)
        for k in range(4):

            @pl.when(pl.program_id(0) == k)
            def _(k=k):
                outs[k][...] = result

    grads = pl.BlockSpec((rows, 2 * HD), lambda i, p: (0, 0))
    weight = pl.BlockSpec((width, cols), lambda i, p: (p[5 + i], 0))
    out = pl.BlockSpec((rows, width), lambda i, p: (0, 0))
    return pl.pallas_call(
        body,
        grid_spec=pltpu.PrefetchScalarGridSpec(
            num_scalar_prefetch=1,
            grid=(4,),
            in_specs=[grads, grads, weight, weight],
            out_specs=[out] * 4,
        ),
        out_shape=[jax.ShapeDtypeStruct((rows, width), BF)] * 4,
        compiler_params=params(10),
        name="input_partials",
    )(place, mine, other, key_weight, value_weight)


def weight_partials(place, grads, own, peer):
    width = own[0].shape[1]
    share = width // 8

    def body(p, g, *refs):
        mine, other = refs[:7], refs[7:14]
        k_outs, v_outs, result = refs[14:18], refs[18:22], refs[22]
        core = p[4]
        grad = g[...]
        for piece in range(4):
            at = slice(max(2 * piece - 1, 0), 2 * piece + 1)
            rows = mine[at] + other[at]
            features = jnp.concatenate([r[...] for r in rows], axis=0)
            result[...] = tn(features, grad)
            line = p[9 + piece]
            for dx in range(4):
                base = p[13 + dx] * (2 * share)
                for r in range(2):
                    start = pl.multiple_of(base + ((core + r) % 2) * share, 16)
                    value = result[pl.ds(start, share), :]
                    k_outs[dx][line * 2 + r] = value[:, :HD].astype(k_outs[dx].dtype)
                    for dy in range(4):

                        @pl.when(line == dy)
                        def _(dy=dy, dx=dx, r=r, value=value):
                            v_outs[dy][dx * 2 + r] = value[:, HD:].astype(v_outs[dy].dtype)

    wide = (8, share, HD)
    shapes = [(wide, F32)] + [(wide, BF)] * 3
    return pl.pallas_call(
        body,
        in_specs=[pl.BlockSpec(memory_space=pltpu.SMEM)]
        + [pl.BlockSpec(memory_space=pltpu.VMEM)] * 15,
        out_specs=[pl.BlockSpec(memory_space=pltpu.VMEM)] * 8,
        out_shape=[jax.ShapeDtypeStruct(s, d) for s, d in shapes + shapes],
        scratch_shapes=[pltpu.VMEM((width, 2 * HD), F32)],
        compiler_params=params(16),
        name="weight_partials",
    )(place, grads, *own, *peer)


def mover(axis, pairs):
    return lambda value: lax.ppermute(value, axis, pairs)


def ring_gather(first, second, ahead, behind):
    back_first = ahead(first)
    next_second = behind(second)
    back_second = ahead(second)
    next_first = behind(first)
    far_first = ahead(back_first)
    far_second = behind(next_second)
    return [
        first,
        second,
        back_first,
        back_second,
        next_first,
        next_second,
        far_first,
        far_second,
    ]


def send_all(values, ahead, behind, across):
    home, back, forth, far = values
    near = ahead(forth)
    distant = across(far)
    other = behind(back)
    return [home, near, other, distant]


def program(hidden, queries, key_weight, value_weight, parents, upstream):
    place_ctx = lax.axis_index("ctx")
    tp = lax.axis_index("tp")
    core = place_ctx % 2
    x = (place_ctx // 2) % 4
    y = place_ctx // 8
    xn = mover("ctx", [(i, i // 8 * 8 + (i + 2) % 8) for i in range(32)])
    xb = mover("ctx", [(i, i // 8 * 8 + (i - 2) % 8) for i in range(32)])
    yn = mover("ctx", [(i, (i + 8) % 32) for i in range(32)])
    yb = mover("ctx", [(i, (i - 8) % 32) for i in range(32)])
    swap = mover("ctx", [(i, i ^ 1) for i in range(32)])
    zn = mover("tp", [(i, (i + 1) % 4) for i in range(4)])
    zb = mover("tp", [(i, (i - 1) % 4) for i in range(4)])
    x2 = mover("ctx", [(i, i // 8 * 8 + (i + 4) % 8) for i in range(32)])
    y2 = mover("ctx", [(i, (i + 16) % 32) for i in range(32)])
    z2 = mover("tp", [(i, (i + 2) % 4) for i in range(4)])

    local_rows = hidden.shape[0]
    half_rows = local_rows // 2
    table, place, depths = device_tables(
        parents, jnp.stack([y, x, core, tp]).astype(jnp.int32)
    )
    cosine, sine = rope_tables(depths)

    width = queries.shape[1] // 2
    top = hidden[:half_rows]
    low = hidden[half_rows:]
    left_top = zn(top)
    right_low = zb(low)
    left_low = zn(low)
    right_top = zb(top)
    far_top = zn(left_top)
    far_low = zb(right_low)
    query_peer = swap(lax.dynamic_slice_in_dim(queries, (1 - core) * width, width, 1))
    upstream_peer = swap(lax.dynamic_slice_in_dim(upstream, (1 - core) * width, width, 1))
    hidden_peer = swap(hidden)
    place, hidden_peer, query_peer, upstream_peer = lax.optimization_barrier(
        (place, hidden_peer, query_peer, upstream_peer)
    )
    key_sum, value_sum = project_near(
        place, hidden, left_top, left_low, right_top, right_low, key_weight, value_weight
    )
    keep, send = project_far(
        place, far_top, far_low, key_weight, value_weight, key_sum, value_sum, cosine, sine
    )
    other = swap(send)
    mine_line = pack(keep, xn(keep), xb(keep), x2(keep))
    other_line = pack(other, yn(other), yb(other), y2(other))
    pieces = ring_gather(*mine_line, yn, yb) + ring_gather(*other_line, xn, xb)

    near_features = [left_top, left_low, right_top, right_low, far_top, far_low]
    own_features = [hidden, *near_features]
    peer_features = [hidden_peer] + [swap(f) for f in near_features]
    pieces, peer_features = lax.optimization_barrier((pieces, peer_features))

    out, *slot_grads = attend(table, queries, query_peer, upstream, upstream_peer, pieces)
    sums = combine(
        send_all(slot_grads[:4], xn, xb, x2) + send_all(slot_grads[4:], yn, yb, y2)
    )
    grads, grads_away = finish_grads(
        send_all(sums[:4], yn, yb, y2) + send_all(sums[4:], xn, xb, x2), cosine, sine
    )
    grads_other = swap(grads_away)
    grads, grads_other = lax.optimization_barrier((grads, grads_other))

    out_other = swap(out[local_rows:])

    def assemble(a, b):
        first = jnp.where(core == 0, a, b)
        second = jnp.where(core == 0, b, a)
        return jnp.concatenate([first, second], axis=1)

    attention = assemble(out[:local_rows, :width], out_other[:, :width])
    query_grad = assemble(out[:local_rows, width:], out_other[:, width:])

    w_parts = weight_partials(place, grads, own_features, peer_features)
    w_sent = send_all(w_parts[:4], xn, xb, x2) + send_all(w_parts[4:], yn, yb, y2)
    parts = input_partials(place, grads, grads_other, key_weight, value_weight)
    _, from_back, from_next, from_far = send_all(parts, zn, zb, z2)
    hidden_grad = (
        parts[0].astype(F32)
        + from_back.astype(F32)
        + from_next.astype(F32)
        + from_far.astype(F32)
    ).astype(BF)
    w_sums = combine(w_sent)
    both, both_away = finish_weights(
        send_all(w_sums[:4], yn, yb, y2) + send_all(w_sums[4:], xn, xb, x2)
    )
    both_other = swap(both_away)
    key_weight_grad, value_weight_grad = join_weights(place, both, both_other)
    return (attention, query_grad, hidden_grad, key_weight_grad, value_weight_grad)


def solution(mesh):
    return jax.shard_map(
        program,
        mesh=mesh,
        in_specs=(
            P("ctx", "tp"),
            P("ctx", "tp"),
            P(None, "tp"),
            P(None, "tp"),
            P(),
            P("ctx", "tp"),
        ),
        out_specs=(P("ctx", "tp"), P("ctx", "tp"), P("ctx", "tp"), P("ctx", "tp"), P("ctx", "tp")),
        check_vma=False,
    )
```

profile of v0, /device:TPU:6, one launch (start us, length us, event | category | flops | bytes accessed | tf_op | source)
XLA Modules:
  0.0 233.7 jit_solution(692567551063647098)
XLA Ops:
  0.7 2.0 fusion.1
  2.7 1.9 collective-permute-start.7
  4.6 2.1 collective-permute-start.5
  8.0 2.0 constant_dynamic-slice_fusion.1
  10.6 2.6 %device_tables.1 = (s32[115]{0:T(128)}, s32[17]{0:T(128)}, s32[4]{0:T(128)}) custom-call(s32[64]{0:T(128)} %links.1, s32[4]{0:T(128)} %pad_add_fusion.where), custom_call_target="tpu_custom_call" | custom-call | tf_op jit(solution)/shard_map/device_tables/pallas_call | solution.py:89
  13.8 2.0 collective-permute-start.8
  16.2 3.1 %collective-permute-start.6 = (bf16[128,1280]{1,0:T(8,128)(2,1)}, bf16[128,1280]{1,0:T(8,128)(2,1)S(1)}, u32[]{:S(2)}, u32[]{:S(2)}) collective-permute-start(bf16[128,1280]{1,0:T(8,128)(2,1)} %collective-permute-done.5.cl.refs_4_), channel_id=1, source_target_pairs={{0,3},{1,0},{2,1},{3,2},{4,7},{5,4},{6,5},{7,6},{8,11},{9,8},{10,9... | collective-permute-start | bytes 983048 | tf_op jit(solution)/shard_map/ppermute | solution.py:532
  19.3 5.3 %collective-permute-done.8.ct.refs_3_ = bf16[128,1280]{1,0:T(8,128)(2,1)S(1)} collective-permute-done((bf16[128,1280]{1,0:T(8,128)(2,1)}, bf16[128,1280]{1,0:T(8,128)(2,1)S(1)}, u32[]{:S(2)}, u32[]{:S(2)}) %collective-permute-start.8) | collective-permute-done | bytes 327712 | tf_op jit(solution)/shard_map/ppermute | solution.py:532
  24.6 2.5 %collective-permute-done.3.bt.refs_1_ = bf16[128,1280]{1,0:T(8,128)(2,1)S(1)} collective-permute-done((bf16[128,1280]{1,0:T(8,128)(2,1)}, bf16[128,1280]{1,0:T(8,128)(2,1)S(1)}, u32[]{:S(2)}, u32[]{:S(2)}) %collective-permute-start.3) | collective-permute-done | bytes 327712 | tf_op jit(solution)/shard_map/ppermute | solution.py:532
  27.1 1.0 fusion
  28.4 1.7 copy-done.1
  30.1 2.8 %project_near.1 = (f32[256,256]{1,0:T(8,128)S(1)}, f32[256,256]{1,0:T(8,128)S(1)}) custom-call(s32[17]{0:T(128)S(1)} %copy-done.19, bf16[256,1280]{1,0:T(8,128)(2,1)S(1)} %copy-done.3, bf16[128,1280]{1,0:T(8,128)(2,1)S(1)} %collective-permute-done.3.bt.refs_1_, bf16[128,1280]{1,0:T(8,128)(2,1)} %collective-permute-done.7.bl.refs_2_, ...), custom_call_target="tpu_custom_call" | custom-call | tf_op jit(solution)/shard_map/project_near/pallas_call | solution.py:152
  32.9 5.6 %collective-permute-done.4.a.refs_5_ = bf16[128,1280]{1,0:T(8,128)(2,1)S(1)} collective-permute-done((bf16[128,1280]{1,0:T(8,128)(2,1)S(1)}, bf16[128,1280]{1,0:T(8,128)(2,1)S(1)}, u32[]{:S(2)}, u32[]{:S(2)}) %collective-permute-start.4) | collective-permute-done | bytes 327712 | tf_op jit(solution)/shard_map/ppermute | solution.py:532
  38.5 1.1 project_far.1
  39.7 1.5 collective-permute-start.11
  41.2 3.2 %collective-permute-start.9 = (bf16[256,256]{1,0:T(8,128)(2,1)S(1)}, bf16[256,256]{1,0:T(8,128)(2,1)S(1)}, u32[]{:S(2)}, u32[]{:S(2)}) collective-permute-start(bf16[256,256]{1,0:T(8,128)(2,1)S(1)} %get-tuple-element.96.a), channel_id=1, source_target_pairs={{0,8},{4,12},{8,16},{12,20},{16,24},{20,28},{24,0},{28,4},{32,40},... | collective-permute-start | bytes 393224 | tf_op jit(solution)/shard_map/ppermute | solution.py:532
  44.4 3.2 %collective-permute-start.21 = (bf16[256,256]{1,0:T(8,128)(2,1)S(1)}, bf16[256,256]{1,0:T(8,128)(2,1)S(1)}, u32[]{:S(2)}, u32[]{:S(2)}) collective-permute-start(bf16[256,256]{1,0:T(8,128)(2,1)S(1)} %collective-permute-done.18.a), channel_id=1, source_target_pairs={{0,64},{4,68},{8,72},{12,76},{16,80},{20,84},{24,88},{28,92},{32,9... | collective-permute-start | bytes 393224 | tf_op jit(solution)/shard_map/ppermute | solution.py:532
  47.6 1.1 collective-permute-start.20
  50.4 1.0 collective-permute-done.21.d
  51.5 2.6 %collective-permute-done.20.c = bf16[256,256]{1,0:T(8,128)(2,1)S(1)} collective-permute-done((bf16[256,256]{1,0:T(8,128)(2,1)S(1)}, bf16[256,256]{1,0:T(8,128)(2,1)S(1)}, u32[]{:S(2)}, u32[]{:S(2)}) %collective-permute-start.20) | collective-permute-done | bytes 131104 | tf_op jit(solution)/shard_map/ppermute | solution.py:532
  54.1 2.7 %collective-permute-start.14 = (bf16[4,128,256]{2,1,0:T(8,128)(2,1)S(1)}, bf16[4,128,256]{2,1,0:T(8,128)(2,1)S(1)}, u32[]{:S(2)}, u32[]{:S(2)}) collective-permute-start(bf16[4,128,256]{2,1,0:T(8,128)(2,1)S(1)} %get-tuple-element.103.refs_0_), channel_id=1, source_target_pairs={{0,96},{4,100},{8,104},{12,108},{16,112},{20,116},{24,120},{28,124... | collective-permute-start | bytes 786440 | tf_op jit(solution)/shard_map/ppermute | solution.py:532
  56.8 3.3 %collective-permute-start.15 = (bf16[4,128,256]{2,1,0:T(8,128)(2,1)S(1)}, bf16[4,128,256]{2,1,0:T(8,128)(2,1)S(1)}, u32[]{:S(2)}, u32[]{:S(2)}) collective-permute-start(bf16[4,128,256]{2,1,0:T(8,128)(2,1)S(1)} %get-tuple-element.104.refs_1_), channel_id=1, source_target_pairs={{0,96},{4,100},{8,104},{12,108},{16,112},{20,116},{24,120},{28,124... | collective-permute-start | bytes 786440 | tf_op jit(solution)/shard_map/ppermute | solution.py:532
  60.4 3.1 %collective-permute-done.14.refs_4_ = bf16[4,128,256]{2,1,0:T(8,128)(2,1)S(1)} collective-permute-done((bf16[4,128,256]{2,1,0:T(8,128)(2,1)S(1)}, bf16[4,128,256]{2,1,0:T(8,128)(2,1)S(1)}, u32[]{:S(2)}, u32[]{:S(2)}) %collective-permute-start.14) | collective-permute-done | bytes 262176 | tf_op jit(solution)/shard_map/ppermute | solution.py:532
  64.3 2.8 %collective-permute-done.12.refs_2_ = bf16[4,128,256]{2,1,0:T(8,128)(2,1)S(1)} collective-permute-done((bf16[4,128,256]{2,1,0:T(8,128)(2,1)S(1)}, bf16[4,128,256]{2,1,0:T(8,128)(2,1)S(1)}, u32[]{:S(2)}, u32[]{:S(2)}) %collective-permute-start.12) | collective-permute-done | bytes 262176 | tf_op jit(solution)/shard_map/ppermute | solution.py:532
  67.7 2.6 %collective-permute-start.23 = (bf16[4,128,256]{2,1,0:T(8,128)(2,1)S(1)}, bf16[4,128,256]{2,1,0:T(8,128)(2,1)S(1)}, u32[]{:S(2)}, u32[]{:S(2)}) collective-permute-start(bf16[4,128,256]{2,1,0:T(8,128)(2,1)S(1)} %get-tuple-element.112.refs_9_), channel_id=1, source_target_pairs={{0,8},{4,12},{8,16},{12,20},{16,24},{20,28},{24,0},{28,4},{32,40},... | collective-permute-start | bytes 786440 | tf_op jit(solution)/shard_map/ppermute | solution.py:532
  71.2 3.2 %collective-permute-start.17 = (bf16[4,128,256]{2,1,0:T(8,128)(2,1)S(1)}, bf16[4,128,256]{2,1,0:T(8,128)(2,1)S(1)}, u32[]{:S(2)}, u32[]{:S(2)}) collective-permute-start(bf16[4,128,256]{2,1,0:T(8,128)(2,1)S(1)} %collective-permute-done.15.refs_5_), channel_id=1, source_target_pairs={{0,96},{4,100},{8,104},{12,108},{16,112},{20,116},{24,120},{28,124... | collective-permute-start | bytes 786440 | tf_op jit(solution)/shard_map/ppermute | solution.py:532
  75.3 1.1 collective-permute-start.27
  76.4 2.7 %collective-permute-done.16.refs_6_ = bf16[4,128,256]{2,1,0:T(8,128)(2,1)S(1)} collective-permute-done((bf16[4,128,256]{2,1,0:T(8,128)(2,1)S(1)}, bf16[4,128,256]{2,1,0:T(8,128)(2,1)S(1)}, u32[]{:S(2)}, u32[]{:S(2)}) %collective-permute-start.16) | collective-permute-done | bytes 262176 | tf_op jit(solution)/shard_map/ppermute | solution.py:532
  79.1 1.9 collective-permute-done.26.refs_14_
  81.0 1.8 collective-permute-done.27.refs_15_
  82.9 14.7 %attend.1 = (bf16[512,1280]{1,0:T(8,128)(2,1)S(1)}, f32[16,128,128]{2,1,0:T(8,128)S(1)}, bf16[16,128,128]{2,1,0:T(8,128)(2,1)S(1)}, bf16[16,128,128]{2,1,0:T(8,1...) custom-call(s32[115]{0:T(128)S(1)} %copy-done.20, ...), custom_call_target="tpu_custom_call" | custom-call | tf_op jit(solution)/shard_map/attend/pallas_call | solution.py:365
  98.3 1.3 collective-permute-start.36
  100.5 3.3 %collective-permute-start.39 = (bf16[16,128,128]{2,1,0:T(8,128)(2,1)S(1)}, bf16[16,128,128]{2,1,0:T(8,128)(2,1)S(1)}, u32[]{:S(2)}, u32[]{:S(2)}) collective-permute-start(bf16[16,128,128]{2,1,0:T(8,128)(2,1)S(1)} %get-tuple-element.126), channel_id=1, source_target_pairs={{0,96},{4,100},{8,104},{12,108},{16,112},{20,116},{24,120},{28,124... | collective-permute-start | bytes 1572872 | tf_op jit(solution)/shard_map/ppermute | solution.py:532
  103.9 15.1 %collective-permute-done.35.refs_1_ = bf16[16,128,128]{2,1,0:T(8,128)(2,1)S(1)} collective-permute-done((bf16[16,128,128]{2,1,0:T(8,128)(2,1)S(1)}, bf16[16,128,128]{2,1,0:T(8,128)(2,1)S(1)}, u32[]{:S(2)}, u32[]{:S(2)}) %collective-permute-start.35) | collective-permute-done | bytes 524320 | tf_op jit(solution)/shard_map/ppermute | solution.py:532
  118.9 2.5 %collective-permute-start.40 = (bf16[16,128,128]{2,1,0:T(8,128)(2,1)S(1)}, bf16[16,128,128]{2,1,0:T(8,128)(2,1)S(1)}, u32[]{:S(2)}, u32[]{:S(2)}) collective-permute-start(bf16[16,128,128]{2,1,0:T(8,128)(2,1)S(1)} %get-tuple-element.127), channel_id=1, source_target_pairs={{0,64},{4,68},{8,72},{12,76},{16,80},{20,84},{24,88},{28,92},{32,9... | collective-permute-start | bytes 1572872 | tf_op jit(solution)/shard_map/ppermute | solution.py:532
  122.3 11.3 %collective-permute-done.40.refs_7_ = bf16[16,128,128]{2,1,0:T(8,128)(2,1)S(1)} collective-permute-done((bf16[16,128,128]{2,1,0:T(8,128)(2,1)S(1)}, bf16[16,128,128]{2,1,0:T(8,128)(2,1)S(1)}, u32[]{:S(2)}, u32[]{:S(2)}) %collective-permute-start.40) | collective-permute-done | bytes 524320 | tf_op jit(solution)/shard_map/ppermute | solution.py:532
  134.1 2.6 %collective-permute-start.41 = (f32[4,128,128]{2,1,0:T(8,128)S(1)}, f32[4,128,128]{2,1,0:T(8,128)S(1)}, u32[]{:S(2)}, u32[]{:S(2)}) collective-permute-start(f32[4,128,128]{2,1,0:T(8,128)S(1)} %get-tuple-element.129), channel_id=1, source_target_pairs={{0,32},{4,36},{8,40},{12,44},{16,48},{20,52},{24,56},{28,60},{32,6... | collective-permute-start | bytes 786440 | tf_op jit(solution)/shard_map/ppermute | solution.py:532
  136.7 2.7 %collective-permute-start.42 = (f32[4,128,128]{2,1,0:T(8,128)S(1)}, f32[4,128,128]{2,1,0:T(8,128)S(1)}, u32[]{:S(2)}, u32[]{:S(2)}) collective-permute-start(f32[4,128,128]{2,1,0:T(8,128)S(1)} %get-tuple-element.130), channel_id=1, source_target_pairs={{0,96},{4,100},{8,104},{12,108},{16,112},{20,116},{24,120},{28,124... | collective-permute-start | bytes 786440 | tf_op jit(solution)/shard_map/ppermute | solution.py:532
  139.4 1.4 collective-permute-start.43
  140.8 1.7 collective-permute-start.44
  143.9 2.2 collective-permute-done.42.refs_2_
  146.1 1.8 collective-permute-done.43.refs_3_
  147.9 4.9 %collective-permute-done.45.refs_6_ = f32[4,128,128]{2,1,0:T(8,128)S(1)} collective-permute-done((f32[4,128,128]{2,1,0:T(8,128)S(1)}, f32[4,128,128]{2,1,0:T(8,128)S(1)}, u32[]{:S(2)}, u32[]{:S(2)}) %collective-permute-start.45) | collective-permute-done | bytes 262176 | tf_op jit(solution)/shard_map/ppermute | solution.py:532
  153.3 1.3 collective-permute-done.47.b
  154.7 5.5 %weight_partials.1 = (f32[8,160,128]{2,1,0:T(8,128)S(1)}, bf16[8,160,128]{2,1,0:T(8,128)(2,1)S(1)}, bf16[8,160,128]{2,1,0:T(8,128)(2,1)S(1)}, bf16[8,160,128]{2,...) custom-call(s32[17]{0:T(128)S(1)} %copy-done.19, ...), custom_call_target="tpu_custom_call" | custom-call | tf_op jit(solution)/shard_map/weight_partials/pallas_call | solution.py:519
  160.2 1.1 collective-permute-start.51
  163.8 1.4 collective-permute-start.54
  165.2 5.6 %collective-permute-done.51.refs_1_ = bf16[8,160,128]{2,1,0:T(8,128)(2,1)S(1)} collective-permute-done((bf16[8,160,128]{2,1,0:T(8,128)(2,1)S(1)}, bf16[8,160,128]{2,1,0:T(8,128)(2,1)S(1)}, u32[]{:S(2)}, u32[]{:S(2)}) %collective-permute-start.51) | collective-permute-done | bytes 327712 | tf_op jit(solution)/shard_map/ppermute | solution.py:532
  170.9 1.9 collective-permute-start.55
  172.7 6.4 %collective-permute-done.52.refs_2_ = bf16[8,160,128]{2,1,0:T(8,128)(2,1)S(1)} collective-permute-done((bf16[8,160,128]{2,1,0:T(8,128)(2,1)S(1)}, bf16[8,160,128]{2,1,0:T(8,128)(2,1)S(1)}, u32[]{:S(2)}, u32[]{:S(2)}) %collective-permute-start.52) | collective-permute-done | bytes 327712 | tf_op jit(solution)/shard_map/ppermute | solution.py:532
  179.1 2.4 %collective-permute-start.56 = (bf16[8,160,128]{2,1,0:T(8,128)(2,1)S(1)}, bf16[8,160,128]{2,1,0:T(8,128)(2,1)S(1)}, u32[]{:S(2)}, u32[]{:S(2)}) collective-permute-start(bf16[8,160,128]{2,1,0:T(8,128)(2,1)S(1)} %get-tuple-element.158), channel_id=1, source_target_pairs={{0,64},{4,68},{8,72},{12,76},{16,80},{20,84},{24,88},{28,92},{32,9... | collective-permute-start | bytes 983048 | tf_op jit(solution)/shard_map/ppermute | solution.py:532
  181.5 7.7 %collective-permute-done.56.refs_7_ = bf16[8,160,128]{2,1,0:T(8,128)(2,1)S(1)} collective-permute-done((bf16[8,160,128]{2,1,0:T(8,128)(2,1)S(1)}, bf16[8,160,128]{2,1,0:T(8,128)(2,1)S(1)}, u32[]{:S(2)}, u32[]{:S(2)}) %collective-permute-start.56) | collective-permute-done | bytes 327712 | tf_op jit(solution)/shard_map/ppermute | solution.py:532
  194.1 1.1 collective-permute-start.57
  195.1 2.2 collective-permute-start.58
  197.3 1.7 copy-done.2
  200.0 3.0 %input_partials.1 = (bf16[256,1280]{1,0:T(8,128)(2,1)S(1)}, bf16[256,1280]{1,0:T(8,128)(2,1)S(1)}, bf16[256,1280]{1,0:T(8,128)(2,1)S(1)}, bf16[256,1280]{1,0:T(8,128)(2,1)S(1)}) custom-call(s32[17]{0:T(128)S(1)} %copy-done.19, bf16[512,256]{1,0:T(8,128)(2,1)S(1)} %get-tuple-element.138.a.g, bf16[256,256]{1,0:T(8,128)(2,1)S(1)} %copy-done.18, ...), custom_call_target="tpu_custom_call" | custom-call | tf_op jit(solution)/shard_map/input_partials/pallas_call | solution.py:476
  203.1 3.2 %collective-permute-start.49 = (bf16[256,1280]{1,0:T(8,128)(2,1)S(1)}, bf16[256,1280]{1,0:T(8,128)(2,1)S(1)}, u32[]{:S(2)}, u32[]{:S(2)}) collective-permute-start(bf16[256,1280]{1,0:T(8,128)(2,1)S(1)} %get-tuple-element.142), channel_id=1, source_target_pairs={{0,3},{1,0},{2,1},{3,2},{4,7},{5,4},{6,5},{7,6},{8,11},{9,8},{10,9... | collective-permute-start | bytes 1966088 | tf_op jit(solution)/shard_map/ppermute | solution.py:532
  207.0 1.2 collective-permute-start.59
  208.9 1.2 broadcast_select_fusion.1
  210.2 3.6 %collective-permute-done.59.refs_3_ = f32[2,160,128]{2,1,0:T(8,128)S(1)} collective-permute-done((f32[2,160,128]{2,1,0:T(8,128)S(1)}, f32[2,160,128]{2,1,0:T(8,128)S(1)}, u32[]{:S(2)}, u32[]{:S(2)}) %collective-permute-start.59) | collective-permute-done | bytes 163872 | tf_op jit(solution)/shard_map/ppermute | solution.py:532
  215.2 6.9 %collective-permute-done.61.refs_6_ = f32[2,160,128]{2,1,0:T(8,128)S(1)} collective-permute-done((f32[2,160,128]{2,1,0:T(8,128)S(1)}, f32[2,160,128]{2,1,0:T(8,128)S(1)}, u32[]{:S(2)}, u32[]{:S(2)}) %collective-permute-start.61) | collective-permute-done | bytes 163872 | tf_op jit(solution)/shard_map/ppermute | solution.py:532
  223.7 1.3 join_weights.1
  225.0 7.6 %collective-permute-done.48 = bf16[256,1280]{1,0:T(8,128)(2,1)S(1)} collective-permute-done((bf16[256,1280]{1,0:T(8,128)(2,1)S(1)}, bf16[256,1280]{1,0:T(8,128)(2,1)S(1)}, u32[]{:S(2)}, u32[]{:S(2)}) %collective-permute-start.48) | collective-permute-done | bytes 655392 | tf_op jit(solution)/shard_map/ppermute | solution.py:532
  232.6 1.2 add_convert_fusion
  (149 shorter events, 26.0 us)
Async XLA Ops:
  2.7 13.5 %collective-permute-start.7 = (bf16[128,1280]{1,0:T(8,128)(2,1)}, bf16[128,1280]{1,0:T(8,128)(2,1)}, u32[]{:S(2)}, u32[]{:S(2)}) collective-permute-start(bf16[128,1280]{1,0:T(8,128)(2,1)} %get-tuple-element.175), channel_id=1, source_target_pairs={{0,1},{1,2},{2,3},{3,0},{4,5},{5,6},{6,7},{7,4},{8,9},{9,10},{10,1... | collective-permute-start | bytes 983048 | tf_op jit(solution)/shard_map/ppermute | solution.py:532
  4.6 11.3 %collective-permute-start.5 = (bf16[128,1280]{1,0:T(8,128)(2,1)}, bf16[128,1280]{1,0:T(8,128)(2,1)}, u32[]{:S(2)}, u32[]{:S(2)}) collective-permute-start(bf16[128,1280]{1,0:T(8,128)(2,1)} %get-tuple-element.175), channel_id=1, source_target_pairs={{0,3},{1,0},{2,1},{3,2},{4,7},{5,4},{6,5},{7,6},{8,11},{9,8},{10,9... | collective-permute-start | bytes 983048 | tf_op jit(solution)/shard_map/ppermute | solution.py:532
  6.7 20.4 %collective-permute-start = (bf16[256,1280]{1,0:T(8,128)(2,1)S(1)}, bf16[256,1280]{1,0:T(8,128)(2,1)}, u32[]{:S(2)}, u32[]{:S(2)}) collective-permute-start(bf16[256,1280]{1,0:T(8,128)(2,1)S(1)} %copy-done.3), channel_id=1, source_target_pairs={{0,4},{4,0},{8,12},{12,8},{16,20},{20,16},{24,28},{28,24},{32,36},... | collective-permute-start | bytes 1966088 | tf_op jit(solution)/shard_map/ppermute | solution.py:532
  7.5 6.3 %collective-permute-start.2 = (bf16[256,640]{1,0:T(8,128)(2,1)}, bf16[256,640]{1,0:T(8,128)(2,1)}, u32[]{:S(2)}, u32[]{:S(2)}) collective-permute-start(bf16[256,640]{1,0:T(8,128)(2,1)} %constant_dynamic-slice_fusion), channel_id=1, source_target_pairs={{0,4},{4,0},{8,12},{12,8},{16,20},{20,16},{24,28},{28,24},{32,36},... | collective-permute-start | bytes 983048 | tf_op jit(solution)/shard_map/ppermute | solution.py:532
  10.0 5.9 %collective-permute-start.1 = (bf16[256,640]{1,0:T(8,128)(2,1)}, bf16[256,640]{1,0:T(8,128)(2,1)}, u32[]{:S(2)}, u32[]{:S(2)}) collective-permute-start(bf16[256,640]{1,0:T(8,128)(2,1)} %constant_dynamic-slice_fusion.1), channel_id=1, source_target_pairs={{0,4},{4,0},{8,12},{12,8},{16,20},{20,16},{24,28},{28,24},{32,36},... | collective-permute-start | bytes 983048 | tf_op jit(solution)/shard_map/ppermute | solution.py:532
  13.8 10.8 %collective-permute-start.8 = (bf16[128,1280]{1,0:T(8,128)(2,1)}, bf16[128,1280]{1,0:T(8,128)(2,1)S(1)}, u32[]{:S(2)}, u32[]{:S(2)}) collective-permute-start(bf16[128,1280]{1,0:T(8,128)(2,1)} %get-tuple-element.176), channel_id=1, source_target_pairs={{0,3},{1,0},{2,1},{3,2},{4,7},{5,4},{6,5},{7,6},{8,11},{9,8},{10,9... | collective-permute-start | bytes 983048 | tf_op jit(solution)/shard_map/ppermute | solution.py:532
  15.8 11.3 %collective-permute-start.3 = (bf16[128,1280]{1,0:T(8,128)(2,1)}, bf16[128,1280]{1,0:T(8,128)(2,1)S(1)}, u32[]{:S(2)}, u32[]{:S(2)}) collective-permute-start(bf16[128,1280]{1,0:T(8,128)(2,1)} %get-tuple-element.176), channel_id=1, source_target_pairs={{0,1},{1,2},{2,3},{3,0},{4,5},{5,6},{6,7},{7,4},{8,9},{9,10},{10,1... | collective-permute-start | bytes 983048 | tf_op jit(solution)/shard_map/ppermute | solution.py:532
  15.9 25.3 %collective-permute-start.31 = (bf16[128,1280]{1,0:T(8,128)(2,1)}, bf16[128,1280]{1,0:T(8,128)(2,1)S(1)}, u32[]{:S(2)}, u32[]{:S(2)}) collective-permute-start(bf16[128,1280]{1,0:T(8,128)(2,1)} %collective-permute-done.5.cl.refs_4_), channel_id=1, source_target_pairs={{0,4},{4,0},{8,12},{12,8},{16,20},{20,16},{24,28},{28,24},{32,36},... | collective-permute-start | bytes 983048 | tf_op jit(solution)/shard_map/ppermute | solution.py:532
  16.2 16.7 %collective-permute-start.6 = (bf16[128,1280]{1,0:T(8,128)(2,1)}, bf16[128,1280]{1,0:T(8,128)(2,1)S(1)}, u32[]{:S(2)}, u32[]{:S(2)}) collective-permute-start(bf16[128,1280]{1,0:T(8,128)(2,1)} %collective-permute-done.5.cl.refs_4_), channel_id=1, source_target_pairs={{0,3},{1,0},{2,1},{3,2},{4,7},{5,4},{6,5},{7,6},{8,11},{9,8},{10,9... | collective-permute-start | bytes 983048 | tf_op jit(solution)/shard_map/ppermute | solution.py:532
  24.6 16.6 %collective-permute-start.29 = (bf16[128,1280]{1,0:T(8,128)(2,1)}, bf16[128,1280]{1,0:T(8,128)(2,1)S(1)}, u32[]{:S(2)}, u32[]{:S(2)}) collective-permute-start(bf16[128,1280]{1,0:T(8,128)(2,1)} %collective-permute-done.7.bl.refs_2_), channel_id=1, source_target_pairs={{0,4},{4,0},{8,12},{12,8},{16,20},{20,16},{24,28},{28,24},{32,36},... | collective-permute-start | bytes 983048 | tf_op jit(solution)/shard_map/ppermute | solution.py:532
  27.1 20.5 %collective-permute-start.30 = (bf16[128,1280]{1,0:T(8,128)(2,1)S(1)}, bf16[128,1280]{1,0:T(8,128)(2,1)S(1)}, u32[]{:S(2)}, u32[]{:S(2)}) collective-permute-start(bf16[128,1280]{1,0:T(8,128)(2,1)S(1)} %collective-permute-done.8.ct.refs_3_), channel_id=1, source_target_pairs={{0,4},{4,0},{8,12},{12,8},{16,20},{20,16},{24,28},{28,24},{32,36},... | collective-permute-start | bytes 983048 | tf_op jit(solution)/shard_map/ppermute | solution.py:532
  27.1 11.3 %collective-permute-start.4 = (bf16[128,1280]{1,0:T(8,128)(2,1)S(1)}, bf16[128,1280]{1,0:T(8,128)(2,1)S(1)}, u32[]{:S(2)}, u32[]{:S(2)}) collective-permute-start(bf16[128,1280]{1,0:T(8,128)(2,1)S(1)} %collective-permute-done.3.bt.refs_1_), channel_id=1, source_target_pairs={{0,1},{1,2},{2,3},{3,0},{4,5},{5,6},{6,7},{7,4},{8,9},{9,10},{10,1... | collective-permute-start | bytes 983048 | tf_op jit(solution)/shard_map/ppermute | solution.py:532
  39.6 4.8 %collective-permute-start.18 = (bf16[256,256]{1,0:T(8,128)(2,1)S(1)}, bf16[256,256]{1,0:T(8,128)(2,1)S(1)}, u32[]{:S(2)}, u32[]{:S(2)}) collective-permute-start(bf16[256,256]{1,0:T(8,128)(2,1)S(1)} %get-tuple-element.99), channel_id=1, source_target_pairs={{0,4},{4,0},{8,12},{12,8},{16,20},{20,16},{24,28},{28,24},{32,36},... | collective-permute-start | bytes 393224 | tf_op jit(solution)/shard_map/ppermute | solution.py:532
  39.7 9.0 %collective-permute-start.11 = (bf16[256,256]{1,0:T(8,128)(2,1)S(1)}, bf16[256,256]{1,0:T(8,128)(2,1)S(1)}, u32[]{:S(2)}, u32[]{:S(2)}) collective-permute-start(bf16[256,256]{1,0:T(8,128)(2,1)S(1)} %get-tuple-element.96.a), channel_id=1, source_target_pairs={{0,16},{4,20},{8,24},{12,28},{16,0},{20,4},{24,8},{28,12},{32,48},... | collective-permute-start | bytes 393224 | tf_op jit(solution)/shard_map/ppermute | solution.py:532
  41.2 8.7 %collective-permute-start.10 = (bf16[256,256]{1,0:T(8,128)(2,1)S(1)}, bf16[256,256]{1,0:T(8,128)(2,1)S(1)}, u32[]{:S(2)}, u32[]{:S(2)}) collective-permute-start(bf16[256,256]{1,0:T(8,128)(2,1)S(1)} %get-tuple-element.96.a), channel_id=1, source_target_pairs={{0,24},{4,28},{8,0},{12,4},{16,8},{20,12},{24,16},{28,20},{32,56},... | collective-permute-start | bytes 393224 | tf_op jit(solution)/shard_map/ppermute | solution.py:532
  41.2 8.8 %collective-permute-start.9 = (bf16[256,256]{1,0:T(8,128)(2,1)S(1)}, bf16[256,256]{1,0:T(8,128)(2,1)S(1)}, u32[]{:S(2)}, u32[]{:S(2)}) collective-permute-start(bf16[256,256]{1,0:T(8,128)(2,1)S(1)} %get-tuple-element.96.a), channel_id=1, source_target_pairs={{0,8},{4,12},{8,16},{12,20},{16,24},{20,28},{24,0},{28,4},{32,40},... | collective-permute-start | bytes 393224 | tf_op jit(solution)/shard_map/ppermute | solution.py:532
  44.4 7.0 %collective-permute-start.21 = (bf16[256,256]{1,0:T(8,128)(2,1)S(1)}, bf16[256,256]{1,0:T(8,128)(2,1)S(1)}, u32[]{:S(2)}, u32[]{:S(2)}) collective-permute-start(bf16[256,256]{1,0:T(8,128)(2,1)S(1)} %collective-permute-done.18.a), channel_id=1, source_target_pairs={{0,64},{4,68},{8,72},{12,76},{16,80},{20,84},{24,88},{28,92},{32,9... | collective-permute-start | bytes 393224 | tf_op jit(solution)/shard_map/ppermute | solution.py:532
  47.6 6.4 %collective-permute-start.20 = (bf16[256,256]{1,0:T(8,128)(2,1)S(1)}, bf16[256,256]{1,0:T(8,128)(2,1)S(1)}, u32[]{:S(2)}, u32[]{:S(2)}) collective-permute-start(bf16[256,256]{1,0:T(8,128)(2,1)S(1)} %collective-permute-done.18.a), channel_id=1, source_target_pairs={{0,96},{4,100},{8,104},{12,108},{16,112},{20,116},{24,120},{28,124... | collective-permute-start | bytes 393224 | tf_op jit(solution)/shard_map/ppermute | solution.py:532
  48.7 8.1 %collective-permute-start.19 = (bf16[256,256]{1,0:T(8,128)(2,1)S(1)}, bf16[256,256]{1,0:T(8,128)(2,1)S(1)}, u32[]{:S(2)}, u32[]{:S(2)}) collective-permute-start(bf16[256,256]{1,0:T(8,128)(2,1)S(1)} %collective-permute-done.18.a), channel_id=1, source_target_pairs={{0,32},{4,36},{8,40},{12,44},{16,48},{20,52},{24,56},{28,60},{32,6... | collective-permute-start | bytes 393224 | tf_op jit(solution)/shard_map/ppermute | solution.py:532
  49.9 6.9 %collective-permute-start.28 = (bf16[128,1280]{1,0:T(8,128)(2,1)S(1)}, bf16[128,1280]{1,0:T(8,128)(2,1)S(1)}, u32[]{:S(2)}, u32[]{:S(2)}) collective-permute-start(bf16[128,1280]{1,0:T(8,128)(2,1)S(1)} %collective-permute-done.3.bt.refs_1_), channel_id=1, source_target_pairs={{0,4},{4,0},{8,12},{12,8},{16,20},{20,16},{24,28},{28,24},{32,36},... | collective-permute-start | bytes 983048 | tf_op jit(solution)/shard_map/ppermute | solution.py:532
  49.9 10.2 %collective-permute-start.33 = (bf16[128,1280]{1,0:T(8,128)(2,1)S(1)}, bf16[128,1280]{1,0:T(8,128)(2,1)S(1)}, u32[]{:S(2)}, u32[]{:S(2)}) collective-permute-start(bf16[128,1280]{1,0:T(8,128)(2,1)S(1)} %collective-permute-done.6.b.refs_6_), channel_id=1, source_target_pairs={{0,4},{4,0},{8,12},{12,8},{16,20},{20,16},{24,28},{28,24},{32,36},... | collective-permute-start | bytes 983048 | tf_op jit(solution)/shard_map/ppermute | solution.py:532
  51.5 8.6 %collective-permute-start.32 = (bf16[128,1280]{1,0:T(8,128)(2,1)S(1)}, bf16[128,1280]{1,0:T(8,128)(2,1)S(1)}, u32[]{:S(2)}, u32[]{:S(2)}) collective-permute-start(bf16[128,1280]{1,0:T(8,128)(2,1)S(1)} %collective-permute-done.4.a.refs_5_), channel_id=1, source_target_pairs={{0,4},{4,0},{8,12},{12,8},{16,20},{20,16},{24,28},{28,24},{32,36},... | collective-permute-start | bytes 983048 | tf_op jit(solution)/shard_map/ppermute | solution.py:532
  54.1 9.4 %collective-permute-start.14 = (bf16[4,128,256]{2,1,0:T(8,128)(2,1)S(1)}, bf16[4,128,256]{2,1,0:T(8,128)(2,1)S(1)}, u32[]{:S(2)}, u32[]{:S(2)}) collective-permute-start(bf16[4,128,256]{2,1,0:T(8,128)(2,1)S(1)} %get-tuple-element.103.refs_0_), channel_id=1, source_target_pairs={{0,96},{4,100},{8,104},{12,108},{16,112},{20,116},{24,120},{28,124... | collective-permute-start | bytes 786440 | tf_op jit(solution)/shard_map/ppermute | solution.py:532
  56.7 10.4 %collective-permute-start.12 = (bf16[4,128,256]{2,1,0:T(8,128)(2,1)S(1)}, bf16[4,128,256]{2,1,0:T(8,128)(2,1)S(1)}, u32[]{:S(2)}, u32[]{:S(2)}) collective-permute-start(bf16[4,128,256]{2,1,0:T(8,128)(2,1)S(1)} %get-tuple-element.103.refs_0_), channel_id=1, source_target_pairs={{0,32},{4,36},{8,40},{12,44},{16,48},{20,52},{24,56},{28,60},{32,6... | collective-permute-start | bytes 786440 | tf_op jit(solution)/shard_map/ppermute | solution.py:532
  56.8 10.9 %collective-permute-start.15 = (bf16[4,128,256]{2,1,0:T(8,128)(2,1)S(1)}, bf16[4,128,256]{2,1,0:T(8,128)(2,1)S(1)}, u32[]{:S(2)}, u32[]{:S(2)}) collective-permute-start(bf16[4,128,256]{2,1,0:T(8,128)(2,1)S(1)} %get-tuple-element.104.refs_1_), channel_id=1, source_target_pairs={{0,96},{4,100},{8,104},{12,108},{16,112},{20,116},{24,120},{28,124... | collective-permute-start | bytes 786440 | tf_op jit(solution)/shard_map/ppermute | solution.py:532
  60.1 11.1 %collective-permute-start.13 = (bf16[4,128,256]{2,1,0:T(8,128)(2,1)S(1)}, bf16[4,128,256]{2,1,0:T(8,128)(2,1)S(1)}, u32[]{:S(2)}, u32[]{:S(2)}) collective-permute-start(bf16[4,128,256]{2,1,0:T(8,128)(2,1)S(1)} %get-tuple-element.104.refs_1_), channel_id=1, source_target_pairs={{0,32},{4,36},{8,40},{12,44},{16,48},{20,52},{24,56},{28,60},{32,6... | collective-permute-start | bytes 786440 | tf_op jit(solution)/shard_map/ppermute | solution.py:532
  60.1 11.1 %collective-permute-start.24 = (bf16[4,128,256]{2,1,0:T(8,128)(2,1)S(1)}, bf16[4,128,256]{2,1,0:T(8,128)(2,1)S(1)}, u32[]{:S(2)}, u32[]{:S(2)}) collective-permute-start(bf16[4,128,256]{2,1,0:T(8,128)(2,1)S(1)} %get-tuple-element.111.refs_8_), channel_id=1, source_target_pairs={{0,24},{4,28},{8,0},{12,4},{16,8},{20,12},{24,16},{28,20},{32,56},... | collective-permute-start | bytes 786440 | tf_op jit(solution)/shard_map/ppermute | solution.py:532
  63.4 11.0 %collective-permute-start.22 = (bf16[4,128,256]{2,1,0:T(8,128)(2,1)S(1)}, bf16[4,128,256]{2,1,0:T(8,128)(2,1)S(1)}, u32[]{:S(2)}, u32[]{:S(2)}) collective-permute-start(bf16[4,128,256]{2,1,0:T(8,128)(2,1)S(1)} %get-tuple-element.111.refs_8_), channel_id=1, source_target_pairs={{0,8},{4,12},{8,16},{12,20},{16,24},{20,28},{24,0},{28,4},{32,40},... | collective-permute-start | bytes 786440 | tf_op jit(solution)/shard_map/ppermute | solution.py:532
  67.1 8.2 %collective-permute-start.25 = (bf16[4,128,256]{2,1,0:T(8,128)(2,1)S(1)}, bf16[4,128,256]{2,1,0:T(8,128)(2,1)S(1)}, u32[]{:S(2)}, u32[]{:S(2)}) collective-permute-start(bf16[4,128,256]{2,1,0:T(8,128)(2,1)S(1)} %get-tuple-element.112.refs_9_), channel_id=1, source_target_pairs={{0,24},{4,28},{8,0},{12,4},{16,8},{20,12},{24,16},{28,20},{32,56},... | collective-permute-start | bytes 786440 | tf_op jit(solution)/shard_map/ppermute | solution.py:532
  67.7 8.7 %collective-permute-start.23 = (bf16[4,128,256]{2,1,0:T(8,128)(2,1)S(1)}, bf16[4,128,256]{2,1,0:T(8,128)(2,1)S(1)}, u32[]{:S(2)}, u32[]{:S(2)}) collective-permute-start(bf16[4,128,256]{2,1,0:T(8,128)(2,1)S(1)} %get-tuple-element.112.refs_9_), channel_id=1, source_target_pairs={{0,8},{4,12},{8,16},{12,20},{16,24},{20,28},{24,0},{28,4},{32,40},... | collective-permute-start | bytes 786440 | tf_op jit(solution)/shard_map/ppermute | solution.py:532
  71.2 7.9 %collective-permute-start.16 = (bf16[4,128,256]{2,1,0:T(8,128)(2,1)S(1)}, bf16[4,128,256]{2,1,0:T(8,128)(2,1)S(1)}, u32[]{:S(2)}, u32[]{:S(2)}) collective-permute-start(bf16[4,128,256]{2,1,0:T(8,128)(2,1)S(1)} %collective-permute-done.12.refs_2_), channel_id=1, source_target_pairs={{0,32},{4,36},{8,40},{12,44},{16,48},{20,52},{24,56},{28,60},{32,6... | collective-permute-start | bytes 786440 | tf_op jit(solution)/shard_map/ppermute | solution.py:532
  71.2 7.9 %collective-permute-start.17 = (bf16[4,128,256]{2,1,0:T(8,128)(2,1)S(1)}, bf16[4,128,256]{2,1,0:T(8,128)(2,1)S(1)}, u32[]{:S(2)}, u32[]{:S(2)}) collective-permute-start(bf16[4,128,256]{2,1,0:T(8,128)(2,1)S(1)} %collective-permute-done.15.refs_5_), channel_id=1, source_target_pairs={{0,96},{4,100},{8,104},{12,108},{16,112},{20,116},{24,120},{28,124... | collective-permute-start | bytes 786440 | tf_op jit(solution)/shard_map/ppermute | solution.py:532
  74.4 6.6 %collective-permute-start.26 = (bf16[4,128,256]{2,1,0:T(8,128)(2,1)S(1)}, bf16[4,128,256]{2,1,0:T(8,128)(2,1)S(1)}, u32[]{:S(2)}, u32[]{:S(2)}) collective-permute-start(bf16[4,128,256]{2,1,0:T(8,128)(2,1)S(1)} %collective-permute-done.22.refs_10_), channel_id=1, source_target_pairs={{0,8},{4,12},{8,16},{12,20},{16,24},{20,28},{24,0},{28,4},{32,40},... | collective-permute-start | bytes 786440 | tf_op jit(solution)/shard_map/ppermute | solution.py:532
  75.3 7.6 %collective-permute-start.27 = (bf16[4,128,256]{2,1,0:T(8,128)(2,1)S(1)}, bf16[4,128,256]{2,1,0:T(8,128)(2,1)S(1)}, u32[]{:S(2)}, u32[]{:S(2)}) collective-permute-start(bf16[4,128,256]{2,1,0:T(8,128)(2,1)S(1)} %collective-permute-done.25.refs_13_), channel_id=1, source_target_pairs={{0,24},{4,28},{8,0},{12,4},{16,8},{20,12},{24,16},{28,20},{32,56},... | collective-permute-start | bytes 786440 | tf_op jit(solution)/shard_map/ppermute | solution.py:532
  97.5 21.4 %collective-permute-start.35 = (bf16[16,128,128]{2,1,0:T(8,128)(2,1)S(1)}, bf16[16,128,128]{2,1,0:T(8,128)(2,1)S(1)}, u32[]{:S(2)}, u32[]{:S(2)}) collective-permute-start(bf16[16,128,128]{2,1,0:T(8,128)(2,1)S(1)} %get-tuple-element.121), channel_id=1, source_target_pairs={{0,8},{4,12},{8,16},{12,20},{16,24},{20,28},{24,0},{28,4},{32,40},... | collective-permute-start | bytes 1572872 | tf_op jit(solution)/shard_map/ppermute | solution.py:532
  98.3 24.0 %collective-permute-start.36 = (bf16[16,128,128]{2,1,0:T(8,128)(2,1)S(1)}, bf16[16,128,128]{2,1,0:T(8,128)(2,1)S(1)}, u32[]{:S(2)}, u32[]{:S(2)}) collective-permute-start(bf16[16,128,128]{2,1,0:T(8,128)(2,1)S(1)} %get-tuple-element.122), channel_id=1, source_target_pairs={{0,24},{4,28},{8,0},{12,4},{16,8},{20,12},{24,16},{28,20},{32,56},... | collective-permute-start | bytes 1572872 | tf_op jit(solution)/shard_map/ppermute | solution.py:532
  99.6 22.7 %collective-permute-start.37 = (bf16[16,128,128]{2,1,0:T(8,128)(2,1)S(1)}, bf16[16,128,128]{2,1,0:T(8,128)(2,1)S(1)}, u32[]{:S(2)}, u32[]{:S(2)}) collective-permute-start(bf16[16,128,128]{2,1,0:T(8,128)(2,1)S(1)} %get-tuple-element.123), channel_id=1, source_target_pairs={{0,16},{4,20},{8,24},{12,28},{16,0},{20,4},{24,8},{28,12},{32,48},... | collective-permute-start | bytes 1572872 | tf_op jit(solution)/shard_map/ppermute | solution.py:532
  100.3 22.0 %collective-permute-start.38 = (bf16[16,128,128]{2,1,0:T(8,128)(2,1)S(1)}, bf16[16,128,128]{2,1,0:T(8,128)(2,1)S(1)}, u32[]{:S(2)}, u32[]{:S(2)}) collective-permute-start(bf16[16,128,128]{2,1,0:T(8,128)(2,1)S(1)} %get-tuple-element.125), channel_id=1, source_target_pairs={{0,32},{4,36},{8,40},{12,44},{16,48},{20,52},{24,56},{28,60},{32,6... | collective-permute-start | bytes 1572872 | tf_op jit(solution)/shard_map/ppermute | solution.py:532
  100.5 21.8 %collective-permute-start.39 = (bf16[16,128,128]{2,1,0:T(8,128)(2,1)S(1)}, bf16[16,128,128]{2,1,0:T(8,128)(2,1)S(1)}, u32[]{:S(2)}, u32[]{:S(2)}) collective-permute-start(bf16[16,128,128]{2,1,0:T(8,128)(2,1)S(1)} %get-tuple-element.126), channel_id=1, source_target_pairs={{0,96},{4,100},{8,104},{12,108},{16,112},{20,116},{24,120},{28,124... | collective-permute-start | bytes 1572872 | tf_op jit(solution)/shard_map/ppermute | solution.py:532
  118.9 14.7 %collective-permute-start.40 = (bf16[16,128,128]{2,1,0:T(8,128)(2,1)S(1)}, bf16[16,128,128]{2,1,0:T(8,128)(2,1)S(1)}, u32[]{:S(2)}, u32[]{:S(2)}) collective-permute-start(bf16[16,128,128]{2,1,0:T(8,128)(2,1)S(1)} %get-tuple-element.127), channel_id=1, source_target_pairs={{0,64},{4,68},{8,72},{12,76},{16,80},{20,84},{24,88},{28,92},{32,9... | collective-permute-start | bytes 1572872 | tf_op jit(solution)/shard_map/ppermute | solution.py:532
  134.1 9.6 %collective-permute-start.41 = (f32[4,128,128]{2,1,0:T(8,128)S(1)}, f32[4,128,128]{2,1,0:T(8,128)S(1)}, u32[]{:S(2)}, u32[]{:S(2)}) collective-permute-start(f32[4,128,128]{2,1,0:T(8,128)S(1)} %get-tuple-element.129), channel_id=1, source_target_pairs={{0,32},{4,36},{8,40},{12,44},{16,48},{20,52},{24,56},{28,60},{32,6... | collective-permute-start | bytes 786440 | tf_op jit(solution)/shard_map/ppermute | solution.py:532
  136.7 9.4 %collective-permute-start.42 = (f32[4,128,128]{2,1,0:T(8,128)S(1)}, f32[4,128,128]{2,1,0:T(8,128)S(1)}, u32[]{:S(2)}, u32[]{:S(2)}) collective-permute-start(f32[4,128,128]{2,1,0:T(8,128)S(1)} %get-tuple-element.130), channel_id=1, source_target_pairs={{0,96},{4,100},{8,104},{12,108},{16,112},{20,116},{24,120},{28,124... | collective-permute-start | bytes 786440 | tf_op jit(solution)/shard_map/ppermute | solution.py:532
  139.4 8.5 %collective-permute-start.43 = (f32[4,128,128]{2,1,0:T(8,128)S(1)}, f32[4,128,128]{2,1,0:T(8,128)S(1)}, u32[]{:S(2)}, u32[]{:S(2)}) collective-permute-start(f32[4,128,128]{2,1,0:T(8,128)S(1)} %get-tuple-element.131), channel_id=1, source_target_pairs={{0,64},{4,68},{8,72},{12,76},{16,80},{20,84},{24,88},{28,92},{32,9... | collective-permute-start | bytes 786440 | tf_op jit(solution)/shard_map/ppermute | solution.py:532
  140.8 7.2 %collective-permute-start.44 = (f32[4,128,128]{2,1,0:T(8,128)S(1)}, f32[4,128,128]{2,1,0:T(8,128)S(1)}, u32[]{:S(2)}, u32[]{:S(2)}) collective-permute-start(f32[4,128,128]{2,1,0:T(8,128)S(1)} %get-tuple-element.133), channel_id=1, source_target_pairs={{0,8},{4,12},{8,16},{12,20},{16,24},{20,28},{24,0},{28,4},{32,40},... | collective-permute-start | bytes 786440 | tf_op jit(solution)/shard_map/ppermute | solution.py:532
  142.5 10.4 %collective-permute-start.45 = (f32[4,128,128]{2,1,0:T(8,128)S(1)}, f32[4,128,128]{2,1,0:T(8,128)S(1)}, u32[]{:S(2)}, u32[]{:S(2)}) collective-permute-start(f32[4,128,128]{2,1,0:T(8,128)S(1)} %get-tuple-element.134), channel_id=1, source_target_pairs={{0,24},{4,28},{8,0},{12,4},{16,8},{20,12},{24,16},{28,20},{32,56},... | collective-permute-start | bytes 786440 | tf_op jit(solution)/shard_map/ppermute | solution.py:532
  143.6 9.2 %collective-permute-start.46 = (f32[4,128,128]{2,1,0:T(8,128)S(1)}, f32[4,128,128]{2,1,0:T(8,128)S(1)}, u32[]{:S(2)}, u32[]{:S(2)}) collective-permute-start(f32[4,128,128]{2,1,0:T(8,128)S(1)} %get-tuple-element.135), channel_id=1, source_target_pairs={{0,16},{4,20},{8,24},{12,28},{16,0},{20,4},{24,8},{28,12},{32,48},... | collective-permute-start | bytes 786440 | tf_op jit(solution)/shard_map/ppermute | solution.py:532
  153.0 1.6 collective-permute-start.47
  160.2 10.7 %collective-permute-start.51 = (bf16[8,160,128]{2,1,0:T(8,128)(2,1)S(1)}, bf16[8,160,128]{2,1,0:T(8,128)(2,1)S(1)}, u32[]{:S(2)}, u32[]{:S(2)}) collective-permute-start(bf16[8,160,128]{2,1,0:T(8,128)(2,1)S(1)} %get-tuple-element.152), channel_id=1, source_target_pairs={{0,8},{4,12},{8,16},{12,20},{16,24},{20,28},{24,0},{28,4},{32,40},... | collective-permute-start | bytes 983048 | tf_op jit(solution)/shard_map/ppermute | solution.py:532
  161.4 17.7 %collective-permute-start.52 = (bf16[8,160,128]{2,1,0:T(8,128)(2,1)S(1)}, bf16[8,160,128]{2,1,0:T(8,128)(2,1)S(1)}, u32[]{:S(2)}, u32[]{:S(2)}) collective-permute-start(bf16[8,160,128]{2,1,0:T(8,128)(2,1)S(1)} %get-tuple-element.153), channel_id=1, source_target_pairs={{0,24},{4,28},{8,0},{12,4},{16,8},{20,12},{24,16},{28,20},{32,56},... | collective-permute-start | bytes 983048 | tf_op jit(solution)/shard_map/ppermute | solution.py:532
  163.2 43.1 %collective-permute-start.34 = (bf16[256,1280]{1,0:T(8,128)(2,1)}, bf16[256,1280]{1,0:T(8,128)(2,1)}, u32[]{:S(2)}, u32[]{:S(2)}) collective-permute-start(bf16[256,1280]{1,0:T(8,128)(2,1)} %slice.24), channel_id=1, source_target_pairs={{0,4},{4,0},{8,12},{12,8},{16,20},{20,16},{24,28},{28,24},{32,36},... | collective-permute-start | bytes 1966088 | tf_op jit(solution)/shard_map/ppermute | solution.py:532
  163.2 18.3 %collective-permute-start.53 = (bf16[8,160,128]{2,1,0:T(8,128)(2,1)S(1)}, bf16[8,160,128]{2,1,0:T(8,128)(2,1)S(1)}, u32[]{:S(2)}, u32[]{:S(2)}) collective-permute-start(bf16[8,160,128]{2,1,0:T(8,128)(2,1)S(1)} %get-tuple-element.154), channel_id=1, source_target_pairs={{0,16},{4,20},{8,24},{12,28},{16,0},{20,4},{24,8},{28,12},{32,48},... | collective-permute-start | bytes 983048 | tf_op jit(solution)/shard_map/ppermute | solution.py:532
  163.8 17.7 %collective-permute-start.54 = (bf16[8,160,128]{2,1,0:T(8,128)(2,1)S(1)}, bf16[8,160,128]{2,1,0:T(8,128)(2,1)S(1)}, u32[]{:S(2)}, u32[]{:S(2)}) collective-permute-start(bf16[8,160,128]{2,1,0:T(8,128)(2,1)S(1)} %get-tuple-element.156), channel_id=1, source_target_pairs={{0,32},{4,36},{8,40},{12,44},{16,48},{20,52},{24,56},{28,60},{32,6... | collective-permute-start | bytes 983048 | tf_op jit(solution)/shard_map/ppermute | solution.py:532
  170.9 10.6 %collective-permute-start.55 = (bf16[8,160,128]{2,1,0:T(8,128)(2,1)S(1)}, bf16[8,160,128]{2,1,0:T(8,128)(2,1)S(1)}, u32[]{:S(2)}, u32[]{:S(2)}) collective-permute-start(bf16[8,160,128]{2,1,0:T(8,128)(2,1)S(1)} %get-tuple-element.157), channel_id=1, source_target_pairs={{0,96},{4,100},{8,104},{12,108},{16,112},{20,116},{24,120},{28,124... | collective-permute-start | bytes 983048 | tf_op jit(solution)/shard_map/ppermute | solution.py:532
  179.1 10.1 %collective-permute-start.56 = (bf16[8,160,128]{2,1,0:T(8,128)(2,1)S(1)}, bf16[8,160,128]{2,1,0:T(8,128)(2,1)S(1)}, u32[]{:S(2)}, u32[]{:S(2)}) collective-permute-start(bf16[8,160,128]{2,1,0:T(8,128)(2,1)S(1)} %get-tuple-element.158), channel_id=1, source_target_pairs={{0,64},{4,68},{8,72},{12,76},{16,80},{20,84},{24,88},{28,92},{32,9... | collective-permute-start | bytes 983048 | tf_op jit(solution)/shard_map/ppermute | solution.py:532
  194.1 12.2 %collective-permute-start.57 = (f32[2,160,128]{2,1,0:T(8,128)}, f32[2,160,128]{2,1,0:T(8,128)S(1)}, u32[]{:S(2)}, u32[]{:S(2)}) collective-permute-start(f32[2,160,128]{2,1,0:T(8,128)} %get-tuple-element.160), channel_id=1, source_target_pairs={{0,32},{4,36},{8,40},{12,44},{16,48},{20,52},{24,56},{28,60},{32,6... | collective-permute-start | bytes 491528 | tf_op jit(solution)/shard_map/ppermute | solution.py:532
  195.1 13.1 %collective-permute-start.58 = (f32[2,160,128]{2,1,0:T(8,128)}, f32[2,160,128]{2,1,0:T(8,128)S(1)}, u32[]{:S(2)}, u32[]{:S(2)}) collective-permute-start(f32[2,160,128]{2,1,0:T(8,128)} %get-tuple-element.161), channel_id=1, source_target_pairs={{0,96},{4,100},{8,104},{12,108},{16,112},{20,116},{24,120},{28,124... | collective-permute-start | bytes 491528 | tf_op jit(solution)/shard_map/ppermute | solution.py:532
  203.0 29.6 %collective-permute-start.48 = (bf16[256,1280]{1,0:T(8,128)(2,1)S(1)}, bf16[256,1280]{1,0:T(8,128)(2,1)S(1)}, u32[]{:S(2)}, u32[]{:S(2)}) collective-permute-start(bf16[256,1280]{1,0:T(8,128)(2,1)S(1)} %get-tuple-element.141), channel_id=1, source_target_pairs={{0,1},{1,2},{2,3},{3,0},{4,5},{5,6},{6,7},{7,4},{8,9},{9,10},{10,1... | collective-permute-start | bytes 1966088 | tf_op jit(solution)/shard_map/ppermute | solution.py:532
  203.1 29.5 %collective-permute-start.49 = (bf16[256,1280]{1,0:T(8,128)(2,1)S(1)}, bf16[256,1280]{1,0:T(8,128)(2,1)S(1)}, u32[]{:S(2)}, u32[]{:S(2)}) collective-permute-start(bf16[256,1280]{1,0:T(8,128)(2,1)S(1)} %get-tuple-element.142), channel_id=1, source_target_pairs={{0,3},{1,0},{2,1},{3,2},{4,7},{5,4},{6,5},{7,6},{8,11},{9,8},{10,9... | collective-permute-start | bytes 1966088 | tf_op jit(solution)/shard_map/ppermute | solution.py:532
  206.3 26.3 %collective-permute-start.50 = (bf16[256,1280]{1,0:T(8,128)(2,1)S(1)}, bf16[256,1280]{1,0:T(8,128)(2,1)S(1)}, u32[]{:S(2)}, u32[]{:S(2)}) collective-permute-start(bf16[256,1280]{1,0:T(8,128)(2,1)S(1)} %get-tuple-element.143), channel_id=1, source_target_pairs={{0,2},{1,3},{2,0},{3,1},{4,6},{5,7},{6,4},{7,5},{8,10},{9,11},{10,... | collective-permute-start | bytes 1966088 | tf_op jit(solution)/shard_map/ppermute | solution.py:532
  207.0 6.8 %collective-permute-start.59 = (f32[2,160,128]{2,1,0:T(8,128)S(1)}, f32[2,160,128]{2,1,0:T(8,128)S(1)}, u32[]{:S(2)}, u32[]{:S(2)}) collective-permute-start(f32[2,160,128]{2,1,0:T(8,128)S(1)} %copy-done.28), channel_id=1, source_target_pairs={{0,64},{4,68},{8,72},{12,76},{16,80},{20,84},{24,88},{28,92},{32,9... | collective-permute-start | bytes 491528 | tf_op jit(solution)/shard_map/ppermute | solution.py:532
  208.9 5.4 %collective-permute-start.60 = (f32[2,160,128]{2,1,0:T(8,128)S(1)}, f32[2,160,128]{2,1,0:T(8,128)S(1)}, u32[]{:S(2)}, u32[]{:S(2)}) collective-permute-start(f32[2,160,128]{2,1,0:T(8,128)S(1)} %copy-done.26), channel_id=1, source_target_pairs={{0,8},{4,12},{8,16},{12,20},{16,24},{20,28},{24,0},{28,4},{32,40},... | collective-permute-start | bytes 491528 | tf_op jit(solution)/shard_map/ppermute | solution.py:532
  213.8 8.3 %collective-permute-start.61 = (f32[2,160,128]{2,1,0:T(8,128)S(1)}, f32[2,160,128]{2,1,0:T(8,128)S(1)}, u32[]{:S(2)}, u32[]{:S(2)}) collective-permute-start(f32[2,160,128]{2,1,0:T(8,128)S(1)} %copy-done.24), channel_id=1, source_target_pairs={{0,24},{4,28},{8,0},{12,4},{16,8},{20,12},{24,16},{28,20},{32,56},... | collective-permute-start | bytes 491528 | tf_op jit(solution)/shard_map/ppermute | solution.py:532
  214.3 7.8 %collective-permute-start.62 = (f32[2,160,128]{2,1,0:T(8,128)S(1)}, f32[2,160,128]{2,1,0:T(8,128)S(1)}, u32[]{:S(2)}, u32[]{:S(2)}) collective-permute-start(f32[2,160,128]{2,1,0:T(8,128)S(1)} %copy-done.22), channel_id=1, source_target_pairs={{0,16},{4,20},{8,24},{12,28},{16,0},{20,4},{24,8},{28,12},{32,48},... | collective-permute-start | bytes 491528 | tf_op jit(solution)/shard_map/ppermute | solution.py:532
  222.2 1.5 collective-permute-start.63
  (29 other events, 343.4 us)
where the time goes:
time: 234 us
  waiting for transfers between devices  108 us (46%)
  starting transfers between devices  69.8 us (30%)
  Pallas kernels  32.6 us (14%)
  local copies, waits for them, and re-layouts  15.4 us (7%)
  other arithmetic  6.69 us (3%)
    ppermute x64, waiting for transfers between devices, mover(): return lambda value: lax.ppermute(value, axis, pairs)  108 us
    ppermute x64, starting transfers between devices, mover(): return lambda value: lax.ppermute(value, axis, pairs)  69.8 us
    pallas_call x1, Pallas kernels, attend(): pl.pallas_call(body, grid_spec=pltpu.PrefetchScalarGridSpec(num_scalar_pr...  14.7 us
    unnamed x58, local copies, waits for them, and re-layouts  9.75 us
    pallas_call x1, Pallas kernels, weight_partials(): pl.pallas_call(body, in_specs=[pl.BlockSpec(memory_space=pltpu.SMEM)] + [...  5.53 us
  transfers between devices with their start and end apart: 64, of which 29 were waited for; matrix products, arithmetic and copies ran while one was open for 4% of the time, Pallas kernels for 5%

commit v1 on v0

--- a/solution.py
+++ b/solution.py
@@ -135,6 +135,30 @@
     return pltpu.CompilerParams(vmem_limit_bytes=mib * 1024 * 1024)
 
 
+def halve(value):
+    half = value.shape[0] // 2
+
+    def body(source, top, low, sems):
+        copies = [
+            pltpu.make_async_copy(source.at[pl.ds(k * half, half)], out, sems.at[k])
+            for k, out in enumerate((top, low))
+        ]
+        for copy in copies:
+            copy.start()
+        for copy in copies:
+            copy.wait()
+
+    anywhere = pl.BlockSpec(memory_space=pl.ANY)
+    return pl.pallas_call(
+        body,
+        in_specs=[anywhere],
+        out_specs=[anywhere] * 2,
+        out_shape=[jax.ShapeDtypeStruct((half, value.shape[1]), value.dtype)] * 2,
+        scratch_shapes=[pltpu.SemaphoreType.DMA((2,))],
+        name="halve",
+    )(value)
+
+
 def project_near(place, own, left_top, left_low, right_top, right_low, key_weight, value_weight):
     rows, width = own.shape
     cols = key_weight.shape[1]
@@ -183,7 +207,7 @@
         in_specs=[pl.BlockSpec(memory_space=pltpu.VMEM)] * 4,
         out_specs=[pl.BlockSpec(memory_space=pltpu.VMEM)] * 2,
         out_shape=[jax.ShapeDtypeStruct((4, BLOCK, 2 * HD), BF)] * 2,
-        compiler_params=params(6),
+        compiler_params=params(3),
         name="pack",
     )(own, back, forth, far)
 
@@ -206,7 +230,7 @@
         + [pl.BlockSpec(memory_space=pltpu.VMEM)] * 2,
         out_specs=[pl.BlockSpec(memory_space=pltpu.VMEM)] * 2,
         out_shape=[jax.ShapeDtypeStruct((share, 2 * HD), F32)] * 2,
-        compiler_params=params(6),
+        compiler_params=params(2),
         name="join_weights",
     )(place, mine, other)
 
@@ -244,7 +268,7 @@
             out_specs=[sums, sums],
         ),
         out_shape=[jax.ShapeDtypeStruct((rows, cols), BF)] * 2,
-        compiler_params=params(10),
+        compiler_params=params(8),
         name="project_far",
     )(place, top, bottom, key_weight, value_weight, key_sum, value_sum, cosine, sine)
 
@@ -402,7 +426,7 @@
         in_specs=[pl.BlockSpec(memory_space=pltpu.VMEM)] * 8,
         out_specs=[pl.BlockSpec(memory_space=pltpu.VMEM)] * 8,
         out_shape=[jax.ShapeDtypeStruct(part, F32)] * 8,
-        compiler_params=params(12),
+        compiler_params=params(8),
         name="combine",
     )(*sums)
 
@@ -428,7 +452,7 @@
             jax.ShapeDtypeStruct((rows, 2 * HD), BF),
             jax.ShapeDtypeStruct((rows // 2, 2 * HD), BF),
         ],
-        compiler_params=params(8),
+        compiler_params=params(5),
         name="finish_grads",
     )(*sums, cosine, sine)
 
@@ -447,7 +471,7 @@
         in_specs=[pl.BlockSpec(memory_space=pltpu.VMEM)] * 8,
         out_specs=[pl.BlockSpec(memory_space=pltpu.VMEM)] * 2,
         out_shape=[jax.ShapeDtypeStruct((share, 2 * HD), F32)] * 2,
-        compiler_params=params(6),
+        compiler_params=params(4),
         name="finish_weights",
     )(*sums)
 
@@ -472,7 +496,7 @@
 
     grads = pl.BlockSpec((rows, 2 * HD), lambda i, p: (0, 0))
     weight = pl.BlockSpec((width, cols), lambda i, p: (p[5 + i], 0))
-    out = pl.BlockSpec((rows, width), lambda i, p: (0, 0))
+    out = pl.BlockSpec((rows, width), lambda i, p: (0, 0), pipeline_mode=pl.Buffered(1))
     return pl.pallas_call(
         body,
         grid_spec=pltpu.PrefetchScalarGridSpec(
@@ -482,25 +506,42 @@
             out_specs=[out] * 4,
         ),
         out_shape=[jax.ShapeDtypeStruct((rows, width), BF)] * 4,
-        compiler_params=params(10),
+        compiler_params=params(7),
         name="input_partials",
     )(place, mine, other, key_weight, value_weight)
 
 
-def weight_partials(place, grads, own, peer):
+def flip(own, peer):
     width = own[0].shape[1]
+    rows = 4 * BLOCK
+
+    def body(*refs):
+        mine, other, outs = refs[:7], refs[7:14], refs[14:]
+        for piece in range(4):
+            at = slice(max(2 * piece - 1, 0), 2 * piece + 1)
+            features = jnp.concatenate([r[...] for r in mine[at] + other[at]], axis=0)
+            outs[piece][...] = features.T
+
+    return pl.pallas_call(
+        body,
+        in_specs=[pl.BlockSpec(memory_space=pltpu.VMEM)] * 14,
+        out_specs=[pl.BlockSpec(memory_space=pltpu.VMEM)] * 4,
+        out_shape=[jax.ShapeDtypeStruct((width, rows), BF)] * 4,
+        compiler_params=params(12),
+        name="flip",
+    )(*own, *peer)
+
+
+def weight_partials(place, grads, features):
+    width = features[0].shape[0]
     share = width // 8
 
     def body(p, g, *refs):
-        mine, other = refs[:7], refs[7:14]
-        k_outs, v_outs, result = refs[14:18], refs[18:22], refs[22]
+        k_outs, v_outs, result = refs[4:8], refs[8:12], refs[12]
         core = p[4]
         grad = g[...]
         for piece in range(4):
-            at = slice(max(2 * piece - 1, 0), 2 * piece + 1)
-            rows = mine[at] + other[at]
-            features = jnp.concatenate([r[...] for r in rows], axis=0)
-            result[...] = tn(features, grad)
+            result[...] = nn(refs[piece][...], grad)
             line = p[9 + piece]
             for dx in range(4):
                 base = p[13 + dx] * (2 * share)
@@ -519,13 +560,13 @@
     return pl.pallas_call(
         body,
         in_specs=[pl.BlockSpec(memory_space=pltpu.SMEM)]
-        + [pl.BlockSpec(memory_space=pltpu.VMEM)] * 15,
+        + [pl.BlockSpec(memory_space=pltpu.VMEM)] * 5,
         out_specs=[pl.BlockSpec(memory_space=pltpu.VMEM)] * 8,
         out_shape=[jax.ShapeDtypeStruct(s, d) for s, d in shapes + shapes],
         scratch_shapes=[pltpu.VMEM((width, 2 * HD), F32)],
-        compiler_params=params(16),
+        compiler_params=params(11),
         name="weight_partials",
-    )(place, grads, *own, *peer)
+    )(place, grads, *features)
 
 
 def mover(axis, pairs):
@@ -577,15 +618,13 @@
     z2 = mover("tp", [(i, (i + 2) % 4) for i in range(4)])
 
     local_rows = hidden.shape[0]
-    half_rows = local_rows // 2
     table, place, depths = device_tables(
         parents, jnp.stack([y, x, core, tp]).astype(jnp.int32)
     )
     cosine, sine = rope_tables(depths)
 
     width = queries.shape[1] // 2
-    top = hidden[:half_rows]
-    low = hidden[half_rows:]
+    top, low = halve(hidden)
     left_top = zn(top)
     right_low = zb(low)
     left_low = zn(low)
@@ -611,13 +650,13 @@
 
     near_features = [left_top, left_low, right_top, right_low, far_top, far_low]
     own_features = [hidden, *near_features]
-    peer_features = [hidden_peer] + [swap(f) for f in near_features]
-    pieces, peer_features = lax.optimization_barrier((pieces, peer_features))
+    peer_features = [hidden_peer]
+    for feature in near_features:
+        peer_features.append(swap(feature))
+    features = flip(own_features, peer_features)
 
     out, *slot_grads = attend(table, queries, query_peer, upstream, upstream_peer, pieces)
-    sums = combine(
-        send_all(slot_grads[:4], xn, xb, x2) + send_all(slot_grads[4:], yn, yb, y2)
-    )
+    sums = combine(send_all(slot_grads[:4], xn, xb, x2) + send_all(slot_grads[4:], yn, yb, y2))
     grads, grads_away = finish_grads(
         send_all(sums[:4], yn, yb, y2) + send_all(sums[4:], xn, xb, x2), cosine, sine
     )
@@ -634,7 +673,7 @@
     attention = assemble(out[:local_rows, :width], out_other[:, :width])
     query_grad = assemble(out[:local_rows, width:], out_other[:, width:])
 
-    w_parts = weight_partials(place, grads, own_features, peer_features)
+    w_parts = weight_partials(place, grads, features)
     w_sent = send_all(w_parts[:4], xn, xb, x2) + send_all(w_parts[4:], yn, yb, y2)
     parts = input_partials(place, grads, grads_other, key_weight, value_weight)
     _, from_back, from_next, from_far = send_all(parts, zn, zb, z2)

time: 234 us -> 254 us (1.085)
  the two profiles are of different devices: /device:TPU:6 before, /device:TPU:1 now
where the time goes in v1:
time: 254 us; the launch traced here: 250 us
  starting transfers between devices  112 us (44%)
  waiting for transfers between devices  61.9 us (24%)
  Pallas kernels  55.7 us (22%)
  local copies, waits for them, and re-layouts  12.6 us (5%)
  other arithmetic  6.81 us (3%)
    ppermute x64, starting transfers between devices, mover(): return lambda value: lax.ppermute(value, axis, pairs)  112 us
    ppermute x64, waiting for transfers between devices, mover(): return lambda value: lax.ppermute(value, axis, pairs)  61.9 us
    pallas_call x1, Pallas kernels, halve(): pl.pallas_call(body, in_specs=[anywhere], out_specs=[anywhere] * 2, out_s...  21 us
    pallas_call x1, Pallas kernels, attend(): pl.pallas_call(body, grid_spec=pltpu.PrefetchScalarGridSpec(num_scalar_pr...  14.9 us
    unnamed x44, local copies, waits for them, and re-layouts  8.16 us
  transfers between devices with their start and end apart: 64, of which 26 were waited for; matrix products, arithmetic and copies ran while one was open for 3% of the time, Pallas kernels for 14%

profile of v1, /device:TPU:1, one launch (start us, length us, event | category | flops | bytes accessed | tf_op | source)
XLA Modules:
  0.0 249.9 jit_solution(2013708293245895955)
XLA Ops:
  0.7 1.8 constant_dynamic-slice_fusion.1
  2.5 1.4 collective-permute-start.1
  3.8 1.7 constant_dynamic-slice_fusion
  6.1 21.0 %halve.1 = (bf16[128,1280]{1,0:T(8,128)(2,1)}, bf16[128,1280]{1,0:T(8,128)(2,1)}) custom-call(bf16[256,1280]{1,0:T(8,128)(2,1)} %refs_0_.1), custom_call_target="tpu_custom_call" | custom-call | tf_op jit(solution)/shard_map/halve/pallas_call | solution.py:152
  27.1 1.8 collective-permute-start.3
  28.9 2.2 collective-permute-start.5
  31.7 2.6 %device_tables.1 = (s32[115]{0:T(128)}, s32[17]{0:T(128)}, s32[4]{0:T(128)}) custom-call(s32[64]{0:T(128)} %links.1, s32[4]{0:T(128)} %pad_add_fusion.where), custom_call_target="tpu_custom_call" | custom-call | tf_op jit(solution)/shard_map/device_tables/pallas_call | solution.py:89
  35.1 2.7 %collective-permute-start.8 = (bf16[128,1280]{1,0:T(8,128)(2,1)}, bf16[128,1280]{1,0:T(8,128)(2,1)S(1)}, u32[]{:S(2)}, u32[]{:S(2)}) collective-permute-start(bf16[128,1280]{1,0:T(8,128)(2,1)} %get-tuple-element.76), channel_id=1, source_target_pairs={{0,3},{1,0},{2,1},{3,2},{4,7},{5,4},{6,5},{7,6},{8,11},{9,8},{10,9... | collective-permute-start | bytes 983048 | tf_op jit(solution)/shard_map/ppermute | solution.py:573
  37.8 1.5 collective-permute-done.3.bt.refs_1_
  39.3 2.7 %collective-permute-start.6 = (bf16[128,1280]{1,0:T(8,128)(2,1)}, bf16[128,1280]{1,0:T(8,128)(2,1)S(1)}, u32[]{:S(2)}, u32[]{:S(2)}) collective-permute-start(bf16[128,1280]{1,0:T(8,128)(2,1)} %collective-permute-done.5.cl.refs_4_), channel_id=1, source_target_pairs={{0,3},{1,0},{2,1},{3,2},{4,7},{5,4},{6,5},{7,6},{8,11},{9,8},{10,9... | collective-permute-start | bytes 983048 | tf_op jit(solution)/shard_map/ppermute | solution.py:573
  43.2 2.7 %collective-permute-done.7.bl.refs_2_ = bf16[128,1280]{1,0:T(8,128)(2,1)S(1)} collective-permute-done((bf16[128,1280]{1,0:T(8,128)(2,1)}, bf16[128,1280]{1,0:T(8,128)(2,1)S(1)}, u32[]{:S(2)}, u32[]{:S(2)}) %collective-permute-start.7) | collective-permute-done | bytes 327712 | tf_op jit(solution)/shard_map/ppermute | solution.py:573
  45.9 1.7 copy-done.1
  48.7 2.8 %project_near.1 = (f32[256,256]{1,0:T(8,128)S(1)}, f32[256,256]{1,0:T(8,128)S(1)}) custom-call(s32[17]{0:T(128)S(1)} %copy-done.12, bf16[256,1280]{1,0:T(8,128)(2,1)S(1)} %copy-done.4, bf16[128,1280]{1,0:T(8,128)(2,1)} %collective-permute-done.3.bt.refs_1_, bf16[128,1280]{1,0:T(8,128)(2,1)S(1)} %collective-permute-done.7.bl.refs_2_, ...), custom_call_target="tpu_custom_call" | custom-call | tf_op jit(solution)/shard_map/project_near/pallas_call | solution.py:176
  51.5 1.4 collective-permute-done.4.a.refs_5_
  54.1 2.5 %collective-permute-start.10 = (bf16[256,256]{1,0:T(8,128)(2,1)S(1)}, bf16[256,256]{1,0:T(8,128)(2,1)S(1)}, u32[]{:S(2)}, u32[]{:S(2)}) collective-permute-start(bf16[256,256]{1,0:T(8,128)(2,1)S(1)} %get-tuple-element.81.a), channel_id=1, source_target_pairs={{0,24},{4,28},{8,0},{12,4},{16,8},{20,12},{24,16},{28,20},{32,56},... | collective-permute-start | bytes 393224 | tf_op jit(solution)/shard_map/ppermute | solution.py:573
  57.7 1.8 collective-permute-start.18
  59.6 2.5 collective-permute-done.11.d
  62.0 3.8 %collective-permute-done.9.b = bf16[256,256]{1,0:T(8,128)(2,1)S(1)} collective-permute-done((bf16[256,256]{1,0:T(8,128)(2,1)S(1)}, bf16[256,256]{1,0:T(8,128)(2,1)S(1)}, u32[]{:S(2)}, u32[]{:S(2)}) %collective-permute-start.9) | collective-permute-done | bytes 131104 | tf_op jit(solution)/shard_map/ppermute | solution.py:573
  65.9 1.4 collective-permute-start.12
  67.3 1.5 collective-permute-start.15
  68.8 2.7 %collective-permute-start.20 = (bf16[256,256]{1,0:T(8,128)(2,1)S(1)}, bf16[256,256]{1,0:T(8,128)(2,1)S(1)}, u32[]{:S(2)}, u32[]{:S(2)}) collective-permute-start(bf16[256,256]{1,0:T(8,128)(2,1)S(1)} %collective-permute-done.18.a), channel_id=1, source_target_pairs={{0,96},{4,100},{8,104},{12,108},{16,112},{20,116},{24,120},{28,124... | collective-permute-start | bytes 393224 | tf_op jit(solution)/shard_map/ppermute | solution.py:573
  71.8 5.2 %collective-permute-done.19.b = bf16[256,256]{1,0:T(8,128)(2,1)S(1)} collective-permute-done((bf16[256,256]{1,0:T(8,128)(2,1)S(1)}, bf16[256,256]{1,0:T(8,128)(2,1)S(1)}, u32[]{:S(2)}, u32[]{:S(2)}) %collective-permute-start.19) | collective-permute-done | bytes 131104 | tf_op jit(solution)/shard_map/ppermute | solution.py:573
  77.0 3.0 %collective-permute-start.14 = (bf16[4,128,256]{2,1,0:T(8,128)(2,1)S(1)}, bf16[4,128,256]{2,1,0:T(8,128)(2,1)S(1)}, u32[]{:S(2)}, u32[]{:S(2)}) collective-permute-start(bf16[4,128,256]{2,1,0:T(8,128)(2,1)S(1)} %get-tuple-element.82.refs_0_), channel_id=1, source_target_pairs={{0,96},{4,100},{8,104},{12,108},{16,112},{20,116},{24,120},{28,124... | collective-permute-start | bytes 786440 | tf_op jit(solution)/shard_map/ppermute | solution.py:573
  80.8 2.7 %collective-permute-start.25 = (bf16[4,128,256]{2,1,0:T(8,128)(2,1)S(1)}, bf16[4,128,256]{2,1,0:T(8,128)(2,1)S(1)}, u32[]{:S(2)}, u32[]{:S(2)}) collective-permute-start(bf16[4,128,256]{2,1,0:T(8,128)(2,1)S(1)} %get-tuple-element.86.refs_9_), channel_id=1, source_target_pairs={{0,24},{4,28},{8,0},{12,4},{16,8},{20,12},{24,16},{28,20},{32,56},... | collective-permute-start | bytes 786440 | tf_op jit(solution)/shard_map/ppermute | solution.py:573
  83.4 3.2 %collective-permute-done.13.refs_3_ = bf16[4,128,256]{2,1,0:T(8,128)(2,1)S(1)} collective-permute-done((bf16[4,128,256]{2,1,0:T(8,128)(2,1)S(1)}, bf16[4,128,256]{2,1,0:T(8,128)(2,1)S(1)}, u32[]{:S(2)}, u32[]{:S(2)}) %collective-permute-start.13) | collective-permute-done | bytes 262176 | tf_op jit(solution)/shard_map/ppermute | solution.py:573
  87.5 1.9 collective-permute-start.17
  89.4 1.5 collective-permute-start.26
  92.1 2.8 %collective-permute-done.24.refs_12_ = bf16[4,128,256]{2,1,0:T(8,128)(2,1)S(1)} collective-permute-done((bf16[4,128,256]{2,1,0:T(8,128)(2,1)S(1)}, bf16[4,128,256]{2,1,0:T(8,128)(2,1)S(1)}, u32[]{:S(2)}, u32[]{:S(2)}) %collective-permute-start.24) | collective-permute-done | bytes 262176 | tf_op jit(solution)/shard_map/ppermute | solution.py:573
  94.9 3.6 %collective-permute-done.26.refs_14_ = bf16[4,128,256]{2,1,0:T(8,128)(2,1)S(1)} collective-permute-done((bf16[4,128,256]{2,1,0:T(8,128)(2,1)S(1)}, bf16[4,128,256]{2,1,0:T(8,128)(2,1)S(1)}, u32[]{:S(2)}, u32[]{:S(2)}) %collective-permute-start.26) | collective-permute-done | bytes 262176 | tf_op jit(solution)/shard_map/ppermute | solution.py:573
  98.8 14.9 %attend.1 = (bf16[512,1280]{1,0:T(8,128)(2,1)S(1)}, f32[16,128,128]{2,1,0:T(8,128)S(1)}, bf16[16,128,128]{2,1,0:T(8,128)(2,1)S(1)}, bf16[16,128,128]{2,1,0:T(8,1...) custom-call(s32[115]{0:T(128)S(1)} %copy-done.13, ...), custom_call_target="tpu_custom_call" | custom-call | tf_op jit(solution)/shard_map/attend/pallas_call | solution.py:389
  113.8 2.9 %collective-permute-start.30 = (bf16[16,128,128]{2,1,0:T(8,128)(2,1)S(1)}, bf16[16,128,128]{2,1,0:T(8,128)(2,1)S(1)}, u32[]{:S(2)}, u32[]{:S(2)}) collective-permute-start(bf16[16,128,128]{2,1,0:T(8,128)(2,1)S(1)} %get-tuple-element.90), channel_id=1, source_target_pairs={{0,24},{4,28},{8,0},{12,4},{16,8},{20,12},{24,16},{28,20},{32,56},... | collective-permute-start | bytes 1572872 | tf_op jit(solution)/shard_map/ppermute | solution.py:573
  118.6 1.8 collective-permute-start.33
  120.5 2.7 %collective-permute-done.29.refs_1_ = bf16[16,128,128]{2,1,0:T(8,128)(2,1)S(1)} collective-permute-done((bf16[16,128,128]{2,1,0:T(8,128)(2,1)S(1)}, bf16[16,128,128]{2,1,0:T(8,128)(2,1)S(1)}, u32[]{:S(2)}, u32[]{:S(2)}) %collective-permute-start.29) | collective-permute-done | bytes 524320 | tf_op jit(solution)/shard_map/ppermute | solution.py:573
  124.1 2.7 %collective-permute-done.30.refs_2_ = bf16[16,128,128]{2,1,0:T(8,128)(2,1)S(1)} collective-permute-done((bf16[16,128,128]{2,1,0:T(8,128)(2,1)S(1)}, bf16[16,128,128]{2,1,0:T(8,128)(2,1)S(1)}, u32[]{:S(2)}, u32[]{:S(2)}) %collective-permute-start.30) | collective-permute-done | bytes 524320 | tf_op jit(solution)/shard_map/ppermute | solution.py:573
  126.7 13.3 %collective-permute-start.45 = (bf16[128,1280]{1,0:T(8,128)(2,1)}, bf16[128,1280]{1,0:T(8,128)(2,1)S(1)}, u32[]{:S(2)}, u32[]{:S(2)}) collective-permute-start(bf16[128,1280]{1,0:T(8,128)(2,1)} %collective-permute-done.3.bt.refs_1_), channel_id=1, source_target_pairs={{0,4},{4,0},{8,12},{12,8},{16,20},{20,16},{24,28},{28,24},{32,36},... | collective-permute-start | bytes 983048 | tf_op jit(solution)/shard_map/ppermute | solution.py:573
  140.6 4.2 %collective-permute-start.35 = (f32[4,128,128]{2,1,0:T(8,128)S(1)}, f32[4,128,128]{2,1,0:T(8,128)S(1)}, u32[]{:S(2)}, u32[]{:S(2)}) collective-permute-start(f32[4,128,128]{2,1,0:T(8,128)S(1)} %get-tuple-element.97), channel_id=1, source_target_pairs={{0,32},{4,36},{8,40},{12,44},{16,48},{20,52},{24,56},{28,60},{32,6... | collective-permute-start | bytes 786440 | tf_op jit(solution)/shard_map/ppermute | solution.py:573
  144.7 1.9 collective-permute-start.37
  146.6 2.7 %collective-permute-start.39 = (f32[4,128,128]{2,1,0:T(8,128)S(1)}, f32[4,128,128]{2,1,0:T(8,128)S(1)}, u32[]{:S(2)}, u32[]{:S(2)}) collective-permute-start(f32[4,128,128]{2,1,0:T(8,128)S(1)} %get-tuple-element.102), channel_id=1, source_target_pairs={{0,24},{4,28},{8,0},{12,4},{16,8},{20,12},{24,16},{28,20},{32,56},... | collective-permute-start | bytes 786440 | tf_op jit(solution)/shard_map/ppermute | solution.py:573
  149.3 2.8 %collective-permute-start.40 = (f32[4,128,128]{2,1,0:T(8,128)S(1)}, f32[4,128,128]{2,1,0:T(8,128)S(1)}, u32[]{:S(2)}, u32[]{:S(2)}) collective-permute-start(f32[4,128,128]{2,1,0:T(8,128)S(1)} %get-tuple-element.103), channel_id=1, source_target_pairs={{0,16},{4,20},{8,24},{12,28},{16,0},{20,4},{24,8},{28,12},{32,48},... | collective-permute-start | bytes 786440 | tf_op jit(solution)/shard_map/ppermute | solution.py:573
  152.7 12.6 %collective-permute-start.48 = (bf16[128,1280]{1,0:T(8,128)(2,1)}, bf16[128,1280]{1,0:T(8,128)(2,1)S(1)}, u32[]{:S(2)}, u32[]{:S(2)}) collective-permute-start(bf16[128,1280]{1,0:T(8,128)(2,1)} %collective-permute-done.5.cl.refs_4_), channel_id=1, source_target_pairs={{0,4},{4,0},{8,12},{12,8},{16,20},{20,16},{24,28},{28,24},{32,36},... | collective-permute-start | bytes 983048 | tf_op jit(solution)/shard_map/ppermute | solution.py:573
  165.4 1.8 collective-permute-start.46
  167.6 2.4 collective-permute-start.49
  172.4 2.7 %flip.1 = (bf16[1280,512]{1,0:T(8,128)(2,1)S(1)}, bf16[1280,512]{1,0:T(8,128)(2,1)S(1)}, bf16[1280,512]{1,0:T(8,128)(2,1)S(1)}, bf16[1280,512]{1,0:T(8,128)(2,1)S(1)}) custom-call(bf16[256,1280]{1,0:T(8,128)(2,1)S(1)} %copy-done.5, bf16[128,1280]{1,0:T(8,128)(2,1)} %collective-permute-done.3.bt.refs_1_, ...), custom_call_target="tpu_custom_call" | custom-call | tf_op jit(solution)/shard_map/flip/pallas_call | solution.py:525
  175.1 4.6 %weight_partials.1 = (f32[8,160,128]{2,1,0:T(8,128)S(1)}, bf16[8,160,128]{2,1,0:T(8,128)(2,1)S(1)}, bf16[8,160,128]{2,1,0:T(8,128)(2,1)S(1)}, bf16[8,160,128]{2,...) custom-call(s32[17]{0:T(128)S(1)} %copy-done.12, ...), custom_call_target="tpu_custom_call" | custom-call | tf_op jit(solution)/shard_map/weight_partials/pallas_call | solution.py:560
  179.8 2.8 %collective-permute-start.52 = (bf16[8,160,128]{2,1,0:T(8,128)(2,1)S(1)}, bf16[8,160,128]{2,1,0:T(8,128)(2,1)S(1)}, u32[]{:S(2)}, u32[]{:S(2)}) collective-permute-start(bf16[8,160,128]{2,1,0:T(8,128)(2,1)S(1)} %get-tuple-element.119), channel_id=1, source_target_pairs={{0,24},{4,28},{8,0},{12,4},{16,8},{20,12},{24,16},{28,20},{32,56},... | collective-permute-start | bytes 983048 | tf_op jit(solution)/shard_map/ppermute | solution.py:573
  186.4 3.6 %collective-permute-done.51.refs_1_ = bf16[8,160,128]{2,1,0:T(8,128)(2,1)S(1)} collective-permute-done((bf16[8,160,128]{2,1,0:T(8,128)(2,1)S(1)}, bf16[8,160,128]{2,1,0:T(8,128)(2,1)S(1)}, u32[]{:S(2)}, u32[]{:S(2)}) %collective-permute-start.51) | collective-permute-done | bytes 327712 | tf_op jit(solution)/shard_map/ppermute | solution.py:573
  190.0 1.3 collective-permute-start.55
  191.3 4.7 %collective-permute-done.52.refs_2_ = bf16[8,160,128]{2,1,0:T(8,128)(2,1)S(1)} collective-permute-done((bf16[8,160,128]{2,1,0:T(8,128)(2,1)S(1)}, bf16[8,160,128]{2,1,0:T(8,128)(2,1)S(1)}, u32[]{:S(2)}, u32[]{:S(2)}) %collective-permute-start.52) | collective-permute-done | bytes 327712 | tf_op jit(solution)/shard_map/ppermute | solution.py:573
  196.0 1.9 collective-permute-start.56
  198.2 7.1 %collective-permute-done.56.refs_7_ = bf16[8,160,128]{2,1,0:T(8,128)(2,1)S(1)} collective-permute-done((bf16[8,160,128]{2,1,0:T(8,128)(2,1)S(1)}, bf16[8,160,128]{2,1,0:T(8,128)(2,1)S(1)}, u32[]{:S(2)}, u32[]{:S(2)}) %collective-permute-start.56) | collective-permute-done | bytes 327712 | tf_op jit(solution)/shard_map/ppermute | solution.py:573
  209.9 1.5 collective-permute-start.58
  211.5 1.7 copy-done.2
  214.1 3.0 %input_partials.1 = (bf16[256,1280]{1,0:T(8,128)(2,1)S(1)}, bf16[256,1280]{1,0:T(8,128)(2,1)S(1)}, bf16[256,1280]{1,0:T(8,128)(2,1)S(1)}, bf16[256,1280]{1,0:T(8,128)(2,1)S(1)}) custom-call(s32[17]{0:T(128)S(1)} %copy-done.12, bf16[512,256]{1,0:T(8,128)(2,1)S(1)} %get-tuple-element.106.a.g, bf16[256,256]{1,0:T(8,128)(2,1)S(1)} %copy-done.11, ...), custom_call_target="tpu_custom_call" | custom-call | tf_op jit(solution)/shard_map/input_partials/pallas_call | solution.py:500
  217.1 2.3 collective-permute-start.42
  219.5 1.9 collective-permute-start.43
  222.6 1.4 collective-permute-start.59
  224.2 1.3 broadcast_select_fusion.1
  225.4 2.9 %collective-permute-done.59.refs_3_ = f32[2,160,128]{2,1,0:T(8,128)S(1)} collective-permute-done((f32[2,160,128]{2,1,0:T(8,128)S(1)}, f32[2,160,128]{2,1,0:T(8,128)S(1)}, u32[]{:S(2)}, u32[]{:S(2)}) %collective-permute-start.59) | collective-permute-done | bytes 163872 | tf_op jit(solution)/shard_map/ppermute | solution.py:573
  228.3 3.9 %collective-permute-start.61 = (f32[2,160,128]{2,1,0:T(8,128)S(1)}, f32[2,160,128]{2,1,0:T(8,128)S(1)}, u32[]{:S(2)}, u32[]{:S(2)}) collective-permute-start(f32[2,160,128]{2,1,0:T(8,128)S(1)} %copy-done.17), channel_id=1, source_target_pairs={{0,24},{4,28},{8,0},{12,4},{16,8},{20,12},{24,16},{28,20},{32,56},... | collective-permute-start | bytes 491528 | tf_op jit(solution)/shard_map/ppermute | solution.py:573
  233.1 3.1 %collective-permute-done.61.refs_6_ = f32[2,160,128]{2,1,0:T(8,128)S(1)} collective-permute-done((f32[2,160,128]{2,1,0:T(8,128)S(1)}, f32[2,160,128]{2,1,0:T(8,128)S(1)}, u32[]{:S(2)}, u32[]{:S(2)}) %collective-permute-start.61) | collective-permute-done | bytes 163872 | tf_op jit(solution)/shard_map/ppermute | solution.py:573
  236.2 1.7 collective-permute-done.62.refs_7_
  237.9 6.4 %collective-permute-start.63 = (f32[160,256]{1,0:T(8,128)S(1)}, f32[160,256]{1,0:T(8,128)S(1)}, u32[]{:S(2)}, u32[]{:S(2)}) collective-permute-start(f32[160,256]{1,0:T(8,128)S(1)} %get-tuple-element.134), channel_id=1, source_target_pairs={{0,4},{4,0},{8,12},{12,8},{16,20},{20,16},{24,28},{28,24},{32,36},... | collective-permute-start | bytes 491528 | tf_op jit(solution)/shard_map/ppermute | solution.py:573
  245.4 1.3 join_weights.1
  246.7 2.1 collective-permute-done.44
  (136 shorter events, 31.1 us)
Async XLA Ops:
  2.5 32.7 %collective-permute-start.1 = (bf16[256,640]{1,0:T(8,128)(2,1)}, bf16[256,640]{1,0:T(8,128)(2,1)}, u32[]{:S(2)}, u32[]{:S(2)}) collective-permute-start(bf16[256,640]{1,0:T(8,128)(2,1)} %constant_dynamic-slice_fusion.1), channel_id=1, source_target_pairs={{0,4},{4,0},{8,12},{12,8},{16,20},{20,16},{24,28},{28,24},{32,36},... | collective-permute-start | bytes 983048 | tf_op jit(solution)/shard_map/ppermute | solution.py:573
  5.6 29.6 %collective-permute-start.2 = (bf16[256,640]{1,0:T(8,128)(2,1)}, bf16[256,640]{1,0:T(8,128)(2,1)}, u32[]{:S(2)}, u32[]{:S(2)}) collective-permute-start(bf16[256,640]{1,0:T(8,128)(2,1)} %constant_dynamic-slice_fusion), channel_id=1, source_target_pairs={{0,4},{4,0},{8,12},{12,8},{16,20},{20,16},{24,28},{28,24},{32,36},... | collective-permute-start | bytes 983048 | tf_op jit(solution)/shard_map/ppermute | solution.py:573
  5.6 37.6 %collective-permute-start = (bf16[256,1280]{1,0:T(8,128)(2,1)S(1)}, bf16[256,1280]{1,0:T(8,128)(2,1)}, u32[]{:S(2)}, u32[]{:S(2)}) collective-permute-start(bf16[256,1280]{1,0:T(8,128)(2,1)S(1)} %copy-done.3), channel_id=1, source_target_pairs={{0,4},{4,0},{8,12},{12,8},{16,20},{20,16},{24,28},{28,24},{32,36},... | collective-permute-start | bytes 1966088 | tf_op jit(solution)/shard_map/ppermute | solution.py:573
  27.1 12.3 %collective-permute-start.3 = (bf16[128,1280]{1,0:T(8,128)(2,1)}, bf16[128,1280]{1,0:T(8,128)(2,1)}, u32[]{:S(2)}, u32[]{:S(2)}) collective-permute-start(bf16[128,1280]{1,0:T(8,128)(2,1)} %get-tuple-element.76), channel_id=1, source_target_pairs={{0,1},{1,2},{2,3},{3,0},{4,5},{5,6},{6,7},{7,4},{8,9},{9,10},{10,1... | collective-permute-start | bytes 983048 | tf_op jit(solution)/shard_map/ppermute | solution.py:573
  28.9 10.4 %collective-permute-start.5 = (bf16[128,1280]{1,0:T(8,128)(2,1)}, bf16[128,1280]{1,0:T(8,128)(2,1)}, u32[]{:S(2)}, u32[]{:S(2)}) collective-permute-start(bf16[128,1280]{1,0:T(8,128)(2,1)} %get-tuple-element.77), channel_id=1, source_target_pairs={{0,3},{1,0},{2,1},{3,2},{4,7},{5,4},{6,5},{7,6},{8,11},{9,8},{10,9... | collective-permute-start | bytes 983048 | tf_op jit(solution)/shard_map/ppermute | solution.py:573
  35.1 10.8 %collective-permute-start.7 = (bf16[128,1280]{1,0:T(8,128)(2,1)}, bf16[128,1280]{1,0:T(8,128)(2,1)S(1)}, u32[]{:S(2)}, u32[]{:S(2)}) collective-permute-start(bf16[128,1280]{1,0:T(8,128)(2,1)} %get-tuple-element.77), channel_id=1, source_target_pairs={{0,1},{1,2},{2,3},{3,0},{4,5},{5,6},{6,7},{7,4},{8,9},{9,10},{10,1... | collective-permute-start | bytes 983048 | tf_op jit(solution)/shard_map/ppermute | solution.py:573
  35.1 10.8 %collective-permute-start.8 = (bf16[128,1280]{1,0:T(8,128)(2,1)}, bf16[128,1280]{1,0:T(8,128)(2,1)S(1)}, u32[]{:S(2)}, u32[]{:S(2)}) collective-permute-start(bf16[128,1280]{1,0:T(8,128)(2,1)} %get-tuple-element.76), channel_id=1, source_target_pairs={{0,3},{1,0},{2,1},{3,2},{4,7},{5,4},{6,5},{7,6},{8,11},{9,8},{10,9... | collective-permute-start | bytes 983048 | tf_op jit(solution)/shard_map/ppermute | solution.py:573
  39.3 13.6 %collective-permute-start.4 = (bf16[128,1280]{1,0:T(8,128)(2,1)}, bf16[128,1280]{1,0:T(8,128)(2,1)S(1)}, u32[]{:S(2)}, u32[]{:S(2)}) collective-permute-start(bf16[128,1280]{1,0:T(8,128)(2,1)} %collective-permute-done.3.bt.refs_1_), channel_id=1, source_target_pairs={{0,1},{1,2},{2,3},{3,0},{4,5},{5,6},{6,7},{7,4},{8,9},{9,10},{10,1... | collective-permute-start | bytes 983048 | tf_op jit(solution)/shard_map/ppermute | solution.py:573
  39.3 13.6 %collective-permute-start.6 = (bf16[128,1280]{1,0:T(8,128)(2,1)}, bf16[128,1280]{1,0:T(8,128)(2,1)S(1)}, u32[]{:S(2)}, u32[]{:S(2)}) collective-permute-start(bf16[128,1280]{1,0:T(8,128)(2,1)} %collective-permute-done.5.cl.refs_4_), channel_id=1, source_target_pairs={{0,3},{1,0},{2,1},{3,2},{4,7},{5,4},{6,5},{7,6},{8,11},{9,8},{10,9... | collective-permute-start | bytes 983048 | tf_op jit(solution)/shard_map/ppermute | solution.py:573
  54.1 5.5 %collective-permute-start.10 = (bf16[256,256]{1,0:T(8,128)(2,1)S(1)}, bf16[256,256]{1,0:T(8,128)(2,1)S(1)}, u32[]{:S(2)}, u32[]{:S(2)}) collective-permute-start(bf16[256,256]{1,0:T(8,128)(2,1)S(1)} %get-tuple-element.81.a), channel_id=1, source_target_pairs={{0,24},{4,28},{8,0},{12,4},{16,8},{20,12},{24,16},{28,20},{32,56},... | collective-permute-start | bytes 393224 | tf_op jit(solution)/shard_map/ppermute | solution.py:573
  56.6 5.4 %collective-permute-start.11 = (bf16[256,256]{1,0:T(8,128)(2,1)S(1)}, bf16[256,256]{1,0:T(8,128)(2,1)S(1)}, u32[]{:S(2)}, u32[]{:S(2)}) collective-permute-start(bf16[256,256]{1,0:T(8,128)(2,1)S(1)} %get-tuple-element.81.a), channel_id=1, source_target_pairs={{0,16},{4,20},{8,24},{12,28},{16,0},{20,4},{24,8},{28,12},{32,48},... | collective-permute-start | bytes 393224 | tf_op jit(solution)/shard_map/ppermute | solution.py:573
  57.1 8.7 %collective-permute-start.9 = (bf16[256,256]{1,0:T(8,128)(2,1)S(1)}, bf16[256,256]{1,0:T(8,128)(2,1)S(1)}, u32[]{:S(2)}, u32[]{:S(2)}) collective-permute-start(bf16[256,256]{1,0:T(8,128)(2,1)S(1)} %get-tuple-element.81.a), channel_id=1, source_target_pairs={{0,8},{4,12},{8,16},{12,20},{16,24},{20,28},{24,0},{28,4},{32,40},... | collective-permute-start | bytes 393224 | tf_op jit(solution)/shard_map/ppermute | solution.py:573
  57.7 11.1 %collective-permute-start.18 = (bf16[256,256]{1,0:T(8,128)(2,1)S(1)}, bf16[256,256]{1,0:T(8,128)(2,1)S(1)}, u32[]{:S(2)}, u32[]{:S(2)}) collective-permute-start(bf16[256,256]{1,0:T(8,128)(2,1)S(1)} %get-tuple-element.84), channel_id=1, source_target_pairs={{0,4},{4,0},{8,12},{12,8},{16,20},{20,16},{24,28},{28,24},{32,36},... | collective-permute-start | bytes 393224 | tf_op jit(solution)/shard_map/ppermute | solution.py:573
  65.9 14.9 %collective-permute-start.12 = (bf16[4,128,256]{2,1,0:T(8,128)(2,1)S(1)}, bf16[4,128,256]{2,1,0:T(8,128)(2,1)S(1)}, u32[]{:S(2)}, u32[]{:S(2)}) collective-permute-start(bf16[4,128,256]{2,1,0:T(8,128)(2,1)S(1)} %get-tuple-element.82.refs_0_), channel_id=1, source_target_pairs={{0,32},{4,36},{8,40},{12,44},{16,48},{20,52},{24,56},{28,60},{32,6... | collective-permute-start | bytes 786440 | tf_op jit(solution)/shard_map/ppermute | solution.py:573
  67.3 16.2 %collective-permute-start.15 = (bf16[4,128,256]{2,1,0:T(8,128)(2,1)S(1)}, bf16[4,128,256]{2,1,0:T(8,128)(2,1)S(1)}, u32[]{:S(2)}, u32[]{:S(2)}) collective-permute-start(bf16[4,128,256]{2,1,0:T(8,128)(2,1)S(1)} %get-tuple-element.83.refs_1_), channel_id=1, source_target_pairs={{0,96},{4,100},{8,104},{12,108},{16,112},{20,116},{24,120},{28,124... | collective-permute-start | bytes 786440 | tf_op jit(solution)/shard_map/ppermute | solution.py:573
  68.8 8.2 %collective-permute-start.19 = (bf16[256,256]{1,0:T(8,128)(2,1)S(1)}, bf16[256,256]{1,0:T(8,128)(2,1)S(1)}, u32[]{:S(2)}, u32[]{:S(2)}) collective-permute-start(bf16[256,256]{1,0:T(8,128)(2,1)S(1)} %collective-permute-done.18.a), channel_id=1, source_target_pairs={{0,32},{4,36},{8,40},{12,44},{16,48},{20,52},{24,56},{28,60},{32,6... | collective-permute-start | bytes 393224 | tf_op jit(solution)/shard_map/ppermute | solution.py:573
  68.8 8.2 %collective-permute-start.20 = (bf16[256,256]{1,0:T(8,128)(2,1)S(1)}, bf16[256,256]{1,0:T(8,128)(2,1)S(1)}, u32[]{:S(2)}, u32[]{:S(2)}) collective-permute-start(bf16[256,256]{1,0:T(8,128)(2,1)S(1)} %collective-permute-done.18.a), channel_id=1, source_target_pairs={{0,96},{4,100},{8,104},{12,108},{16,112},{20,116},{24,120},{28,124... | collective-permute-start | bytes 393224 | tf_op jit(solution)/shard_map/ppermute | solution.py:573
  71.5 9.2 %collective-permute-start.21 = (bf16[256,256]{1,0:T(8,128)(2,1)S(1)}, bf16[256,256]{1,0:T(8,128)(2,1)S(1)}, u32[]{:S(2)}, u32[]{:S(2)}) collective-permute-start(bf16[256,256]{1,0:T(8,128)(2,1)S(1)} %collective-permute-done.18.a), channel_id=1, source_target_pairs={{0,64},{4,68},{8,72},{12,76},{16,80},{20,84},{24,88},{28,92},{32,9... | collective-permute-start | bytes 393224 | tf_op jit(solution)/shard_map/ppermute | solution.py:573
  77.0 9.7 %collective-permute-start.13 = (bf16[4,128,256]{2,1,0:T(8,128)(2,1)S(1)}, bf16[4,128,256]{2,1,0:T(8,128)(2,1)S(1)}, u32[]{:S(2)}, u32[]{:S(2)}) collective-permute-start(bf16[4,128,256]{2,1,0:T(8,128)(2,1)S(1)} %get-tuple-element.83.refs_1_), channel_id=1, source_target_pairs={{0,32},{4,36},{8,40},{12,44},{16,48},{20,52},{24,56},{28,60},{32,6... | collective-permute-start | bytes 786440 | tf_op jit(solution)/shard_map/ppermute | solution.py:573
  77.0 9.7 %collective-permute-start.14 = (bf16[4,128,256]{2,1,0:T(8,128)(2,1)S(1)}, bf16[4,128,256]{2,1,0:T(8,128)(2,1)S(1)}, u32[]{:S(2)}, u32[]{:S(2)}) collective-permute-start(bf16[4,128,256]{2,1,0:T(8,128)(2,1)S(1)} %get-tuple-element.82.refs_0_), channel_id=1, source_target_pairs={{0,96},{4,100},{8,104},{12,108},{16,112},{20,116},{24,120},{28,124... | collective-permute-start | bytes 786440 | tf_op jit(solution)/shard_map/ppermute | solution.py:573
  80.7 6.8 %collective-permute-start.22 = (bf16[4,128,256]{2,1,0:T(8,128)(2,1)S(1)}, bf16[4,128,256]{2,1,0:T(8,128)(2,1)S(1)}, u32[]{:S(2)}, u32[]{:S(2)}) collective-permute-start(bf16[4,128,256]{2,1,0:T(8,128)(2,1)S(1)} %get-tuple-element.85.refs_8_), channel_id=1, source_target_pairs={{0,8},{4,12},{8,16},{12,20},{16,24},{20,28},{24,0},{28,4},{32,40},... | collective-permute-start | bytes 786440 | tf_op jit(solution)/shard_map/ppermute | solution.py:573
  80.8 8.6 %collective-permute-start.25 = (bf16[4,128,256]{2,1,0:T(8,128)(2,1)S(1)}, bf16[4,128,256]{2,1,0:T(8,128)(2,1)S(1)}, u32[]{:S(2)}, u32[]{:S(2)}) collective-permute-start(bf16[4,128,256]{2,1,0:T(8,128)(2,1)S(1)} %get-tuple-element.86.refs_9_), channel_id=1, source_target_pairs={{0,24},{4,28},{8,0},{12,4},{16,8},{20,12},{24,16},{28,20},{32,56},... | collective-permute-start | bytes 786440 | tf_op jit(solution)/shard_map/ppermute | solution.py:573
  83.4 8.4 %collective-permute-start.23 = (bf16[4,128,256]{2,1,0:T(8,128)(2,1)S(1)}, bf16[4,128,256]{2,1,0:T(8,128)(2,1)S(1)}, u32[]{:S(2)}, u32[]{:S(2)}) collective-permute-start(bf16[4,128,256]{2,1,0:T(8,128)(2,1)S(1)} %get-tuple-element.86.refs_9_), channel_id=1, source_target_pairs={{0,8},{4,12},{8,16},{12,20},{16,24},{20,28},{24,0},{28,4},{32,40},... | collective-permute-start | bytes 786440 | tf_op jit(solution)/shard_map/ppermute | solution.py:573
  86.7 8.2 %collective-permute-start.24 = (bf16[4,128,256]{2,1,0:T(8,128)(2,1)S(1)}, bf16[4,128,256]{2,1,0:T(8,128)(2,1)S(1)}, u32[]{:S(2)}, u32[]{:S(2)}) collective-permute-start(bf16[4,128,256]{2,1,0:T(8,128)(2,1)S(1)} %get-tuple-element.85.refs_8_), channel_id=1, source_target_pairs={{0,24},{4,28},{8,0},{12,4},{16,8},{20,12},{24,16},{28,20},{32,56},... | collective-permute-start | bytes 786440 | tf_op jit(solution)/shard_map/ppermute | solution.py:573
  86.7 8.2 %collective-permute-start.16 = (bf16[4,128,256]{2,1,0:T(8,128)(2,1)S(1)}, bf16[4,128,256]{2,1,0:T(8,128)(2,1)S(1)}, u32[]{:S(2)}, u32[]{:S(2)}) collective-permute-start(bf16[4,128,256]{2,1,0:T(8,128)(2,1)S(1)} %collective-permute-done.12.refs_2_), channel_id=1, source_target_pairs={{0,32},{4,36},{8,40},{12,44},{16,48},{20,52},{24,56},{28,60},{32,6... | collective-permute-start | bytes 786440 | tf_op jit(solution)/shard_map/ppermute | solution.py:573
  87.5 7.4 %collective-permute-start.17 = (bf16[4,128,256]{2,1,0:T(8,128)(2,1)S(1)}, bf16[4,128,256]{2,1,0:T(8,128)(2,1)S(1)}, u32[]{:S(2)}, u32[]{:S(2)}) collective-permute-start(bf16[4,128,256]{2,1,0:T(8,128)(2,1)S(1)} %collective-permute-done.15.refs_5_), channel_id=1, source_target_pairs={{0,96},{4,100},{8,104},{12,108},{16,112},{20,116},{24,120},{28,124... | collective-permute-start | bytes 786440 | tf_op jit(solution)/shard_map/ppermute | solution.py:573
  89.4 9.1 %collective-permute-start.26 = (bf16[4,128,256]{2,1,0:T(8,128)(2,1)S(1)}, bf16[4,128,256]{2,1,0:T(8,128)(2,1)S(1)}, u32[]{:S(2)}, u32[]{:S(2)}) collective-permute-start(bf16[4,128,256]{2,1,0:T(8,128)(2,1)S(1)} %collective-permute-done.22.refs_10_), channel_id=1, source_target_pairs={{0,8},{4,12},{8,16},{12,20},{16,24},{20,28},{24,0},{28,4},{32,40},... | collective-permute-start | bytes 786440 | tf_op jit(solution)/shard_map/ppermute | solution.py:573
  91.9 6.9 %collective-permute-start.27 = (bf16[4,128,256]{2,1,0:T(8,128)(2,1)S(1)}, bf16[4,128,256]{2,1,0:T(8,128)(2,1)S(1)}, u32[]{:S(2)}, u32[]{:S(2)}) collective-permute-start(bf16[4,128,256]{2,1,0:T(8,128)(2,1)S(1)} %collective-permute-done.25.refs_13_), channel_id=1, source_target_pairs={{0,24},{4,28},{8,0},{12,4},{16,8},{20,12},{24,16},{28,20},{32,56},... | collective-permute-start | bytes 786440 | tf_op jit(solution)/shard_map/ppermute | solution.py:573
  113.7 9.4 %collective-permute-start.29 = (bf16[16,128,128]{2,1,0:T(8,128)(2,1)S(1)}, bf16[16,128,128]{2,1,0:T(8,128)(2,1)S(1)}, u32[]{:S(2)}, u32[]{:S(2)}) collective-permute-start(bf16[16,128,128]{2,1,0:T(8,128)(2,1)S(1)} %get-tuple-element.89), channel_id=1, source_target_pairs={{0,8},{4,12},{8,16},{12,20},{16,24},{20,28},{24,0},{28,4},{32,40},... | collective-permute-start | bytes 1572872 | tf_op jit(solution)/shard_map/ppermute | solution.py:573
  113.8 12.9 %collective-permute-start.30 = (bf16[16,128,128]{2,1,0:T(8,128)(2,1)S(1)}, bf16[16,128,128]{2,1,0:T(8,128)(2,1)S(1)}, u32[]{:S(2)}, u32[]{:S(2)}) collective-permute-start(bf16[16,128,128]{2,1,0:T(8,128)(2,1)S(1)} %get-tuple-element.90), channel_id=1, source_target_pairs={{0,24},{4,28},{8,0},{12,4},{16,8},{20,12},{24,16},{28,20},{32,56},... | collective-permute-start | bytes 1572872 | tf_op jit(solution)/shard_map/ppermute | solution.py:573
  116.7 23.4 %collective-permute-start.31 = (bf16[16,128,128]{2,1,0:T(8,128)(2,1)S(1)}, bf16[16,128,128]{2,1,0:T(8,128)(2,1)S(1)}, u32[]{:S(2)}, u32[]{:S(2)}) collective-permute-start(bf16[16,128,128]{2,1,0:T(8,128)(2,1)S(1)} %get-tuple-element.91), channel_id=1, source_target_pairs={{0,16},{4,20},{8,24},{12,28},{16,0},{20,4},{24,8},{28,12},{32,48},... | collective-permute-start | bytes 1572872 | tf_op jit(solution)/shard_map/ppermute | solution.py:573
  117.8 22.3 %collective-permute-start.32 = (bf16[16,128,128]{2,1,0:T(8,128)(2,1)S(1)}, bf16[16,128,128]{2,1,0:T(8,128)(2,1)S(1)}, u32[]{:S(2)}, u32[]{:S(2)}) collective-permute-start(bf16[16,128,128]{2,1,0:T(8,128)(2,1)S(1)} %get-tuple-element.93), channel_id=1, source_target_pairs={{0,32},{4,36},{8,40},{12,44},{16,48},{20,52},{24,56},{28,60},{32,6... | collective-permute-start | bytes 1572872 | tf_op jit(solution)/shard_map/ppermute | solution.py:573
  118.6 21.4 %collective-permute-start.33 = (bf16[16,128,128]{2,1,0:T(8,128)(2,1)S(1)}, bf16[16,128,128]{2,1,0:T(8,128)(2,1)S(1)}, u32[]{:S(2)}, u32[]{:S(2)}) collective-permute-start(bf16[16,128,128]{2,1,0:T(8,128)(2,1)S(1)} %get-tuple-element.94), channel_id=1, source_target_pairs={{0,96},{4,100},{8,104},{12,108},{16,112},{20,116},{24,120},{28,124... | collective-permute-start | bytes 1572872 | tf_op jit(solution)/shard_map/ppermute | solution.py:573
  123.2 16.9 %collective-permute-start.34 = (bf16[16,128,128]{2,1,0:T(8,128)(2,1)S(1)}, bf16[16,128,128]{2,1,0:T(8,128)(2,1)S(1)}, u32[]{:S(2)}, u32[]{:S(2)}) collective-permute-start(bf16[16,128,128]{2,1,0:T(8,128)(2,1)S(1)} %get-tuple-element.95), channel_id=1, source_target_pairs={{0,64},{4,68},{8,72},{12,76},{16,80},{20,84},{24,88},{28,92},{32,9... | collective-permute-start | bytes 1572872 | tf_op jit(solution)/shard_map/ppermute | solution.py:573
  126.7 19.8 %collective-permute-start.45 = (bf16[128,1280]{1,0:T(8,128)(2,1)}, bf16[128,1280]{1,0:T(8,128)(2,1)S(1)}, u32[]{:S(2)}, u32[]{:S(2)}) collective-permute-start(bf16[128,1280]{1,0:T(8,128)(2,1)} %collective-permute-done.3.bt.refs_1_), channel_id=1, source_target_pairs={{0,4},{4,0},{8,12},{12,8},{16,20},{20,16},{24,28},{28,24},{32,36},... | collective-permute-start | bytes 983048 | tf_op jit(solution)/shard_map/ppermute | solution.py:573
  140.6 8.7 %collective-permute-start.35 = (f32[4,128,128]{2,1,0:T(8,128)S(1)}, f32[4,128,128]{2,1,0:T(8,128)S(1)}, u32[]{:S(2)}, u32[]{:S(2)}) collective-permute-start(f32[4,128,128]{2,1,0:T(8,128)S(1)} %get-tuple-element.97), channel_id=1, source_target_pairs={{0,32},{4,36},{8,40},{12,44},{16,48},{20,52},{24,56},{28,60},{32,6... | collective-permute-start | bytes 786440 | tf_op jit(solution)/shard_map/ppermute | solution.py:573
  144.7 8.0 %collective-permute-start.36 = (f32[4,128,128]{2,1,0:T(8,128)S(1)}, f32[4,128,128]{2,1,0:T(8,128)S(1)}, u32[]{:S(2)}, u32[]{:S(2)}) collective-permute-start(f32[4,128,128]{2,1,0:T(8,128)S(1)} %get-tuple-element.98), channel_id=1, source_target_pairs={{0,96},{4,100},{8,104},{12,108},{16,112},{20,116},{24,120},{28,124... | collective-permute-start | bytes 786440 | tf_op jit(solution)/shard_map/ppermute | solution.py:573
  144.7 20.6 %collective-permute-start.37 = (f32[4,128,128]{2,1,0:T(8,128)S(1)}, f32[4,128,128]{2,1,0:T(8,128)S(1)}, u32[]{:S(2)}, u32[]{:S(2)}) collective-permute-start(f32[4,128,128]{2,1,0:T(8,128)S(1)} %get-tuple-element.99), channel_id=1, source_target_pairs={{0,64},{4,68},{8,72},{12,76},{16,80},{20,84},{24,88},{28,92},{32,9... | collective-permute-start | bytes 786440 | tf_op jit(solution)/shard_map/ppermute | solution.py:573
  146.6 20.6 %collective-permute-start.38 = (f32[4,128,128]{2,1,0:T(8,128)S(1)}, f32[4,128,128]{2,1,0:T(8,128)S(1)}, u32[]{:S(2)}, u32[]{:S(2)}) collective-permute-start(f32[4,128,128]{2,1,0:T(8,128)S(1)} %get-tuple-element.101), channel_id=1, source_target_pairs={{0,8},{4,12},{8,16},{12,20},{16,24},{20,28},{24,0},{28,4},{32,40},... | collective-permute-start | bytes 786440 | tf_op jit(solution)/shard_map/ppermute | solution.py:573
  146.6 21.0 %collective-permute-start.39 = (f32[4,128,128]{2,1,0:T(8,128)S(1)}, f32[4,128,128]{2,1,0:T(8,128)S(1)}, u32[]{:S(2)}, u32[]{:S(2)}) collective-permute-start(f32[4,128,128]{2,1,0:T(8,128)S(1)} %get-tuple-element.102), channel_id=1, source_target_pairs={{0,24},{4,28},{8,0},{12,4},{16,8},{20,12},{24,16},{28,20},{32,56},... | collective-permute-start | bytes 786440 | tf_op jit(solution)/shard_map/ppermute | solution.py:573
  149.3 20.7 %collective-permute-start.40 = (f32[4,128,128]{2,1,0:T(8,128)S(1)}, f32[4,128,128]{2,1,0:T(8,128)S(1)}, u32[]{:S(2)}, u32[]{:S(2)}) collective-permute-start(f32[4,128,128]{2,1,0:T(8,128)S(1)} %get-tuple-element.103), channel_id=1, source_target_pairs={{0,16},{4,20},{8,24},{12,28},{16,0},{20,4},{24,8},{28,12},{32,48},... | collective-permute-start | bytes 786440 | tf_op jit(solution)/shard_map/ppermute | solution.py:573
  152.7 18.5 %collective-permute-start.48 = (bf16[128,1280]{1,0:T(8,128)(2,1)}, bf16[128,1280]{1,0:T(8,128)(2,1)S(1)}, u32[]{:S(2)}, u32[]{:S(2)}) collective-permute-start(bf16[128,1280]{1,0:T(8,128)(2,1)} %collective-permute-done.5.cl.refs_4_), channel_id=1, source_target_pairs={{0,4},{4,0},{8,12},{12,8},{16,20},{20,16},{24,28},{28,24},{32,36},... | collective-permute-start | bytes 983048 | tf_op jit(solution)/shard_map/ppermute | solution.py:573
  165.4 6.3 %collective-permute-start.46 = (bf16[128,1280]{1,0:T(8,128)(2,1)S(1)}, bf16[128,1280]{1,0:T(8,128)(2,1)S(1)}, u32[]{:S(2)}, u32[]{:S(2)}) collective-permute-start(bf16[128,1280]{1,0:T(8,128)(2,1)S(1)} %collective-permute-done.7.bl.refs_2_), channel_id=1, source_target_pairs={{0,4},{4,0},{8,12},{12,8},{16,20},{20,16},{24,28},{28,24},{32,36},... | collective-permute-start | bytes 983048 | tf_op jit(solution)/shard_map/ppermute | solution.py:573
  167.2 4.5 %collective-permute-start.47 = (bf16[128,1280]{1,0:T(8,128)(2,1)S(1)}, bf16[128,1280]{1,0:T(8,128)(2,1)S(1)}, u32[]{:S(2)}, u32[]{:S(2)}) collective-permute-start(bf16[128,1280]{1,0:T(8,128)(2,1)S(1)} %collective-permute-done.8.ct.refs_3_), channel_id=1, source_target_pairs={{0,4},{4,0},{8,12},{12,8},{16,20},{20,16},{24,28},{28,24},{32,36},... | collective-permute-start | bytes 983048 | tf_op jit(solution)/shard_map/ppermute | solution.py:573
  167.6 4.0 %collective-permute-start.49 = (bf16[128,1280]{1,0:T(8,128)(2,1)S(1)}, bf16[128,1280]{1,0:T(8,128)(2,1)S(1)}, u32[]{:S(2)}, u32[]{:S(2)}) collective-permute-start(bf16[128,1280]{1,0:T(8,128)(2,1)S(1)} %collective-permute-done.4.a.refs_5_), channel_id=1, source_target_pairs={{0,4},{4,0},{8,12},{12,8},{16,20},{20,16},{24,28},{28,24},{32,36},... | collective-permute-start | bytes 983048 | tf_op jit(solution)/shard_map/ppermute | solution.py:573
  169.9 2.4 collective-permute-start.50
  171.3 3.8 %collective-permute-start.41 = (bf16[256,256]{1,0:T(8,128)(2,1)S(1)}, bf16[256,256]{1,0:T(8,128)(2,1)S(1)}, u32[]{:S(2)}, u32[]{:S(2)}) collective-permute-start(bf16[256,256]{1,0:T(8,128)(2,1)S(1)} %get-tuple-element.105), channel_id=1, source_target_pairs={{0,4},{4,0},{8,12},{12,8},{16,20},{20,16},{24,28},{28,24},{32,36},... | collective-permute-start | bytes 393224 | tf_op jit(solution)/shard_map/ppermute | solution.py:573
  179.8 10.2 %collective-permute-start.51 = (bf16[8,160,128]{2,1,0:T(8,128)(2,1)S(1)}, bf16[8,160,128]{2,1,0:T(8,128)(2,1)S(1)}, u32[]{:S(2)}, u32[]{:S(2)}) collective-permute-start(bf16[8,160,128]{2,1,0:T(8,128)(2,1)S(1)} %get-tuple-element.118), channel_id=1, source_target_pairs={{0,8},{4,12},{8,16},{12,20},{16,24},{20,28},{24,0},{28,4},{32,40},... | collective-permute-start | bytes 983048 | tf_op jit(solution)/shard_map/ppermute | solution.py:573
  179.8 16.2 %collective-permute-start.52 = (bf16[8,160,128]{2,1,0:T(8,128)(2,1)S(1)}, bf16[8,160,128]{2,1,0:T(8,128)(2,1)S(1)}, u32[]{:S(2)}, u32[]{:S(2)}) collective-permute-start(bf16[8,160,128]{2,1,0:T(8,128)(2,1)S(1)} %get-tuple-element.119), channel_id=1, source_target_pairs={{0,24},{4,28},{8,0},{12,4},{16,8},{20,12},{24,16},{28,20},{32,56},... | collective-permute-start | bytes 983048 | tf_op jit(solution)/shard_map/ppermute | solution.py:573
  183.5 37.9 %collective-permute-start.28 = (bf16[256,1280]{1,0:T(8,128)(2,1)}, bf16[256,1280]{1,0:T(8,128)(2,1)}, u32[]{:S(2)}, u32[]{:S(2)}) collective-permute-start(bf16[256,1280]{1,0:T(8,128)(2,1)} %slice.16), channel_id=1, source_target_pairs={{0,4},{4,0},{8,12},{12,8},{16,20},{20,16},{24,28},{28,24},{32,36},... | collective-permute-start | bytes 1966088 | tf_op jit(solution)/shard_map/ppermute | solution.py:573
  184.3 13.8 %collective-permute-start.53 = (bf16[8,160,128]{2,1,0:T(8,128)(2,1)S(1)}, bf16[8,160,128]{2,1,0:T(8,128)(2,1)S(1)}, u32[]{:S(2)}, u32[]{:S(2)}) collective-permute-start(bf16[8,160,128]{2,1,0:T(8,128)(2,1)S(1)} %get-tuple-element.120), channel_id=1, source_target_pairs={{0,16},{4,20},{8,24},{12,28},{16,0},{20,4},{24,8},{28,12},{32,48},... | collective-permute-start | bytes 983048 | tf_op jit(solution)/shard_map/ppermute | solution.py:573
  185.3 12.9 %collective-permute-start.54 = (bf16[8,160,128]{2,1,0:T(8,128)(2,1)S(1)}, bf16[8,160,128]{2,1,0:T(8,128)(2,1)S(1)}, u32[]{:S(2)}, u32[]{:S(2)}) collective-permute-start(bf16[8,160,128]{2,1,0:T(8,128)(2,1)S(1)} %get-tuple-element.122), channel_id=1, source_target_pairs={{0,32},{4,36},{8,40},{12,44},{16,48},{20,52},{24,56},{28,60},{32,6... | collective-permute-start | bytes 983048 | tf_op jit(solution)/shard_map/ppermute | solution.py:573
  190.0 8.2 %collective-permute-start.55 = (bf16[8,160,128]{2,1,0:T(8,128)(2,1)S(1)}, bf16[8,160,128]{2,1,0:T(8,128)(2,1)S(1)}, u32[]{:S(2)}, u32[]{:S(2)}) collective-permute-start(bf16[8,160,128]{2,1,0:T(8,128)(2,1)S(1)} %get-tuple-element.123), channel_id=1, source_target_pairs={{0,96},{4,100},{8,104},{12,108},{16,112},{20,116},{24,120},{28,124... | collective-permute-start | bytes 983048 | tf_op jit(solution)/shard_map/ppermute | solution.py:573
  196.0 9.2 %collective-permute-start.56 = (bf16[8,160,128]{2,1,0:T(8,128)(2,1)S(1)}, bf16[8,160,128]{2,1,0:T(8,128)(2,1)S(1)}, u32[]{:S(2)}, u32[]{:S(2)}) collective-permute-start(bf16[8,160,128]{2,1,0:T(8,128)(2,1)S(1)} %get-tuple-element.124), channel_id=1, source_target_pairs={{0,64},{4,68},{8,72},{12,76},{16,80},{20,84},{24,88},{28,92},{32,9... | collective-permute-start | bytes 983048 | tf_op jit(solution)/shard_map/ppermute | solution.py:573
  208.8 13.8 %collective-permute-start.57 = (f32[2,160,128]{2,1,0:T(8,128)}, f32[2,160,128]{2,1,0:T(8,128)S(1)}, u32[]{:S(2)}, u32[]{:S(2)}) collective-permute-start(f32[2,160,128]{2,1,0:T(8,128)} %get-tuple-element.126), channel_id=1, source_target_pairs={{0,32},{4,36},{8,40},{12,44},{16,48},{20,52},{24,56},{28,60},{32,6... | collective-permute-start | bytes 491528 | tf_op jit(solution)/shard_map/ppermute | solution.py:573
  209.9 14.1 %collective-permute-start.58 = (f32[2,160,128]{2,1,0:T(8,128)}, f32[2,160,128]{2,1,0:T(8,128)S(1)}, u32[]{:S(2)}, u32[]{:S(2)}) collective-permute-start(f32[2,160,128]{2,1,0:T(8,128)} %get-tuple-element.127), channel_id=1, source_target_pairs={{0,96},{4,100},{8,104},{12,108},{16,112},{20,116},{24,120},{28,124... | collective-permute-start | bytes 491528 | tf_op jit(solution)/shard_map/ppermute | solution.py:573
  217.1 29.5 %collective-permute-start.42 = (bf16[256,1280]{1,0:T(8,128)(2,1)S(1)}, bf16[256,1280]{1,0:T(8,128)(2,1)S(1)}, u32[]{:S(2)}, u32[]{:S(2)}) collective-permute-start(bf16[256,1280]{1,0:T(8,128)(2,1)S(1)} %get-tuple-element.109), channel_id=1, source_target_pairs={{0,1},{1,2},{2,3},{3,0},{4,5},{5,6},{6,7},{7,4},{8,9},{9,10},{10,1... | collective-permute-start | bytes 1966088 | tf_op jit(solution)/shard_map/ppermute | solution.py:573
  219.5 27.2 %collective-permute-start.43 = (bf16[256,1280]{1,0:T(8,128)(2,1)S(1)}, bf16[256,1280]{1,0:T(8,128)(2,1)S(1)}, u32[]{:S(2)}, u32[]{:S(2)}) collective-permute-start(bf16[256,1280]{1,0:T(8,128)(2,1)S(1)} %get-tuple-element.110), channel_id=1, source_target_pairs={{0,3},{1,0},{2,1},{3,2},{4,7},{5,4},{6,5},{7,6},{8,11},{9,8},{10,9... | collective-permute-start | bytes 1966088 | tf_op jit(solution)/shard_map/ppermute | solution.py:573
  221.4 27.3 %collective-permute-start.44 = (bf16[256,1280]{1,0:T(8,128)(2,1)S(1)}, bf16[256,1280]{1,0:T(8,128)(2,1)S(1)}, u32[]{:S(2)}, u32[]{:S(2)}) collective-permute-start(bf16[256,1280]{1,0:T(8,128)(2,1)S(1)} %get-tuple-element.111), channel_id=1, source_target_pairs={{0,2},{1,3},{2,0},{3,1},{4,6},{5,7},{6,4},{7,5},{8,10},{9,11},{10,... | collective-permute-start | bytes 1966088 | tf_op jit(solution)/shard_map/ppermute | solution.py:573
  222.6 5.7 %collective-permute-start.59 = (f32[2,160,128]{2,1,0:T(8,128)S(1)}, f32[2,160,128]{2,1,0:T(8,128)S(1)}, u32[]{:S(2)}, u32[]{:S(2)}) collective-permute-start(f32[2,160,128]{2,1,0:T(8,128)S(1)} %copy-done.21), channel_id=1, source_target_pairs={{0,64},{4,68},{8,72},{12,76},{16,80},{20,84},{24,88},{28,92},{32,9... | collective-permute-start | bytes 491528 | tf_op jit(solution)/shard_map/ppermute | solution.py:573
  224.1 8.1 %collective-permute-start.60 = (f32[2,160,128]{2,1,0:T(8,128)S(1)}, f32[2,160,128]{2,1,0:T(8,128)S(1)}, u32[]{:S(2)}, u32[]{:S(2)}) collective-permute-start(f32[2,160,128]{2,1,0:T(8,128)S(1)} %copy-done.19), channel_id=1, source_target_pairs={{0,8},{4,12},{8,16},{12,20},{16,24},{20,28},{24,0},{28,4},{32,40},... | collective-permute-start | bytes 491528 | tf_op jit(solution)/shard_map/ppermute | solution.py:573
  228.3 7.9 %collective-permute-start.61 = (f32[2,160,128]{2,1,0:T(8,128)S(1)}, f32[2,160,128]{2,1,0:T(8,128)S(1)}, u32[]{:S(2)}, u32[]{:S(2)}) collective-permute-start(f32[2,160,128]{2,1,0:T(8,128)S(1)} %copy-done.17), channel_id=1, source_target_pairs={{0,24},{4,28},{8,0},{12,4},{16,8},{20,12},{24,16},{28,20},{32,56},... | collective-permute-start | bytes 491528 | tf_op jit(solution)/shard_map/ppermute | solution.py:573
  232.2 5.7 %collective-permute-start.62 = (f32[2,160,128]{2,1,0:T(8,128)S(1)}, f32[2,160,128]{2,1,0:T(8,128)S(1)}, u32[]{:S(2)}, u32[]{:S(2)}) collective-permute-start(f32[2,160,128]{2,1,0:T(8,128)S(1)} %copy-done.15), channel_id=1, source_target_pairs={{0,16},{4,20},{8,24},{12,28},{16,0},{20,4},{24,8},{28,12},{32,48},... | collective-permute-start | bytes 491528 | tf_op jit(solution)/shard_map/ppermute | solution.py:573
  237.9 7.4 %collective-permute-start.63 = (f32[160,256]{1,0:T(8,128)S(1)}, f32[160,256]{1,0:T(8,128)S(1)}, u32[]{:S(2)}, u32[]{:S(2)}) collective-permute-start(f32[160,256]{1,0:T(8,128)S(1)} %get-tuple-element.134), channel_id=1, source_target_pairs={{0,4},{4,0},{8,12},{12,8},{16,20},{20,16},{24,28},{28,24},{32,36},... | collective-permute-start | bytes 491528 | tf_op jit(solution)/shard_map/ppermute | solution.py:573
  (22 other events, 317.2 us)

commit v2 on v1

--- a/solution.py
+++ b/solution.py
@@ -44,7 +44,7 @@
         place[4] = core
         for k, o in enumerate(OFFSETS):
             place[5 + k] = (tp + o) % 4
-            place[9 + k] = side((tp + o - y + 4) % 4)
+            place[9 + k] = side((y + o - tp + 4) % 4)
             place[13 + k] = (x + o) % 4
         table[AT_CORE] = core
 
@@ -138,23 +138,16 @@
 def halve(value):
     half = value.shape[0] // 2
 
-    def body(source, top, low, sems):
-        copies = [
-            pltpu.make_async_copy(source.at[pl.ds(k * half, half)], out, sems.at[k])
-            for k, out in enumerate((top, low))
-        ]
-        for copy in copies:
-            copy.start()
-        for copy in copies:
-            copy.wait()
-
-    anywhere = pl.BlockSpec(memory_space=pl.ANY)
-    return pl.pallas_call(
-        body,
-        in_specs=[anywhere],
-        out_specs=[anywhere] * 2,
+    def body(source, top, low):
+        top[...] = source[:half]
+        low[...] = source[half:]
+
+    return pl.pallas_call(
+        body,
+        in_specs=[pl.BlockSpec(memory_space=pltpu.VMEM)],
+        out_specs=[pl.BlockSpec(memory_space=pltpu.VMEM)] * 2,
         out_shape=[jax.ShapeDtypeStruct((half, value.shape[1]), value.dtype)] * 2,
-        scratch_shapes=[pltpu.SemaphoreType.DMA((2,))],
+        compiler_params=params(3),
         name="halve",
     )(value)
 
@@ -516,57 +509,52 @@
     rows = 4 * BLOCK
 
     def body(*refs):
-        mine, other, outs = refs[:7], refs[7:14], refs[14:]
+        mine, other, out = refs[:7], refs[7:14], refs[14]
         for piece in range(4):
             at = slice(max(2 * piece - 1, 0), 2 * piece + 1)
             features = jnp.concatenate([r[...] for r in mine[at] + other[at]], axis=0)
-            outs[piece][...] = features.T
+            out[piece] = features.T
 
     return pl.pallas_call(
         body,
         in_specs=[pl.BlockSpec(memory_space=pltpu.VMEM)] * 14,
-        out_specs=[pl.BlockSpec(memory_space=pltpu.VMEM)] * 4,
-        out_shape=[jax.ShapeDtypeStruct((width, rows), BF)] * 4,
+        out_specs=pl.BlockSpec(memory_space=pltpu.VMEM),
+        out_shape=jax.ShapeDtypeStruct((4, width, rows), BF),
         compiler_params=params(12),
         name="flip",
     )(*own, *peer)
 
 
 def weight_partials(place, grads, features):
-    width = features[0].shape[0]
+    width = features.shape[1]
     share = width // 8
 
-    def body(p, g, *refs):
-        k_outs, v_outs, result = refs[4:8], refs[8:12], refs[12]
+    def body(p, g, ft, *refs):
+        k_outs, v_outs, result = refs[:4], refs[4:8], refs[8]
         core = p[4]
         grad = g[...]
-        for piece in range(4):
-            result[...] = nn(refs[piece][...], grad)
-            line = p[9 + piece]
+        for dy in range(4):
+            result[...] = nn(ft[p[9 + dy]], grad)
             for dx in range(4):
                 base = p[13 + dx] * (2 * share)
                 for r in range(2):
                     start = pl.multiple_of(base + ((core + r) % 2) * share, 16)
                     value = result[pl.ds(start, share), :]
-                    k_outs[dx][line * 2 + r] = value[:, :HD].astype(k_outs[dx].dtype)
-                    for dy in range(4):
-
-                        @pl.when(line == dy)
-                        def _(dy=dy, dx=dx, r=r, value=value):
-                            v_outs[dy][dx * 2 + r] = value[:, HD:].astype(v_outs[dy].dtype)
+                    k_outs[dx][dy * 2 + r] = value[:, :HD].astype(k_outs[dx].dtype)
+                    v_outs[dy][dx * 2 + r] = value[:, HD:].astype(v_outs[dy].dtype)
 
     wide = (8, share, HD)
     shapes = [(wide, F32)] + [(wide, BF)] * 3
     return pl.pallas_call(
         body,
         in_specs=[pl.BlockSpec(memory_space=pltpu.SMEM)]
-        + [pl.BlockSpec(memory_space=pltpu.VMEM)] * 5,
+        + [pl.BlockSpec(memory_space=pltpu.VMEM)] * 2,
         out_specs=[pl.BlockSpec(memory_space=pltpu.VMEM)] * 8,
         out_shape=[jax.ShapeDtypeStruct(s, d) for s, d in shapes + shapes],
         scratch_shapes=[pltpu.VMEM((width, 2 * HD), F32)],
         compiler_params=params(11),
         name="weight_partials",
-    )(place, grads, *features)
+    )(place, grads, features)
 
 
 def mover(axis, pairs):
@@ -631,8 +619,10 @@
     right_top = zb(top)
     far_top = zn(left_top)
     far_low = zb(right_low)
-    query_peer = swap(lax.dynamic_slice_in_dim(queries, (1 - core) * width, width, 1))
-    upstream_peer = swap(lax.dynamic_slice_in_dim(upstream, (1 - core) * width, width, 1))
+    query_away = lax.dynamic_slice_in_dim(queries, (1 - core) * width, width, 1)
+    upstream_away = lax.dynamic_slice_in_dim(upstream, (1 - core) * width, width, 1)
+    query_peer = swap(query_away)
+    upstream_peer = swap(upstream_away)
     hidden_peer = swap(hidden)
     place, hidden_peer, query_peer, upstream_peer = lax.optimization_barrier(
         (place, hidden_peer, query_peer, upstream_peer)

time: 254 us -> 233 us (0.917)
  Pallas kernels: 55.7 us -> 34.2 us
  waiting for transfers between devices: 61.9 us -> 65 us
  starting transfers between devices: 112 us -> 109 us
    pallas_call x1, Pallas kernels: 21 us -> 0.87 us  [halve(): pl.pallas_call(body, in_specs=[pl.BlockSpec(memory_space=pltpu.VMEM)], ou...]
    ppermute x64, waiting for transfers between devices: 61.9 us -> 65 us  [mover(): return lambda value: lax.ppermute(value, axis, pairs)]
    ppermute x64, starting transfers between devices: 112 us -> 109 us  [mover(): return lambda value: lax.ppermute(value, axis, pairs)]
    unnamed x44 -> x48, local copies, waits for them, and re-layouts: 8.16 us -> 8.42 us
  transfers between devices with their start and end apart: 64 -> 64, of which waited for: 26 -> 23; matrix products, arithmetic and copies ran while one was open for 3% -> 4% of each run, Pallas kernels for 14% -> 7%
where the time goes in v2:
time: 233 us; the launch traced here: 229 us
  starting transfers between devices  109 us (47%)
  waiting for transfers between devices  65 us (28%)
  Pallas kernels  34.2 us (15%)
  local copies, waits for them, and re-layouts  12.8 us (5%)
  other arithmetic  6.79 us (3%)
    ppermute x64, starting transfers between devices, mover(): return lambda value: lax.ppermute(value, axis, pairs)  109 us
    ppermute x64, waiting for transfers between devices, mover(): return lambda value: lax.ppermute(value, axis, pairs)  65 us
    pallas_call x1, Pallas kernels, attend(): pl.pallas_call(body, grid_spec=pltpu.PrefetchScalarGridSpec(num_scalar_pr...  14.6 us
    unnamed x48, local copies, waits for them, and re-layouts  8.42 us
  transfers between devices with their start and end apart: 64, of which 23 were waited for; matrix products, arithmetic and copies ran while one was open for 4% of the time, Pallas kernels for 7%

profile of v2, /device:TPU:1, one launch (start us, length us, event | category | flops | bytes accessed | tf_op | source)
XLA Modules:
  0.0 228.8 jit_solution(2468152508145564952)
XLA Ops:
  0.7 1.8 constant_dynamic-slice_fusion.1
  2.5 1.4 collective-permute-start.1
  3.8 1.7 constant_dynamic-slice_fusion
  6.9 1.7 collective-permute-start.3
  8.7 2.1 collective-permute-start.5
  11.5 2.6 %device_tables.1 = (s32[115]{0:T(128)}, s32[17]{0:T(128)}, s32[4]{0:T(128)}) custom-call(s32[64]{0:T(128)} %links.1, s32[4]{0:T(128)} %pad_add_fusion.where), custom_call_target="tpu_custom_call" | custom-call | tf_op jit(solution)/shard_map/device_tables/pallas_call | solution.py:89
  14.9 2.7 %collective-permute-start.8 = (bf16[128,1280]{1,0:T(8,128)(2,1)}, bf16[128,1280]{1,0:T(8,128)(2,1)S(1)}, u32[]{:S(2)}, u32[]{:S(2)}) collective-permute-start(bf16[128,1280]{1,0:T(8,128)(2,1)} %get-tuple-element.72), channel_id=1, source_target_pairs={{0,3},{1,0},{2,1},{3,2},{4,7},{5,4},{6,5},{7,6},{8,11},{9,8},{10,9... | collective-permute-start | bytes 983048 | tf_op jit(solution)/shard_map/ppermute | solution.py:561
  17.5 1.6 collective-permute-done.3.bt.refs_1_
  19.1 2.7 %collective-permute-start.6 = (bf16[128,1280]{1,0:T(8,128)(2,1)}, bf16[128,1280]{1,0:T(8,128)(2,1)S(1)}, u32[]{:S(2)}, u32[]{:S(2)}) collective-permute-start(bf16[128,1280]{1,0:T(8,128)(2,1)} %collective-permute-done.5.cl.refs_4_), channel_id=1, source_target_pairs={{0,3},{1,0},{2,1},{3,2},{4,7},{5,4},{6,5},{7,6},{8,11},{9,8},{10,9... | collective-permute-start | bytes 983048 | tf_op jit(solution)/shard_map/ppermute | solution.py:561
  23.0 2.8 %collective-permute-done.7.bl.refs_2_ = bf16[128,1280]{1,0:T(8,128)(2,1)S(1)} collective-permute-done((bf16[128,1280]{1,0:T(8,128)(2,1)}, bf16[128,1280]{1,0:T(8,128)(2,1)S(1)}, u32[]{:S(2)}, u32[]{:S(2)}) %collective-permute-start.7) | collective-permute-done | bytes 327712 | tf_op jit(solution)/shard_map/ppermute | solution.py:561
  25.8 1.7 copy-done.1
  27.6 2.8 %project_near.1 = (f32[256,256]{1,0:T(8,128)S(1)}, f32[256,256]{1,0:T(8,128)S(1)}) custom-call(s32[17]{0:T(128)S(1)} %copy-done.14, bf16[256,1280]{1,0:T(8,128)(2,1)S(1)} %copy-done.3, bf16[128,1280]{1,0:T(8,128)(2,1)} %collective-permute-done.3.bt.refs_1_, bf16[128,1280]{1,0:T(8,128)(2,1)S(1)} %collective-permute-done.7.bl.refs_2_, ...), custom_call_target="tpu_custom_call" | custom-call | tf_op jit(solution)/shard_map/project_near/pallas_call | solution.py:169
  30.3 2.5 %collective-permute-done.4.a.refs_5_ = bf16[128,1280]{1,0:T(8,128)(2,1)S(1)} collective-permute-done((bf16[128,1280]{1,0:T(8,128)(2,1)}, bf16[128,1280]{1,0:T(8,128)(2,1)S(1)}, u32[]{:S(2)}, u32[]{:S(2)}) %collective-permute-start.4) | collective-permute-done | bytes 327712 | tf_op jit(solution)/shard_map/ppermute | solution.py:561
  32.8 1.1 project_far.1
  34.0 2.5 %collective-permute-start.10 = (bf16[256,256]{1,0:T(8,128)(2,1)S(1)}, bf16[256,256]{1,0:T(8,128)(2,1)S(1)}, u32[]{:S(2)}, u32[]{:S(2)}) collective-permute-start(bf16[256,256]{1,0:T(8,128)(2,1)S(1)} %get-tuple-element.77.a), channel_id=1, source_target_pairs={{0,24},{4,28},{8,0},{12,4},{16,8},{20,12},{24,16},{28,20},{32,56},... | collective-permute-start | bytes 393224 | tf_op jit(solution)/shard_map/ppermute | solution.py:561
  37.6 1.7 collective-permute-start.18
  39.4 2.5 %collective-permute-done.11.d = bf16[256,256]{1,0:T(8,128)(2,1)S(1)} collective-permute-done((bf16[256,256]{1,0:T(8,128)(2,1)S(1)}, bf16[256,256]{1,0:T(8,128)(2,1)S(1)}, u32[]{:S(2)}, u32[]{:S(2)}) %collective-permute-start.11) | collective-permute-done | bytes 131104 | tf_op jit(solution)/shard_map/ppermute | solution.py:561
  41.9 3.9 %collective-permute-done.9.b = bf16[256,256]{1,0:T(8,128)(2,1)S(1)} collective-permute-done((bf16[256,256]{1,0:T(8,128)(2,1)S(1)}, bf16[256,256]{1,0:T(8,128)(2,1)S(1)}, u32[]{:S(2)}, u32[]{:S(2)}) %collective-permute-start.9) | collective-permute-done | bytes 131104 | tf_op jit(solution)/shard_map/ppermute | solution.py:561
  45.9 1.4 collective-permute-start.12
  47.3 1.5 collective-permute-start.15
  48.8 2.7 %collective-permute-start.20 = (bf16[256,256]{1,0:T(8,128)(2,1)S(1)}, bf16[256,256]{1,0:T(8,128)(2,1)S(1)}, u32[]{:S(2)}, u32[]{:S(2)}) collective-permute-start(bf16[256,256]{1,0:T(8,128)(2,1)S(1)} %collective-permute-done.18.a), channel_id=1, source_target_pairs={{0,96},{4,100},{8,104},{12,108},{16,112},{20,116},{24,120},{28,124... | collective-permute-start | bytes 393224 | tf_op jit(solution)/shard_map/ppermute | solution.py:561
  51.8 5.3 %collective-permute-done.19.b = bf16[256,256]{1,0:T(8,128)(2,1)S(1)} collective-permute-done((bf16[256,256]{1,0:T(8,128)(2,1)S(1)}, bf16[256,256]{1,0:T(8,128)(2,1)S(1)}, u32[]{:S(2)}, u32[]{:S(2)}) %collective-permute-start.19) | collective-permute-done | bytes 131104 | tf_op jit(solution)/shard_map/ppermute | solution.py:561
  57.1 3.0 %collective-permute-start.14 = (bf16[4,128,256]{2,1,0:T(8,128)(2,1)S(1)}, bf16[4,128,256]{2,1,0:T(8,128)(2,1)S(1)}, u32[]{:S(2)}, u32[]{:S(2)}) collective-permute-start(bf16[4,128,256]{2,1,0:T(8,128)(2,1)S(1)} %get-tuple-element.78.refs_0_), channel_id=1, source_target_pairs={{0,96},{4,100},{8,104},{12,108},{16,112},{20,116},{24,120},{28,124... | collective-permute-start | bytes 786440 | tf_op jit(solution)/shard_map/ppermute | solution.py:561
  61.1 2.7 %collective-permute-start.25 = (bf16[4,128,256]{2,1,0:T(8,128)(2,1)S(1)}, bf16[4,128,256]{2,1,0:T(8,128)(2,1)S(1)}, u32[]{:S(2)}, u32[]{:S(2)}) collective-permute-start(bf16[4,128,256]{2,1,0:T(8,128)(2,1)S(1)} %get-tuple-element.82.refs_9_), channel_id=1, source_target_pairs={{0,24},{4,28},{8,0},{12,4},{16,8},{20,12},{24,16},{28,20},{32,56},... | collective-permute-start | bytes 786440 | tf_op jit(solution)/shard_map/ppermute | solution.py:561
  63.8 3.0 %collective-permute-done.13.refs_3_ = bf16[4,128,256]{2,1,0:T(8,128)(2,1)S(1)} collective-permute-done((bf16[4,128,256]{2,1,0:T(8,128)(2,1)S(1)}, bf16[4,128,256]{2,1,0:T(8,128)(2,1)S(1)}, u32[]{:S(2)}, u32[]{:S(2)}) %collective-permute-start.13) | collective-permute-done | bytes 262176 | tf_op jit(solution)/shard_map/ppermute | solution.py:561
  67.8 1.7 collective-permute-start.17
  69.5 1.5 collective-permute-start.26
  71.0 1.7 collective-permute-done.23.refs_11_
  72.7 1.9 collective-permute-done.24.refs_12_
  74.6 4.4 %collective-permute-done.26.refs_14_ = bf16[4,128,256]{2,1,0:T(8,128)(2,1)S(1)} collective-permute-done((bf16[4,128,256]{2,1,0:T(8,128)(2,1)S(1)}, bf16[4,128,256]{2,1,0:T(8,128)(2,1)S(1)}, u32[]{:S(2)}, u32[]{:S(2)}) %collective-permute-start.26) | collective-permute-done | bytes 262176 | tf_op jit(solution)/shard_map/ppermute | solution.py:561
  79.1 14.6 %attend.1 = (bf16[512,1280]{1,0:T(8,128)(2,1)S(1)}, f32[16,128,128]{2,1,0:T(8,128)S(1)}, bf16[16,128,128]{2,1,0:T(8,128)(2,1)S(1)}, bf16[16,128,128]{2,1,0:T(8,1...) custom-call(s32[115]{0:T(128)S(1)} %copy-done.15, ...), custom_call_target="tpu_custom_call" | custom-call | tf_op jit(solution)/shard_map/attend/pallas_call | solution.py:382
  93.8 2.7 %collective-permute-start.30 = (bf16[16,128,128]{2,1,0:T(8,128)(2,1)S(1)}, bf16[16,128,128]{2,1,0:T(8,128)(2,1)S(1)}, u32[]{:S(2)}, u32[]{:S(2)}) collective-permute-start(bf16[16,128,128]{2,1,0:T(8,128)(2,1)S(1)} %get-tuple-element.86), channel_id=1, source_target_pairs={{0,24},{4,28},{8,0},{12,4},{16,8},{20,12},{24,16},{28,20},{32,56},... | collective-permute-start | bytes 1572872 | tf_op jit(solution)/shard_map/ppermute | solution.py:561
  98.6 1.7 collective-permute-start.33
  100.3 2.7 %collective-permute-done.29.refs_1_ = bf16[16,128,128]{2,1,0:T(8,128)(2,1)S(1)} collective-permute-done((bf16[16,128,128]{2,1,0:T(8,128)(2,1)S(1)}, bf16[16,128,128]{2,1,0:T(8,128)(2,1)S(1)}, u32[]{:S(2)}, u32[]{:S(2)}) %collective-permute-start.29) | collective-permute-done | bytes 524320 | tf_op jit(solution)/shard_map/ppermute | solution.py:561
  103.8 2.4 %collective-permute-done.30.refs_2_ = bf16[16,128,128]{2,1,0:T(8,128)(2,1)S(1)} collective-permute-done((bf16[16,128,128]{2,1,0:T(8,128)(2,1)S(1)}, bf16[16,128,128]{2,1,0:T(8,128)(2,1)S(1)}, u32[]{:S(2)}, u32[]{:S(2)}) %collective-permute-start.30) | collective-permute-done | bytes 524320 | tf_op jit(solution)/shard_map/ppermute | solution.py:561
  106.2 16.9 %collective-permute-start.45 = (bf16[128,1280]{1,0:T(8,128)(2,1)}, bf16[128,1280]{1,0:T(8,128)(2,1)S(1)}, u32[]{:S(2)}, u32[]{:S(2)}) collective-permute-start(bf16[128,1280]{1,0:T(8,128)(2,1)} %collective-permute-done.3.bt.refs_1_), channel_id=1, source_target_pairs={{0,4},{4,0},{8,12},{12,8},{16,20},{20,16},{24,28},{28,24},{32,36},... | collective-permute-start | bytes 983048 | tf_op jit(solution)/shard_map/ppermute | solution.py:561
  123.5 1.1 collective-permute-start.35
  124.6 1.6 collective-permute-start.36
  127.3 2.7 %collective-permute-start.39 = (f32[4,128,128]{2,1,0:T(8,128)S(1)}, f32[4,128,128]{2,1,0:T(8,128)S(1)}, u32[]{:S(2)}, u32[]{:S(2)}) collective-permute-start(f32[4,128,128]{2,1,0:T(8,128)S(1)} %get-tuple-element.98), channel_id=1, source_target_pairs={{0,24},{4,28},{8,0},{12,4},{16,8},{20,12},{24,16},{28,20},{32,56},... | collective-permute-start | bytes 786440 | tf_op jit(solution)/shard_map/ppermute | solution.py:561
  129.9 7.9 %collective-permute-done.35.refs_1_ = f32[4,128,128]{2,1,0:T(8,128)S(1)} collective-permute-done((f32[4,128,128]{2,1,0:T(8,128)S(1)}, f32[4,128,128]{2,1,0:T(8,128)S(1)}, u32[]{:S(2)}, u32[]{:S(2)}) %collective-permute-start.35) | collective-permute-done | bytes 262176 | tf_op jit(solution)/shard_map/ppermute | solution.py:561
  137.9 10.6 %collective-permute-start.48 = (bf16[128,1280]{1,0:T(8,128)(2,1)}, bf16[128,1280]{1,0:T(8,128)(2,1)S(1)}, u32[]{:S(2)}, u32[]{:S(2)}) collective-permute-start(bf16[128,1280]{1,0:T(8,128)(2,1)} %collective-permute-done.5.cl.refs_4_), channel_id=1, source_target_pairs={{0,4},{4,0},{8,12},{12,8},{16,20},{20,16},{24,28},{28,24},{32,36},... | collective-permute-start | bytes 983048 | tf_op jit(solution)/shard_map/ppermute | solution.py:561
  148.5 1.2 collective-permute-start.46
  150.1 1.6 collective-permute-start.49
  151.7 2.3 collective-permute-start.50
  155.3 2.7 %flip.1.ft = bf16[4,1280,512]{2,1,0:T(8,128)(2,1)S(1)} custom-call(bf16[256,1280]{1,0:T(8,128)(2,1)S(1)} %copy-done.3, bf16[128,1280]{1,0:T(8,128)(2,1)} %collective-permute-done.3.bt.refs_1_, bf16[128,1280]{1,0:T(8,128)(2,1)S(1)} %collective-permute-done.7.bl.refs_2_, bf16[128,1280]{1,0:T(8,128)(2,1)S(1)} %collective-permute-done.8.ct.refs_3_, ...), custom_call_target="tpu_custom_call" | custom-call | tf_op jit(solution)/shard_map/flip/pallas_call | solution.py:518
  158.0 2.5 %weight_partials.1 = (f32[8,160,128]{2,1,0:T(8,128)S(1)}, bf16[8,160,128]{2,1,0:T(8,128)(2,1)S(1)}, bf16[8,160,128]{2,1,0:T(8,128)(2,1)S(1)}, bf16[8,160,128]{2,...) custom-call(s32[17]{0:T(128)S(1)} %copy-done.14, ...), custom_call_target="tpu_custom_call" | custom-call | tf_op jit(solution)/shard_map/weight_partials/pallas_call | solution.py:548
  160.6 2.7 %collective-permute-start.52 = (bf16[8,160,128]{2,1,0:T(8,128)(2,1)S(1)}, bf16[8,160,128]{2,1,0:T(8,128)(2,1)S(1)}, u32[]{:S(2)}, u32[]{:S(2)}) collective-permute-start(bf16[8,160,128]{2,1,0:T(8,128)(2,1)S(1)} %get-tuple-element.111), channel_id=1, source_target_pairs={{0,24},{4,28},{8,0},{12,4},{16,8},{20,12},{24,16},{28,20},{32,56},... | collective-permute-start | bytes 983048 | tf_op jit(solution)/shard_map/ppermute | solution.py:561
  165.5 5.2 %collective-permute-done.51.refs_1_ = bf16[8,160,128]{2,1,0:T(8,128)(2,1)S(1)} collective-permute-done((bf16[8,160,128]{2,1,0:T(8,128)(2,1)S(1)}, bf16[8,160,128]{2,1,0:T(8,128)(2,1)S(1)}, u32[]{:S(2)}, u32[]{:S(2)}) %collective-permute-start.51) | collective-permute-done | bytes 327712 | tf_op jit(solution)/shard_map/ppermute | solution.py:561
  170.9 8.0 %collective-permute-start.56 = (bf16[8,160,128]{2,1,0:T(8,128)(2,1)S(1)}, bf16[8,160,128]{2,1,0:T(8,128)(2,1)S(1)}, u32[]{:S(2)}, u32[]{:S(2)}) collective-permute-start(bf16[8,160,128]{2,1,0:T(8,128)(2,1)S(1)} %get-tuple-element.116), channel_id=1, source_target_pairs={{0,64},{4,68},{8,72},{12,76},{16,80},{20,84},{24,88},{28,92},{32,9... | collective-permute-start | bytes 983048 | tf_op jit(solution)/shard_map/ppermute | solution.py:561
  179.0 5.5 %collective-permute-done.56.refs_7_ = bf16[8,160,128]{2,1,0:T(8,128)(2,1)S(1)} collective-permute-done((bf16[8,160,128]{2,1,0:T(8,128)(2,1)S(1)}, bf16[8,160,128]{2,1,0:T(8,128)(2,1)S(1)}, u32[]{:S(2)}, u32[]{:S(2)}) %collective-permute-start.56) | collective-permute-done | bytes 327712 | tf_op jit(solution)/shard_map/ppermute | solution.py:561
  189.4 3.0 %collective-permute-start.57 = (f32[2,160,128]{2,1,0:T(8,128)}, f32[2,160,128]{2,1,0:T(8,128)}, u32[]{:S(2)}, u32[]{:S(2)}) collective-permute-start(f32[2,160,128]{2,1,0:T(8,128)} %get-tuple-element.118), channel_id=1, source_target_pairs={{0,32},{4,36},{8,40},{12,44},{16,48},{20,52},{24,56},{28,60},{32,6... | collective-permute-start | bytes 491528 | tf_op jit(solution)/shard_map/ppermute | solution.py:561
  193.1 1.7 copy-done.2
  195.8 3.0 %input_partials.1 = (bf16[256,1280]{1,0:T(8,128)(2,1)S(1)}, bf16[256,1280]{1,0:T(8,128)(2,1)S(1)}, bf16[256,1280]{1,0:T(8,128)(2,1)S(1)}, bf16[256,1280]{1,0:T(8,128)(2,1)S(1)}) custom-call(s32[17]{0:T(128)S(1)} %copy-done.14, bf16[512,256]{1,0:T(8,128)(2,1)S(1)} %get-tuple-element.102.a.g, bf16[256,256]{1,0:T(8,128)(2,1)S(1)} %copy-done.13, ...), custom_call_target="tpu_custom_call" | custom-call | tf_op jit(solution)/shard_map/input_partials/pallas_call | solution.py:493
  198.9 2.7 %collective-permute-start.43 = (bf16[256,1280]{1,0:T(8,128)(2,1)S(1)}, bf16[256,1280]{1,0:T(8,128)(2,1)S(1)}, u32[]{:S(2)}, u32[]{:S(2)}) collective-permute-start(bf16[256,1280]{1,0:T(8,128)(2,1)S(1)} %get-tuple-element.106), channel_id=1, source_target_pairs={{0,3},{1,0},{2,1},{3,2},{4,7},{5,4},{6,5},{7,6},{8,11},{9,8},{10,9... | collective-permute-start | bytes 1966088 | tf_op jit(solution)/shard_map/ppermute | solution.py:561
  201.6 1.5 collective-permute-start.59
  203.2 1.3 broadcast_select_fusion.1
  204.4 2.9 %collective-permute-done.59.refs_3_ = f32[2,160,128]{2,1,0:T(8,128)S(1)} collective-permute-done((f32[2,160,128]{2,1,0:T(8,128)S(1)}, f32[2,160,128]{2,1,0:T(8,128)S(1)}, u32[]{:S(2)}, u32[]{:S(2)}) %collective-permute-start.59) | collective-permute-done | bytes 163872 | tf_op jit(solution)/shard_map/ppermute | solution.py:561
  207.3 3.9 %collective-permute-start.61 = (f32[2,160,128]{2,1,0:T(8,128)S(1)}, f32[2,160,128]{2,1,0:T(8,128)S(1)}, u32[]{:S(2)}, u32[]{:S(2)}) collective-permute-start(f32[2,160,128]{2,1,0:T(8,128)S(1)} %copy-done.19), channel_id=1, source_target_pairs={{0,24},{4,28},{8,0},{12,4},{16,8},{20,12},{24,16},{28,20},{32,56},... | collective-permute-start | bytes 491528 | tf_op jit(solution)/shard_map/ppermute | solution.py:561
  212.1 3.1 %collective-permute-done.61.refs_6_ = f32[2,160,128]{2,1,0:T(8,128)S(1)} collective-permute-done((f32[2,160,128]{2,1,0:T(8,128)S(1)}, f32[2,160,128]{2,1,0:T(8,128)S(1)}, u32[]{:S(2)}, u32[]{:S(2)}) %collective-permute-start.61) | collective-permute-done | bytes 163872 | tf_op jit(solution)/shard_map/ppermute | solution.py:561
  215.2 1.7 collective-permute-done.62.refs_7_
  217.9 6.2 %collective-permute-start.63 = (f32[160,256]{1,0:T(8,128)S(1)}, f32[160,256]{1,0:T(8,128)S(1)}, u32[]{:S(2)}, u32[]{:S(2)}) collective-permute-start(f32[160,256]{1,0:T(8,128)S(1)} %get-tuple-element.126), channel_id=1, source_target_pairs={{0,4},{4,0},{8,12},{12,8},{16,20},{20,16},{24,28},{28,24},{32,36},... | collective-permute-start | bytes 491528 | tf_op jit(solution)/shard_map/ppermute | solution.py:561
  225.2 1.3 join_weights.1
  226.5 1.1 collective-permute-done.44
  227.6 1.2 add_convert_fusion
  (140 shorter events, 25.9 us)
Async XLA Ops:
  2.5 12.4 %collective-permute-start.1 = (bf16[256,640]{1,0:T(8,128)(2,1)}, bf16[256,640]{1,0:T(8,128)(2,1)}, u32[]{:S(2)}, u32[]{:S(2)}) collective-permute-start(bf16[256,640]{1,0:T(8,128)(2,1)} %constant_dynamic-slice_fusion.1), channel_id=1, source_target_pairs={{0,4},{4,0},{8,12},{12,8},{16,20},{20,16},{24,28},{28,24},{32,36},... | collective-permute-start | bytes 983048 | tf_op jit(solution)/shard_map/ppermute | solution.py:561
  5.6 9.3 %collective-permute-start.2 = (bf16[256,640]{1,0:T(8,128)(2,1)}, bf16[256,640]{1,0:T(8,128)(2,1)}, u32[]{:S(2)}, u32[]{:S(2)}) collective-permute-start(bf16[256,640]{1,0:T(8,128)(2,1)} %constant_dynamic-slice_fusion), channel_id=1, source_target_pairs={{0,4},{4,0},{8,12},{12,8},{16,20},{20,16},{24,28},{28,24},{32,36},... | collective-permute-start | bytes 983048 | tf_op jit(solution)/shard_map/ppermute | solution.py:561
  5.6 17.4 %collective-permute-start = (bf16[256,1280]{1,0:T(8,128)(2,1)S(1)}, bf16[256,1280]{1,0:T(8,128)(2,1)}, u32[]{:S(2)}, u32[]{:S(2)}) collective-permute-start(bf16[256,1280]{1,0:T(8,128)(2,1)S(1)} %copy-done.3), channel_id=1, source_target_pairs={{0,4},{4,0},{8,12},{12,8},{16,20},{20,16},{24,28},{28,24},{32,36},... | collective-permute-start | bytes 1966088 | tf_op jit(solution)/shard_map/ppermute | solution.py:561
  6.9 12.2 %collective-permute-start.3 = (bf16[128,1280]{1,0:T(8,128)(2,1)}, bf16[128,1280]{1,0:T(8,128)(2,1)}, u32[]{:S(2)}, u32[]{:S(2)}) collective-permute-start(bf16[128,1280]{1,0:T(8,128)(2,1)} %get-tuple-element.72), channel_id=1, source_target_pairs={{0,1},{1,2},{2,3},{3,0},{4,5},{5,6},{6,7},{7,4},{8,9},{9,10},{10,1... | collective-permute-start | bytes 983048 | tf_op jit(solution)/shard_map/ppermute | solution.py:561
  8.7 10.4 %collective-permute-start.5 = (bf16[128,1280]{1,0:T(8,128)(2,1)}, bf16[128,1280]{1,0:T(8,128)(2,1)}, u32[]{:S(2)}, u32[]{:S(2)}) collective-permute-start(bf16[128,1280]{1,0:T(8,128)(2,1)} %get-tuple-element.73), channel_id=1, source_target_pairs={{0,3},{1,0},{2,1},{3,2},{4,7},{5,4},{6,5},{7,6},{8,11},{9,8},{10,9... | collective-permute-start | bytes 983048 | tf_op jit(solution)/shard_map/ppermute | solution.py:561
  14.8 11.0 %collective-permute-start.7 = (bf16[128,1280]{1,0:T(8,128)(2,1)}, bf16[128,1280]{1,0:T(8,128)(2,1)S(1)}, u32[]{:S(2)}, u32[]{:S(2)}) collective-permute-start(bf16[128,1280]{1,0:T(8,128)(2,1)} %get-tuple-element.73), channel_id=1, source_target_pairs={{0,1},{1,2},{2,3},{3,0},{4,5},{5,6},{6,7},{7,4},{8,9},{9,10},{10,1... | collective-permute-start | bytes 983048 | tf_op jit(solution)/shard_map/ppermute | solution.py:561
  14.9 10.9 %collective-permute-start.8 = (bf16[128,1280]{1,0:T(8,128)(2,1)}, bf16[128,1280]{1,0:T(8,128)(2,1)S(1)}, u32[]{:S(2)}, u32[]{:S(2)}) collective-permute-start(bf16[128,1280]{1,0:T(8,128)(2,1)} %get-tuple-element.72), channel_id=1, source_target_pairs={{0,3},{1,0},{2,1},{3,2},{4,7},{5,4},{6,5},{7,6},{8,11},{9,8},{10,9... | collective-permute-start | bytes 983048 | tf_op jit(solution)/shard_map/ppermute | solution.py:561
  19.1 13.7 %collective-permute-start.4 = (bf16[128,1280]{1,0:T(8,128)(2,1)}, bf16[128,1280]{1,0:T(8,128)(2,1)S(1)}, u32[]{:S(2)}, u32[]{:S(2)}) collective-permute-start(bf16[128,1280]{1,0:T(8,128)(2,1)} %collective-permute-done.3.bt.refs_1_), channel_id=1, source_target_pairs={{0,1},{1,2},{2,3},{3,0},{4,5},{5,6},{6,7},{7,4},{8,9},{9,10},{10,1... | collective-permute-start | bytes 983048 | tf_op jit(solution)/shard_map/ppermute | solution.py:561
  19.1 13.7 %collective-permute-start.6 = (bf16[128,1280]{1,0:T(8,128)(2,1)}, bf16[128,1280]{1,0:T(8,128)(2,1)S(1)}, u32[]{:S(2)}, u32[]{:S(2)}) collective-permute-start(bf16[128,1280]{1,0:T(8,128)(2,1)} %collective-permute-done.5.cl.refs_4_), channel_id=1, source_target_pairs={{0,3},{1,0},{2,1},{3,2},{4,7},{5,4},{6,5},{7,6},{8,11},{9,8},{10,9... | collective-permute-start | bytes 983048 | tf_op jit(solution)/shard_map/ppermute | solution.py:561
  34.0 5.4 %collective-permute-start.10 = (bf16[256,256]{1,0:T(8,128)(2,1)S(1)}, bf16[256,256]{1,0:T(8,128)(2,1)S(1)}, u32[]{:S(2)}, u32[]{:S(2)}) collective-permute-start(bf16[256,256]{1,0:T(8,128)(2,1)S(1)} %get-tuple-element.77.a), channel_id=1, source_target_pairs={{0,24},{4,28},{8,0},{12,4},{16,8},{20,12},{24,16},{28,20},{32,56},... | collective-permute-start | bytes 393224 | tf_op jit(solution)/shard_map/ppermute | solution.py:561
  36.5 5.4 %collective-permute-start.11 = (bf16[256,256]{1,0:T(8,128)(2,1)S(1)}, bf16[256,256]{1,0:T(8,128)(2,1)S(1)}, u32[]{:S(2)}, u32[]{:S(2)}) collective-permute-start(bf16[256,256]{1,0:T(8,128)(2,1)S(1)} %get-tuple-element.77.a), channel_id=1, source_target_pairs={{0,16},{4,20},{8,24},{12,28},{16,0},{20,4},{24,8},{28,12},{32,48},... | collective-permute-start | bytes 393224 | tf_op jit(solution)/shard_map/ppermute | solution.py:561
  37.0 8.8 %collective-permute-start.9 = (bf16[256,256]{1,0:T(8,128)(2,1)S(1)}, bf16[256,256]{1,0:T(8,128)(2,1)S(1)}, u32[]{:S(2)}, u32[]{:S(2)}) collective-permute-start(bf16[256,256]{1,0:T(8,128)(2,1)S(1)} %get-tuple-element.77.a), channel_id=1, source_target_pairs={{0,8},{4,12},{8,16},{12,20},{16,24},{20,28},{24,0},{28,4},{32,40},... | collective-permute-start | bytes 393224 | tf_op jit(solution)/shard_map/ppermute | solution.py:561
  37.6 11.1 %collective-permute-start.18 = (bf16[256,256]{1,0:T(8,128)(2,1)S(1)}, bf16[256,256]{1,0:T(8,128)(2,1)S(1)}, u32[]{:S(2)}, u32[]{:S(2)}) collective-permute-start(bf16[256,256]{1,0:T(8,128)(2,1)S(1)} %get-tuple-element.80), channel_id=1, source_target_pairs={{0,4},{4,0},{8,12},{12,8},{16,20},{20,16},{24,28},{28,24},{32,36},... | collective-permute-start | bytes 393224 | tf_op jit(solution)/shard_map/ppermute | solution.py:561
  45.9 15.2 %collective-permute-start.12 = (bf16[4,128,256]{2,1,0:T(8,128)(2,1)S(1)}, bf16[4,128,256]{2,1,0:T(8,128)(2,1)S(1)}, u32[]{:S(2)}, u32[]{:S(2)}) collective-permute-start(bf16[4,128,256]{2,1,0:T(8,128)(2,1)S(1)} %get-tuple-element.78.refs_0_), channel_id=1, source_target_pairs={{0,32},{4,36},{8,40},{12,44},{16,48},{20,52},{24,56},{28,60},{32,6... | collective-permute-start | bytes 786440 | tf_op jit(solution)/shard_map/ppermute | solution.py:561
  47.3 16.5 %collective-permute-start.15 = (bf16[4,128,256]{2,1,0:T(8,128)(2,1)S(1)}, bf16[4,128,256]{2,1,0:T(8,128)(2,1)S(1)}, u32[]{:S(2)}, u32[]{:S(2)}) collective-permute-start(bf16[4,128,256]{2,1,0:T(8,128)(2,1)S(1)} %get-tuple-element.79.refs_1_), channel_id=1, source_target_pairs={{0,96},{4,100},{8,104},{12,108},{16,112},{20,116},{24,120},{28,124... | collective-permute-start | bytes 786440 | tf_op jit(solution)/shard_map/ppermute | solution.py:561
  48.8 8.3 %collective-permute-start.19 = (bf16[256,256]{1,0:T(8,128)(2,1)S(1)}, bf16[256,256]{1,0:T(8,128)(2,1)S(1)}, u32[]{:S(2)}, u32[]{:S(2)}) collective-permute-start(bf16[256,256]{1,0:T(8,128)(2,1)S(1)} %collective-permute-done.18.a), channel_id=1, source_target_pairs={{0,32},{4,36},{8,40},{12,44},{16,48},{20,52},{24,56},{28,60},{32,6... | collective-permute-start | bytes 393224 | tf_op jit(solution)/shard_map/ppermute | solution.py:561
  48.8 8.3 %collective-permute-start.20 = (bf16[256,256]{1,0:T(8,128)(2,1)S(1)}, bf16[256,256]{1,0:T(8,128)(2,1)S(1)}, u32[]{:S(2)}, u32[]{:S(2)}) collective-permute-start(bf16[256,256]{1,0:T(8,128)(2,1)S(1)} %collective-permute-done.18.a), channel_id=1, source_target_pairs={{0,96},{4,100},{8,104},{12,108},{16,112},{20,116},{24,120},{28,124... | collective-permute-start | bytes 393224 | tf_op jit(solution)/shard_map/ppermute | solution.py:561
  51.5 9.5 %collective-permute-start.21 = (bf16[256,256]{1,0:T(8,128)(2,1)S(1)}, bf16[256,256]{1,0:T(8,128)(2,1)S(1)}, u32[]{:S(2)}, u32[]{:S(2)}) collective-permute-start(bf16[256,256]{1,0:T(8,128)(2,1)S(1)} %collective-permute-done.18.a), channel_id=1, source_target_pairs={{0,64},{4,68},{8,72},{12,76},{16,80},{20,84},{24,88},{28,92},{32,9... | collective-permute-start | bytes 393224 | tf_op jit(solution)/shard_map/ppermute | solution.py:561
  57.1 9.7 %collective-permute-start.13 = (bf16[4,128,256]{2,1,0:T(8,128)(2,1)S(1)}, bf16[4,128,256]{2,1,0:T(8,128)(2,1)S(1)}, u32[]{:S(2)}, u32[]{:S(2)}) collective-permute-start(bf16[4,128,256]{2,1,0:T(8,128)(2,1)S(1)} %get-tuple-element.79.refs_1_), channel_id=1, source_target_pairs={{0,32},{4,36},{8,40},{12,44},{16,48},{20,52},{24,56},{28,60},{32,6... | collective-permute-start | bytes 786440 | tf_op jit(solution)/shard_map/ppermute | solution.py:561
  57.1 9.7 %collective-permute-start.14 = (bf16[4,128,256]{2,1,0:T(8,128)(2,1)S(1)}, bf16[4,128,256]{2,1,0:T(8,128)(2,1)S(1)}, u32[]{:S(2)}, u32[]{:S(2)}) collective-permute-start(bf16[4,128,256]{2,1,0:T(8,128)(2,1)S(1)} %get-tuple-element.78.refs_0_), channel_id=1, source_target_pairs={{0,96},{4,100},{8,104},{12,108},{16,112},{20,116},{24,120},{28,124... | collective-permute-start | bytes 786440 | tf_op jit(solution)/shard_map/ppermute | solution.py:561
  61.0 6.8 %collective-permute-start.22 = (bf16[4,128,256]{2,1,0:T(8,128)(2,1)S(1)}, bf16[4,128,256]{2,1,0:T(8,128)(2,1)S(1)}, u32[]{:S(2)}, u32[]{:S(2)}) collective-permute-start(bf16[4,128,256]{2,1,0:T(8,128)(2,1)S(1)} %get-tuple-element.81.refs_8_), channel_id=1, source_target_pairs={{0,8},{4,12},{8,16},{12,20},{16,24},{20,28},{24,0},{28,4},{32,40},... | collective-permute-start | bytes 786440 | tf_op jit(solution)/shard_map/ppermute | solution.py:561
  61.1 8.4 %collective-permute-start.25 = (bf16[4,128,256]{2,1,0:T(8,128)(2,1)S(1)}, bf16[4,128,256]{2,1,0:T(8,128)(2,1)S(1)}, u32[]{:S(2)}, u32[]{:S(2)}) collective-permute-start(bf16[4,128,256]{2,1,0:T(8,128)(2,1)S(1)} %get-tuple-element.82.refs_9_), channel_id=1, source_target_pairs={{0,24},{4,28},{8,0},{12,4},{16,8},{20,12},{24,16},{28,20},{32,56},... | collective-permute-start | bytes 786440 | tf_op jit(solution)/shard_map/ppermute | solution.py:561
  63.8 8.9 %collective-permute-start.23 = (bf16[4,128,256]{2,1,0:T(8,128)(2,1)S(1)}, bf16[4,128,256]{2,1,0:T(8,128)(2,1)S(1)}, u32[]{:S(2)}, u32[]{:S(2)}) collective-permute-start(bf16[4,128,256]{2,1,0:T(8,128)(2,1)S(1)} %get-tuple-element.82.refs_9_), channel_id=1, source_target_pairs={{0,8},{4,12},{8,16},{12,20},{16,24},{20,28},{24,0},{28,4},{32,40},... | collective-permute-start | bytes 786440 | tf_op jit(solution)/shard_map/ppermute | solution.py:561
  66.8 7.8 %collective-permute-start.24 = (bf16[4,128,256]{2,1,0:T(8,128)(2,1)S(1)}, bf16[4,128,256]{2,1,0:T(8,128)(2,1)S(1)}, u32[]{:S(2)}, u32[]{:S(2)}) collective-permute-start(bf16[4,128,256]{2,1,0:T(8,128)(2,1)S(1)} %get-tuple-element.81.refs_8_), channel_id=1, source_target_pairs={{0,24},{4,28},{8,0},{12,4},{16,8},{20,12},{24,16},{28,20},{32,56},... | collective-permute-start | bytes 786440 | tf_op jit(solution)/shard_map/ppermute | solution.py:561
  66.8 7.8 %collective-permute-start.16 = (bf16[4,128,256]{2,1,0:T(8,128)(2,1)S(1)}, bf16[4,128,256]{2,1,0:T(8,128)(2,1)S(1)}, u32[]{:S(2)}, u32[]{:S(2)}) collective-permute-start(bf16[4,128,256]{2,1,0:T(8,128)(2,1)S(1)} %collective-permute-done.12.refs_2_), channel_id=1, source_target_pairs={{0,32},{4,36},{8,40},{12,44},{16,48},{20,52},{24,56},{28,60},{32,6... | collective-permute-start | bytes 786440 | tf_op jit(solution)/shard_map/ppermute | solution.py:561
  67.8 6.8 %collective-permute-start.17 = (bf16[4,128,256]{2,1,0:T(8,128)(2,1)S(1)}, bf16[4,128,256]{2,1,0:T(8,128)(2,1)S(1)}, u32[]{:S(2)}, u32[]{:S(2)}) collective-permute-start(bf16[4,128,256]{2,1,0:T(8,128)(2,1)S(1)} %collective-permute-done.15.refs_5_), channel_id=1, source_target_pairs={{0,96},{4,100},{8,104},{12,108},{16,112},{20,116},{24,120},{28,124... | collective-permute-start | bytes 786440 | tf_op jit(solution)/shard_map/ppermute | solution.py:561
  69.5 9.5 %collective-permute-start.26 = (bf16[4,128,256]{2,1,0:T(8,128)(2,1)S(1)}, bf16[4,128,256]{2,1,0:T(8,128)(2,1)S(1)}, u32[]{:S(2)}, u32[]{:S(2)}) collective-permute-start(bf16[4,128,256]{2,1,0:T(8,128)(2,1)S(1)} %collective-permute-done.22.refs_10_), channel_id=1, source_target_pairs={{0,8},{4,12},{8,16},{12,20},{16,24},{20,28},{24,0},{28,4},{32,40},... | collective-permute-start | bytes 786440 | tf_op jit(solution)/shard_map/ppermute | solution.py:561
  72.7 6.3 %collective-permute-start.27 = (bf16[4,128,256]{2,1,0:T(8,128)(2,1)S(1)}, bf16[4,128,256]{2,1,0:T(8,128)(2,1)S(1)}, u32[]{:S(2)}, u32[]{:S(2)}) collective-permute-start(bf16[4,128,256]{2,1,0:T(8,128)(2,1)S(1)} %collective-permute-done.25.refs_13_), channel_id=1, source_target_pairs={{0,24},{4,28},{8,0},{12,4},{16,8},{20,12},{24,16},{28,20},{32,56},... | collective-permute-start | bytes 786440 | tf_op jit(solution)/shard_map/ppermute | solution.py:561
  93.7 9.3 %collective-permute-start.29 = (bf16[16,128,128]{2,1,0:T(8,128)(2,1)S(1)}, bf16[16,128,128]{2,1,0:T(8,128)(2,1)S(1)}, u32[]{:S(2)}, u32[]{:S(2)}) collective-permute-start(bf16[16,128,128]{2,1,0:T(8,128)(2,1)S(1)} %get-tuple-element.85), channel_id=1, source_target_pairs={{0,8},{4,12},{8,16},{12,20},{16,24},{20,28},{24,0},{28,4},{32,40},... | collective-permute-start | bytes 1572872 | tf_op jit(solution)/shard_map/ppermute | solution.py:561
  93.8 12.4 %collective-permute-start.30 = (bf16[16,128,128]{2,1,0:T(8,128)(2,1)S(1)}, bf16[16,128,128]{2,1,0:T(8,128)(2,1)S(1)}, u32[]{:S(2)}, u32[]{:S(2)}) collective-permute-start(bf16[16,128,128]{2,1,0:T(8,128)(2,1)S(1)} %get-tuple-element.86), channel_id=1, source_target_pairs={{0,24},{4,28},{8,0},{12,4},{16,8},{20,12},{24,16},{28,20},{32,56},... | collective-permute-start | bytes 1572872 | tf_op jit(solution)/shard_map/ppermute | solution.py:561
  96.5 26.5 %collective-permute-start.31 = (bf16[16,128,128]{2,1,0:T(8,128)(2,1)S(1)}, bf16[16,128,128]{2,1,0:T(8,128)(2,1)S(1)}, u32[]{:S(2)}, u32[]{:S(2)}) collective-permute-start(bf16[16,128,128]{2,1,0:T(8,128)(2,1)S(1)} %get-tuple-element.87), channel_id=1, source_target_pairs={{0,16},{4,20},{8,24},{12,28},{16,0},{20,4},{24,8},{28,12},{32,48},... | collective-permute-start | bytes 1572872 | tf_op jit(solution)/shard_map/ppermute | solution.py:561
  97.6 25.4 %collective-permute-start.32 = (bf16[16,128,128]{2,1,0:T(8,128)(2,1)S(1)}, bf16[16,128,128]{2,1,0:T(8,128)(2,1)S(1)}, u32[]{:S(2)}, u32[]{:S(2)}) collective-permute-start(bf16[16,128,128]{2,1,0:T(8,128)(2,1)S(1)} %get-tuple-element.89), channel_id=1, source_target_pairs={{0,32},{4,36},{8,40},{12,44},{16,48},{20,52},{24,56},{28,60},{32,6... | collective-permute-start | bytes 1572872 | tf_op jit(solution)/shard_map/ppermute | solution.py:561
  98.6 24.5 %collective-permute-start.33 = (bf16[16,128,128]{2,1,0:T(8,128)(2,1)S(1)}, bf16[16,128,128]{2,1,0:T(8,128)(2,1)S(1)}, u32[]{:S(2)}, u32[]{:S(2)}) collective-permute-start(bf16[16,128,128]{2,1,0:T(8,128)(2,1)S(1)} %get-tuple-element.90), channel_id=1, source_target_pairs={{0,96},{4,100},{8,104},{12,108},{16,112},{20,116},{24,120},{28,124... | collective-permute-start | bytes 1572872 | tf_op jit(solution)/shard_map/ppermute | solution.py:561
  103.0 20.0 %collective-permute-start.34 = (bf16[16,128,128]{2,1,0:T(8,128)(2,1)S(1)}, bf16[16,128,128]{2,1,0:T(8,128)(2,1)S(1)}, u32[]{:S(2)}, u32[]{:S(2)}) collective-permute-start(bf16[16,128,128]{2,1,0:T(8,128)(2,1)S(1)} %get-tuple-element.91), channel_id=1, source_target_pairs={{0,64},{4,68},{8,72},{12,76},{16,80},{20,84},{24,88},{28,92},{32,9... | collective-permute-start | bytes 1572872 | tf_op jit(solution)/shard_map/ppermute | solution.py:561
  106.2 21.1 %collective-permute-start.45 = (bf16[128,1280]{1,0:T(8,128)(2,1)}, bf16[128,1280]{1,0:T(8,128)(2,1)S(1)}, u32[]{:S(2)}, u32[]{:S(2)}) collective-permute-start(bf16[128,1280]{1,0:T(8,128)(2,1)} %collective-permute-done.3.bt.refs_1_), channel_id=1, source_target_pairs={{0,4},{4,0},{8,12},{12,8},{16,20},{20,16},{24,28},{28,24},{32,36},... | collective-permute-start | bytes 983048 | tf_op jit(solution)/shard_map/ppermute | solution.py:561
  123.5 14.4 %collective-permute-start.35 = (f32[4,128,128]{2,1,0:T(8,128)S(1)}, f32[4,128,128]{2,1,0:T(8,128)S(1)}, u32[]{:S(2)}, u32[]{:S(2)}) collective-permute-start(f32[4,128,128]{2,1,0:T(8,128)S(1)} %get-tuple-element.93), channel_id=1, source_target_pairs={{0,32},{4,36},{8,40},{12,44},{16,48},{20,52},{24,56},{28,60},{32,6... | collective-permute-start | bytes 786440 | tf_op jit(solution)/shard_map/ppermute | solution.py:561
  124.6 13.2 %collective-permute-start.36 = (f32[4,128,128]{2,1,0:T(8,128)S(1)}, f32[4,128,128]{2,1,0:T(8,128)S(1)}, u32[]{:S(2)}, u32[]{:S(2)}) collective-permute-start(f32[4,128,128]{2,1,0:T(8,128)S(1)} %get-tuple-element.94), channel_id=1, source_target_pairs={{0,96},{4,100},{8,104},{12,108},{16,112},{20,116},{24,120},{28,124... | collective-permute-start | bytes 786440 | tf_op jit(solution)/shard_map/ppermute | solution.py:561
  126.2 22.3 %collective-permute-start.37 = (f32[4,128,128]{2,1,0:T(8,128)S(1)}, f32[4,128,128]{2,1,0:T(8,128)S(1)}, u32[]{:S(2)}, u32[]{:S(2)}) collective-permute-start(f32[4,128,128]{2,1,0:T(8,128)S(1)} %get-tuple-element.95), channel_id=1, source_target_pairs={{0,64},{4,68},{8,72},{12,76},{16,80},{20,84},{24,88},{28,92},{32,9... | collective-permute-start | bytes 786440 | tf_op jit(solution)/shard_map/ppermute | solution.py:561
  127.3 22.4 %collective-permute-start.38 = (f32[4,128,128]{2,1,0:T(8,128)S(1)}, f32[4,128,128]{2,1,0:T(8,128)S(1)}, u32[]{:S(2)}, u32[]{:S(2)}) collective-permute-start(f32[4,128,128]{2,1,0:T(8,128)S(1)} %get-tuple-element.97), channel_id=1, source_target_pairs={{0,8},{4,12},{8,16},{12,20},{16,24},{20,28},{24,0},{28,4},{32,40},... | collective-permute-start | bytes 786440 | tf_op jit(solution)/shard_map/ppermute | solution.py:561
  127.3 22.8 %collective-permute-start.39 = (f32[4,128,128]{2,1,0:T(8,128)S(1)}, f32[4,128,128]{2,1,0:T(8,128)S(1)}, u32[]{:S(2)}, u32[]{:S(2)}) collective-permute-start(f32[4,128,128]{2,1,0:T(8,128)S(1)} %get-tuple-element.98), channel_id=1, source_target_pairs={{0,24},{4,28},{8,0},{12,4},{16,8},{20,12},{24,16},{28,20},{32,56},... | collective-permute-start | bytes 786440 | tf_op jit(solution)/shard_map/ppermute | solution.py:561
  137.9 13.9 %collective-permute-start.40 = (f32[4,128,128]{2,1,0:T(8,128)S(1)}, f32[4,128,128]{2,1,0:T(8,128)S(1)}, u32[]{:S(2)}, u32[]{:S(2)}) collective-permute-start(f32[4,128,128]{2,1,0:T(8,128)S(1)} %get-tuple-element.99), channel_id=1, source_target_pairs={{0,16},{4,20},{8,24},{12,28},{16,0},{20,4},{24,8},{28,12},{32,48},... | collective-permute-start | bytes 786440 | tf_op jit(solution)/shard_map/ppermute | solution.py:561
  137.9 16.3 %collective-permute-start.48 = (bf16[128,1280]{1,0:T(8,128)(2,1)}, bf16[128,1280]{1,0:T(8,128)(2,1)S(1)}, u32[]{:S(2)}, u32[]{:S(2)}) collective-permute-start(bf16[128,1280]{1,0:T(8,128)(2,1)} %collective-permute-done.5.cl.refs_4_), channel_id=1, source_target_pairs={{0,4},{4,0},{8,12},{12,8},{16,20},{20,16},{24,28},{28,24},{32,36},... | collective-permute-start | bytes 983048 | tf_op jit(solution)/shard_map/ppermute | solution.py:561
  148.5 6.0 %collective-permute-start.46 = (bf16[128,1280]{1,0:T(8,128)(2,1)S(1)}, bf16[128,1280]{1,0:T(8,128)(2,1)S(1)}, u32[]{:S(2)}, u32[]{:S(2)}) collective-permute-start(bf16[128,1280]{1,0:T(8,128)(2,1)S(1)} %collective-permute-done.7.bl.refs_2_), channel_id=1, source_target_pairs={{0,4},{4,0},{8,12},{12,8},{16,20},{20,16},{24,28},{28,24},{32,36},... | collective-permute-start | bytes 983048 | tf_op jit(solution)/shard_map/ppermute | solution.py:561
  149.7 4.9 %collective-permute-start.47 = (bf16[128,1280]{1,0:T(8,128)(2,1)S(1)}, bf16[128,1280]{1,0:T(8,128)(2,1)S(1)}, u32[]{:S(2)}, u32[]{:S(2)}) collective-permute-start(bf16[128,1280]{1,0:T(8,128)(2,1)S(1)} %collective-permute-done.8.ct.refs_3_), channel_id=1, source_target_pairs={{0,4},{4,0},{8,12},{12,8},{16,20},{20,16},{24,28},{28,24},{32,36},... | collective-permute-start | bytes 983048 | tf_op jit(solution)/shard_map/ppermute | solution.py:561
  150.1 4.4 %collective-permute-start.49 = (bf16[128,1280]{1,0:T(8,128)(2,1)S(1)}, bf16[128,1280]{1,0:T(8,128)(2,1)S(1)}, u32[]{:S(2)}, u32[]{:S(2)}) collective-permute-start(bf16[128,1280]{1,0:T(8,128)(2,1)S(1)} %collective-permute-done.4.a.refs_5_), channel_id=1, source_target_pairs={{0,4},{4,0},{8,12},{12,8},{16,20},{20,16},{24,28},{28,24},{32,36},... | collective-permute-start | bytes 983048 | tf_op jit(solution)/shard_map/ppermute | solution.py:561
  151.7 3.5 %collective-permute-start.50 = (bf16[128,1280]{1,0:T(8,128)(2,1)S(1)}, bf16[128,1280]{1,0:T(8,128)(2,1)S(1)}, u32[]{:S(2)}, u32[]{:S(2)}) collective-permute-start(bf16[128,1280]{1,0:T(8,128)(2,1)S(1)} %collective-permute-done.6.b.refs_6_), channel_id=1, source_target_pairs={{0,4},{4,0},{8,12},{12,8},{16,20},{20,16},{24,28},{28,24},{32,36},... | collective-permute-start | bytes 983048 | tf_op jit(solution)/shard_map/ppermute | solution.py:561
  154.2 3.8 %collective-permute-start.41 = (bf16[256,256]{1,0:T(8,128)(2,1)S(1)}, bf16[256,256]{1,0:T(8,128)(2,1)S(1)}, u32[]{:S(2)}, u32[]{:S(2)}) collective-permute-start(bf16[256,256]{1,0:T(8,128)(2,1)S(1)} %get-tuple-element.101), channel_id=1, source_target_pairs={{0,4},{4,0},{8,12},{12,8},{16,20},{20,16},{24,28},{28,24},{32,36},... | collective-permute-start | bytes 393224 | tf_op jit(solution)/shard_map/ppermute | solution.py:561
  160.5 10.2 %collective-permute-start.51 = (bf16[8,160,128]{2,1,0:T(8,128)(2,1)S(1)}, bf16[8,160,128]{2,1,0:T(8,128)(2,1)S(1)}, u32[]{:S(2)}, u32[]{:S(2)}) collective-permute-start(bf16[8,160,128]{2,1,0:T(8,128)(2,1)S(1)} %get-tuple-element.110), channel_id=1, source_target_pairs={{0,8},{4,12},{8,16},{12,20},{16,24},{20,28},{24,0},{28,4},{32,40},... | collective-permute-start | bytes 983048 | tf_op jit(solution)/shard_map/ppermute | solution.py:561
  160.6 10.3 %collective-permute-start.52 = (bf16[8,160,128]{2,1,0:T(8,128)(2,1)S(1)}, bf16[8,160,128]{2,1,0:T(8,128)(2,1)S(1)}, u32[]{:S(2)}, u32[]{:S(2)}) collective-permute-start(bf16[8,160,128]{2,1,0:T(8,128)(2,1)S(1)} %get-tuple-element.111), channel_id=1, source_target_pairs={{0,24},{4,28},{8,0},{12,4},{16,8},{20,12},{24,16},{28,20},{32,56},... | collective-permute-start | bytes 983048 | tf_op jit(solution)/shard_map/ppermute | solution.py:561
  164.2 37.4 %collective-permute-start.28 = (bf16[256,1280]{1,0:T(8,128)(2,1)}, bf16[256,1280]{1,0:T(8,128)(2,1)}, u32[]{:S(2)}, u32[]{:S(2)}) collective-permute-start(bf16[256,1280]{1,0:T(8,128)(2,1)} %slice.16), channel_id=1, source_target_pairs={{0,4},{4,0},{8,12},{12,8},{16,20},{20,16},{24,28},{28,24},{32,36},... | collective-permute-start | bytes 1966088 | tf_op jit(solution)/shard_map/ppermute | solution.py:561
  165.1 13.8 %collective-permute-start.53 = (bf16[8,160,128]{2,1,0:T(8,128)(2,1)S(1)}, bf16[8,160,128]{2,1,0:T(8,128)(2,1)S(1)}, u32[]{:S(2)}, u32[]{:S(2)}) collective-permute-start(bf16[8,160,128]{2,1,0:T(8,128)(2,1)S(1)} %get-tuple-element.112), channel_id=1, source_target_pairs={{0,16},{4,20},{8,24},{12,28},{16,0},{20,4},{24,8},{28,12},{32,48},... | collective-permute-start | bytes 983048 | tf_op jit(solution)/shard_map/ppermute | solution.py:561
  165.1 13.8 %collective-permute-start.54 = (bf16[8,160,128]{2,1,0:T(8,128)(2,1)S(1)}, bf16[8,160,128]{2,1,0:T(8,128)(2,1)S(1)}, u32[]{:S(2)}, u32[]{:S(2)}) collective-permute-start(bf16[8,160,128]{2,1,0:T(8,128)(2,1)S(1)} %get-tuple-element.114), channel_id=1, source_target_pairs={{0,32},{4,36},{8,40},{12,44},{16,48},{20,52},{24,56},{28,60},{32,6... | collective-permute-start | bytes 983048 | tf_op jit(solution)/shard_map/ppermute | solution.py:561
  170.7 8.2 %collective-permute-start.55 = (bf16[8,160,128]{2,1,0:T(8,128)(2,1)S(1)}, bf16[8,160,128]{2,1,0:T(8,128)(2,1)S(1)}, u32[]{:S(2)}, u32[]{:S(2)}) collective-permute-start(bf16[8,160,128]{2,1,0:T(8,128)(2,1)S(1)} %get-tuple-element.115), channel_id=1, source_target_pairs={{0,96},{4,100},{8,104},{12,108},{16,112},{20,116},{24,120},{28,124... | collective-permute-start | bytes 983048 | tf_op jit(solution)/shard_map/ppermute | solution.py:561
  170.9 13.5 %collective-permute-start.56 = (bf16[8,160,128]{2,1,0:T(8,128)(2,1)S(1)}, bf16[8,160,128]{2,1,0:T(8,128)(2,1)S(1)}, u32[]{:S(2)}, u32[]{:S(2)}) collective-permute-start(bf16[8,160,128]{2,1,0:T(8,128)(2,1)S(1)} %get-tuple-element.116), channel_id=1, source_target_pairs={{0,64},{4,68},{8,72},{12,76},{16,80},{20,84},{24,88},{28,92},{32,9... | collective-permute-start | bytes 983048 | tf_op jit(solution)/shard_map/ppermute | solution.py:561
  189.4 12.2 %collective-permute-start.57 = (f32[2,160,128]{2,1,0:T(8,128)}, f32[2,160,128]{2,1,0:T(8,128)}, u32[]{:S(2)}, u32[]{:S(2)}) collective-permute-start(f32[2,160,128]{2,1,0:T(8,128)} %get-tuple-element.118), channel_id=1, source_target_pairs={{0,32},{4,36},{8,40},{12,44},{16,48},{20,52},{24,56},{28,60},{32,6... | collective-permute-start | bytes 491528 | tf_op jit(solution)/shard_map/ppermute | solution.py:561
  192.4 10.7 %collective-permute-start.58 = (f32[2,160,128]{2,1,0:T(8,128)}, f32[2,160,128]{2,1,0:T(8,128)}, u32[]{:S(2)}, u32[]{:S(2)}) collective-permute-start(f32[2,160,128]{2,1,0:T(8,128)} %get-tuple-element.119), channel_id=1, source_target_pairs={{0,96},{4,100},{8,104},{12,108},{16,112},{20,116},{24,120},{28,124... | collective-permute-start | bytes 491528 | tf_op jit(solution)/shard_map/ppermute | solution.py:561
  198.8 27.7 %collective-permute-start.42 = (bf16[256,1280]{1,0:T(8,128)(2,1)S(1)}, bf16[256,1280]{1,0:T(8,128)(2,1)S(1)}, u32[]{:S(2)}, u32[]{:S(2)}) collective-permute-start(bf16[256,1280]{1,0:T(8,128)(2,1)S(1)} %get-tuple-element.105), channel_id=1, source_target_pairs={{0,1},{1,2},{2,3},{3,0},{4,5},{5,6},{6,7},{7,4},{8,9},{9,10},{10,1... | collective-permute-start | bytes 1966088 | tf_op jit(solution)/shard_map/ppermute | solution.py:561
  198.9 27.6 %collective-permute-start.43 = (bf16[256,1280]{1,0:T(8,128)(2,1)S(1)}, bf16[256,1280]{1,0:T(8,128)(2,1)S(1)}, u32[]{:S(2)}, u32[]{:S(2)}) collective-permute-start(bf16[256,1280]{1,0:T(8,128)(2,1)S(1)} %get-tuple-element.106), channel_id=1, source_target_pairs={{0,3},{1,0},{2,1},{3,2},{4,7},{5,4},{6,5},{7,6},{8,11},{9,8},{10,9... | collective-permute-start | bytes 1966088 | tf_op jit(solution)/shard_map/ppermute | solution.py:561
  201.5 26.1 %collective-permute-start.44 = (bf16[256,1280]{1,0:T(8,128)(2,1)S(1)}, bf16[256,1280]{1,0:T(8,128)(2,1)S(1)}, u32[]{:S(2)}, u32[]{:S(2)}) collective-permute-start(bf16[256,1280]{1,0:T(8,128)(2,1)S(1)} %get-tuple-element.107), channel_id=1, source_target_pairs={{0,2},{1,3},{2,0},{3,1},{4,6},{5,7},{6,4},{7,5},{8,10},{9,11},{10,... | collective-permute-start | bytes 1966088 | tf_op jit(solution)/shard_map/ppermute | solution.py:561
  201.6 5.8 %collective-permute-start.59 = (f32[2,160,128]{2,1,0:T(8,128)S(1)}, f32[2,160,128]{2,1,0:T(8,128)S(1)}, u32[]{:S(2)}, u32[]{:S(2)}) collective-permute-start(f32[2,160,128]{2,1,0:T(8,128)S(1)} %copy-done.23), channel_id=1, source_target_pairs={{0,64},{4,68},{8,72},{12,76},{16,80},{20,84},{24,88},{28,92},{32,9... | collective-permute-start | bytes 491528 | tf_op jit(solution)/shard_map/ppermute | solution.py:561
  203.1 8.1 %collective-permute-start.60 = (f32[2,160,128]{2,1,0:T(8,128)S(1)}, f32[2,160,128]{2,1,0:T(8,128)S(1)}, u32[]{:S(2)}, u32[]{:S(2)}) collective-permute-start(f32[2,160,128]{2,1,0:T(8,128)S(1)} %copy-done.21), channel_id=1, source_target_pairs={{0,8},{4,12},{8,16},{12,20},{16,24},{20,28},{24,0},{28,4},{32,40},... | collective-permute-start | bytes 491528 | tf_op jit(solution)/shard_map/ppermute | solution.py:561
  207.3 7.9 %collective-permute-start.61 = (f32[2,160,128]{2,1,0:T(8,128)S(1)}, f32[2,160,128]{2,1,0:T(8,128)S(1)}, u32[]{:S(2)}, u32[]{:S(2)}) collective-permute-start(f32[2,160,128]{2,1,0:T(8,128)S(1)} %copy-done.19), channel_id=1, source_target_pairs={{0,24},{4,28},{8,0},{12,4},{16,8},{20,12},{24,16},{28,20},{32,56},... | collective-permute-start | bytes 491528 | tf_op jit(solution)/shard_map/ppermute | solution.py:561
  211.2 5.7 %collective-permute-start.62 = (f32[2,160,128]{2,1,0:T(8,128)S(1)}, f32[2,160,128]{2,1,0:T(8,128)S(1)}, u32[]{:S(2)}, u32[]{:S(2)}) collective-permute-start(f32[2,160,128]{2,1,0:T(8,128)S(1)} %copy-done.17), channel_id=1, source_target_pairs={{0,16},{4,20},{8,24},{12,28},{16,0},{20,4},{24,8},{28,12},{32,48},... | collective-permute-start | bytes 491528 | tf_op jit(solution)/shard_map/ppermute | solution.py:561
  217.9 7.3 %collective-permute-start.63 = (f32[160,256]{1,0:T(8,128)S(1)}, f32[160,256]{1,0:T(8,128)S(1)}, u32[]{:S(2)}, u32[]{:S(2)}) collective-permute-start(f32[160,256]{1,0:T(8,128)S(1)} %get-tuple-element.126), channel_id=1, source_target_pairs={{0,4},{4,0},{8,12},{12,8},{16,20},{20,16},{24,28},{28,24},{32,36},... | collective-permute-start | bytes 491528 | tf_op jit(solution)/shard_map/ppermute | solution.py:561
  (24 other events, 312.7 us)

commit v3 on v2

--- a/solution.py
+++ b/solution.py
@@ -96,6 +96,7 @@
             jax.ShapeDtypeStruct((4,), jnp.int32),
         ],
         scratch_shapes=[pltpu.SMEM((block_total,), jnp.int32)],
+        compiler_params=params(1),
         name="device_tables",
     )(parents, position)
 
@@ -203,6 +204,29 @@
         compiler_params=params(3),
         name="pack",
     )(own, back, forth, far)
+
+
+def join_rows(place, mine, other):
+    rows, cols = other.shape
+    width = cols // 2
+
+    def body(p, a, b, out, grad):
+        swap = p[4] == 1
+        for low, ref in ((0, out), (width, grad)):
+            first = a[:rows, low : low + width]
+            second = b[:, low : low + width]
+            ref[:, :width] = jnp.where(swap, second, first)
+            ref[:, width:] = jnp.where(swap, first, second)
+
+    return pl.pallas_call(
+        body,
+        in_specs=[pl.BlockSpec(memory_space=pltpu.SMEM)]
+        + [pl.BlockSpec(memory_space=pltpu.VMEM)] * 2,
+        out_specs=[pl.BlockSpec(memory_space=pltpu.VMEM)] * 2,
+        out_shape=[jax.ShapeDtypeStruct((rows, cols), BF)] * 2,
+        compiler_params=params(5),
+        name="join_rows",
+    )(place, mine, other)
 
 
 def join_weights(place, mine, other):
@@ -646,22 +670,16 @@
     features = flip(own_features, peer_features)
 
     out, *slot_grads = attend(table, queries, query_peer, upstream, upstream_peer, pieces)
-    sums = combine(send_all(slot_grads[:4], xn, xb, x2) + send_all(slot_grads[4:], yn, yb, y2))
-    grads, grads_away = finish_grads(
-        send_all(sums[:4], yn, yb, y2) + send_all(sums[4:], xn, xb, x2), cosine, sine
-    )
+    t_sent = send_all(slot_grads[:4], xn, xb, x2) + send_all(slot_grads[4:], yn, yb, y2)
+    sums = combine(t_sent)
+    t_last = send_all(sums[:4], yn, yb, y2) + send_all(sums[4:], xn, xb, x2)
+    grads, grads_away = finish_grads(t_last, cosine, sine)
     grads_other = swap(grads_away)
     grads, grads_other = lax.optimization_barrier((grads, grads_other))
 
     out_other = swap(out[local_rows:])
 
-    def assemble(a, b):
-        first = jnp.where(core == 0, a, b)
-        second = jnp.where(core == 0, b, a)
-        return jnp.concatenate([first, second], axis=1)
-
-    attention = assemble(out[:local_rows, :width], out_other[:, :width])
-    query_grad = assemble(out[:local_rows, width:], out_other[:, width:])
+    attention, query_grad = join_rows(place, out, out_other)
 
     w_parts = weight_partials(place, grads, features)
     w_sent = send_all(w_parts[:4], xn, xb, x2) + send_all(w_parts[4:], yn, yb, y2)

time: 233 us -> 225 us (0.966); the launches traced: 229 us -> 225 us
  local copies, waits for them, and re-layouts: 12.8 us -> 5.32 us
  waiting for transfers between devices: 65 us -> 70.3 us
  other arithmetic: 6.79 us -> 2.55 us
    unnamed x48 -> x14, local copies, waits for them, and re-layouts: 8.42 us -> 1.76 us
    ppermute x64, waiting for transfers between devices: 65 us -> 70.3 us  [mover(): return lambda value: lax.ppermute(value, axis, pairs)]
    ppermute x64, starting transfers between devices: 109 us -> 111 us  [mover(): return lambda value: lax.ppermute(value, axis, pairs)]
  transfers between devices with their start and end apart: 64 -> 64, of which waited for: 23 -> 24; matrix products, arithmetic and copies ran while one was open for 4% -> 1% of each run, Pallas kernels for 7% -> 7%
where the time goes in v3:
time: 225 us
  starting transfers between devices  111 us (49%)
  waiting for transfers between devices  70.3 us (31%)
  Pallas kernels  34.2 us (15%)
  local copies, waits for them, and re-layouts  5.32 us (2%)
  other arithmetic  2.55 us (1%)
    ppermute x64, starting transfers between devices, mover(): return lambda value: lax.ppermute(value, axis, pairs)  111 us
    ppermute x64, waiting for transfers between devices, mover(): return lambda value: lax.ppermute(value, axis, pairs)  70.3 us
    pallas_call x1, Pallas kernels, attend(): pl.pallas_call(body, grid_spec=pltpu.PrefetchScalarGridSpec(num_scalar_pr...  14.6 us
  transfers between devices with their start and end apart: 64, of which 24 were waited for; matrix products, arithmetic and copies ran while one was open for 1% of the time, Pallas kernels for 7%

profile of v3, /device:TPU:1, one launch (start us, length us, event | category | flops | bytes accessed | tf_op | source)
XLA Modules:
  0.0 224.7 jit_solution(10980567088925237993)
XLA Ops:
  0.7 1.8 constant_dynamic-slice_fusion.1
  2.5 1.4 collective-permute-start.1
  3.8 1.7 constant_dynamic-slice_fusion
  7.0 1.7 collective-permute-start.3
  8.7 2.1 collective-permute-start.5
  10.9 2.5 %device_tables.1 = (s32[115]{0:T(128)S(1)}, s32[17]{0:T(128)S(1)}, s32[4]{0:T(128)S(1)}) custom-call(s32[64]{0:T(128)S(1)} %copy-done.6, s32[4]{0:T(128)S(1)} %pad_add_fusion.where), custom_call_target="tpu_custom_call" | custom-call | tf_op jit(solution)/shard_map/device_tables/pallas_call | solution.py:89
  13.6 2.7 %collective-permute-start.8 = (bf16[128,1280]{1,0:T(8,128)(2,1)}, bf16[128,1280]{1,0:T(8,128)(2,1)S(1)}, u32[]{:S(2)}, u32[]{:S(2)}) collective-permute-start(bf16[128,1280]{1,0:T(8,128)(2,1)} %get-tuple-element.74), channel_id=1, source_target_pairs={{0,3},{1,0},{2,1},{3,2},{4,7},{5,4},{6,5},{7,6},{8,11},{9,8},{10,9... | collective-permute-start | bytes 983048 | tf_op jit(solution)/shard_map/ppermute | solution.py:585
  16.2 2.9 %collective-permute-done.3.bt.refs_1_ = bf16[128,1280]{1,0:T(8,128)(2,1)} collective-permute-done((bf16[128,1280]{1,0:T(8,128)(2,1)}, bf16[128,1280]{1,0:T(8,128)(2,1)}, u32[]{:S(2)}, u32[]{:S(2)}) %collective-permute-start.3) | collective-permute-done | bytes 327712 | tf_op jit(solution)/shard_map/ppermute | solution.py:585
  19.2 2.7 %collective-permute-start.6 = (bf16[128,1280]{1,0:T(8,128)(2,1)}, bf16[128,1280]{1,0:T(8,128)(2,1)S(1)}, u32[]{:S(2)}, u32[]{:S(2)}) collective-permute-start(bf16[128,1280]{1,0:T(8,128)(2,1)} %collective-permute-done.5.cl.refs_4_), channel_id=1, source_target_pairs={{0,3},{1,0},{2,1},{3,2},{4,7},{5,4},{6,5},{7,6},{8,11},{9,8},{10,9... | collective-permute-start | bytes 983048 | tf_op jit(solution)/shard_map/ppermute | solution.py:585
  23.0 3.0 %collective-permute-done.7.bl.refs_2_ = bf16[128,1280]{1,0:T(8,128)(2,1)S(1)} collective-permute-done((bf16[128,1280]{1,0:T(8,128)(2,1)}, bf16[128,1280]{1,0:T(8,128)(2,1)S(1)}, u32[]{:S(2)}, u32[]{:S(2)}) %collective-permute-start.7) | collective-permute-done | bytes 327712 | tf_op jit(solution)/shard_map/ppermute | solution.py:585
  26.1 1.7 copy-done.1
  27.8 2.8 %project_near.1 = (f32[256,256]{1,0:T(8,128)S(1)}, f32[256,256]{1,0:T(8,128)S(1)}) custom-call(s32[17]{0:T(128)S(1)} %get-tuple-element.70.place_ref.p, bf16[256,1280]{1,0:T(8,128)(2,1)S(1)} %copy-done.3, bf16[128,1280]{1,0:T(8,128)(2,1)} %collective-permute-done.3.bt.refs_1_, bf16[128,1280]{1,0:T(8,128)(2,1)S(1)} %collective-permute-done.7.bl.refs_2_, ...), custom_call_target="tpu_custom_call" | custom-call | tf_op jit(solution)/shard_map/project_near/pallas_call | solution.py:170
  30.6 2.5 %collective-permute-done.4.a.refs_5_ = bf16[128,1280]{1,0:T(8,128)(2,1)S(1)} collective-permute-done((bf16[128,1280]{1,0:T(8,128)(2,1)}, bf16[128,1280]{1,0:T(8,128)(2,1)S(1)}, u32[]{:S(2)}, u32[]{:S(2)}) %collective-permute-start.4) | collective-permute-done | bytes 327712 | tf_op jit(solution)/shard_map/ppermute | solution.py:585
  34.2 2.5 %collective-permute-start.10 = (bf16[256,256]{1,0:T(8,128)(2,1)S(1)}, bf16[256,256]{1,0:T(8,128)(2,1)S(1)}, u32[]{:S(2)}, u32[]{:S(2)}) collective-permute-start(bf16[256,256]{1,0:T(8,128)(2,1)S(1)} %get-tuple-element.79.a), channel_id=1, source_target_pairs={{0,24},{4,28},{8,0},{12,4},{16,8},{20,12},{24,16},{28,20},{32,56},... | collective-permute-start | bytes 393224 | tf_op jit(solution)/shard_map/ppermute | solution.py:585
  37.9 1.5 collective-permute-start.18
  39.6 2.6 %collective-permute-done.11.d = bf16[256,256]{1,0:T(8,128)(2,1)S(1)} collective-permute-done((bf16[256,256]{1,0:T(8,128)(2,1)S(1)}, bf16[256,256]{1,0:T(8,128)(2,1)S(1)}, u32[]{:S(2)}, u32[]{:S(2)}) %collective-permute-start.11) | collective-permute-done | bytes 131104 | tf_op jit(solution)/shard_map/ppermute | solution.py:585
  42.2 4.2 %collective-permute-done.9.b = bf16[256,256]{1,0:T(8,128)(2,1)S(1)} collective-permute-done((bf16[256,256]{1,0:T(8,128)(2,1)S(1)}, bf16[256,256]{1,0:T(8,128)(2,1)S(1)}, u32[]{:S(2)}, u32[]{:S(2)}) %collective-permute-start.9) | collective-permute-done | bytes 131104 | tf_op jit(solution)/shard_map/ppermute | solution.py:585
  46.4 1.4 collective-permute-start.12
  47.8 1.5 collective-permute-start.15
  49.3 2.7 %collective-permute-start.20 = (bf16[256,256]{1,0:T(8,128)(2,1)S(1)}, bf16[256,256]{1,0:T(8,128)(2,1)S(1)}, u32[]{:S(2)}, u32[]{:S(2)}) collective-permute-start(bf16[256,256]{1,0:T(8,128)(2,1)S(1)} %collective-permute-done.18.a), channel_id=1, source_target_pairs={{0,96},{4,100},{8,104},{12,108},{16,112},{20,116},{24,120},{28,124... | collective-permute-start | bytes 393224 | tf_op jit(solution)/shard_map/ppermute | solution.py:585
  52.3 5.5 %collective-permute-done.19.b = bf16[256,256]{1,0:T(8,128)(2,1)S(1)} collective-permute-done((bf16[256,256]{1,0:T(8,128)(2,1)S(1)}, bf16[256,256]{1,0:T(8,128)(2,1)S(1)}, u32[]{:S(2)}, u32[]{:S(2)}) %collective-permute-start.19) | collective-permute-done | bytes 131104 | tf_op jit(solution)/shard_map/ppermute | solution.py:585
  57.8 3.0 %collective-permute-start.14 = (bf16[4,128,256]{2,1,0:T(8,128)(2,1)S(1)}, bf16[4,128,256]{2,1,0:T(8,128)(2,1)S(1)}, u32[]{:S(2)}, u32[]{:S(2)}) collective-permute-start(bf16[4,128,256]{2,1,0:T(8,128)(2,1)S(1)} %get-tuple-element.80.refs_0_), channel_id=1, source_target_pairs={{0,96},{4,100},{8,104},{12,108},{16,112},{20,116},{24,120},{28,124... | collective-permute-start | bytes 786440 | tf_op jit(solution)/shard_map/ppermute | solution.py:585
  61.9 2.7 %collective-permute-start.25 = (bf16[4,128,256]{2,1,0:T(8,128)(2,1)S(1)}, bf16[4,128,256]{2,1,0:T(8,128)(2,1)S(1)}, u32[]{:S(2)}, u32[]{:S(2)}) collective-permute-start(bf16[4,128,256]{2,1,0:T(8,128)(2,1)S(1)} %get-tuple-element.84.refs_9_), channel_id=1, source_target_pairs={{0,24},{4,28},{8,0},{12,4},{16,8},{20,12},{24,16},{28,20},{32,56},... | collective-permute-start | bytes 786440 | tf_op jit(solution)/shard_map/ppermute | solution.py:585
  64.6 3.0 %collective-permute-done.13.refs_3_ = bf16[4,128,256]{2,1,0:T(8,128)(2,1)S(1)} collective-permute-done((bf16[4,128,256]{2,1,0:T(8,128)(2,1)S(1)}, bf16[4,128,256]{2,1,0:T(8,128)(2,1)S(1)}, u32[]{:S(2)}, u32[]{:S(2)}) %collective-permute-start.13) | collective-permute-done | bytes 262176 | tf_op jit(solution)/shard_map/ppermute | solution.py:585
  68.5 1.7 collective-permute-start.17
  70.2 1.5 collective-permute-start.26
  71.7 2.3 %collective-permute-done.23.refs_11_ = bf16[4,128,256]{2,1,0:T(8,128)(2,1)S(1)} collective-permute-done((bf16[4,128,256]{2,1,0:T(8,128)(2,1)S(1)}, bf16[4,128,256]{2,1,0:T(8,128)(2,1)S(1)}, u32[]{:S(2)}, u32[]{:S(2)}) %collective-permute-start.23) | collective-permute-done | bytes 262176 | tf_op jit(solution)/shard_map/ppermute | solution.py:585
  74.7 5.1 %collective-permute-done.26.refs_14_ = bf16[4,128,256]{2,1,0:T(8,128)(2,1)S(1)} collective-permute-done((bf16[4,128,256]{2,1,0:T(8,128)(2,1)S(1)}, bf16[4,128,256]{2,1,0:T(8,128)(2,1)S(1)}, u32[]{:S(2)}, u32[]{:S(2)}) %collective-permute-start.26) | collective-permute-done | bytes 262176 | tf_op jit(solution)/shard_map/ppermute | solution.py:585
  79.8 14.6 %attend.1 = (bf16[512,1280]{1,0:T(8,128)(2,1)S(1)}, f32[16,128,128]{2,1,0:T(8,128)S(1)}, bf16[16,128,128]{2,1,0:T(8,128)(2,1)S(1)}, bf16[16,128,128]{2,1,0:T(8,1...) custom-call(s32[115]{0:T(128)S(1)} %get-tuple-element.71.t, ...), custom_call_target="tpu_custom_call" | custom-call | tf_op jit(solution)/shard_map/attend/pallas_call | solution.py:406
  94.8 2.4 %collective-permute-start.30 = (bf16[16,128,128]{2,1,0:T(8,128)(2,1)S(1)}, bf16[16,128,128]{2,1,0:T(8,128)(2,1)S(1)}, u32[]{:S(2)}, u32[]{:S(2)}) collective-permute-start(bf16[16,128,128]{2,1,0:T(8,128)(2,1)S(1)} %get-tuple-element.90), channel_id=1, source_target_pairs={{0,24},{4,28},{8,0},{12,4},{16,8},{20,12},{24,16},{28,20},{32,56},... | collective-permute-start | bytes 1572872 | tf_op jit(solution)/shard_map/ppermute | solution.py:585
  99.3 1.6 collective-permute-start.33
  101.0 2.8 %collective-permute-done.29.refs_1_ = bf16[16,128,128]{2,1,0:T(8,128)(2,1)S(1)} collective-permute-done((bf16[16,128,128]{2,1,0:T(8,128)(2,1)S(1)}, bf16[16,128,128]{2,1,0:T(8,128)(2,1)S(1)}, u32[]{:S(2)}, u32[]{:S(2)}) %collective-permute-start.29) | collective-permute-done | bytes 524320 | tf_op jit(solution)/shard_map/ppermute | solution.py:585
  104.8 1.2 collective-permute-done.30.refs_2_
  106.0 16.7 %collective-permute-start.45 = (bf16[128,1280]{1,0:T(8,128)(2,1)}, bf16[128,1280]{1,0:T(8,128)(2,1)S(1)}, u32[]{:S(2)}, u32[]{:S(2)}) collective-permute-start(bf16[128,1280]{1,0:T(8,128)(2,1)} %collective-permute-done.3.bt.refs_1_), channel_id=1, source_target_pairs={{0,4},{4,0},{8,12},{12,8},{16,20},{20,16},{24,28},{28,24},{32,36},... | collective-permute-start | bytes 983048 | tf_op jit(solution)/shard_map/ppermute | solution.py:585
  123.1 2.4 %collective-permute-start.35 = (f32[4,128,128]{2,1,0:T(8,128)S(1)}, f32[4,128,128]{2,1,0:T(8,128)S(1)}, u32[]{:S(2)}, u32[]{:S(2)}) collective-permute-start(f32[4,128,128]{2,1,0:T(8,128)S(1)} %get-tuple-element.97), channel_id=1, source_target_pairs={{0,32},{4,36},{8,40},{12,44},{16,48},{20,52},{24,56},{28,60},{32,6... | collective-permute-start | bytes 786440 | tf_op jit(solution)/shard_map/ppermute | solution.py:585
  125.9 2.0 collective-permute-start.37
  127.9 2.7 %collective-permute-start.39 = (f32[4,128,128]{2,1,0:T(8,128)S(1)}, f32[4,128,128]{2,1,0:T(8,128)S(1)}, u32[]{:S(2)}, u32[]{:S(2)}) collective-permute-start(f32[4,128,128]{2,1,0:T(8,128)S(1)} %get-tuple-element.102), channel_id=1, source_target_pairs={{0,24},{4,28},{8,0},{12,4},{16,8},{20,12},{24,16},{28,20},{32,56},... | collective-permute-start | bytes 786440 | tf_op jit(solution)/shard_map/ppermute | solution.py:585
  130.6 2.2 collective-permute-done.35.refs_1_
  133.8 15.2 %collective-permute-start.48 = (bf16[128,1280]{1,0:T(8,128)(2,1)}, bf16[128,1280]{1,0:T(8,128)(2,1)S(1)}, u32[]{:S(2)}, u32[]{:S(2)}) collective-permute-start(bf16[128,1280]{1,0:T(8,128)(2,1)} %collective-permute-done.5.cl.refs_4_), channel_id=1, source_target_pairs={{0,4},{4,0},{8,12},{12,8},{16,20},{20,16},{24,28},{28,24},{32,36},... | collective-permute-start | bytes 983048 | tf_op jit(solution)/shard_map/ppermute | solution.py:585
  150.2 2.1 collective-permute-start.49
  152.3 2.3 %collective-permute-start.50 = (bf16[128,1280]{1,0:T(8,128)(2,1)S(1)}, bf16[128,1280]{1,0:T(8,128)(2,1)S(1)}, u32[]{:S(2)}, u32[]{:S(2)}) collective-permute-start(bf16[128,1280]{1,0:T(8,128)(2,1)S(1)} %collective-permute-done.6.b.refs_6_), channel_id=1, source_target_pairs={{0,4},{4,0},{8,12},{12,8},{16,20},{20,16},{24,28},{28,24},{32,36},... | collective-permute-start | bytes 983048 | tf_op jit(solution)/shard_map/ppermute | solution.py:585
  155.8 2.7 %flip.1.ft = bf16[4,1280,512]{2,1,0:T(8,128)(2,1)S(1)} custom-call(bf16[256,1280]{1,0:T(8,128)(2,1)S(1)} %copy-done.3, bf16[128,1280]{1,0:T(8,128)(2,1)} %collective-permute-done.3.bt.refs_1_, bf16[128,1280]{1,0:T(8,128)(2,1)S(1)} %collective-permute-done.7.bl.refs_2_, bf16[128,1280]{1,0:T(8,128)(2,1)S(1)} %collective-permute-done.8.ct.refs_3_, ...), custom_call_target="tpu_custom_call" | custom-call | tf_op jit(solution)/shard_map/flip/pallas_call | solution.py:542
  158.5 2.5 %weight_partials.1 = (f32[8,160,128]{2,1,0:T(8,128)S(1)}, bf16[8,160,128]{2,1,0:T(8,128)(2,1)S(1)}, bf16[8,160,128]{2,1,0:T(8,128)(2,1)S(1)}, bf16[8,160,128]{2,...) custom-call(s32[17]{0:T(128)S(1)} %get-tuple-element.70.place_ref.p,, ...), custom_call_target="tpu_custom_call" | custom-call | tf_op jit(solution)/shard_map/weight_partials/pallas_call | solution.py:572
  161.1 2.7 %collective-permute-start.52 = (bf16[8,160,128]{2,1,0:T(8,128)(2,1)S(1)}, bf16[8,160,128]{2,1,0:T(8,128)(2,1)S(1)}, u32[]{:S(2)}, u32[]{:S(2)}) collective-permute-start(bf16[8,160,128]{2,1,0:T(8,128)(2,1)S(1)} %get-tuple-element.115), channel_id=1, source_target_pairs={{0,24},{4,28},{8,0},{12,4},{16,8},{20,12},{24,16},{28,20},{32,56},... | collective-permute-start | bytes 983048 | tf_op jit(solution)/shard_map/ppermute | solution.py:585
  164.5 2.1 collective-permute-start.55
  166.6 4.6 %collective-permute-done.51.refs_1_ = bf16[8,160,128]{2,1,0:T(8,128)(2,1)S(1)} collective-permute-done((bf16[8,160,128]{2,1,0:T(8,128)(2,1)S(1)}, bf16[8,160,128]{2,1,0:T(8,128)(2,1)S(1)}, u32[]{:S(2)}, u32[]{:S(2)}) %collective-permute-start.51) | collective-permute-done | bytes 327712 | tf_op jit(solution)/shard_map/ppermute | solution.py:585
  171.2 2.2 collective-permute-start.56
  173.4 4.9 %collective-permute-done.53.refs_3_ = bf16[8,160,128]{2,1,0:T(8,128)(2,1)S(1)} collective-permute-done((bf16[8,160,128]{2,1,0:T(8,128)(2,1)S(1)}, bf16[8,160,128]{2,1,0:T(8,128)(2,1)S(1)}, u32[]{:S(2)}, u32[]{:S(2)}) %collective-permute-start.53) | collective-permute-done | bytes 327712 | tf_op jit(solution)/shard_map/ppermute | solution.py:585
  178.4 1.7 collective-permute-done.56.refs_7_
  180.4 2.0 collective-permute-start.57
  183.6 1.3 collective-permute-start.59
  185.3 3.0 %collective-permute-start.28 = (bf16[256,1280]{1,0:T(8,128)(2,1)S(1)}, bf16[256,1280]{1,0:T(8,128)(2,1)S(1)}, u32[]{:S(2)}, u32[]{:S(2)}) collective-permute-start(bf16[256,1280]{1,0:T(8,128)(2,1)S(1)} %slice.3), channel_id=1, source_target_pairs={{0,4},{4,0},{8,12},{12,8},{16,20},{20,16},{24,28},{28,24},{32,36},... | collective-permute-start | bytes 1966088 | tf_op jit(solution)/shard_map/ppermute | solution.py:585
  188.3 3.0 %input_partials.1 = (bf16[256,1280]{1,0:T(8,128)(2,1)S(1)}, bf16[256,1280]{1,0:T(8,128)(2,1)S(1)}, bf16[256,1280]{1,0:T(8,128)(2,1)S(1)}, bf16[256,1280]{1,0:T(8,128)(2,1)S(1)}) custom-call(s32[17]{0:T(128)S(1)} %get-tuple-element.70.place_ref.p, bf16[512,256]{1,0:T(8,128)(2,1)S(1)} %get-tuple-element.106.a.g, ...), custom_call_target="tpu_custom_call" | custom-call | tf_op jit(solution)/shard_map/input_partials/pallas_call | solution.py:517
  191.5 2.7 %collective-permute-start.43 = (bf16[256,1280]{1,0:T(8,128)(2,1)S(1)}, bf16[256,1280]{1,0:T(8,128)(2,1)S(1)}, u32[]{:S(2)}, u32[]{:S(2)}) collective-permute-start(bf16[256,1280]{1,0:T(8,128)(2,1)S(1)} %get-tuple-element.110), channel_id=1, source_target_pairs={{0,3},{1,0},{2,1},{3,2},{4,7},{5,4},{6,5},{7,6},{8,11},{9,8},{10,9... | collective-permute-start | bytes 1966088 | tf_op jit(solution)/shard_map/ppermute | solution.py:585
  194.8 2.5 %collective-permute-start.61 = (f32[2,160,128]{2,1,0:T(8,128)S(1)}, f32[2,160,128]{2,1,0:T(8,128)S(1)}, u32[]{:S(2)}, u32[]{:S(2)}) collective-permute-start(f32[2,160,128]{2,1,0:T(8,128)S(1)} %get-tuple-element.127), channel_id=1, source_target_pairs={{0,24},{4,28},{8,0},{12,4},{16,8},{20,12},{24,16},{28,20},{32,56},... | collective-permute-start | bytes 491528 | tf_op jit(solution)/shard_map/ppermute | solution.py:585
  197.3 3.1 %collective-permute-done.61.refs_6_ = f32[2,160,128]{2,1,0:T(8,128)S(1)} collective-permute-done((f32[2,160,128]{2,1,0:T(8,128)S(1)}, f32[2,160,128]{2,1,0:T(8,128)S(1)}, u32[]{:S(2)}, u32[]{:S(2)}) %collective-permute-start.61) | collective-permute-done | bytes 163872 | tf_op jit(solution)/shard_map/ppermute | solution.py:585
  200.4 2.2 collective-permute-start.62
  202.5 3.5 %collective-permute-done.62.refs_7_ = f32[2,160,128]{2,1,0:T(8,128)S(1)} collective-permute-done((f32[2,160,128]{2,1,0:T(8,128)S(1)}, f32[2,160,128]{2,1,0:T(8,128)S(1)}, u32[]{:S(2)}, u32[]{:S(2)}) %collective-permute-start.62) | collective-permute-done | bytes 163872 | tf_op jit(solution)/shard_map/ppermute | solution.py:585
  206.1 2.6 %collective-permute-start.63 = (f32[160,256]{1,0:T(8,128)S(1)}, f32[160,256]{1,0:T(8,128)S(1)}, u32[]{:S(2)}, u32[]{:S(2)}) collective-permute-start(f32[160,256]{1,0:T(8,128)S(1)} %get-tuple-element.130), channel_id=1, source_target_pairs={{0,4},{4,0},{8,12},{12,8},{16,20},{20,16},{24,28},{28,24},{32,36},... | collective-permute-start | bytes 491528 | tf_op jit(solution)/shard_map/ppermute | solution.py:585
  208.7 1.7 join_rows.1
  210.4 1.3 join_weights.1
  211.6 10.2 %collective-permute-done.43 = bf16[256,1280]{1,0:T(8,128)(2,1)S(1)} collective-permute-done((bf16[256,1280]{1,0:T(8,128)(2,1)S(1)}, bf16[256,1280]{1,0:T(8,128)(2,1)S(1)}, u32[]{:S(2)}, u32[]{:S(2)}) %collective-permute-start.43) | collective-permute-done | bytes 655392 | tf_op jit(solution)/shard_map/ppermute | solution.py:585
  221.8 1.7 collective-permute-done.44
  223.5 1.2 add_convert_fusion
  (104 shorter events, 19.6 us)
Async XLA Ops:
  2.5 11.1 %collective-permute-start.1 = (bf16[256,640]{1,0:T(8,128)(2,1)}, bf16[256,640]{1,0:T(8,128)(2,1)}, u32[]{:S(2)}, u32[]{:S(2)}) collective-permute-start(bf16[256,640]{1,0:T(8,128)(2,1)} %constant_dynamic-slice_fusion.1), channel_id=1, source_target_pairs={{0,4},{4,0},{8,12},{12,8},{16,20},{20,16},{24,28},{28,24},{32,36},... | collective-permute-start | bytes 983048 | tf_op jit(solution)/shard_map/ppermute | solution.py:585
  5.6 8.0 %collective-permute-start.2 = (bf16[256,640]{1,0:T(8,128)(2,1)}, bf16[256,640]{1,0:T(8,128)(2,1)}, u32[]{:S(2)}, u32[]{:S(2)}) collective-permute-start(bf16[256,640]{1,0:T(8,128)(2,1)} %constant_dynamic-slice_fusion), channel_id=1, source_target_pairs={{0,4},{4,0},{8,12},{12,8},{16,20},{20,16},{24,28},{28,24},{32,36},... | collective-permute-start | bytes 983048 | tf_op jit(solution)/shard_map/ppermute | solution.py:585
  5.6 17.5 %collective-permute-start = (bf16[256,1280]{1,0:T(8,128)(2,1)S(1)}, bf16[256,1280]{1,0:T(8,128)(2,1)}, u32[]{:S(2)}, u32[]{:S(2)}) collective-permute-start(bf16[256,1280]{1,0:T(8,128)(2,1)S(1)} %copy-done.3), channel_id=1, source_target_pairs={{0,4},{4,0},{8,12},{12,8},{16,20},{20,16},{24,28},{28,24},{32,36},... | collective-permute-start | bytes 1966088 | tf_op jit(solution)/shard_map/ppermute | solution.py:585
  7.0 12.2 %collective-permute-start.3 = (bf16[128,1280]{1,0:T(8,128)(2,1)}, bf16[128,1280]{1,0:T(8,128)(2,1)}, u32[]{:S(2)}, u32[]{:S(2)}) collective-permute-start(bf16[128,1280]{1,0:T(8,128)(2,1)} %get-tuple-element.74), channel_id=1, source_target_pairs={{0,1},{1,2},{2,3},{3,0},{4,5},{5,6},{6,7},{7,4},{8,9},{9,10},{10,1... | collective-permute-start | bytes 983048 | tf_op jit(solution)/shard_map/ppermute | solution.py:585
  8.7 10.4 %collective-permute-start.5 = (bf16[128,1280]{1,0:T(8,128)(2,1)}, bf16[128,1280]{1,0:T(8,128)(2,1)}, u32[]{:S(2)}, u32[]{:S(2)}) collective-permute-start(bf16[128,1280]{1,0:T(8,128)(2,1)} %get-tuple-element.75), channel_id=1, source_target_pairs={{0,3},{1,0},{2,1},{3,2},{4,7},{5,4},{6,5},{7,6},{8,11},{9,8},{10,9... | collective-permute-start | bytes 983048 | tf_op jit(solution)/shard_map/ppermute | solution.py:585
  13.5 12.5 %collective-permute-start.7 = (bf16[128,1280]{1,0:T(8,128)(2,1)}, bf16[128,1280]{1,0:T(8,128)(2,1)S(1)}, u32[]{:S(2)}, u32[]{:S(2)}) collective-permute-start(bf16[128,1280]{1,0:T(8,128)(2,1)} %get-tuple-element.75), channel_id=1, source_target_pairs={{0,1},{1,2},{2,3},{3,0},{4,5},{5,6},{6,7},{7,4},{8,9},{9,10},{10,1... | collective-permute-start | bytes 983048 | tf_op jit(solution)/shard_map/ppermute | solution.py:585
  13.6 12.5 %collective-permute-start.8 = (bf16[128,1280]{1,0:T(8,128)(2,1)}, bf16[128,1280]{1,0:T(8,128)(2,1)S(1)}, u32[]{:S(2)}, u32[]{:S(2)}) collective-permute-start(bf16[128,1280]{1,0:T(8,128)(2,1)} %get-tuple-element.74), channel_id=1, source_target_pairs={{0,3},{1,0},{2,1},{3,2},{4,7},{5,4},{6,5},{7,6},{8,11},{9,8},{10,9... | collective-permute-start | bytes 983048 | tf_op jit(solution)/shard_map/ppermute | solution.py:585
  19.1 13.9 %collective-permute-start.4 = (bf16[128,1280]{1,0:T(8,128)(2,1)}, bf16[128,1280]{1,0:T(8,128)(2,1)S(1)}, u32[]{:S(2)}, u32[]{:S(2)}) collective-permute-start(bf16[128,1280]{1,0:T(8,128)(2,1)} %collective-permute-done.3.bt.refs_1_), channel_id=1, source_target_pairs={{0,1},{1,2},{2,3},{3,0},{4,5},{5,6},{6,7},{7,4},{8,9},{9,10},{10,1... | collective-permute-start | bytes 983048 | tf_op jit(solution)/shard_map/ppermute | solution.py:585
  19.2 13.9 %collective-permute-start.6 = (bf16[128,1280]{1,0:T(8,128)(2,1)}, bf16[128,1280]{1,0:T(8,128)(2,1)S(1)}, u32[]{:S(2)}, u32[]{:S(2)}) collective-permute-start(bf16[128,1280]{1,0:T(8,128)(2,1)} %collective-permute-done.5.cl.refs_4_), channel_id=1, source_target_pairs={{0,3},{1,0},{2,1},{3,2},{4,7},{5,4},{6,5},{7,6},{8,11},{9,8},{10,9... | collective-permute-start | bytes 983048 | tf_op jit(solution)/shard_map/ppermute | solution.py:585
  34.2 5.4 %collective-permute-start.10 = (bf16[256,256]{1,0:T(8,128)(2,1)S(1)}, bf16[256,256]{1,0:T(8,128)(2,1)S(1)}, u32[]{:S(2)}, u32[]{:S(2)}) collective-permute-start(bf16[256,256]{1,0:T(8,128)(2,1)S(1)} %get-tuple-element.79.a), channel_id=1, source_target_pairs={{0,24},{4,28},{8,0},{12,4},{16,8},{20,12},{24,16},{28,20},{32,56},... | collective-permute-start | bytes 393224 | tf_op jit(solution)/shard_map/ppermute | solution.py:585
  36.8 5.4 %collective-permute-start.11 = (bf16[256,256]{1,0:T(8,128)(2,1)S(1)}, bf16[256,256]{1,0:T(8,128)(2,1)S(1)}, u32[]{:S(2)}, u32[]{:S(2)}) collective-permute-start(bf16[256,256]{1,0:T(8,128)(2,1)S(1)} %get-tuple-element.79.a), channel_id=1, source_target_pairs={{0,16},{4,20},{8,24},{12,28},{16,0},{20,4},{24,8},{28,12},{32,48},... | collective-permute-start | bytes 393224 | tf_op jit(solution)/shard_map/ppermute | solution.py:585
  37.3 9.1 %collective-permute-start.9 = (bf16[256,256]{1,0:T(8,128)(2,1)S(1)}, bf16[256,256]{1,0:T(8,128)(2,1)S(1)}, u32[]{:S(2)}, u32[]{:S(2)}) collective-permute-start(bf16[256,256]{1,0:T(8,128)(2,1)S(1)} %get-tuple-element.79.a), channel_id=1, source_target_pairs={{0,8},{4,12},{8,16},{12,20},{16,24},{20,28},{24,0},{28,4},{32,40},... | collective-permute-start | bytes 393224 | tf_op jit(solution)/shard_map/ppermute | solution.py:585
  37.9 11.4 %collective-permute-start.18 = (bf16[256,256]{1,0:T(8,128)(2,1)S(1)}, bf16[256,256]{1,0:T(8,128)(2,1)S(1)}, u32[]{:S(2)}, u32[]{:S(2)}) collective-permute-start(bf16[256,256]{1,0:T(8,128)(2,1)S(1)} %get-tuple-element.82), channel_id=1, source_target_pairs={{0,4},{4,0},{8,12},{12,8},{16,20},{20,16},{24,28},{28,24},{32,36},... | collective-permute-start | bytes 393224 | tf_op jit(solution)/shard_map/ppermute | solution.py:585
  46.4 15.5 %collective-permute-start.12 = (bf16[4,128,256]{2,1,0:T(8,128)(2,1)S(1)}, bf16[4,128,256]{2,1,0:T(8,128)(2,1)S(1)}, u32[]{:S(2)}, u32[]{:S(2)}) collective-permute-start(bf16[4,128,256]{2,1,0:T(8,128)(2,1)S(1)} %get-tuple-element.80.refs_0_), channel_id=1, source_target_pairs={{0,32},{4,36},{8,40},{12,44},{16,48},{20,52},{24,56},{28,60},{32,6... | collective-permute-start | bytes 786440 | tf_op jit(solution)/shard_map/ppermute | solution.py:585
  47.8 16.8 %collective-permute-start.15 = (bf16[4,128,256]{2,1,0:T(8,128)(2,1)S(1)}, bf16[4,128,256]{2,1,0:T(8,128)(2,1)S(1)}, u32[]{:S(2)}, u32[]{:S(2)}) collective-permute-start(bf16[4,128,256]{2,1,0:T(8,128)(2,1)S(1)} %get-tuple-element.81.refs_1_), channel_id=1, source_target_pairs={{0,96},{4,100},{8,104},{12,108},{16,112},{20,116},{24,120},{28,124... | collective-permute-start | bytes 786440 | tf_op jit(solution)/shard_map/ppermute | solution.py:585
  49.3 8.5 %collective-permute-start.19 = (bf16[256,256]{1,0:T(8,128)(2,1)S(1)}, bf16[256,256]{1,0:T(8,128)(2,1)S(1)}, u32[]{:S(2)}, u32[]{:S(2)}) collective-permute-start(bf16[256,256]{1,0:T(8,128)(2,1)S(1)} %collective-permute-done.18.a), channel_id=1, source_target_pairs={{0,32},{4,36},{8,40},{12,44},{16,48},{20,52},{24,56},{28,60},{32,6... | collective-permute-start | bytes 393224 | tf_op jit(solution)/shard_map/ppermute | solution.py:585
  49.3 8.5 %collective-permute-start.20 = (bf16[256,256]{1,0:T(8,128)(2,1)S(1)}, bf16[256,256]{1,0:T(8,128)(2,1)S(1)}, u32[]{:S(2)}, u32[]{:S(2)}) collective-permute-start(bf16[256,256]{1,0:T(8,128)(2,1)S(1)} %collective-permute-done.18.a), channel_id=1, source_target_pairs={{0,96},{4,100},{8,104},{12,108},{16,112},{20,116},{24,120},{28,124... | collective-permute-start | bytes 393224 | tf_op jit(solution)/shard_map/ppermute | solution.py:585
  52.0 9.8 %collective-permute-start.21 = (bf16[256,256]{1,0:T(8,128)(2,1)S(1)}, bf16[256,256]{1,0:T(8,128)(2,1)S(1)}, u32[]{:S(2)}, u32[]{:S(2)}) collective-permute-start(bf16[256,256]{1,0:T(8,128)(2,1)S(1)} %collective-permute-done.18.a), channel_id=1, source_target_pairs={{0,64},{4,68},{8,72},{12,76},{16,80},{20,84},{24,88},{28,92},{32,9... | collective-permute-start | bytes 393224 | tf_op jit(solution)/shard_map/ppermute | solution.py:585
  57.8 9.7 %collective-permute-start.13 = (bf16[4,128,256]{2,1,0:T(8,128)(2,1)S(1)}, bf16[4,128,256]{2,1,0:T(8,128)(2,1)S(1)}, u32[]{:S(2)}, u32[]{:S(2)}) collective-permute-start(bf16[4,128,256]{2,1,0:T(8,128)(2,1)S(1)} %get-tuple-element.81.refs_1_), channel_id=1, source_target_pairs={{0,32},{4,36},{8,40},{12,44},{16,48},{20,52},{24,56},{28,60},{32,6... | collective-permute-start | bytes 786440 | tf_op jit(solution)/shard_map/ppermute | solution.py:585
  57.8 9.7 %collective-permute-start.14 = (bf16[4,128,256]{2,1,0:T(8,128)(2,1)S(1)}, bf16[4,128,256]{2,1,0:T(8,128)(2,1)S(1)}, u32[]{:S(2)}, u32[]{:S(2)}) collective-permute-start(bf16[4,128,256]{2,1,0:T(8,128)(2,1)S(1)} %get-tuple-element.80.refs_0_), channel_id=1, source_target_pairs={{0,96},{4,100},{8,104},{12,108},{16,112},{20,116},{24,120},{28,124... | collective-permute-start | bytes 786440 | tf_op jit(solution)/shard_map/ppermute | solution.py:585
  61.8 6.7 %collective-permute-start.22 = (bf16[4,128,256]{2,1,0:T(8,128)(2,1)S(1)}, bf16[4,128,256]{2,1,0:T(8,128)(2,1)S(1)}, u32[]{:S(2)}, u32[]{:S(2)}) collective-permute-start(bf16[4,128,256]{2,1,0:T(8,128)(2,1)S(1)} %get-tuple-element.83.refs_8_), channel_id=1, source_target_pairs={{0,8},{4,12},{8,16},{12,20},{16,24},{20,28},{24,0},{28,4},{32,40},... | collective-permute-start | bytes 786440 | tf_op jit(solution)/shard_map/ppermute | solution.py:585
  61.9 8.3 %collective-permute-start.25 = (bf16[4,128,256]{2,1,0:T(8,128)(2,1)S(1)}, bf16[4,128,256]{2,1,0:T(8,128)(2,1)S(1)}, u32[]{:S(2)}, u32[]{:S(2)}) collective-permute-start(bf16[4,128,256]{2,1,0:T(8,128)(2,1)S(1)} %get-tuple-element.84.refs_9_), channel_id=1, source_target_pairs={{0,24},{4,28},{8,0},{12,4},{16,8},{20,12},{24,16},{28,20},{32,56},... | collective-permute-start | bytes 786440 | tf_op jit(solution)/shard_map/ppermute | solution.py:585
  64.5 9.4 %collective-permute-start.23 = (bf16[4,128,256]{2,1,0:T(8,128)(2,1)S(1)}, bf16[4,128,256]{2,1,0:T(8,128)(2,1)S(1)}, u32[]{:S(2)}, u32[]{:S(2)}) collective-permute-start(bf16[4,128,256]{2,1,0:T(8,128)(2,1)S(1)} %get-tuple-element.84.refs_9_), channel_id=1, source_target_pairs={{0,8},{4,12},{8,16},{12,20},{16,24},{20,28},{24,0},{28,4},{32,40},... | collective-permute-start | bytes 786440 | tf_op jit(solution)/shard_map/ppermute | solution.py:585
  67.5 7.1 %collective-permute-start.24 = (bf16[4,128,256]{2,1,0:T(8,128)(2,1)S(1)}, bf16[4,128,256]{2,1,0:T(8,128)(2,1)S(1)}, u32[]{:S(2)}, u32[]{:S(2)}) collective-permute-start(bf16[4,128,256]{2,1,0:T(8,128)(2,1)S(1)} %get-tuple-element.83.refs_8_), channel_id=1, source_target_pairs={{0,24},{4,28},{8,0},{12,4},{16,8},{20,12},{24,16},{28,20},{32,56},... | collective-permute-start | bytes 786440 | tf_op jit(solution)/shard_map/ppermute | solution.py:585
  67.5 7.1 %collective-permute-start.16 = (bf16[4,128,256]{2,1,0:T(8,128)(2,1)S(1)}, bf16[4,128,256]{2,1,0:T(8,128)(2,1)S(1)}, u32[]{:S(2)}, u32[]{:S(2)}) collective-permute-start(bf16[4,128,256]{2,1,0:T(8,128)(2,1)S(1)} %collective-permute-done.12.refs_2_), channel_id=1, source_target_pairs={{0,32},{4,36},{8,40},{12,44},{16,48},{20,52},{24,56},{28,60},{32,6... | collective-permute-start | bytes 786440 | tf_op jit(solution)/shard_map/ppermute | solution.py:585
  68.5 6.2 %collective-permute-start.17 = (bf16[4,128,256]{2,1,0:T(8,128)(2,1)S(1)}, bf16[4,128,256]{2,1,0:T(8,128)(2,1)S(1)}, u32[]{:S(2)}, u32[]{:S(2)}) collective-permute-start(bf16[4,128,256]{2,1,0:T(8,128)(2,1)S(1)} %collective-permute-done.15.refs_5_), channel_id=1, source_target_pairs={{0,96},{4,100},{8,104},{12,108},{16,112},{20,116},{24,120},{28,124... | collective-permute-start | bytes 786440 | tf_op jit(solution)/shard_map/ppermute | solution.py:585
  70.2 9.5 %collective-permute-start.26 = (bf16[4,128,256]{2,1,0:T(8,128)(2,1)S(1)}, bf16[4,128,256]{2,1,0:T(8,128)(2,1)S(1)}, u32[]{:S(2)}, u32[]{:S(2)}) collective-permute-start(bf16[4,128,256]{2,1,0:T(8,128)(2,1)S(1)} %collective-permute-done.22.refs_10_), channel_id=1, source_target_pairs={{0,8},{4,12},{8,16},{12,20},{16,24},{20,28},{24,0},{28,4},{32,40},... | collective-permute-start | bytes 786440 | tf_op jit(solution)/shard_map/ppermute | solution.py:585
  74.0 5.8 %collective-permute-start.27 = (bf16[4,128,256]{2,1,0:T(8,128)(2,1)S(1)}, bf16[4,128,256]{2,1,0:T(8,128)(2,1)S(1)}, u32[]{:S(2)}, u32[]{:S(2)}) collective-permute-start(bf16[4,128,256]{2,1,0:T(8,128)(2,1)S(1)} %collective-permute-done.25.refs_13_), channel_id=1, source_target_pairs={{0,24},{4,28},{8,0},{12,4},{16,8},{20,12},{24,16},{28,20},{32,56},... | collective-permute-start | bytes 786440 | tf_op jit(solution)/shard_map/ppermute | solution.py:585
  94.4 9.3 %collective-permute-start.29 = (bf16[16,128,128]{2,1,0:T(8,128)(2,1)S(1)}, bf16[16,128,128]{2,1,0:T(8,128)(2,1)S(1)}, u32[]{:S(2)}, u32[]{:S(2)}) collective-permute-start(bf16[16,128,128]{2,1,0:T(8,128)(2,1)S(1)} %get-tuple-element.89), channel_id=1, source_target_pairs={{0,8},{4,12},{8,16},{12,20},{16,24},{20,28},{24,0},{28,4},{32,40},... | collective-permute-start | bytes 1572872 | tf_op jit(solution)/shard_map/ppermute | solution.py:585
  94.8 11.2 %collective-permute-start.30 = (bf16[16,128,128]{2,1,0:T(8,128)(2,1)S(1)}, bf16[16,128,128]{2,1,0:T(8,128)(2,1)S(1)}, u32[]{:S(2)}, u32[]{:S(2)}) collective-permute-start(bf16[16,128,128]{2,1,0:T(8,128)(2,1)S(1)} %get-tuple-element.90), channel_id=1, source_target_pairs={{0,24},{4,28},{8,0},{12,4},{16,8},{20,12},{24,16},{28,20},{32,56},... | collective-permute-start | bytes 1572872 | tf_op jit(solution)/shard_map/ppermute | solution.py:585
  97.2 25.5 %collective-permute-start.31 = (bf16[16,128,128]{2,1,0:T(8,128)(2,1)S(1)}, bf16[16,128,128]{2,1,0:T(8,128)(2,1)S(1)}, u32[]{:S(2)}, u32[]{:S(2)}) collective-permute-start(bf16[16,128,128]{2,1,0:T(8,128)(2,1)S(1)} %get-tuple-element.91), channel_id=1, source_target_pairs={{0,16},{4,20},{8,24},{12,28},{16,0},{20,4},{24,8},{28,12},{32,48},... | collective-permute-start | bytes 1572872 | tf_op jit(solution)/shard_map/ppermute | solution.py:585
  98.3 24.4 %collective-permute-start.32 = (bf16[16,128,128]{2,1,0:T(8,128)(2,1)S(1)}, bf16[16,128,128]{2,1,0:T(8,128)(2,1)S(1)}, u32[]{:S(2)}, u32[]{:S(2)}) collective-permute-start(bf16[16,128,128]{2,1,0:T(8,128)(2,1)S(1)} %get-tuple-element.93), channel_id=1, source_target_pairs={{0,32},{4,36},{8,40},{12,44},{16,48},{20,52},{24,56},{28,60},{32,6... | collective-permute-start | bytes 1572872 | tf_op jit(solution)/shard_map/ppermute | solution.py:585
  99.3 23.3 %collective-permute-start.33 = (bf16[16,128,128]{2,1,0:T(8,128)(2,1)S(1)}, bf16[16,128,128]{2,1,0:T(8,128)(2,1)S(1)}, u32[]{:S(2)}, u32[]{:S(2)}) collective-permute-start(bf16[16,128,128]{2,1,0:T(8,128)(2,1)S(1)} %get-tuple-element.94), channel_id=1, source_target_pairs={{0,96},{4,100},{8,104},{12,108},{16,112},{20,116},{24,120},{28,124... | collective-permute-start | bytes 1572872 | tf_op jit(solution)/shard_map/ppermute | solution.py:585
  103.7 18.9 %collective-permute-start.34 = (bf16[16,128,128]{2,1,0:T(8,128)(2,1)S(1)}, bf16[16,128,128]{2,1,0:T(8,128)(2,1)S(1)}, u32[]{:S(2)}, u32[]{:S(2)}) collective-permute-start(bf16[16,128,128]{2,1,0:T(8,128)(2,1)S(1)} %get-tuple-element.95), channel_id=1, source_target_pairs={{0,64},{4,68},{8,72},{12,76},{16,80},{20,84},{24,88},{28,92},{32,9... | collective-permute-start | bytes 1572872 | tf_op jit(solution)/shard_map/ppermute | solution.py:585
  106.0 21.9 %collective-permute-start.45 = (bf16[128,1280]{1,0:T(8,128)(2,1)}, bf16[128,1280]{1,0:T(8,128)(2,1)S(1)}, u32[]{:S(2)}, u32[]{:S(2)}) collective-permute-start(bf16[128,1280]{1,0:T(8,128)(2,1)} %collective-permute-done.3.bt.refs_1_), channel_id=1, source_target_pairs={{0,4},{4,0},{8,12},{12,8},{16,20},{20,16},{24,28},{28,24},{32,36},... | collective-permute-start | bytes 983048 | tf_op jit(solution)/shard_map/ppermute | solution.py:585
  123.1 9.7 %collective-permute-start.35 = (f32[4,128,128]{2,1,0:T(8,128)S(1)}, f32[4,128,128]{2,1,0:T(8,128)S(1)}, u32[]{:S(2)}, u32[]{:S(2)}) collective-permute-start(f32[4,128,128]{2,1,0:T(8,128)S(1)} %get-tuple-element.97), channel_id=1, source_target_pairs={{0,32},{4,36},{8,40},{12,44},{16,48},{20,52},{24,56},{28,60},{32,6... | collective-permute-start | bytes 786440 | tf_op jit(solution)/shard_map/ppermute | solution.py:585
  125.5 8.3 %collective-permute-start.36 = (f32[4,128,128]{2,1,0:T(8,128)S(1)}, f32[4,128,128]{2,1,0:T(8,128)S(1)}, u32[]{:S(2)}, u32[]{:S(2)}) collective-permute-start(f32[4,128,128]{2,1,0:T(8,128)S(1)} %get-tuple-element.98), channel_id=1, source_target_pairs={{0,96},{4,100},{8,104},{12,108},{16,112},{20,116},{24,120},{28,124... | collective-permute-start | bytes 786440 | tf_op jit(solution)/shard_map/ppermute | solution.py:585
  125.9 23.2 %collective-permute-start.37 = (f32[4,128,128]{2,1,0:T(8,128)S(1)}, f32[4,128,128]{2,1,0:T(8,128)S(1)}, u32[]{:S(2)}, u32[]{:S(2)}) collective-permute-start(f32[4,128,128]{2,1,0:T(8,128)S(1)} %get-tuple-element.99), channel_id=1, source_target_pairs={{0,64},{4,68},{8,72},{12,76},{16,80},{20,84},{24,88},{28,92},{32,9... | collective-permute-start | bytes 786440 | tf_op jit(solution)/shard_map/ppermute | solution.py:585
  127.9 22.3 %collective-permute-start.38 = (f32[4,128,128]{2,1,0:T(8,128)S(1)}, f32[4,128,128]{2,1,0:T(8,128)S(1)}, u32[]{:S(2)}, u32[]{:S(2)}) collective-permute-start(f32[4,128,128]{2,1,0:T(8,128)S(1)} %get-tuple-element.101), channel_id=1, source_target_pairs={{0,8},{4,12},{8,16},{12,20},{16,24},{20,28},{24,0},{28,4},{32,40},... | collective-permute-start | bytes 786440 | tf_op jit(solution)/shard_map/ppermute | solution.py:585
  127.9 22.3 %collective-permute-start.39 = (f32[4,128,128]{2,1,0:T(8,128)S(1)}, f32[4,128,128]{2,1,0:T(8,128)S(1)}, u32[]{:S(2)}, u32[]{:S(2)}) collective-permute-start(f32[4,128,128]{2,1,0:T(8,128)S(1)} %get-tuple-element.102), channel_id=1, source_target_pairs={{0,24},{4,28},{8,0},{12,4},{16,8},{20,12},{24,16},{28,20},{32,56},... | collective-permute-start | bytes 786440 | tf_op jit(solution)/shard_map/ppermute | solution.py:585
  132.8 19.5 %collective-permute-start.40 = (f32[4,128,128]{2,1,0:T(8,128)S(1)}, f32[4,128,128]{2,1,0:T(8,128)S(1)}, u32[]{:S(2)}, u32[]{:S(2)}) collective-permute-start(f32[4,128,128]{2,1,0:T(8,128)S(1)} %get-tuple-element.103), channel_id=1, source_target_pairs={{0,16},{4,20},{8,24},{12,28},{16,0},{20,4},{24,8},{28,12},{32,48},... | collective-permute-start | bytes 786440 | tf_op jit(solution)/shard_map/ppermute | solution.py:585
  133.8 20.9 %collective-permute-start.48 = (bf16[128,1280]{1,0:T(8,128)(2,1)}, bf16[128,1280]{1,0:T(8,128)(2,1)S(1)}, u32[]{:S(2)}, u32[]{:S(2)}) collective-permute-start(bf16[128,1280]{1,0:T(8,128)(2,1)} %collective-permute-done.5.cl.refs_4_), channel_id=1, source_target_pairs={{0,4},{4,0},{8,12},{12,8},{16,20},{20,16},{24,28},{28,24},{32,36},... | collective-permute-start | bytes 983048 | tf_op jit(solution)/shard_map/ppermute | solution.py:585
  149.0 6.0 %collective-permute-start.46 = (bf16[128,1280]{1,0:T(8,128)(2,1)S(1)}, bf16[128,1280]{1,0:T(8,128)(2,1)S(1)}, u32[]{:S(2)}, u32[]{:S(2)}) collective-permute-start(bf16[128,1280]{1,0:T(8,128)(2,1)S(1)} %collective-permute-done.7.bl.refs_2_), channel_id=1, source_target_pairs={{0,4},{4,0},{8,12},{12,8},{16,20},{20,16},{24,28},{28,24},{32,36},... | collective-permute-start | bytes 983048 | tf_op jit(solution)/shard_map/ppermute | solution.py:585
  150.2 4.9 %collective-permute-start.47 = (bf16[128,1280]{1,0:T(8,128)(2,1)S(1)}, bf16[128,1280]{1,0:T(8,128)(2,1)S(1)}, u32[]{:S(2)}, u32[]{:S(2)}) collective-permute-start(bf16[128,1280]{1,0:T(8,128)(2,1)S(1)} %collective-permute-done.8.ct.refs_3_), channel_id=1, source_target_pairs={{0,4},{4,0},{8,12},{12,8},{16,20},{20,16},{24,28},{28,24},{32,36},... | collective-permute-start | bytes 983048 | tf_op jit(solution)/shard_map/ppermute | solution.py:585
  150.2 4.9 %collective-permute-start.49 = (bf16[128,1280]{1,0:T(8,128)(2,1)S(1)}, bf16[128,1280]{1,0:T(8,128)(2,1)S(1)}, u32[]{:S(2)}, u32[]{:S(2)}) collective-permute-start(bf16[128,1280]{1,0:T(8,128)(2,1)S(1)} %collective-permute-done.4.a.refs_5_), channel_id=1, source_target_pairs={{0,4},{4,0},{8,12},{12,8},{16,20},{20,16},{24,28},{28,24},{32,36},... | collective-permute-start | bytes 983048 | tf_op jit(solution)/shard_map/ppermute | solution.py:585
  152.3 3.5 %collective-permute-start.50 = (bf16[128,1280]{1,0:T(8,128)(2,1)S(1)}, bf16[128,1280]{1,0:T(8,128)(2,1)S(1)}, u32[]{:S(2)}, u32[]{:S(2)}) collective-permute-start(bf16[128,1280]{1,0:T(8,128)(2,1)S(1)} %collective-permute-done.6.b.refs_6_), channel_id=1, source_target_pairs={{0,4},{4,0},{8,12},{12,8},{16,20},{20,16},{24,28},{28,24},{32,36},... | collective-permute-start | bytes 983048 | tf_op jit(solution)/shard_map/ppermute | solution.py:585
  154.7 3.8 %collective-permute-start.41 = (bf16[256,256]{1,0:T(8,128)(2,1)S(1)}, bf16[256,256]{1,0:T(8,128)(2,1)S(1)}, u32[]{:S(2)}, u32[]{:S(2)}) collective-permute-start(bf16[256,256]{1,0:T(8,128)(2,1)S(1)} %get-tuple-element.105), channel_id=1, source_target_pairs={{0,4},{4,0},{8,12},{12,8},{16,20},{20,16},{24,28},{28,24},{32,36},... | collective-permute-start | bytes 393224 | tf_op jit(solution)/shard_map/ppermute | solution.py:585
  161.1 10.2 %collective-permute-start.51 = (bf16[8,160,128]{2,1,0:T(8,128)(2,1)S(1)}, bf16[8,160,128]{2,1,0:T(8,128)(2,1)S(1)}, u32[]{:S(2)}, u32[]{:S(2)}) collective-permute-start(bf16[8,160,128]{2,1,0:T(8,128)(2,1)S(1)} %get-tuple-element.114), channel_id=1, source_target_pairs={{0,8},{4,12},{8,16},{12,20},{16,24},{20,28},{24,0},{28,4},{32,40},... | collective-permute-start | bytes 983048 | tf_op jit(solution)/shard_map/ppermute | solution.py:585
  161.1 12.3 %collective-permute-start.52 = (bf16[8,160,128]{2,1,0:T(8,128)(2,1)S(1)}, bf16[8,160,128]{2,1,0:T(8,128)(2,1)S(1)}, u32[]{:S(2)}, u32[]{:S(2)}) collective-permute-start(bf16[8,160,128]{2,1,0:T(8,128)(2,1)S(1)} %get-tuple-element.115), channel_id=1, source_target_pairs={{0,24},{4,28},{8,0},{12,4},{16,8},{20,12},{24,16},{28,20},{32,56},... | collective-permute-start | bytes 983048 | tf_op jit(solution)/shard_map/ppermute | solution.py:585
  163.8 14.6 %collective-permute-start.53 = (bf16[8,160,128]{2,1,0:T(8,128)(2,1)S(1)}, bf16[8,160,128]{2,1,0:T(8,128)(2,1)S(1)}, u32[]{:S(2)}, u32[]{:S(2)}) collective-permute-start(bf16[8,160,128]{2,1,0:T(8,128)(2,1)S(1)} %get-tuple-element.116), channel_id=1, source_target_pairs={{0,16},{4,20},{8,24},{12,28},{16,0},{20,4},{24,8},{28,12},{32,48},... | collective-permute-start | bytes 983048 | tf_op jit(solution)/shard_map/ppermute | solution.py:585
  163.9 14.5 %collective-permute-start.54 = (bf16[8,160,128]{2,1,0:T(8,128)(2,1)S(1)}, bf16[8,160,128]{2,1,0:T(8,128)(2,1)S(1)}, u32[]{:S(2)}, u32[]{:S(2)}) collective-permute-start(bf16[8,160,128]{2,1,0:T(8,128)(2,1)S(1)} %get-tuple-element.118), channel_id=1, source_target_pairs={{0,32},{4,36},{8,40},{12,44},{16,48},{20,52},{24,56},{28,60},{32,6... | collective-permute-start | bytes 983048 | tf_op jit(solution)/shard_map/ppermute | solution.py:585
  164.5 13.9 %collective-permute-start.55 = (bf16[8,160,128]{2,1,0:T(8,128)(2,1)S(1)}, bf16[8,160,128]{2,1,0:T(8,128)(2,1)S(1)}, u32[]{:S(2)}, u32[]{:S(2)}) collective-permute-start(bf16[8,160,128]{2,1,0:T(8,128)(2,1)S(1)} %get-tuple-element.119), channel_id=1, source_target_pairs={{0,96},{4,100},{8,104},{12,108},{16,112},{20,116},{24,120},{28,124... | collective-permute-start | bytes 983048 | tf_op jit(solution)/shard_map/ppermute | solution.py:585
  171.2 8.8 %collective-permute-start.56 = (bf16[8,160,128]{2,1,0:T(8,128)(2,1)S(1)}, bf16[8,160,128]{2,1,0:T(8,128)(2,1)S(1)}, u32[]{:S(2)}, u32[]{:S(2)}) collective-permute-start(bf16[8,160,128]{2,1,0:T(8,128)(2,1)S(1)} %get-tuple-element.120), channel_id=1, source_target_pairs={{0,64},{4,68},{8,72},{12,76},{16,80},{20,84},{24,88},{28,92},{32,9... | collective-permute-start | bytes 983048 | tf_op jit(solution)/shard_map/ppermute | solution.py:585
  180.4 11.0 %collective-permute-start.57 = (f32[2,160,128]{2,1,0:T(8,128)S(1)}, f32[2,160,128]{2,1,0:T(8,128)S(1)}, u32[]{:S(2)}, u32[]{:S(2)}) collective-permute-start(f32[2,160,128]{2,1,0:T(8,128)S(1)} %get-tuple-element.122), channel_id=1, source_target_pairs={{0,32},{4,36},{8,40},{12,44},{16,48},{20,52},{24,56},{28,60},{32,6... | collective-permute-start | bytes 491528 | tf_op jit(solution)/shard_map/ppermute | solution.py:585
  182.4 9.1 %collective-permute-start.58 = (f32[2,160,128]{2,1,0:T(8,128)S(1)}, f32[2,160,128]{2,1,0:T(8,128)S(1)}, u32[]{:S(2)}, u32[]{:S(2)}) collective-permute-start(f32[2,160,128]{2,1,0:T(8,128)S(1)} %get-tuple-element.123), channel_id=1, source_target_pairs={{0,96},{4,100},{8,104},{12,108},{16,112},{20,116},{24,120},{28,124... | collective-permute-start | bytes 491528 | tf_op jit(solution)/shard_map/ppermute | solution.py:585
  183.6 10.6 %collective-permute-start.59 = (f32[2,160,128]{2,1,0:T(8,128)S(1)}, f32[2,160,128]{2,1,0:T(8,128)S(1)}, u32[]{:S(2)}, u32[]{:S(2)}) collective-permute-start(f32[2,160,128]{2,1,0:T(8,128)S(1)} %get-tuple-element.124), channel_id=1, source_target_pairs={{0,64},{4,68},{8,72},{12,76},{16,80},{20,84},{24,88},{28,92},{32,9... | collective-permute-start | bytes 491528 | tf_op jit(solution)/shard_map/ppermute | solution.py:585
  184.9 9.9 %collective-permute-start.60 = (f32[2,160,128]{2,1,0:T(8,128)S(1)}, f32[2,160,128]{2,1,0:T(8,128)S(1)}, u32[]{:S(2)}, u32[]{:S(2)}) collective-permute-start(f32[2,160,128]{2,1,0:T(8,128)S(1)} %get-tuple-element.126), channel_id=1, source_target_pairs={{0,8},{4,12},{8,16},{12,20},{16,24},{20,28},{24,0},{28,4},{32,40},... | collective-permute-start | bytes 491528 | tf_op jit(solution)/shard_map/ppermute | solution.py:585
  185.3 23.3 %collective-permute-start.28 = (bf16[256,1280]{1,0:T(8,128)(2,1)S(1)}, bf16[256,1280]{1,0:T(8,128)(2,1)S(1)}, u32[]{:S(2)}, u32[]{:S(2)}) collective-permute-start(bf16[256,1280]{1,0:T(8,128)(2,1)S(1)} %slice.3), channel_id=1, source_target_pairs={{0,4},{4,0},{8,12},{12,8},{16,20},{20,16},{24,28},{28,24},{32,36},... | collective-permute-start | bytes 1966088 | tf_op jit(solution)/shard_map/ppermute | solution.py:585
  191.4 20.2 %collective-permute-start.42 = (bf16[256,1280]{1,0:T(8,128)(2,1)S(1)}, bf16[256,1280]{1,0:T(8,128)(2,1)S(1)}, u32[]{:S(2)}, u32[]{:S(2)}) collective-permute-start(bf16[256,1280]{1,0:T(8,128)(2,1)S(1)} %get-tuple-element.109), channel_id=1, source_target_pairs={{0,1},{1,2},{2,3},{3,0},{4,5},{5,6},{6,7},{7,4},{8,9},{9,10},{10,1... | collective-permute-start | bytes 1966088 | tf_op jit(solution)/shard_map/ppermute | solution.py:585
  191.5 30.3 %collective-permute-start.43 = (bf16[256,1280]{1,0:T(8,128)(2,1)S(1)}, bf16[256,1280]{1,0:T(8,128)(2,1)S(1)}, u32[]{:S(2)}, u32[]{:S(2)}) collective-permute-start(bf16[256,1280]{1,0:T(8,128)(2,1)S(1)} %get-tuple-element.110), channel_id=1, source_target_pairs={{0,3},{1,0},{2,1},{3,2},{4,7},{5,4},{6,5},{7,6},{8,11},{9,8},{10,9... | collective-permute-start | bytes 1966088 | tf_op jit(solution)/shard_map/ppermute | solution.py:585
  194.2 29.4 %collective-permute-start.44 = (bf16[256,1280]{1,0:T(8,128)(2,1)S(1)}, bf16[256,1280]{1,0:T(8,128)(2,1)S(1)}, u32[]{:S(2)}, u32[]{:S(2)}) collective-permute-start(bf16[256,1280]{1,0:T(8,128)(2,1)S(1)} %get-tuple-element.111), channel_id=1, source_target_pairs={{0,2},{1,3},{2,0},{3,1},{4,6},{5,7},{6,4},{7,5},{8,10},{9,11},{10,... | collective-permute-start | bytes 1966088 | tf_op jit(solution)/shard_map/ppermute | solution.py:585
  194.8 5.6 %collective-permute-start.61 = (f32[2,160,128]{2,1,0:T(8,128)S(1)}, f32[2,160,128]{2,1,0:T(8,128)S(1)}, u32[]{:S(2)}, u32[]{:S(2)}) collective-permute-start(f32[2,160,128]{2,1,0:T(8,128)S(1)} %get-tuple-element.127), channel_id=1, source_target_pairs={{0,24},{4,28},{8,0},{12,4},{16,8},{20,12},{24,16},{28,20},{32,56},... | collective-permute-start | bytes 491528 | tf_op jit(solution)/shard_map/ppermute | solution.py:585
  200.4 5.7 %collective-permute-start.62 = (f32[2,160,128]{2,1,0:T(8,128)S(1)}, f32[2,160,128]{2,1,0:T(8,128)S(1)}, u32[]{:S(2)}, u32[]{:S(2)}) collective-permute-start(f32[2,160,128]{2,1,0:T(8,128)S(1)} %get-tuple-element.128), channel_id=1, source_target_pairs={{0,16},{4,20},{8,24},{12,28},{16,0},{20,4},{24,8},{28,12},{32,48},... | collective-permute-start | bytes 491528 | tf_op jit(solution)/shard_map/ppermute | solution.py:585
  206.1 4.3 %collective-permute-start.63 = (f32[160,256]{1,0:T(8,128)S(1)}, f32[160,256]{1,0:T(8,128)S(1)}, u32[]{:S(2)}, u32[]{:S(2)}) collective-permute-start(f32[160,256]{1,0:T(8,128)S(1)} %get-tuple-element.130), channel_id=1, source_target_pairs={{0,4},{4,0},{8,12},{12,8},{16,20},{20,16},{24,28},{28,24},{32,36},... | collective-permute-start | bytes 491528 | tf_op jit(solution)/shard_map/ppermute | solution.py:585
  (7 other events, 138.0 us)

commit v4 on v3

--- a/solution.py
+++ b/solution.py
@@ -692,9 +692,8 @@
         + from_far.astype(F32)
     ).astype(BF)
     w_sums = combine(w_sent)
-    both, both_away = finish_weights(
-        send_all(w_sums[:4], yn, yb, y2) + send_all(w_sums[4:], xn, xb, x2)
-    )
+    w_last = send_all(w_sums[:4], yn, yb, y2) + send_all(w_sums[4:], xn, xb, x2)
+    both, both_away = finish_weights(w_last)
     both_other = swap(both_away)
     key_weight_grad, value_weight_grad = join_weights(place, both, both_other)
     return (attention, query_grad, hidden_grad, key_weight_grad, value_weight_grad)

time: 225 us -> 225 us (level)
  no operation moved by 1% of the time
where the time goes in v4:
time: 225 us
  starting transfers between devices  111 us (49%)
  waiting for transfers between devices  70.3 us (31%)
  Pallas kernels  34.2 us (15%)
  local copies, waits for them, and re-layouts  5.32 us (2%)
  other arithmetic  2.55 us (1%)
    ppermute x64, starting transfers between devices, mover(): return lambda value: lax.ppermute(value, axis, pairs)  111 us
    ppermute x64, waiting for transfers between devices, mover(): return lambda value: lax.ppermute(value, axis, pairs)  70.3 us
    pallas_call x1, Pallas kernels, attend(): pl.pallas_call(body, grid_spec=pltpu.PrefetchScalarGridSpec(num_scalar_pr...  14.6 us
  transfers between devices with their start and end apart: 64, of which 24 were waited for; matrix products, arithmetic and copies ran while one was open for 1% of the time, Pallas kernels for 7%

profile of v4, /device:TPU:1, one launch (start us, length us, event | category | flops | bytes accessed | tf_op | source)
XLA Modules:
  0.0 224.7 jit_solution(10980567088925237993)
XLA Ops:
  0.7 1.8 constant_dynamic-slice_fusion.1
  2.5 1.4 collective-permute-start.1
  3.8 1.7 constant_dynamic-slice_fusion
  7.0 1.7 collective-permute-start.3
  8.7 2.1 collective-permute-start.5
  10.9 2.5 %device_tables.1 = (s32[115]{0:T(128)S(1)}, s32[17]{0:T(128)S(1)}, s32[4]{0:T(128)S(1)}) custom-call(s32[64]{0:T(128)S(1)} %copy-done.6, s32[4]{0:T(128)S(1)} %pad_add_fusion.where), custom_call_target="tpu_custom_call" | custom-call | tf_op jit(solution)/shard_map/device_tables/pallas_call | solution.py:89
  13.6 2.7 %collective-permute-start.8 = (bf16[128,1280]{1,0:T(8,128)(2,1)}, bf16[128,1280]{1,0:T(8,128)(2,1)S(1)}, u32[]{:S(2)}, u32[]{:S(2)}) collective-permute-start(bf16[128,1280]{1,0:T(8,128)(2,1)} %get-tuple-element.74), channel_id=1, source_target_pairs={{0,3},{1,0},{2,1},{3,2},{4,7},{5,4},{6,5},{7,6},{8,11},{9,8},{10,9... | collective-permute-start | bytes 983048 | tf_op jit(solution)/shard_map/ppermute | solution.py:585
  16.2 2.9 %collective-permute-done.3.bt.refs_1_ = bf16[128,1280]{1,0:T(8,128)(2,1)} collective-permute-done((bf16[128,1280]{1,0:T(8,128)(2,1)}, bf16[128,1280]{1,0:T(8,128)(2,1)}, u32[]{:S(2)}, u32[]{:S(2)}) %collective-permute-start.3) | collective-permute-done | bytes 327712 | tf_op jit(solution)/shard_map/ppermute | solution.py:585
  19.2 2.7 %collective-permute-start.6 = (bf16[128,1280]{1,0:T(8,128)(2,1)}, bf16[128,1280]{1,0:T(8,128)(2,1)S(1)}, u32[]{:S(2)}, u32[]{:S(2)}) collective-permute-start(bf16[128,1280]{1,0:T(8,128)(2,1)} %collective-permute-done.5.cl.refs_4_), channel_id=1, source_target_pairs={{0,3},{1,0},{2,1},{3,2},{4,7},{5,4},{6,5},{7,6},{8,11},{9,8},{10,9... | collective-permute-start | bytes 983048 | tf_op jit(solution)/shard_map/ppermute | solution.py:585
  23.0 3.0 %collective-permute-done.7.bl.refs_2_ = bf16[128,1280]{1,0:T(8,128)(2,1)S(1)} collective-permute-done((bf16[128,1280]{1,0:T(8,128)(2,1)}, bf16[128,1280]{1,0:T(8,128)(2,1)S(1)}, u32[]{:S(2)}, u32[]{:S(2)}) %collective-permute-start.7) | collective-permute-done | bytes 327712 | tf_op jit(solution)/shard_map/ppermute | solution.py:585
  26.1 1.7 copy-done.1
  27.8 2.8 %project_near.1 = (f32[256,256]{1,0:T(8,128)S(1)}, f32[256,256]{1,0:T(8,128)S(1)}) custom-call(s32[17]{0:T(128)S(1)} %get-tuple-element.70.place_ref.p, bf16[256,1280]{1,0:T(8,128)(2,1)S(1)} %copy-done.3, bf16[128,1280]{1,0:T(8,128)(2,1)} %collective-permute-done.3.bt.refs_1_, bf16[128,1280]{1,0:T(8,128)(2,1)S(1)} %collective-permute-done.7.bl.refs_2_, ...), custom_call_target="tpu_custom_call" | custom-call | tf_op jit(solution)/shard_map/project_near/pallas_call | solution.py:170
  30.6 2.5 %collective-permute-done.4.a.refs_5_ = bf16[128,1280]{1,0:T(8,128)(2,1)S(1)} collective-permute-done((bf16[128,1280]{1,0:T(8,128)(2,1)}, bf16[128,1280]{1,0:T(8,128)(2,1)S(1)}, u32[]{:S(2)}, u32[]{:S(2)}) %collective-permute-start.4) | collective-permute-done | bytes 327712 | tf_op jit(solution)/shard_map/ppermute | solution.py:585
  34.2 2.5 %collective-permute-start.10 = (bf16[256,256]{1,0:T(8,128)(2,1)S(1)}, bf16[256,256]{1,0:T(8,128)(2,1)S(1)}, u32[]{:S(2)}, u32[]{:S(2)}) collective-permute-start(bf16[256,256]{1,0:T(8,128)(2,1)S(1)} %get-tuple-element.79.a), channel_id=1, source_target_pairs={{0,24},{4,28},{8,0},{12,4},{16,8},{20,12},{24,16},{28,20},{32,56},... | collective-permute-start | bytes 393224 | tf_op jit(solution)/shard_map/ppermute | solution.py:585
  37.9 1.5 collective-permute-start.18
  39.6 2.6 %collective-permute-done.11.d = bf16[256,256]{1,0:T(8,128)(2,1)S(1)} collective-permute-done((bf16[256,256]{1,0:T(8,128)(2,1)S(1)}, bf16[256,256]{1,0:T(8,128)(2,1)S(1)}, u32[]{:S(2)}, u32[]{:S(2)}) %collective-permute-start.11) | collective-permute-done | bytes 131104 | tf_op jit(solution)/shard_map/ppermute | solution.py:585
  42.2 4.2 %collective-permute-done.9.b = bf16[256,256]{1,0:T(8,128)(2,1)S(1)} collective-permute-done((bf16[256,256]{1,0:T(8,128)(2,1)S(1)}, bf16[256,256]{1,0:T(8,128)(2,1)S(1)}, u32[]{:S(2)}, u32[]{:S(2)}) %collective-permute-start.9) | collective-permute-done | bytes 131104 | tf_op jit(solution)/shard_map/ppermute | solution.py:585
  46.4 1.4 collective-permute-start.12
  47.8 1.5 collective-permute-start.15
  49.3 2.7 %collective-permute-start.20 = (bf16[256,256]{1,0:T(8,128)(2,1)S(1)}, bf16[256,256]{1,0:T(8,128)(2,1)S(1)}, u32[]{:S(2)}, u32[]{:S(2)}) collective-permute-start(bf16[256,256]{1,0:T(8,128)(2,1)S(1)} %collective-permute-done.18.a), channel_id=1, source_target_pairs={{0,96},{4,100},{8,104},{12,108},{16,112},{20,116},{24,120},{28,124... | collective-permute-start | bytes 393224 | tf_op jit(solution)/shard_map/ppermute | solution.py:585
  52.3 5.5 %collective-permute-done.19.b = bf16[256,256]{1,0:T(8,128)(2,1)S(1)} collective-permute-done((bf16[256,256]{1,0:T(8,128)(2,1)S(1)}, bf16[256,256]{1,0:T(8,128)(2,1)S(1)}, u32[]{:S(2)}, u32[]{:S(2)}) %collective-permute-start.19) | collective-permute-done | bytes 131104 | tf_op jit(solution)/shard_map/ppermute | solution.py:585
  57.8 3.0 %collective-permute-start.14 = (bf16[4,128,256]{2,1,0:T(8,128)(2,1)S(1)}, bf16[4,128,256]{2,1,0:T(8,128)(2,1)S(1)}, u32[]{:S(2)}, u32[]{:S(2)}) collective-permute-start(bf16[4,128,256]{2,1,0:T(8,128)(2,1)S(1)} %get-tuple-element.80.refs_0_), channel_id=1, source_target_pairs={{0,96},{4,100},{8,104},{12,108},{16,112},{20,116},{24,120},{28,124... | collective-permute-start | bytes 786440 | tf_op jit(solution)/shard_map/ppermute | solution.py:585
  61.9 2.7 %collective-permute-start.25 = (bf16[4,128,256]{2,1,0:T(8,128)(2,1)S(1)}, bf16[4,128,256]{2,1,0:T(8,128)(2,1)S(1)}, u32[]{:S(2)}, u32[]{:S(2)}) collective-permute-start(bf16[4,128,256]{2,1,0:T(8,128)(2,1)S(1)} %get-tuple-element.84.refs_9_), channel_id=1, source_target_pairs={{0,24},{4,28},{8,0},{12,4},{16,8},{20,12},{24,16},{28,20},{32,56},... | collective-permute-start | bytes 786440 | tf_op jit(solution)/shard_map/ppermute | solution.py:585
  64.6 3.0 %collective-permute-done.13.refs_3_ = bf16[4,128,256]{2,1,0:T(8,128)(2,1)S(1)} collective-permute-done((bf16[4,128,256]{2,1,0:T(8,128)(2,1)S(1)}, bf16[4,128,256]{2,1,0:T(8,128)(2,1)S(1)}, u32[]{:S(2)}, u32[]{:S(2)}) %collective-permute-start.13) | collective-permute-done | bytes 262176 | tf_op jit(solution)/shard_map/ppermute | solution.py:585
  68.5 1.7 collective-permute-start.17
  70.2 1.5 collective-permute-start.26
  71.7 2.3 %collective-permute-done.23.refs_11_ = bf16[4,128,256]{2,1,0:T(8,128)(2,1)S(1)} collective-permute-done((bf16[4,128,256]{2,1,0:T(8,128)(2,1)S(1)}, bf16[4,128,256]{2,1,0:T(8,128)(2,1)S(1)}, u32[]{:S(2)}, u32[]{:S(2)}) %collective-permute-start.23) | collective-permute-done | bytes 262176 | tf_op jit(solution)/shard_map/ppermute | solution.py:585
  74.7 5.1 %collective-permute-done.26.refs_14_ = bf16[4,128,256]{2,1,0:T(8,128)(2,1)S(1)} collective-permute-done((bf16[4,128,256]{2,1,0:T(8,128)(2,1)S(1)}, bf16[4,128,256]{2,1,0:T(8,128)(2,1)S(1)}, u32[]{:S(2)}, u32[]{:S(2)}) %collective-permute-start.26) | collective-permute-done | bytes 262176 | tf_op jit(solution)/shard_map/ppermute | solution.py:585
  79.8 14.6 %attend.1 = (bf16[512,1280]{1,0:T(8,128)(2,1)S(1)}, f32[16,128,128]{2,1,0:T(8,128)S(1)}, bf16[16,128,128]{2,1,0:T(8,128)(2,1)S(1)}, bf16[16,128,128]{2,1,0:T(8,1...) custom-call(s32[115]{0:T(128)S(1)} %get-tuple-element.71.t, ...), custom_call_target="tpu_custom_call" | custom-call | tf_op jit(solution)/shard_map/attend/pallas_call | solution.py:406
  94.8 2.4 %collective-permute-start.30 = (bf16[16,128,128]{2,1,0:T(8,128)(2,1)S(1)}, bf16[16,128,128]{2,1,0:T(8,128)(2,1)S(1)}, u32[]{:S(2)}, u32[]{:S(2)}) collective-permute-start(bf16[16,128,128]{2,1,0:T(8,128)(2,1)S(1)} %get-tuple-element.90), channel_id=1, source_target_pairs={{0,24},{4,28},{8,0},{12,4},{16,8},{20,12},{24,16},{28,20},{32,56},... | collective-permute-start | bytes 1572872 | tf_op jit(solution)/shard_map/ppermute | solution.py:585
  99.3 1.6 collective-permute-start.33
  101.0 2.8 %collective-permute-done.29.refs_1_ = bf16[16,128,128]{2,1,0:T(8,128)(2,1)S(1)} collective-permute-done((bf16[16,128,128]{2,1,0:T(8,128)(2,1)S(1)}, bf16[16,128,128]{2,1,0:T(8,128)(2,1)S(1)}, u32[]{:S(2)}, u32[]{:S(2)}) %collective-permute-start.29) | collective-permute-done | bytes 524320 | tf_op jit(solution)/shard_map/ppermute | solution.py:585
  104.8 1.2 collective-permute-done.30.refs_2_
  106.0 16.7 %collective-permute-start.45 = (bf16[128,1280]{1,0:T(8,128)(2,1)}, bf16[128,1280]{1,0:T(8,128)(2,1)S(1)}, u32[]{:S(2)}, u32[]{:S(2)}) collective-permute-start(bf16[128,1280]{1,0:T(8,128)(2,1)} %collective-permute-done.3.bt.refs_1_), channel_id=1, source_target_pairs={{0,4},{4,0},{8,12},{12,8},{16,20},{20,16},{24,28},{28,24},{32,36},... | collective-permute-start | bytes 983048 | tf_op jit(solution)/shard_map/ppermute | solution.py:585
  123.1 2.4 %collective-permute-start.35 = (f32[4,128,128]{2,1,0:T(8,128)S(1)}, f32[4,128,128]{2,1,0:T(8,128)S(1)}, u32[]{:S(2)}, u32[]{:S(2)}) collective-permute-start(f32[4,128,128]{2,1,0:T(8,128)S(1)} %get-tuple-element.97), channel_id=1, source_target_pairs={{0,32},{4,36},{8,40},{12,44},{16,48},{20,52},{24,56},{28,60},{32,6... | collective-permute-start | bytes 786440 | tf_op jit(solution)/shard_map/ppermute | solution.py:585
  125.9 2.0 collective-permute-start.37
  127.9 2.7 %collective-permute-start.39 = (f32[4,128,128]{2,1,0:T(8,128)S(1)}, f32[4,128,128]{2,1,0:T(8,128)S(1)}, u32[]{:S(2)}, u32[]{:S(2)}) collective-permute-start(f32[4,128,128]{2,1,0:T(8,128)S(1)} %get-tuple-element.102), channel_id=1, source_target_pairs={{0,24},{4,28},{8,0},{12,4},{16,8},{20,12},{24,16},{28,20},{32,56},... | collective-permute-start | bytes 786440 | tf_op jit(solution)/shard_map/ppermute | solution.py:585
  130.6 2.2 collective-permute-done.35.refs_1_
  133.8 15.2 %collective-permute-start.48 = (bf16[128,1280]{1,0:T(8,128)(2,1)}, bf16[128,1280]{1,0:T(8,128)(2,1)S(1)}, u32[]{:S(2)}, u32[]{:S(2)}) collective-permute-start(bf16[128,1280]{1,0:T(8,128)(2,1)} %collective-permute-done.5.cl.refs_4_), channel_id=1, source_target_pairs={{0,4},{4,0},{8,12},{12,8},{16,20},{20,16},{24,28},{28,24},{32,36},... | collective-permute-start | bytes 983048 | tf_op jit(solution)/shard_map/ppermute | solution.py:585
  150.2 2.1 collective-permute-start.49
  152.3 2.3 %collective-permute-start.50 = (bf16[128,1280]{1,0:T(8,128)(2,1)S(1)}, bf16[128,1280]{1,0:T(8,128)(2,1)S(1)}, u32[]{:S(2)}, u32[]{:S(2)}) collective-permute-start(bf16[128,1280]{1,0:T(8,128)(2,1)S(1)} %collective-permute-done.6.b.refs_6_), channel_id=1, source_target_pairs={{0,4},{4,0},{8,12},{12,8},{16,20},{20,16},{24,28},{28,24},{32,36},... | collective-permute-start | bytes 983048 | tf_op jit(solution)/shard_map/ppermute | solution.py:585
  155.8 2.7 %flip.1.ft = bf16[4,1280,512]{2,1,0:T(8,128)(2,1)S(1)} custom-call(bf16[256,1280]{1,0:T(8,128)(2,1)S(1)} %copy-done.3, bf16[128,1280]{1,0:T(8,128)(2,1)} %collective-permute-done.3.bt.refs_1_, bf16[128,1280]{1,0:T(8,128)(2,1)S(1)} %collective-permute-done.7.bl.refs_2_, bf16[128,1280]{1,0:T(8,128)(2,1)S(1)} %collective-permute-done.8.ct.refs_3_, ...), custom_call_target="tpu_custom_call" | custom-call | tf_op jit(solution)/shard_map/flip/pallas_call | solution.py:542
  158.5 2.5 %weight_partials.1 = (f32[8,160,128]{2,1,0:T(8,128)S(1)}, bf16[8,160,128]{2,1,0:T(8,128)(2,1)S(1)}, bf16[8,160,128]{2,1,0:T(8,128)(2,1)S(1)}, bf16[8,160,128]{2,...) custom-call(s32[17]{0:T(128)S(1)} %get-tuple-element.70.place_ref.p,, ...), custom_call_target="tpu_custom_call" | custom-call | tf_op jit(solution)/shard_map/weight_partials/pallas_call | solution.py:572
  161.1 2.7 %collective-permute-start.52 = (bf16[8,160,128]{2,1,0:T(8,128)(2,1)S(1)}, bf16[8,160,128]{2,1,0:T(8,128)(2,1)S(1)}, u32[]{:S(2)}, u32[]{:S(2)}) collective-permute-start(bf16[8,160,128]{2,1,0:T(8,128)(2,1)S(1)} %get-tuple-element.115), channel_id=1, source_target_pairs={{0,24},{4,28},{8,0},{12,4},{16,8},{20,12},{24,16},{28,20},{32,56},... | collective-permute-start | bytes 983048 | tf_op jit(solution)/shard_map/ppermute | solution.py:585
  164.5 2.1 collective-permute-start.55
  166.6 4.6 %collective-permute-done.51.refs_1_ = bf16[8,160,128]{2,1,0:T(8,128)(2,1)S(1)} collective-permute-done((bf16[8,160,128]{2,1,0:T(8,128)(2,1)S(1)}, bf16[8,160,128]{2,1,0:T(8,128)(2,1)S(1)}, u32[]{:S(2)}, u32[]{:S(2)}) %collective-permute-start.51) | collective-permute-done | bytes 327712 | tf_op jit(solution)/shard_map/ppermute | solution.py:585
  171.2 2.2 collective-permute-start.56
  173.4 4.9 %collective-permute-done.53.refs_3_ = bf16[8,160,128]{2,1,0:T(8,128)(2,1)S(1)} collective-permute-done((bf16[8,160,128]{2,1,0:T(8,128)(2,1)S(1)}, bf16[8,160,128]{2,1,0:T(8,128)(2,1)S(1)}, u32[]{:S(2)}, u32[]{:S(2)}) %collective-permute-start.53) | collective-permute-done | bytes 327712 | tf_op jit(solution)/shard_map/ppermute | solution.py:585
  178.4 1.7 collective-permute-done.56.refs_7_
  180.4 2.0 collective-permute-start.57
  183.6 1.3 collective-permute-start.59
  185.3 3.0 %collective-permute-start.28 = (bf16[256,1280]{1,0:T(8,128)(2,1)S(1)}, bf16[256,1280]{1,0:T(8,128)(2,1)S(1)}, u32[]{:S(2)}, u32[]{:S(2)}) collective-permute-start(bf16[256,1280]{1,0:T(8,128)(2,1)S(1)} %slice.3), channel_id=1, source_target_pairs={{0,4},{4,0},{8,12},{12,8},{16,20},{20,16},{24,28},{28,24},{32,36},... | collective-permute-start | bytes 1966088 | tf_op jit(solution)/shard_map/ppermute | solution.py:585
  188.3 3.0 %input_partials.1 = (bf16[256,1280]{1,0:T(8,128)(2,1)S(1)}, bf16[256,1280]{1,0:T(8,128)(2,1)S(1)}, bf16[256,1280]{1,0:T(8,128)(2,1)S(1)}, bf16[256,1280]{1,0:T(8,128)(2,1)S(1)}) custom-call(s32[17]{0:T(128)S(1)} %get-tuple-element.70.place_ref.p, bf16[512,256]{1,0:T(8,128)(2,1)S(1)} %get-tuple-element.106.a.g, ...), custom_call_target="tpu_custom_call" | custom-call | tf_op jit(solution)/shard_map/input_partials/pallas_call | solution.py:517
  191.5 2.7 %collective-permute-start.43 = (bf16[256,1280]{1,0:T(8,128)(2,1)S(1)}, bf16[256,1280]{1,0:T(8,128)(2,1)S(1)}, u32[]{:S(2)}, u32[]{:S(2)}) collective-permute-start(bf16[256,1280]{1,0:T(8,128)(2,1)S(1)} %get-tuple-element.110), channel_id=1, source_target_pairs={{0,3},{1,0},{2,1},{3,2},{4,7},{5,4},{6,5},{7,6},{8,11},{9,8},{10,9... | collective-permute-start | bytes 1966088 | tf_op jit(solution)/shard_map/ppermute | solution.py:585
  194.8 2.5 %collective-permute-start.61 = (f32[2,160,128]{2,1,0:T(8,128)S(1)}, f32[2,160,128]{2,1,0:T(8,128)S(1)}, u32[]{:S(2)}, u32[]{:S(2)}) collective-permute-start(f32[2,160,128]{2,1,0:T(8,128)S(1)} %get-tuple-element.127), channel_id=1, source_target_pairs={{0,24},{4,28},{8,0},{12,4},{16,8},{20,12},{24,16},{28,20},{32,56},... | collective-permute-start | bytes 491528 | tf_op jit(solution)/shard_map/ppermute | solution.py:585
  197.3 3.1 %collective-permute-done.61.refs_6_ = f32[2,160,128]{2,1,0:T(8,128)S(1)} collective-permute-done((f32[2,160,128]{2,1,0:T(8,128)S(1)}, f32[2,160,128]{2,1,0:T(8,128)S(1)}, u32[]{:S(2)}, u32[]{:S(2)}) %collective-permute-start.61) | collective-permute-done | bytes 163872 | tf_op jit(solution)/shard_map/ppermute | solution.py:585
  200.4 2.2 collective-permute-start.62
  202.5 3.5 %collective-permute-done.62.refs_7_ = f32[2,160,128]{2,1,0:T(8,128)S(1)} collective-permute-done((f32[2,160,128]{2,1,0:T(8,128)S(1)}, f32[2,160,128]{2,1,0:T(8,128)S(1)}, u32[]{:S(2)}, u32[]{:S(2)}) %collective-permute-start.62) | collective-permute-done | bytes 163872 | tf_op jit(solution)/shard_map/ppermute | solution.py:585
  206.1 2.6 %collective-permute-start.63 = (f32[160,256]{1,0:T(8,128)S(1)}, f32[160,256]{1,0:T(8,128)S(1)}, u32[]{:S(2)}, u32[]{:S(2)}) collective-permute-start(f32[160,256]{1,0:T(8,128)S(1)} %get-tuple-element.130), channel_id=1, source_target_pairs={{0,4},{4,0},{8,12},{12,8},{16,20},{20,16},{24,28},{28,24},{32,36},... | collective-permute-start | bytes 491528 | tf_op jit(solution)/shard_map/ppermute | solution.py:585
  208.7 1.7 join_rows.1
  210.4 1.3 join_weights.1
  211.6 10.2 %collective-permute-done.43 = bf16[256,1280]{1,0:T(8,128)(2,1)S(1)} collective-permute-done((bf16[256,1280]{1,0:T(8,128)(2,1)S(1)}, bf16[256,1280]{1,0:T(8,128)(2,1)S(1)}, u32[]{:S(2)}, u32[]{:S(2)}) %collective-permute-start.43) | collective-permute-done | bytes 655392 | tf_op jit(solution)/shard_map/ppermute | solution.py:585
  221.8 1.7 collective-permute-done.44
  223.5 1.2 add_convert_fusion
  (104 shorter events, 19.6 us)
Async XLA Ops:
  2.5 11.1 %collective-permute-start.1 = (bf16[256,640]{1,0:T(8,128)(2,1)}, bf16[256,640]{1,0:T(8,128)(2,1)}, u32[]{:S(2)}, u32[]{:S(2)}) collective-permute-start(bf16[256,640]{1,0:T(8,128)(2,1)} %constant_dynamic-slice_fusion.1), channel_id=1, source_target_pairs={{0,4},{4,0},{8,12},{12,8},{16,20},{20,16},{24,28},{28,24},{32,36},... | collective-permute-start | bytes 983048 | tf_op jit(solution)/shard_map/ppermute | solution.py:585
  5.6 8.0 %collective-permute-start.2 = (bf16[256,640]{1,0:T(8,128)(2,1)}, bf16[256,640]{1,0:T(8,128)(2,1)}, u32[]{:S(2)}, u32[]{:S(2)}) collective-permute-start(bf16[256,640]{1,0:T(8,128)(2,1)} %constant_dynamic-slice_fusion), channel_id=1, source_target_pairs={{0,4},{4,0},{8,12},{12,8},{16,20},{20,16},{24,28},{28,24},{32,36},... | collective-permute-start | bytes 983048 | tf_op jit(solution)/shard_map/ppermute | solution.py:585
  5.6 17.5 %collective-permute-start = (bf16[256,1280]{1,0:T(8,128)(2,1)S(1)}, bf16[256,1280]{1,0:T(8,128)(2,1)}, u32[]{:S(2)}, u32[]{:S(2)}) collective-permute-start(bf16[256,1280]{1,0:T(8,128)(2,1)S(1)} %copy-done.3), channel_id=1, source_target_pairs={{0,4},{4,0},{8,12},{12,8},{16,20},{20,16},{24,28},{28,24},{32,36},... | collective-permute-start | bytes 1966088 | tf_op jit(solution)/shard_map/ppermute | solution.py:585
  7.0 12.2 %collective-permute-start.3 = (bf16[128,1280]{1,0:T(8,128)(2,1)}, bf16[128,1280]{1,0:T(8,128)(2,1)}, u32[]{:S(2)}, u32[]{:S(2)}) collective-permute-start(bf16[128,1280]{1,0:T(8,128)(2,1)} %get-tuple-element.74), channel_id=1, source_target_pairs={{0,1},{1,2},{2,3},{3,0},{4,5},{5,6},{6,7},{7,4},{8,9},{9,10},{10,1... | collective-permute-start | bytes 983048 | tf_op jit(solution)/shard_map/ppermute | solution.py:585
  8.7 10.4 %collective-permute-start.5 = (bf16[128,1280]{1,0:T(8,128)(2,1)}, bf16[128,1280]{1,0:T(8,128)(2,1)}, u32[]{:S(2)}, u32[]{:S(2)}) collective-permute-start(bf16[128,1280]{1,0:T(8,128)(2,1)} %get-tuple-element.75), channel_id=1, source_target_pairs={{0,3},{1,0},{2,1},{3,2},{4,7},{5,4},{6,5},{7,6},{8,11},{9,8},{10,9... | collective-permute-start | bytes 983048 | tf_op jit(solution)/shard_map/ppermute | solution.py:585
  13.5 12.5 %collective-permute-start.7 = (bf16[128,1280]{1,0:T(8,128)(2,1)}, bf16[128,1280]{1,0:T(8,128)(2,1)S(1)}, u32[]{:S(2)}, u32[]{:S(2)}) collective-permute-start(bf16[128,1280]{1,0:T(8,128)(2,1)} %get-tuple-element.75), channel_id=1, source_target_pairs={{0,1},{1,2},{2,3},{3,0},{4,5},{5,6},{6,7},{7,4},{8,9},{9,10},{10,1... | collective-permute-start | bytes 983048 | tf_op jit(solution)/shard_map/ppermute | solution.py:585
  13.6 12.5 %collective-permute-start.8 = (bf16[128,1280]{1,0:T(8,128)(2,1)}, bf16[128,1280]{1,0:T(8,128)(2,1)S(1)}, u32[]{:S(2)}, u32[]{:S(2)}) collective-permute-start(bf16[128,1280]{1,0:T(8,128)(2,1)} %get-tuple-element.74), channel_id=1, source_target_pairs={{0,3},{1,0},{2,1},{3,2},{4,7},{5,4},{6,5},{7,6},{8,11},{9,8},{10,9... | collective-permute-start | bytes 983048 | tf_op jit(solution)/shard_map/ppermute | solution.py:585
  19.1 13.9 %collective-permute-start.4 = (bf16[128,1280]{1,0:T(8,128)(2,1)}, bf16[128,1280]{1,0:T(8,128)(2,1)S(1)}, u32[]{:S(2)}, u32[]{:S(2)}) collective-permute-start(bf16[128,1280]{1,0:T(8,128)(2,1)} %collective-permute-done.3.bt.refs_1_), channel_id=1, source_target_pairs={{0,1},{1,2},{2,3},{3,0},{4,5},{5,6},{6,7},{7,4},{8,9},{9,10},{10,1... | collective-permute-start | bytes 983048 | tf_op jit(solution)/shard_map/ppermute | solution.py:585
  19.2 13.9 %collective-permute-start.6 = (bf16[128,1280]{1,0:T(8,128)(2,1)}, bf16[128,1280]{1,0:T(8,128)(2,1)S(1)}, u32[]{:S(2)}, u32[]{:S(2)}) collective-permute-start(bf16[128,1280]{1,0:T(8,128)(2,1)} %collective-permute-done.5.cl.refs_4_), channel_id=1, source_target_pairs={{0,3},{1,0},{2,1},{3,2},{4,7},{5,4},{6,5},{7,6},{8,11},{9,8},{10,9... | collective-permute-start | bytes 983048 | tf_op jit(solution)/shard_map/ppermute | solution.py:585
  34.2 5.4 %collective-permute-start.10 = (bf16[256,256]{1,0:T(8,128)(2,1)S(1)}, bf16[256,256]{1,0:T(8,128)(2,1)S(1)}, u32[]{:S(2)}, u32[]{:S(2)}) collective-permute-start(bf16[256,256]{1,0:T(8,128)(2,1)S(1)} %get-tuple-element.79.a), channel_id=1, source_target_pairs={{0,24},{4,28},{8,0},{12,4},{16,8},{20,12},{24,16},{28,20},{32,56},... | collective-permute-start | bytes 393224 | tf_op jit(solution)/shard_map/ppermute | solution.py:585
  36.8 5.4 %collective-permute-start.11 = (bf16[256,256]{1,0:T(8,128)(2,1)S(1)}, bf16[256,256]{1,0:T(8,128)(2,1)S(1)}, u32[]{:S(2)}, u32[]{:S(2)}) collective-permute-start(bf16[256,256]{1,0:T(8,128)(2,1)S(1)} %get-tuple-element.79.a), channel_id=1, source_target_pairs={{0,16},{4,20},{8,24},{12,28},{16,0},{20,4},{24,8},{28,12},{32,48},... | collective-permute-start | bytes 393224 | tf_op jit(solution)/shard_map/ppermute | solution.py:585
  37.3 9.1 %collective-permute-start.9 = (bf16[256,256]{1,0:T(8,128)(2,1)S(1)}, bf16[256,256]{1,0:T(8,128)(2,1)S(1)}, u32[]{:S(2)}, u32[]{:S(2)}) collective-permute-start(bf16[256,256]{1,0:T(8,128)(2,1)S(1)} %get-tuple-element.79.a), channel_id=1, source_target_pairs={{0,8},{4,12},{8,16},{12,20},{16,24},{20,28},{24,0},{28,4},{32,40},... | collective-permute-start | bytes 393224 | tf_op jit(solution)/shard_map/ppermute | solution.py:585
  37.9 11.4 %collective-permute-start.18 = (bf16[256,256]{1,0:T(8,128)(2,1)S(1)}, bf16[256,256]{1,0:T(8,128)(2,1)S(1)}, u32[]{:S(2)}, u32[]{:S(2)}) collective-permute-start(bf16[256,256]{1,0:T(8,128)(2,1)S(1)} %get-tuple-element.82), channel_id=1, source_target_pairs={{0,4},{4,0},{8,12},{12,8},{16,20},{20,16},{24,28},{28,24},{32,36},... | collective-permute-start | bytes 393224 | tf_op jit(solution)/shard_map/ppermute | solution.py:585
  46.4 15.5 %collective-permute-start.12 = (bf16[4,128,256]{2,1,0:T(8,128)(2,1)S(1)}, bf16[4,128,256]{2,1,0:T(8,128)(2,1)S(1)}, u32[]{:S(2)}, u32[]{:S(2)}) collective-permute-start(bf16[4,128,256]{2,1,0:T(8,128)(2,1)S(1)} %get-tuple-element.80.refs_0_), channel_id=1, source_target_pairs={{0,32},{4,36},{8,40},{12,44},{16,48},{20,52},{24,56},{28,60},{32,6... | collective-permute-start | bytes 786440 | tf_op jit(solution)/shard_map/ppermute | solution.py:585
  47.8 16.8 %collective-permute-start.15 = (bf16[4,128,256]{2,1,0:T(8,128)(2,1)S(1)}, bf16[4,128,256]{2,1,0:T(8,128)(2,1)S(1)}, u32[]{:S(2)}, u32[]{:S(2)}) collective-permute-start(bf16[4,128,256]{2,1,0:T(8,128)(2,1)S(1)} %get-tuple-element.81.refs_1_), channel_id=1, source_target_pairs={{0,96},{4,100},{8,104},{12,108},{16,112},{20,116},{24,120},{28,124... | collective-permute-start | bytes 786440 | tf_op jit(solution)/shard_map/ppermute | solution.py:585
  49.3 8.5 %collective-permute-start.19 = (bf16[256,256]{1,0:T(8,128)(2,1)S(1)}, bf16[256,256]{1,0:T(8,128)(2,1)S(1)}, u32[]{:S(2)}, u32[]{:S(2)}) collective-permute-start(bf16[256,256]{1,0:T(8,128)(2,1)S(1)} %collective-permute-done.18.a), channel_id=1, source_target_pairs={{0,32},{4,36},{8,40},{12,44},{16,48},{20,52},{24,56},{28,60},{32,6... | collective-permute-start | bytes 393224 | tf_op jit(solution)/shard_map/ppermute | solution.py:585
  49.3 8.5 %collective-permute-start.20 = (bf16[256,256]{1,0:T(8,128)(2,1)S(1)}, bf16[256,256]{1,0:T(8,128)(2,1)S(1)}, u32[]{:S(2)}, u32[]{:S(2)}) collective-permute-start(bf16[256,256]{1,0:T(8,128)(2,1)S(1)} %collective-permute-done.18.a), channel_id=1, source_target_pairs={{0,96},{4,100},{8,104},{12,108},{16,112},{20,116},{24,120},{28,124... | collective-permute-start | bytes 393224 | tf_op jit(solution)/shard_map/ppermute | solution.py:585
  52.0 9.8 %collective-permute-start.21 = (bf16[256,256]{1,0:T(8,128)(2,1)S(1)}, bf16[256,256]{1,0:T(8,128)(2,1)S(1)}, u32[]{:S(2)}, u32[]{:S(2)}) collective-permute-start(bf16[256,256]{1,0:T(8,128)(2,1)S(1)} %collective-permute-done.18.a), channel_id=1, source_target_pairs={{0,64},{4,68},{8,72},{12,76},{16,80},{20,84},{24,88},{28,92},{32,9... | collective-permute-start | bytes 393224 | tf_op jit(solution)/shard_map/ppermute | solution.py:585
  57.8 9.7 %collective-permute-start.13 = (bf16[4,128,256]{2,1,0:T(8,128)(2,1)S(1)}, bf16[4,128,256]{2,1,0:T(8,128)(2,1)S(1)}, u32[]{:S(2)}, u32[]{:S(2)}) collective-permute-start(bf16[4,128,256]{2,1,0:T(8,128)(2,1)S(1)} %get-tuple-element.81.refs_1_), channel_id=1, source_target_pairs={{0,32},{4,36},{8,40},{12,44},{16,48},{20,52},{24,56},{28,60},{32,6... | collective-permute-start | bytes 786440 | tf_op jit(solution)/shard_map/ppermute | solution.py:585
  57.8 9.7 %collective-permute-start.14 = (bf16[4,128,256]{2,1,0:T(8,128)(2,1)S(1)}, bf16[4,128,256]{2,1,0:T(8,128)(2,1)S(1)}, u32[]{:S(2)}, u32[]{:S(2)}) collective-permute-start(bf16[4,128,256]{2,1,0:T(8,128)(2,1)S(1)} %get-tuple-element.80.refs_0_), channel_id=1, source_target_pairs={{0,96},{4,100},{8,104},{12,108},{16,112},{20,116},{24,120},{28,124... | collective-permute-start | bytes 786440 | tf_op jit(solution)/shard_map/ppermute | solution.py:585
  61.8 6.7 %collective-permute-start.22 = (bf16[4,128,256]{2,1,0:T(8,128)(2,1)S(1)}, bf16[4,128,256]{2,1,0:T(8,128)(2,1)S(1)}, u32[]{:S(2)}, u32[]{:S(2)}) collective-permute-start(bf16[4,128,256]{2,1,0:T(8,128)(2,1)S(1)} %get-tuple-element.83.refs_8_), channel_id=1, source_target_pairs={{0,8},{4,12},{8,16},{12,20},{16,24},{20,28},{24,0},{28,4},{32,40},... | collective-permute-start | bytes 786440 | tf_op jit(solution)/shard_map/ppermute | solution.py:585
  61.9 8.3 %collective-permute-start.25 = (bf16[4,128,256]{2,1,0:T(8,128)(2,1)S(1)}, bf16[4,128,256]{2,1,0:T(8,128)(2,1)S(1)}, u32[]{:S(2)}, u32[]{:S(2)}) collective-permute-start(bf16[4,128,256]{2,1,0:T(8,128)(2,1)S(1)} %get-tuple-element.84.refs_9_), channel_id=1, source_target_pairs={{0,24},{4,28},{8,0},{12,4},{16,8},{20,12},{24,16},{28,20},{32,56},... | collective-permute-start | bytes 786440 | tf_op jit(solution)/shard_map/ppermute | solution.py:585
  64.5 9.4 %collective-permute-start.23 = (bf16[4,128,256]{2,1,0:T(8,128)(2,1)S(1)}, bf16[4,128,256]{2,1,0:T(8,128)(2,1)S(1)}, u32[]{:S(2)}, u32[]{:S(2)}) collective-permute-start(bf16[4,128,256]{2,1,0:T(8,128)(2,1)S(1)} %get-tuple-element.84.refs_9_), channel_id=1, source_target_pairs={{0,8},{4,12},{8,16},{12,20},{16,24},{20,28},{24,0},{28,4},{32,40},... | collective-permute-start | bytes 786440 | tf_op jit(solution)/shard_map/ppermute | solution.py:585
  67.5 7.1 %collective-permute-start.24 = (bf16[4,128,256]{2,1,0:T(8,128)(2,1)S(1)}, bf16[4,128,256]{2,1,0:T(8,128)(2,1)S(1)}, u32[]{:S(2)}, u32[]{:S(2)}) collective-permute-start(bf16[4,128,256]{2,1,0:T(8,128)(2,1)S(1)} %get-tuple-element.83.refs_8_), channel_id=1, source_target_pairs={{0,24},{4,28},{8,0},{12,4},{16,8},{20,12},{24,16},{28,20},{32,56},... | collective-permute-start | bytes 786440 | tf_op jit(solution)/shard_map/ppermute | solution.py:585
  67.5 7.1 %collective-permute-start.16 = (bf16[4,128,256]{2,1,0:T(8,128)(2,1)S(1)}, bf16[4,128,256]{2,1,0:T(8,128)(2,1)S(1)}, u32[]{:S(2)}, u32[]{:S(2)}) collective-permute-start(bf16[4,128,256]{2,1,0:T(8,128)(2,1)S(1)} %collective-permute-done.12.refs_2_), channel_id=1, source_target_pairs={{0,32},{4,36},{8,40},{12,44},{16,48},{20,52},{24,56},{28,60},{32,6... | collective-permute-start | bytes 786440 | tf_op jit(solution)/shard_map/ppermute | solution.py:585
  68.5 6.2 %collective-permute-start.17 = (bf16[4,128,256]{2,1,0:T(8,128)(2,1)S(1)}, bf16[4,128,256]{2,1,0:T(8,128)(2,1)S(1)}, u32[]{:S(2)}, u32[]{:S(2)}) collective-permute-start(bf16[4,128,256]{2,1,0:T(8,128)(2,1)S(1)} %collective-permute-done.15.refs_5_), channel_id=1, source_target_pairs={{0,96},{4,100},{8,104},{12,108},{16,112},{20,116},{24,120},{28,124... | collective-permute-start | bytes 786440 | tf_op jit(solution)/shard_map/ppermute | solution.py:585
  70.2 9.5 %collective-permute-start.26 = (bf16[4,128,256]{2,1,0:T(8,128)(2,1)S(1)}, bf16[4,128,256]{2,1,0:T(8,128)(2,1)S(1)}, u32[]{:S(2)}, u32[]{:S(2)}) collective-permute-start(bf16[4,128,256]{2,1,0:T(8,128)(2,1)S(1)} %collective-permute-done.22.refs_10_), channel_id=1, source_target_pairs={{0,8},{4,12},{8,16},{12,20},{16,24},{20,28},{24,0},{28,4},{32,40},... | collective-permute-start | bytes 786440 | tf_op jit(solution)/shard_map/ppermute | solution.py:585
  74.0 5.8 %collective-permute-start.27 = (bf16[4,128,256]{2,1,0:T(8,128)(2,1)S(1)}, bf16[4,128,256]{2,1,0:T(8,128)(2,1)S(1)}, u32[]{:S(2)}, u32[]{:S(2)}) collective-permute-start(bf16[4,128,256]{2,1,0:T(8,128)(2,1)S(1)} %collective-permute-done.25.refs_13_), channel_id=1, source_target_pairs={{0,24},{4,28},{8,0},{12,4},{16,8},{20,12},{24,16},{28,20},{32,56},... | collective-permute-start | bytes 786440 | tf_op jit(solution)/shard_map/ppermute | solution.py:585
  94.4 9.3 %collective-permute-start.29 = (bf16[16,128,128]{2,1,0:T(8,128)(2,1)S(1)}, bf16[16,128,128]{2,1,0:T(8,128)(2,1)S(1)}, u32[]{:S(2)}, u32[]{:S(2)}) collective-permute-start(bf16[16,128,128]{2,1,0:T(8,128)(2,1)S(1)} %get-tuple-element.89), channel_id=1, source_target_pairs={{0,8},{4,12},{8,16},{12,20},{16,24},{20,28},{24,0},{28,4},{32,40},... | collective-permute-start | bytes 1572872 | tf_op jit(solution)/shard_map/ppermute | solution.py:585
  94.8 11.2 %collective-permute-start.30 = (bf16[16,128,128]{2,1,0:T(8,128)(2,1)S(1)}, bf16[16,128,128]{2,1,0:T(8,128)(2,1)S(1)}, u32[]{:S(2)}, u32[]{:S(2)}) collective-permute-start(bf16[16,128,128]{2,1,0:T(8,128)(2,1)S(1)} %get-tuple-element.90), channel_id=1, source_target_pairs={{0,24},{4,28},{8,0},{12,4},{16,8},{20,12},{24,16},{28,20},{32,56},... | collective-permute-start | bytes 1572872 | tf_op jit(solution)/shard_map/ppermute | solution.py:585
  97.2 25.5 %collective-permute-start.31 = (bf16[16,128,128]{2,1,0:T(8,128)(2,1)S(1)}, bf16[16,128,128]{2,1,0:T(8,128)(2,1)S(1)}, u32[]{:S(2)}, u32[]{:S(2)}) collective-permute-start(bf16[16,128,128]{2,1,0:T(8,128)(2,1)S(1)} %get-tuple-element.91), channel_id=1, source_target_pairs={{0,16},{4,20},{8,24},{12,28},{16,0},{20,4},{24,8},{28,12},{32,48},... | collective-permute-start | bytes 1572872 | tf_op jit(solution)/shard_map/ppermute | solution.py:585
  98.3 24.4 %collective-permute-start.32 = (bf16[16,128,128]{2,1,0:T(8,128)(2,1)S(1)}, bf16[16,128,128]{2,1,0:T(8,128)(2,1)S(1)}, u32[]{:S(2)}, u32[]{:S(2)}) collective-permute-start(bf16[16,128,128]{2,1,0:T(8,128)(2,1)S(1)} %get-tuple-element.93), channel_id=1, source_target_pairs={{0,32},{4,36},{8,40},{12,44},{16,48},{20,52},{24,56},{28,60},{32,6... | collective-permute-start | bytes 1572872 | tf_op jit(solution)/shard_map/ppermute | solution.py:585
  99.3 23.3 %collective-permute-start.33 = (bf16[16,128,128]{2,1,0:T(8,128)(2,1)S(1)}, bf16[16,128,128]{2,1,0:T(8,128)(2,1)S(1)}, u32[]{:S(2)}, u32[]{:S(2)}) collective-permute-start(bf16[16,128,128]{2,1,0:T(8,128)(2,1)S(1)} %get-tuple-element.94), channel_id=1, source_target_pairs={{0,96},{4,100},{8,104},{12,108},{16,112},{20,116},{24,120},{28,124... | collective-permute-start | bytes 1572872 | tf_op jit(solution)/shard_map/ppermute | solution.py:585
  103.7 18.9 %collective-permute-start.34 = (bf16[16,128,128]{2,1,0:T(8,128)(2,1)S(1)}, bf16[16,128,128]{2,1,0:T(8,128)(2,1)S(1)}, u32[]{:S(2)}, u32[]{:S(2)}) collective-permute-start(bf16[16,128,128]{2,1,0:T(8,128)(2,1)S(1)} %get-tuple-element.95), channel_id=1, source_target_pairs={{0,64},{4,68},{8,72},{12,76},{16,80},{20,84},{24,88},{28,92},{32,9... | collective-permute-start | bytes 1572872 | tf_op jit(solution)/shard_map/ppermute | solution.py:585
  106.0 21.9 %collective-permute-start.45 = (bf16[128,1280]{1,0:T(8,128)(2,1)}, bf16[128,1280]{1,0:T(8,128)(2,1)S(1)}, u32[]{:S(2)}, u32[]{:S(2)}) collective-permute-start(bf16[128,1280]{1,0:T(8,128)(2,1)} %collective-permute-done.3.bt.refs_1_), channel_id=1, source_target_pairs={{0,4},{4,0},{8,12},{12,8},{16,20},{20,16},{24,28},{28,24},{32,36},... | collective-permute-start | bytes 983048 | tf_op jit(solution)/shard_map/ppermute | solution.py:585
  123.1 9.7 %collective-permute-start.35 = (f32[4,128,128]{2,1,0:T(8,128)S(1)}, f32[4,128,128]{2,1,0:T(8,128)S(1)}, u32[]{:S(2)}, u32[]{:S(2)}) collective-permute-start(f32[4,128,128]{2,1,0:T(8,128)S(1)} %get-tuple-element.97), channel_id=1, source_target_pairs={{0,32},{4,36},{8,40},{12,44},{16,48},{20,52},{24,56},{28,60},{32,6... | collective-permute-start | bytes 786440 | tf_op jit(solution)/shard_map/ppermute | solution.py:585
  125.5 8.3 %collective-permute-start.36 = (f32[4,128,128]{2,1,0:T(8,128)S(1)}, f32[4,128,128]{2,1,0:T(8,128)S(1)}, u32[]{:S(2)}, u32[]{:S(2)}) collective-permute-start(f32[4,128,128]{2,1,0:T(8,128)S(1)} %get-tuple-element.98), channel_id=1, source_target_pairs={{0,96},{4,100},{8,104},{12,108},{16,112},{20,116},{24,120},{28,124... | collective-permute-start | bytes 786440 | tf_op jit(solution)/shard_map/ppermute | solution.py:585
  125.9 23.2 %collective-permute-start.37 = (f32[4,128,128]{2,1,0:T(8,128)S(1)}, f32[4,128,128]{2,1,0:T(8,128)S(1)}, u32[]{:S(2)}, u32[]{:S(2)}) collective-permute-start(f32[4,128,128]{2,1,0:T(8,128)S(1)} %get-tuple-element.99), channel_id=1, source_target_pairs={{0,64},{4,68},{8,72},{12,76},{16,80},{20,84},{24,88},{28,92},{32,9... | collective-permute-start | bytes 786440 | tf_op jit(solution)/shard_map/ppermute | solution.py:585
  127.9 22.3 %collective-permute-start.38 = (f32[4,128,128]{2,1,0:T(8,128)S(1)}, f32[4,128,128]{2,1,0:T(8,128)S(1)}, u32[]{:S(2)}, u32[]{:S(2)}) collective-permute-start(f32[4,128,128]{2,1,0:T(8,128)S(1)} %get-tuple-element.101), channel_id=1, source_target_pairs={{0,8},{4,12},{8,16},{12,20},{16,24},{20,28},{24,0},{28,4},{32,40},... | collective-permute-start | bytes 786440 | tf_op jit(solution)/shard_map/ppermute | solution.py:585
  127.9 22.3 %collective-permute-start.39 = (f32[4,128,128]{2,1,0:T(8,128)S(1)}, f32[4,128,128]{2,1,0:T(8,128)S(1)}, u32[]{:S(2)}, u32[]{:S(2)}) collective-permute-start(f32[4,128,128]{2,1,0:T(8,128)S(1)} %get-tuple-element.102), channel_id=1, source_target_pairs={{0,24},{4,28},{8,0},{12,4},{16,8},{20,12},{24,16},{28,20},{32,56},... | collective-permute-start | bytes 786440 | tf_op jit(solution)/shard_map/ppermute | solution.py:585
  132.8 19.5 %collective-permute-start.40 = (f32[4,128,128]{2,1,0:T(8,128)S(1)}, f32[4,128,128]{2,1,0:T(8,128)S(1)}, u32[]{:S(2)}, u32[]{:S(2)}) collective-permute-start(f32[4,128,128]{2,1,0:T(8,128)S(1)} %get-tuple-element.103), channel_id=1, source_target_pairs={{0,16},{4,20},{8,24},{12,28},{16,0},{20,4},{24,8},{28,12},{32,48},... | collective-permute-start | bytes 786440 | tf_op jit(solution)/shard_map/ppermute | solution.py:585
  133.8 20.9 %collective-permute-start.48 = (bf16[128,1280]{1,0:T(8,128)(2,1)}, bf16[128,1280]{1,0:T(8,128)(2,1)S(1)}, u32[]{:S(2)}, u32[]{:S(2)}) collective-permute-start(bf16[128,1280]{1,0:T(8,128)(2,1)} %collective-permute-done.5.cl.refs_4_), channel_id=1, source_target_pairs={{0,4},{4,0},{8,12},{12,8},{16,20},{20,16},{24,28},{28,24},{32,36},... | collective-permute-start | bytes 983048 | tf_op jit(solution)/shard_map/ppermute | solution.py:585
  149.0 6.0 %collective-permute-start.46 = (bf16[128,1280]{1,0:T(8,128)(2,1)S(1)}, bf16[128,1280]{1,0:T(8,128)(2,1)S(1)}, u32[]{:S(2)}, u32[]{:S(2)}) collective-permute-start(bf16[128,1280]{1,0:T(8,128)(2,1)S(1)} %collective-permute-done.7.bl.refs_2_), channel_id=1, source_target_pairs={{0,4},{4,0},{8,12},{12,8},{16,20},{20,16},{24,28},{28,24},{32,36},... | collective-permute-start | bytes 983048 | tf_op jit(solution)/shard_map/ppermute | solution.py:585
  150.2 4.9 %collective-permute-start.47 = (bf16[128,1280]{1,0:T(8,128)(2,1)S(1)}, bf16[128,1280]{1,0:T(8,128)(2,1)S(1)}, u32[]{:S(2)}, u32[]{:S(2)}) collective-permute-start(bf16[128,1280]{1,0:T(8,128)(2,1)S(1)} %collective-permute-done.8.ct.refs_3_), channel_id=1, source_target_pairs={{0,4},{4,0},{8,12},{12,8},{16,20},{20,16},{24,28},{28,24},{32,36},... | collective-permute-start | bytes 983048 | tf_op jit(solution)/shard_map/ppermute | solution.py:585
  150.2 4.9 %collective-permute-start.49 = (bf16[128,1280]{1,0:T(8,128)(2,1)S(1)}, bf16[128,1280]{1,0:T(8,128)(2,1)S(1)}, u32[]{:S(2)}, u32[]{:S(2)}) collective-permute-start(bf16[128,1280]{1,0:T(8,128)(2,1)S(1)} %collective-permute-done.4.a.refs_5_), channel_id=1, source_target_pairs={{0,4},{4,0},{8,12},{12,8},{16,20},{20,16},{24,28},{28,24},{32,36},... | collective-permute-start | bytes 983048 | tf_op jit(solution)/shard_map/ppermute | solution.py:585
  152.3 3.5 %collective-permute-start.50 = (bf16[128,1280]{1,0:T(8,128)(2,1)S(1)}, bf16[128,1280]{1,0:T(8,128)(2,1)S(1)}, u32[]{:S(2)}, u32[]{:S(2)}) collective-permute-start(bf16[128,1280]{1,0:T(8,128)(2,1)S(1)} %collective-permute-done.6.b.refs_6_), channel_id=1, source_target_pairs={{0,4},{4,0},{8,12},{12,8},{16,20},{20,16},{24,28},{28,24},{32,36},... | collective-permute-start | bytes 983048 | tf_op jit(solution)/shard_map/ppermute | solution.py:585
  154.7 3.8 %collective-permute-start.41 = (bf16[256,256]{1,0:T(8,128)(2,1)S(1)}, bf16[256,256]{1,0:T(8,128)(2,1)S(1)}, u32[]{:S(2)}, u32[]{:S(2)}) collective-permute-start(bf16[256,256]{1,0:T(8,128)(2,1)S(1)} %get-tuple-element.105), channel_id=1, source_target_pairs={{0,4},{4,0},{8,12},{12,8},{16,20},{20,16},{24,28},{28,24},{32,36},... | collective-permute-start | bytes 393224 | tf_op jit(solution)/shard_map/ppermute | solution.py:585
  161.1 10.2 %collective-permute-start.51 = (bf16[8,160,128]{2,1,0:T(8,128)(2,1)S(1)}, bf16[8,160,128]{2,1,0:T(8,128)(2,1)S(1)}, u32[]{:S(2)}, u32[]{:S(2)}) collective-permute-start(bf16[8,160,128]{2,1,0:T(8,128)(2,1)S(1)} %get-tuple-element.114), channel_id=1, source_target_pairs={{0,8},{4,12},{8,16},{12,20},{16,24},{20,28},{24,0},{28,4},{32,40},... | collective-permute-start | bytes 983048 | tf_op jit(solution)/shard_map/ppermute | solution.py:585
  161.1 12.3 %collective-permute-start.52 = (bf16[8,160,128]{2,1,0:T(8,128)(2,1)S(1)}, bf16[8,160,128]{2,1,0:T(8,128)(2,1)S(1)}, u32[]{:S(2)}, u32[]{:S(2)}) collective-permute-start(bf16[8,160,128]{2,1,0:T(8,128)(2,1)S(1)} %get-tuple-element.115), channel_id=1, source_target_pairs={{0,24},{4,28},{8,0},{12,4},{16,8},{20,12},{24,16},{28,20},{32,56},... | collective-permute-start | bytes 983048 | tf_op jit(solution)/shard_map/ppermute | solution.py:585
  163.8 14.6 %collective-permute-start.53 = (bf16[8,160,128]{2,1,0:T(8,128)(2,1)S(1)}, bf16[8,160,128]{2,1,0:T(8,128)(2,1)S(1)}, u32[]{:S(2)}, u32[]{:S(2)}) collective-permute-start(bf16[8,160,128]{2,1,0:T(8,128)(2,1)S(1)} %get-tuple-element.116), channel_id=1, source_target_pairs={{0,16},{4,20},{8,24},{12,28},{16,0},{20,4},{24,8},{28,12},{32,48},... | collective-permute-start | bytes 983048 | tf_op jit(solution)/shard_map/ppermute | solution.py:585
  163.9 14.5 %collective-permute-start.54 = (bf16[8,160,128]{2,1,0:T(8,128)(2,1)S(1)}, bf16[8,160,128]{2,1,0:T(8,128)(2,1)S(1)}, u32[]{:S(2)}, u32[]{:S(2)}) collective-permute-start(bf16[8,160,128]{2,1,0:T(8,128)(2,1)S(1)} %get-tuple-element.118), channel_id=1, source_target_pairs={{0,32},{4,36},{8,40},{12,44},{16,48},{20,52},{24,56},{28,60},{32,6... | collective-permute-start | bytes 983048 | tf_op jit(solution)/shard_map/ppermute | solution.py:585
  164.5 13.9 %collective-permute-start.55 = (bf16[8,160,128]{2,1,0:T(8,128)(2,1)S(1)}, bf16[8,160,128]{2,1,0:T(8,128)(2,1)S(1)}, u32[]{:S(2)}, u32[]{:S(2)}) collective-permute-start(bf16[8,160,128]{2,1,0:T(8,128)(2,1)S(1)} %get-tuple-element.119), channel_id=1, source_target_pairs={{0,96},{4,100},{8,104},{12,108},{16,112},{20,116},{24,120},{28,124... | collective-permute-start | bytes 983048 | tf_op jit(solution)/shard_map/ppermute | solution.py:585
  171.2 8.8 %collective-permute-start.56 = (bf16[8,160,128]{2,1,0:T(8,128)(2,1)S(1)}, bf16[8,160,128]{2,1,0:T(8,128)(2,1)S(1)}, u32[]{:S(2)}, u32[]{:S(2)}) collective-permute-start(bf16[8,160,128]{2,1,0:T(8,128)(2,1)S(1)} %get-tuple-element.120), channel_id=1, source_target_pairs={{0,64},{4,68},{8,72},{12,76},{16,80},{20,84},{24,88},{28,92},{32,9... | collective-permute-start | bytes 983048 | tf_op jit(solution)/shard_map/ppermute | solution.py:585
  180.4 11.0 %collective-permute-start.57 = (f32[2,160,128]{2,1,0:T(8,128)S(1)}, f32[2,160,128]{2,1,0:T(8,128)S(1)}, u32[]{:S(2)}, u32[]{:S(2)}) collective-permute-start(f32[2,160,128]{2,1,0:T(8,128)S(1)} %get-tuple-element.122), channel_id=1, source_target_pairs={{0,32},{4,36},{8,40},{12,44},{16,48},{20,52},{24,56},{28,60},{32,6... | collective-permute-start | bytes 491528 | tf_op jit(solution)/shard_map/ppermute | solution.py:585
  182.4 9.1 %collective-permute-start.58 = (f32[2,160,128]{2,1,0:T(8,128)S(1)}, f32[2,160,128]{2,1,0:T(8,128)S(1)}, u32[]{:S(2)}, u32[]{:S(2)}) collective-permute-start(f32[2,160,128]{2,1,0:T(8,128)S(1)} %get-tuple-element.123), channel_id=1, source_target_pairs={{0,96},{4,100},{8,104},{12,108},{16,112},{20,116},{24,120},{28,124... | collective-permute-start | bytes 491528 | tf_op jit(solution)/shard_map/ppermute | solution.py:585
  183.6 10.6 %collective-permute-start.59 = (f32[2,160,128]{2,1,0:T(8,128)S(1)}, f32[2,160,128]{2,1,0:T(8,128)S(1)}, u32[]{:S(2)}, u32[]{:S(2)}) collective-permute-start(f32[2,160,128]{2,1,0:T(8,128)S(1)} %get-tuple-element.124), channel_id=1, source_target_pairs={{0,64},{4,68},{8,72},{12,76},{16,80},{20,84},{24,88},{28,92},{32,9... | collective-permute-start | bytes 491528 | tf_op jit(solution)/shard_map/ppermute | solution.py:585
  184.9 9.9 %collective-permute-start.60 = (f32[2,160,128]{2,1,0:T(8,128)S(1)}, f32[2,160,128]{2,1,0:T(8,128)S(1)}, u32[]{:S(2)}, u32[]{:S(2)}) collective-permute-start(f32[2,160,128]{2,1,0:T(8,128)S(1)} %get-tuple-element.126), channel_id=1, source_target_pairs={{0,8},{4,12},{8,16},{12,20},{16,24},{20,28},{24,0},{28,4},{32,40},... | collective-permute-start | bytes 491528 | tf_op jit(solution)/shard_map/ppermute | solution.py:585
  185.3 23.3 %collective-permute-start.28 = (bf16[256,1280]{1,0:T(8,128)(2,1)S(1)}, bf16[256,1280]{1,0:T(8,128)(2,1)S(1)}, u32[]{:S(2)}, u32[]{:S(2)}) collective-permute-start(bf16[256,1280]{1,0:T(8,128)(2,1)S(1)} %slice.3), channel_id=1, source_target_pairs={{0,4},{4,0},{8,12},{12,8},{16,20},{20,16},{24,28},{28,24},{32,36},... | collective-permute-start | bytes 1966088 | tf_op jit(solution)/shard_map/ppermute | solution.py:585
  191.4 20.2 %collective-permute-start.42 = (bf16[256,1280]{1,0:T(8,128)(2,1)S(1)}, bf16[256,1280]{1,0:T(8,128)(2,1)S(1)}, u32[]{:S(2)}, u32[]{:S(2)}) collective-permute-start(bf16[256,1280]{1,0:T(8,128)(2,1)S(1)} %get-tuple-element.109), channel_id=1, source_target_pairs={{0,1},{1,2},{2,3},{3,0},{4,5},{5,6},{6,7},{7,4},{8,9},{9,10},{10,1... | collective-permute-start | bytes 1966088 | tf_op jit(solution)/shard_map/ppermute | solution.py:585
  191.5 30.3 %collective-permute-start.43 = (bf16[256,1280]{1,0:T(8,128)(2,1)S(1)}, bf16[256,1280]{1,0:T(8,128)(2,1)S(1)}, u32[]{:S(2)}, u32[]{:S(2)}) collective-permute-start(bf16[256,1280]{1,0:T(8,128)(2,1)S(1)} %get-tuple-element.110), channel_id=1, source_target_pairs={{0,3},{1,0},{2,1},{3,2},{4,7},{5,4},{6,5},{7,6},{8,11},{9,8},{10,9... | collective-permute-start | bytes 1966088 | tf_op jit(solution)/shard_map/ppermute | solution.py:585
  194.2 29.4 %collective-permute-start.44 = (bf16[256,1280]{1,0:T(8,128)(2,1)S(1)}, bf16[256,1280]{1,0:T(8,128)(2,1)S(1)}, u32[]{:S(2)}, u32[]{:S(2)}) collective-permute-start(bf16[256,1280]{1,0:T(8,128)(2,1)S(1)} %get-tuple-element.111), channel_id=1, source_target_pairs={{0,2},{1,3},{2,0},{3,1},{4,6},{5,7},{6,4},{7,5},{8,10},{9,11},{10,... | collective-permute-start | bytes 1966088 | tf_op jit(solution)/shard_map/ppermute | solution.py:585
  194.8 5.6 %collective-permute-start.61 = (f32[2,160,128]{2,1,0:T(8,128)S(1)}, f32[2,160,128]{2,1,0:T(8,128)S(1)}, u32[]{:S(2)}, u32[]{:S(2)}) collective-permute-start(f32[2,160,128]{2,1,0:T(8,128)S(1)} %get-tuple-element.127), channel_id=1, source_target_pairs={{0,24},{4,28},{8,0},{12,4},{16,8},{20,12},{24,16},{28,20},{32,56},... | collective-permute-start | bytes 491528 | tf_op jit(solution)/shard_map/ppermute | solution.py:585
  200.4 5.7 %collective-permute-start.62 = (f32[2,160,128]{2,1,0:T(8,128)S(1)}, f32[2,160,128]{2,1,0:T(8,128)S(1)}, u32[]{:S(2)}, u32[]{:S(2)}) collective-permute-start(f32[2,160,128]{2,1,0:T(8,128)S(1)} %get-tuple-element.128), channel_id=1, source_target_pairs={{0,16},{4,20},{8,24},{12,28},{16,0},{20,4},{24,8},{28,12},{32,48},... | collective-permute-start | bytes 491528 | tf_op jit(solution)/shard_map/ppermute | solution.py:585
  206.1 4.3 %collective-permute-start.63 = (f32[160,256]{1,0:T(8,128)S(1)}, f32[160,256]{1,0:T(8,128)S(1)}, u32[]{:S(2)}, u32[]{:S(2)}) collective-permute-start(f32[160,256]{1,0:T(8,128)S(1)} %get-tuple-element.130), channel_id=1, source_target_pairs={{0,4},{4,0},{8,12},{12,8},{16,20},{20,16},{24,28},{28,24},{32,36},... | collective-permute-start | bytes 491528 | tf_op jit(solution)/shard_map/ppermute | solution.py:585
  (7 other events, 138.0 us)

commit v5 on v4

--- a/solution.py
+++ b/solution.py
@@ -227,6 +227,22 @@
         compiler_params=params(5),
         name="join_rows",
     )(place, mine, other)
+
+
+def add_partials(*parts):
+    def body(a, b, c, d, out):
+        out[...] = (
+            a[...].astype(F32) + b[...].astype(F32) + c[...].astype(F32) + d[...].astype(F32)
+        ).astype(BF)
+
+    return pl.pallas_call(
+        body,
+        in_specs=[pl.BlockSpec(memory_space=pltpu.VMEM)] * 4,
+        out_specs=pl.BlockSpec(memory_space=pltpu.VMEM),
+        out_shape=jax.ShapeDtypeStruct(parts[0].shape, BF),
+        compiler_params=params(5),
+        name="add_partials",
+    )(*parts)
 
 
 def join_weights(place, mine, other):
@@ -419,7 +435,7 @@
         ),
         out_shape=[jax.ShapeDtypeStruct((4 * BLOCK, 2 * width), BF)]
         + [jax.ShapeDtypeStruct(s, d) for s, d in grads + grads],
-        compiler_params=params(36),
+        compiler_params=pltpu.CompilerParams(vmem_limit_bytes=36 * 1024 * 1024),
         name="attend",
     )(table, queries, query_peer, upstream, upstream_peer, *pieces)
 
@@ -583,6 +599,13 @@
 
 def mover(axis, pairs):
     return lambda value: lax.ppermute(value, axis, pairs)
+
+
+def spread(value, ahead, behind, across):
+    far = across(value)
+    back = ahead(value)
+    forth = behind(value)
+    return [value, back, forth, far]
 
 
 def ring_gather(first, second, ahead, behind):
@@ -658,8 +681,8 @@
         place, far_top, far_low, key_weight, value_weight, key_sum, value_sum, cosine, sine
     )
     other = swap(send)
-    mine_line = pack(keep, xn(keep), xb(keep), x2(keep))
-    other_line = pack(other, yn(other), yb(other), y2(other))
+    mine_line = pack(*spread(keep, xn, xb, x2))
+    other_line = pack(*spread(other, yn, yb, y2))
     pieces = ring_gather(*mine_line, yn, yb) + ring_gather(*other_line, xn, xb)
 
     near_features = [left_top, left_low, right_top, right_low, far_top, far_low]
@@ -675,7 +698,6 @@
     t_last = send_all(sums[:4], yn, yb, y2) + send_all(sums[4:], xn, xb, x2)
     grads, grads_away = finish_grads(t_last, cosine, sine)
     grads_other = swap(grads_away)
-    grads, grads_other = lax.optimization_barrier((grads, grads_other))
 
     out_other = swap(out[local_rows:])
 
@@ -685,12 +707,7 @@
     w_sent = send_all(w_parts[:4], xn, xb, x2) + send_all(w_parts[4:], yn, yb, y2)
     parts = input_partials(place, grads, grads_other, key_weight, value_weight)
     _, from_back, from_next, from_far = send_all(parts, zn, zb, z2)
-    hidden_grad = (
-        parts[0].astype(F32)
-        + from_back.astype(F32)
-        + from_next.astype(F32)
-        + from_far.astype(F32)
-    ).astype(BF)
+    hidden_grad = add_partials(parts[0], from_back, from_next, from_far)
     w_sums = combine(w_sent)
     w_last = send_all(w_sums[:4], yn, yb, y2) + send_all(w_sums[4:], xn, xb, x2)
     both, both_away = finish_weights(w_last)

time: 225 us -> 227 us (level)
  waiting for transfers between devices: 70.3 us -> 88.4 us
  starting transfers between devices: 111 us -> 93.6 us
    ppermute x64, waiting for transfers between devices: 70.3 us -> 88.4 us  [mover(): return lambda value: lax.ppermute(value, axis, pairs)]
    ppermute x64, starting transfers between devices: 111 us -> 93.6 us  [mover(): return lambda value: lax.ppermute(value, axis, pairs)]
  transfers between devices with their start and end apart: 64 -> 64, of which waited for: 24 -> 26; matrix products, arithmetic and copies ran while one was open for 1% -> 1% of each run, Pallas kernels for 7% -> 7%
where the time goes in v5:
time: 227 us
  starting transfers between devices  93.6 us (41%)
  waiting for transfers between devices  88.4 us (39%)
  Pallas kernels  35.4 us (16%)
  local copies, waits for them, and re-layouts  7.15 us (3%)
    ppermute x64, starting transfers between devices, mover(): return lambda value: lax.ppermute(value, axis, pairs)  93.6 us
    ppermute x64, waiting for transfers between devices, mover(): return lambda value: lax.ppermute(value, axis, pairs)  88.4 us
    pallas_call x1, Pallas kernels, attend(): pl.pallas_call(body, grid_spec=pltpu.PrefetchScalarGridSpec(num_scalar_pr...  14.6 us
  transfers between devices with their start and end apart: 64, of which 26 were waited for; matrix products, arithmetic and copies ran while one was open for 1% of the time, Pallas kernels for 7%

profile of v5, /device:TPU:1, one launch (start us, length us, event | category | flops | bytes accessed | tf_op | source)
XLA Modules:
  0.0 226.8 jit_solution(3619351471781482472)
XLA Ops:
  0.7 1.9 constant_dynamic-slice_fusion.1
  2.5 1.4 collective-permute-start.1
  3.9 1.7 constant_dynamic-slice_fusion
  6.2 1.1 copy-done.3
  8.1 1.7 collective-permute-start.3
  9.9 2.1 collective-permute-start.5
  12.7 2.5 %device_tables.1 = (s32[115]{0:T(128)S(1)}, s32[17]{0:T(128)S(1)}, s32[4]{0:T(128)S(1)}) custom-call(s32[64]{0:T(128)S(1)} %copy-done.7, s32[4]{0:T(128)S(1)} %pad_add_fusion.where), custom_call_target="tpu_custom_call" | custom-call | tf_op jit(solution)/shard_map/device_tables/pallas_call | solution.py:89
  15.4 2.7 %collective-permute-start.8 = (bf16[128,1280]{1,0:T(8,128)(2,1)}, bf16[128,1280]{1,0:T(8,128)(2,1)S(1)}, u32[]{:S(2)}, u32[]{:S(2)}) collective-permute-start(bf16[128,1280]{1,0:T(8,128)(2,1)} %get-tuple-element.72), channel_id=1, source_target_pairs={{0,3},{1,0},{2,1},{3,2},{4,7},{5,4},{6,5},{7,6},{8,11},{9,8},{10,9... | collective-permute-start | bytes 983048 | tf_op jit(solution)/shard_map/ppermute | solution.py:601
  18.1 2.3 %collective-permute-done.3.bt.refs_1_ = bf16[128,1280]{1,0:T(8,128)(2,1)} collective-permute-done((bf16[128,1280]{1,0:T(8,128)(2,1)}, bf16[128,1280]{1,0:T(8,128)(2,1)}, u32[]{:S(2)}, u32[]{:S(2)}) %collective-permute-start.3) | collective-permute-done | bytes 327712 | tf_op jit(solution)/shard_map/ppermute | solution.py:601
  20.4 2.7 %collective-permute-start.6 = (bf16[128,1280]{1,0:T(8,128)(2,1)}, bf16[128,1280]{1,0:T(8,128)(2,1)S(1)}, u32[]{:S(2)}, u32[]{:S(2)}) collective-permute-start(bf16[128,1280]{1,0:T(8,128)(2,1)} %collective-permute-done.5.cl.refs_4_), channel_id=1, source_target_pairs={{0,3},{1,0},{2,1},{3,2},{4,7},{5,4},{6,5},{7,6},{8,11},{9,8},{10,9... | collective-permute-start | bytes 983048 | tf_op jit(solution)/shard_map/ppermute | solution.py:601
  24.3 3.0 %collective-permute-done.7.bl.refs_2_ = bf16[128,1280]{1,0:T(8,128)(2,1)S(1)} collective-permute-done((bf16[128,1280]{1,0:T(8,128)(2,1)}, bf16[128,1280]{1,0:T(8,128)(2,1)S(1)}, u32[]{:S(2)}, u32[]{:S(2)}) %collective-permute-start.7) | collective-permute-done | bytes 327712 | tf_op jit(solution)/shard_map/ppermute | solution.py:601
  27.3 1.7 copy-done.1
  29.1 2.8 %project_near.1 = (f32[256,256]{1,0:T(8,128)S(1)}, f32[256,256]{1,0:T(8,128)S(1)}) custom-call(s32[17]{0:T(128)S(1)} %get-tuple-element.68.place_ref.p, bf16[256,1280]{1,0:T(8,128)(2,1)S(1)} %copy-done.4, bf16[128,1280]{1,0:T(8,128)(2,1)} %collective-permute-done.3.bt.refs_1_, bf16[128,1280]{1,0:T(8,128)(2,1)S(1)} %collective-permute-done.7.bl.refs_2_, ...), custom_call_target="tpu_custom_call" | custom-call | tf_op jit(solution)/shard_map/project_near/pallas_call | solution.py:170
  31.9 2.5 %collective-permute-done.4.a.refs_5_ = bf16[128,1280]{1,0:T(8,128)(2,1)S(1)} collective-permute-done((bf16[128,1280]{1,0:T(8,128)(2,1)}, bf16[128,1280]{1,0:T(8,128)(2,1)S(1)}, u32[]{:S(2)}, u32[]{:S(2)}) %collective-permute-start.4) | collective-permute-done | bytes 327712 | tf_op jit(solution)/shard_map/ppermute | solution.py:601
  34.3 1.1 project_far.1
  35.5 2.5 %collective-permute-start.10 = (bf16[256,256]{1,0:T(8,128)(2,1)S(1)}, bf16[256,256]{1,0:T(8,128)(2,1)S(1)}, u32[]{:S(2)}, u32[]{:S(2)}) collective-permute-start(bf16[256,256]{1,0:T(8,128)(2,1)S(1)} %get-tuple-element.77.a), channel_id=1, source_target_pairs={{0,24},{4,28},{8,0},{12,4},{16,8},{20,12},{24,16},{28,20},{32,56},... | collective-permute-start | bytes 393224 | tf_op jit(solution)/shard_map/ppermute | solution.py:601
  39.1 1.4 collective-permute-start.18
  40.9 2.8 %collective-permute-done.11.d = bf16[256,256]{1,0:T(8,128)(2,1)S(1)} collective-permute-done((bf16[256,256]{1,0:T(8,128)(2,1)S(1)}, bf16[256,256]{1,0:T(8,128)(2,1)S(1)}, u32[]{:S(2)}, u32[]{:S(2)}) %collective-permute-start.11) | collective-permute-done | bytes 131104 | tf_op jit(solution)/shard_map/ppermute | solution.py:601
  43.7 4.0 %collective-permute-done.9.b = bf16[256,256]{1,0:T(8,128)(2,1)S(1)} collective-permute-done((bf16[256,256]{1,0:T(8,128)(2,1)S(1)}, bf16[256,256]{1,0:T(8,128)(2,1)S(1)}, u32[]{:S(2)}, u32[]{:S(2)}) %collective-permute-start.9) | collective-permute-done | bytes 131104 | tf_op jit(solution)/shard_map/ppermute | solution.py:601
  47.7 1.4 collective-permute-start.12
  49.1 1.5 collective-permute-start.15
  50.6 2.7 %collective-permute-start.20 = (bf16[256,256]{1,0:T(8,128)(2,1)S(1)}, bf16[256,256]{1,0:T(8,128)(2,1)S(1)}, u32[]{:S(2)}, u32[]{:S(2)}) collective-permute-start(bf16[256,256]{1,0:T(8,128)(2,1)S(1)} %collective-permute-done.18.a), channel_id=1, source_target_pairs={{0,96},{4,100},{8,104},{12,108},{16,112},{20,116},{24,120},{28,124... | collective-permute-start | bytes 393224 | tf_op jit(solution)/shard_map/ppermute | solution.py:601
  53.6 5.6 %collective-permute-done.19.b = bf16[256,256]{1,0:T(8,128)(2,1)S(1)} collective-permute-done((bf16[256,256]{1,0:T(8,128)(2,1)S(1)}, bf16[256,256]{1,0:T(8,128)(2,1)S(1)}, u32[]{:S(2)}, u32[]{:S(2)}) %collective-permute-start.19) | collective-permute-done | bytes 131104 | tf_op jit(solution)/shard_map/ppermute | solution.py:601
  59.2 3.0 %collective-permute-start.14 = (bf16[4,128,256]{2,1,0:T(8,128)(2,1)S(1)}, bf16[4,128,256]{2,1,0:T(8,128)(2,1)S(1)}, u32[]{:S(2)}, u32[]{:S(2)}) collective-permute-start(bf16[4,128,256]{2,1,0:T(8,128)(2,1)S(1)} %get-tuple-element.78.refs_0_), channel_id=1, source_target_pairs={{0,96},{4,100},{8,104},{12,108},{16,112},{20,116},{24,120},{28,124... | collective-permute-start | bytes 786440 | tf_op jit(solution)/shard_map/ppermute | solution.py:601
  63.3 2.7 %collective-permute-start.25 = (bf16[4,128,256]{2,1,0:T(8,128)(2,1)S(1)}, bf16[4,128,256]{2,1,0:T(8,128)(2,1)S(1)}, u32[]{:S(2)}, u32[]{:S(2)}) collective-permute-start(bf16[4,128,256]{2,1,0:T(8,128)(2,1)S(1)} %get-tuple-element.82.refs_9_), channel_id=1, source_target_pairs={{0,24},{4,28},{8,0},{12,4},{16,8},{20,12},{24,16},{28,20},{32,56},... | collective-permute-start | bytes 786440 | tf_op jit(solution)/shard_map/ppermute | solution.py:601
  66.0 2.9 %collective-permute-done.13.refs_3_ = bf16[4,128,256]{2,1,0:T(8,128)(2,1)S(1)} collective-permute-done((bf16[4,128,256]{2,1,0:T(8,128)(2,1)S(1)}, bf16[4,128,256]{2,1,0:T(8,128)(2,1)S(1)}, u32[]{:S(2)}, u32[]{:S(2)}) %collective-permute-start.13) | collective-permute-done | bytes 262176 | tf_op jit(solution)/shard_map/ppermute | solution.py:601
  69.8 1.8 collective-permute-start.17
  71.6 1.5 collective-permute-start.26
  73.0 2.4 %collective-permute-done.23.refs_11_ = bf16[4,128,256]{2,1,0:T(8,128)(2,1)S(1)} collective-permute-done((bf16[4,128,256]{2,1,0:T(8,128)(2,1)S(1)}, bf16[4,128,256]{2,1,0:T(8,128)(2,1)S(1)}, u32[]{:S(2)}, u32[]{:S(2)}) %collective-permute-start.23) | collective-permute-done | bytes 262176 | tf_op jit(solution)/shard_map/ppermute | solution.py:601
  76.0 5.1 %collective-permute-done.26.refs_14_ = bf16[4,128,256]{2,1,0:T(8,128)(2,1)S(1)} collective-permute-done((bf16[4,128,256]{2,1,0:T(8,128)(2,1)S(1)}, bf16[4,128,256]{2,1,0:T(8,128)(2,1)S(1)}, u32[]{:S(2)}, u32[]{:S(2)}) %collective-permute-start.26) | collective-permute-done | bytes 262176 | tf_op jit(solution)/shard_map/ppermute | solution.py:601
  81.1 14.6 %attend.1 = (bf16[512,1280]{1,0:T(8,128)(2,1)S(1)}, f32[16,128,128]{2,1,0:T(8,128)S(1)}, bf16[16,128,128]{2,1,0:T(8,128)(2,1)S(1)}, bf16[16,128,128]{2,1,0:T(8,1...) custom-call(s32[115]{0:T(128)S(1)} %get-tuple-element.69.t, ...), custom_call_target="tpu_custom_call" | custom-call | tf_op jit(solution)/shard_map/attend/pallas_call | solution.py:422
  96.0 6.9 %collective-permute-start.45 = (bf16[128,1280]{1,0:T(8,128)(2,1)}, bf16[128,1280]{1,0:T(8,128)(2,1)S(1)}, u32[]{:S(2)}, u32[]{:S(2)}) collective-permute-start(bf16[128,1280]{1,0:T(8,128)(2,1)} %collective-permute-done.3.bt.refs_1_), channel_id=1, source_target_pairs={{0,4},{4,0},{8,12},{12,8},{16,20},{20,16},{24,28},{28,24},{32,36},... | collective-permute-start | bytes 983048 | tf_op jit(solution)/shard_map/ppermute | solution.py:601
  102.9 2.7 %collective-permute-start.30 = (bf16[16,128,128]{2,1,0:T(8,128)(2,1)S(1)}, bf16[16,128,128]{2,1,0:T(8,128)(2,1)S(1)}, u32[]{:S(2)}, u32[]{:S(2)}) collective-permute-start(bf16[16,128,128]{2,1,0:T(8,128)(2,1)S(1)} %get-tuple-element.88), channel_id=1, source_target_pairs={{0,24},{4,28},{8,0},{12,4},{16,8},{20,12},{24,16},{28,20},{32,56},... | collective-permute-start | bytes 1572872 | tf_op jit(solution)/shard_map/ppermute | solution.py:601
  106.4 1.9 collective-permute-start.33
  108.6 19.4 %collective-permute-done.30.refs_2_ = bf16[16,128,128]{2,1,0:T(8,128)(2,1)S(1)} collective-permute-done((bf16[16,128,128]{2,1,0:T(8,128)(2,1)S(1)}, bf16[16,128,128]{2,1,0:T(8,128)(2,1)S(1)}, u32[]{:S(2)}, u32[]{:S(2)}) %collective-permute-start.30) | collective-permute-done | bytes 524320 | tf_op jit(solution)/shard_map/ppermute | solution.py:601
  129.6 5.4 %collective-permute-start.50 = (bf16[128,1280]{1,0:T(8,128)(2,1)S(1)}, bf16[128,1280]{1,0:T(8,128)(2,1)S(1)}, u32[]{:S(2)}, u32[]{:S(2)}) collective-permute-start(bf16[128,1280]{1,0:T(8,128)(2,1)S(1)} %collective-permute-done.6.b.refs_6_), channel_id=1, source_target_pairs={{0,4},{4,0},{8,12},{12,8},{16,20},{20,16},{24,28},{28,24},{32,36},... | collective-permute-start | bytes 983048 | tf_op jit(solution)/shard_map/ppermute | solution.py:601
  135.5 2.7 %collective-permute-start.36 = (f32[4,128,128]{2,1,0:T(8,128)S(1)}, f32[4,128,128]{2,1,0:T(8,128)S(1)}, u32[]{:S(2)}, u32[]{:S(2)}) collective-permute-start(f32[4,128,128]{2,1,0:T(8,128)S(1)} %get-tuple-element.96), channel_id=1, source_target_pairs={{0,96},{4,100},{8,104},{12,108},{16,112},{20,116},{24,120},{28,124... | collective-permute-start | bytes 786440 | tf_op jit(solution)/shard_map/ppermute | solution.py:601
  138.5 2.7 %collective-permute-start.39 = (f32[4,128,128]{2,1,0:T(8,128)S(1)}, f32[4,128,128]{2,1,0:T(8,128)S(1)}, u32[]{:S(2)}, u32[]{:S(2)}) collective-permute-start(f32[4,128,128]{2,1,0:T(8,128)S(1)} %get-tuple-element.100), channel_id=1, source_target_pairs={{0,24},{4,28},{8,0},{12,4},{16,8},{20,12},{24,16},{28,20},{32,56},... | collective-permute-start | bytes 786440 | tf_op jit(solution)/shard_map/ppermute | solution.py:601
  141.1 3.4 %collective-permute-done.35.refs_1_ = f32[4,128,128]{2,1,0:T(8,128)S(1)} collective-permute-done((f32[4,128,128]{2,1,0:T(8,128)S(1)}, f32[4,128,128]{2,1,0:T(8,128)S(1)}, u32[]{:S(2)}, u32[]{:S(2)}) %collective-permute-start.35) | collective-permute-done | bytes 262176 | tf_op jit(solution)/shard_map/ppermute | solution.py:601
  145.1 2.7 %flip.1.ft = bf16[4,1280,512]{2,1,0:T(8,128)(2,1)S(1)} custom-call(bf16[256,1280]{1,0:T(8,128)(2,1)S(1)} %copy-done.4, bf16[128,1280]{1,0:T(8,128)(2,1)} %collective-permute-done.3.bt.refs_1_, bf16[128,1280]{1,0:T(8,128)(2,1)S(1)} %collective-permute-done.7.bl.refs_2_, bf16[128,1280]{1,0:T(8,128)(2,1)S(1)} %collective-permute-done.8.ct.refs_3_, ...), custom_call_target="tpu_custom_call" | custom-call | tf_op jit(solution)/shard_map/flip/pallas_call | solution.py:558
  147.8 1.2 collective-permute-done.36.refs_2_
  149.0 1.3 collective-permute-done.37.refs_3_
  150.4 2.4 %collective-permute-done.40.refs_7_ = f32[4,128,128]{2,1,0:T(8,128)S(1)} collective-permute-done((f32[4,128,128]{2,1,0:T(8,128)S(1)}, f32[4,128,128]{2,1,0:T(8,128)S(1)}, u32[]{:S(2)}, u32[]{:S(2)}) %collective-permute-start.40) | collective-permute-done | bytes 262176 | tf_op jit(solution)/shard_map/ppermute | solution.py:601
  153.0 2.5 %weight_partials.1 = (f32[8,160,128]{2,1,0:T(8,128)S(1)}, bf16[8,160,128]{2,1,0:T(8,128)(2,1)S(1)}, bf16[8,160,128]{2,1,0:T(8,128)(2,1)S(1)}, bf16[8,160,128]{2,...) custom-call(s32[17]{0:T(128)S(1)} %get-tuple-element.68.place_ref.p,, ...), custom_call_target="tpu_custom_call" | custom-call | tf_op jit(solution)/shard_map/weight_partials/pallas_call | solution.py:588
  156.0 2.3 %collective-permute-start.52 = (bf16[8,160,128]{2,1,0:T(8,128)(2,1)S(1)}, bf16[8,160,128]{2,1,0:T(8,128)(2,1)S(1)}, u32[]{:S(2)}, u32[]{:S(2)}) collective-permute-start(bf16[8,160,128]{2,1,0:T(8,128)(2,1)S(1)} %get-tuple-element.111), channel_id=1, source_target_pairs={{0,24},{4,28},{8,0},{12,4},{16,8},{20,12},{24,16},{28,20},{32,56},... | collective-permute-start | bytes 983048 | tf_op jit(solution)/shard_map/ppermute | solution.py:601
  159.0 2.7 %collective-permute-start.55 = (bf16[8,160,128]{2,1,0:T(8,128)(2,1)S(1)}, bf16[8,160,128]{2,1,0:T(8,128)(2,1)S(1)}, u32[]{:S(2)}, u32[]{:S(2)}) collective-permute-start(bf16[8,160,128]{2,1,0:T(8,128)(2,1)S(1)} %get-tuple-element.115), channel_id=1, source_target_pairs={{0,96},{4,100},{8,104},{12,108},{16,112},{20,116},{24,120},{28,124... | collective-permute-start | bytes 983048 | tf_op jit(solution)/shard_map/ppermute | solution.py:601
  161.6 2.4 %collective-permute-done.51.refs_1_ = bf16[8,160,128]{2,1,0:T(8,128)(2,1)S(1)} collective-permute-done((bf16[8,160,128]{2,1,0:T(8,128)(2,1)S(1)}, bf16[8,160,128]{2,1,0:T(8,128)(2,1)S(1)}, u32[]{:S(2)}, u32[]{:S(2)}) %collective-permute-start.51) | collective-permute-done | bytes 327712 | tf_op jit(solution)/shard_map/ppermute | solution.py:601
  164.1 4.1 %collective-permute-start.56 = (bf16[8,160,128]{2,1,0:T(8,128)(2,1)S(1)}, bf16[8,160,128]{2,1,0:T(8,128)(2,1)S(1)}, u32[]{:S(2)}, u32[]{:S(2)}) collective-permute-start(bf16[8,160,128]{2,1,0:T(8,128)(2,1)S(1)} %get-tuple-element.116), channel_id=1, source_target_pairs={{0,64},{4,68},{8,72},{12,76},{16,80},{20,84},{24,88},{28,92},{32,9... | collective-permute-start | bytes 983048 | tf_op jit(solution)/shard_map/ppermute | solution.py:601
  168.2 3.9 %collective-permute-done.53.refs_3_ = bf16[8,160,128]{2,1,0:T(8,128)(2,1)S(1)} collective-permute-done((bf16[8,160,128]{2,1,0:T(8,128)(2,1)S(1)}, bf16[8,160,128]{2,1,0:T(8,128)(2,1)S(1)}, u32[]{:S(2)}, u32[]{:S(2)}) %collective-permute-start.53) | collective-permute-done | bytes 327712 | tf_op jit(solution)/shard_map/ppermute | solution.py:601
  174.2 2.2 collective-permute-start.58
  176.4 1.2 collective-permute-start.59
  177.6 11.6 %collective-permute-start.41 = (bf16[256,256]{1,0:T(8,128)(2,1)S(1)}, bf16[256,256]{1,0:T(8,128)(2,1)S(1)}, u32[]{:S(2)}, u32[]{:S(2)}) collective-permute-start(bf16[256,256]{1,0:T(8,128)(2,1)S(1)} %get-tuple-element.103), channel_id=1, source_target_pairs={{0,4},{4,0},{8,12},{12,8},{16,20},{20,16},{24,28},{28,24},{32,36},... | collective-permute-start | bytes 393224 | tf_op jit(solution)/shard_map/ppermute | solution.py:601
  190.5 3.0 %input_partials.1 = (bf16[256,1280]{1,0:T(8,128)(2,1)S(1)}, bf16[256,1280]{1,0:T(8,128)(2,1)S(1)}, bf16[256,1280]{1,0:T(8,128)(2,1)S(1)}, bf16[256,1280]{1,0:T(8,128)(2,1)S(1)}) custom-call(s32[17]{0:T(128)S(1)} %get-tuple-element.68.place_ref.p, bf16[512,256]{1,0:T(8,128)(2,1)S(1)} %get-tuple-element.102.a.g, ...), custom_call_target="tpu_custom_call" | custom-call | tf_op jit(solution)/shard_map/input_partials/pallas_call | solution.py:533
  193.7 2.7 %collective-permute-start.43 = (bf16[256,1280]{1,0:T(8,128)(2,1)S(1)}, bf16[256,1280]{1,0:T(8,128)(2,1)S(1)}, u32[]{:S(2)}, u32[]{:S(2)}) collective-permute-start(bf16[256,1280]{1,0:T(8,128)(2,1)S(1)} %get-tuple-element.106), channel_id=1, source_target_pairs={{0,3},{1,0},{2,1},{3,2},{4,7},{5,4},{6,5},{7,6},{8,11},{9,8},{10,9... | collective-permute-start | bytes 1966088 | tf_op jit(solution)/shard_map/ppermute | solution.py:601
  197.1 1.8 collective-permute-start.61
  198.8 3.3 %collective-permute-done.61.refs_6_ = f32[2,160,128]{2,1,0:T(8,128)S(1)} collective-permute-done((f32[2,160,128]{2,1,0:T(8,128)S(1)}, f32[2,160,128]{2,1,0:T(8,128)S(1)}, u32[]{:S(2)}, u32[]{:S(2)}) %collective-permute-start.61) | collective-permute-done | bytes 163872 | tf_op jit(solution)/shard_map/ppermute | solution.py:601
  202.1 1.7 collective-permute-start.62
  203.8 4.0 %collective-permute-done.62.refs_7_ = f32[2,160,128]{2,1,0:T(8,128)S(1)} collective-permute-done((f32[2,160,128]{2,1,0:T(8,128)S(1)}, f32[2,160,128]{2,1,0:T(8,128)S(1)}, u32[]{:S(2)}, u32[]{:S(2)}) %collective-permute-start.62) | collective-permute-done | bytes 163872 | tf_op jit(solution)/shard_map/ppermute | solution.py:601
  207.9 2.8 %collective-permute-start.63 = (f32[160,256]{1,0:T(8,128)S(1)}, f32[160,256]{1,0:T(8,128)S(1)}, u32[]{:S(2)}, u32[]{:S(2)}) collective-permute-start(f32[160,256]{1,0:T(8,128)S(1)} %get-tuple-element.126), channel_id=1, source_target_pairs={{0,4},{4,0},{8,12},{12,8},{16,20},{20,16},{24,28},{28,24},{32,36},... | collective-permute-start | bytes 491528 | tf_op jit(solution)/shard_map/ppermute | solution.py:601
  210.7 1.7 join_rows.1
  212.4 1.3 join_weights.1
  213.6 10.2 %collective-permute-done.43.c = bf16[256,1280]{1,0:T(8,128)(2,1)S(1)} collective-permute-done((bf16[256,1280]{1,0:T(8,128)(2,1)S(1)}, bf16[256,1280]{1,0:T(8,128)(2,1)S(1)}, u32[]{:S(2)}, u32[]{:S(2)}) %collective-permute-start.43) | collective-permute-done | bytes 655392 | tf_op jit(solution)/shard_map/ppermute | solution.py:601
  223.9 1.8 collective-permute-done.44.d
  225.7 1.2 add_partials.1
  (106 shorter events, 17.7 us)
Async XLA Ops:
  2.5 12.8 %collective-permute-start.1 = (bf16[256,640]{1,0:T(8,128)(2,1)}, bf16[256,640]{1,0:T(8,128)(2,1)}, u32[]{:S(2)}, u32[]{:S(2)}) collective-permute-start(bf16[256,640]{1,0:T(8,128)(2,1)} %constant_dynamic-slice_fusion.1), channel_id=1, source_target_pairs={{0,4},{4,0},{8,12},{12,8},{16,20},{20,16},{24,28},{28,24},{32,36},... | collective-permute-start | bytes 983048 | tf_op jit(solution)/shard_map/ppermute | solution.py:601
  5.6 9.7 %collective-permute-start.2 = (bf16[256,640]{1,0:T(8,128)(2,1)}, bf16[256,640]{1,0:T(8,128)(2,1)}, u32[]{:S(2)}, u32[]{:S(2)}) collective-permute-start(bf16[256,640]{1,0:T(8,128)(2,1)} %constant_dynamic-slice_fusion), channel_id=1, source_target_pairs={{0,4},{4,0},{8,12},{12,8},{16,20},{20,16},{24,28},{28,24},{32,36},... | collective-permute-start | bytes 983048 | tf_op jit(solution)/shard_map/ppermute | solution.py:601
  5.7 18.6 %collective-permute-start = (bf16[256,1280]{1,0:T(8,128)(2,1)}, bf16[256,1280]{1,0:T(8,128)(2,1)}, u32[]{:S(2)}, u32[]{:S(2)}) collective-permute-start(bf16[256,1280]{1,0:T(8,128)(2,1)} %refs_0_.1), channel_id=1, source_target_pairs={{0,4},{4,0},{8,12},{12,8},{16,20},{20,16},{24,28},{28,24},{32,36},... | collective-permute-start | bytes 1966088 | tf_op jit(solution)/shard_map/ppermute | solution.py:601
  8.1 12.3 %collective-permute-start.3 = (bf16[128,1280]{1,0:T(8,128)(2,1)}, bf16[128,1280]{1,0:T(8,128)(2,1)}, u32[]{:S(2)}, u32[]{:S(2)}) collective-permute-start(bf16[128,1280]{1,0:T(8,128)(2,1)} %get-tuple-element.72), channel_id=1, source_target_pairs={{0,1},{1,2},{2,3},{3,0},{4,5},{5,6},{6,7},{7,4},{8,9},{9,10},{10,1... | collective-permute-start | bytes 983048 | tf_op jit(solution)/shard_map/ppermute | solution.py:601
  9.9 10.5 %collective-permute-start.5 = (bf16[128,1280]{1,0:T(8,128)(2,1)}, bf16[128,1280]{1,0:T(8,128)(2,1)}, u32[]{:S(2)}, u32[]{:S(2)}) collective-permute-start(bf16[128,1280]{1,0:T(8,128)(2,1)} %get-tuple-element.73), channel_id=1, source_target_pairs={{0,3},{1,0},{2,1},{3,2},{4,7},{5,4},{6,5},{7,6},{8,11},{9,8},{10,9... | collective-permute-start | bytes 983048 | tf_op jit(solution)/shard_map/ppermute | solution.py:601
  15.4 11.9 %collective-permute-start.7 = (bf16[128,1280]{1,0:T(8,128)(2,1)}, bf16[128,1280]{1,0:T(8,128)(2,1)S(1)}, u32[]{:S(2)}, u32[]{:S(2)}) collective-permute-start(bf16[128,1280]{1,0:T(8,128)(2,1)} %get-tuple-element.73), channel_id=1, source_target_pairs={{0,1},{1,2},{2,3},{3,0},{4,5},{5,6},{6,7},{7,4},{8,9},{9,10},{10,1... | collective-permute-start | bytes 983048 | tf_op jit(solution)/shard_map/ppermute | solution.py:601
  15.4 11.9 %collective-permute-start.8 = (bf16[128,1280]{1,0:T(8,128)(2,1)}, bf16[128,1280]{1,0:T(8,128)(2,1)S(1)}, u32[]{:S(2)}, u32[]{:S(2)}) collective-permute-start(bf16[128,1280]{1,0:T(8,128)(2,1)} %get-tuple-element.72), channel_id=1, source_target_pairs={{0,3},{1,0},{2,1},{3,2},{4,7},{5,4},{6,5},{7,6},{8,11},{9,8},{10,9... | collective-permute-start | bytes 983048 | tf_op jit(solution)/shard_map/ppermute | solution.py:601
  20.4 13.9 %collective-permute-start.4 = (bf16[128,1280]{1,0:T(8,128)(2,1)}, bf16[128,1280]{1,0:T(8,128)(2,1)S(1)}, u32[]{:S(2)}, u32[]{:S(2)}) collective-permute-start(bf16[128,1280]{1,0:T(8,128)(2,1)} %collective-permute-done.3.bt.refs_1_), channel_id=1, source_target_pairs={{0,1},{1,2},{2,3},{3,0},{4,5},{5,6},{6,7},{7,4},{8,9},{9,10},{10,1... | collective-permute-start | bytes 983048 | tf_op jit(solution)/shard_map/ppermute | solution.py:601
  20.4 13.9 %collective-permute-start.6 = (bf16[128,1280]{1,0:T(8,128)(2,1)}, bf16[128,1280]{1,0:T(8,128)(2,1)S(1)}, u32[]{:S(2)}, u32[]{:S(2)}) collective-permute-start(bf16[128,1280]{1,0:T(8,128)(2,1)} %collective-permute-done.5.cl.refs_4_), channel_id=1, source_target_pairs={{0,3},{1,0},{2,1},{3,2},{4,7},{5,4},{6,5},{7,6},{8,11},{9,8},{10,9... | collective-permute-start | bytes 983048 | tf_op jit(solution)/shard_map/ppermute | solution.py:601
  35.5 5.4 %collective-permute-start.10 = (bf16[256,256]{1,0:T(8,128)(2,1)S(1)}, bf16[256,256]{1,0:T(8,128)(2,1)S(1)}, u32[]{:S(2)}, u32[]{:S(2)}) collective-permute-start(bf16[256,256]{1,0:T(8,128)(2,1)S(1)} %get-tuple-element.77.a), channel_id=1, source_target_pairs={{0,24},{4,28},{8,0},{12,4},{16,8},{20,12},{24,16},{28,20},{32,56},... | collective-permute-start | bytes 393224 | tf_op jit(solution)/shard_map/ppermute | solution.py:601
  38.0 5.7 %collective-permute-start.11 = (bf16[256,256]{1,0:T(8,128)(2,1)S(1)}, bf16[256,256]{1,0:T(8,128)(2,1)S(1)}, u32[]{:S(2)}, u32[]{:S(2)}) collective-permute-start(bf16[256,256]{1,0:T(8,128)(2,1)S(1)} %get-tuple-element.77.a), channel_id=1, source_target_pairs={{0,16},{4,20},{8,24},{12,28},{16,0},{20,4},{24,8},{28,12},{32,48},... | collective-permute-start | bytes 393224 | tf_op jit(solution)/shard_map/ppermute | solution.py:601
  38.5 9.1 %collective-permute-start.9 = (bf16[256,256]{1,0:T(8,128)(2,1)S(1)}, bf16[256,256]{1,0:T(8,128)(2,1)S(1)}, u32[]{:S(2)}, u32[]{:S(2)}) collective-permute-start(bf16[256,256]{1,0:T(8,128)(2,1)S(1)} %get-tuple-element.77.a), channel_id=1, source_target_pairs={{0,8},{4,12},{8,16},{12,20},{16,24},{20,28},{24,0},{28,4},{32,40},... | collective-permute-start | bytes 393224 | tf_op jit(solution)/shard_map/ppermute | solution.py:601
  39.1 11.5 %collective-permute-start.18 = (bf16[256,256]{1,0:T(8,128)(2,1)S(1)}, bf16[256,256]{1,0:T(8,128)(2,1)S(1)}, u32[]{:S(2)}, u32[]{:S(2)}) collective-permute-start(bf16[256,256]{1,0:T(8,128)(2,1)S(1)} %get-tuple-element.80), channel_id=1, source_target_pairs={{0,4},{4,0},{8,12},{12,8},{16,20},{20,16},{24,28},{28,24},{32,36},... | collective-permute-start | bytes 393224 | tf_op jit(solution)/shard_map/ppermute | solution.py:601
  47.7 15.6 %collective-permute-start.12 = (bf16[4,128,256]{2,1,0:T(8,128)(2,1)S(1)}, bf16[4,128,256]{2,1,0:T(8,128)(2,1)S(1)}, u32[]{:S(2)}, u32[]{:S(2)}) collective-permute-start(bf16[4,128,256]{2,1,0:T(8,128)(2,1)S(1)} %get-tuple-element.78.refs_0_), channel_id=1, source_target_pairs={{0,32},{4,36},{8,40},{12,44},{16,48},{20,52},{24,56},{28,60},{32,6... | collective-permute-start | bytes 786440 | tf_op jit(solution)/shard_map/ppermute | solution.py:601
  49.1 16.9 %collective-permute-start.15 = (bf16[4,128,256]{2,1,0:T(8,128)(2,1)S(1)}, bf16[4,128,256]{2,1,0:T(8,128)(2,1)S(1)}, u32[]{:S(2)}, u32[]{:S(2)}) collective-permute-start(bf16[4,128,256]{2,1,0:T(8,128)(2,1)S(1)} %get-tuple-element.79.refs_1_), channel_id=1, source_target_pairs={{0,96},{4,100},{8,104},{12,108},{16,112},{20,116},{24,120},{28,124... | collective-permute-start | bytes 786440 | tf_op jit(solution)/shard_map/ppermute | solution.py:601
  50.6 8.6 %collective-permute-start.19 = (bf16[256,256]{1,0:T(8,128)(2,1)S(1)}, bf16[256,256]{1,0:T(8,128)(2,1)S(1)}, u32[]{:S(2)}, u32[]{:S(2)}) collective-permute-start(bf16[256,256]{1,0:T(8,128)(2,1)S(1)} %collective-permute-done.18.a), channel_id=1, source_target_pairs={{0,32},{4,36},{8,40},{12,44},{16,48},{20,52},{24,56},{28,60},{32,6... | collective-permute-start | bytes 393224 | tf_op jit(solution)/shard_map/ppermute | solution.py:601
  50.6 8.6 %collective-permute-start.20 = (bf16[256,256]{1,0:T(8,128)(2,1)S(1)}, bf16[256,256]{1,0:T(8,128)(2,1)S(1)}, u32[]{:S(2)}, u32[]{:S(2)}) collective-permute-start(bf16[256,256]{1,0:T(8,128)(2,1)S(1)} %collective-permute-done.18.a), channel_id=1, source_target_pairs={{0,96},{4,100},{8,104},{12,108},{16,112},{20,116},{24,120},{28,124... | collective-permute-start | bytes 393224 | tf_op jit(solution)/shard_map/ppermute | solution.py:601
  53.3 9.9 %collective-permute-start.21 = (bf16[256,256]{1,0:T(8,128)(2,1)S(1)}, bf16[256,256]{1,0:T(8,128)(2,1)S(1)}, u32[]{:S(2)}, u32[]{:S(2)}) collective-permute-start(bf16[256,256]{1,0:T(8,128)(2,1)S(1)} %collective-permute-done.18.a), channel_id=1, source_target_pairs={{0,64},{4,68},{8,72},{12,76},{16,80},{20,84},{24,88},{28,92},{32,9... | collective-permute-start | bytes 393224 | tf_op jit(solution)/shard_map/ppermute | solution.py:601
  59.2 9.7 %collective-permute-start.13 = (bf16[4,128,256]{2,1,0:T(8,128)(2,1)S(1)}, bf16[4,128,256]{2,1,0:T(8,128)(2,1)S(1)}, u32[]{:S(2)}, u32[]{:S(2)}) collective-permute-start(bf16[4,128,256]{2,1,0:T(8,128)(2,1)S(1)} %get-tuple-element.79.refs_1_), channel_id=1, source_target_pairs={{0,32},{4,36},{8,40},{12,44},{16,48},{20,52},{24,56},{28,60},{32,6... | collective-permute-start | bytes 786440 | tf_op jit(solution)/shard_map/ppermute | solution.py:601
  59.2 9.7 %collective-permute-start.14 = (bf16[4,128,256]{2,1,0:T(8,128)(2,1)S(1)}, bf16[4,128,256]{2,1,0:T(8,128)(2,1)S(1)}, u32[]{:S(2)}, u32[]{:S(2)}) collective-permute-start(bf16[4,128,256]{2,1,0:T(8,128)(2,1)S(1)} %get-tuple-element.78.refs_0_), channel_id=1, source_target_pairs={{0,96},{4,100},{8,104},{12,108},{16,112},{20,116},{24,120},{28,124... | collective-permute-start | bytes 786440 | tf_op jit(solution)/shard_map/ppermute | solution.py:601
  63.2 6.6 %collective-permute-start.22 = (bf16[4,128,256]{2,1,0:T(8,128)(2,1)S(1)}, bf16[4,128,256]{2,1,0:T(8,128)(2,1)S(1)}, u32[]{:S(2)}, u32[]{:S(2)}) collective-permute-start(bf16[4,128,256]{2,1,0:T(8,128)(2,1)S(1)} %get-tuple-element.81.refs_8_), channel_id=1, source_target_pairs={{0,8},{4,12},{8,16},{12,20},{16,24},{20,28},{24,0},{28,4},{32,40},... | collective-permute-start | bytes 786440 | tf_op jit(solution)/shard_map/ppermute | solution.py:601
  63.3 8.3 %collective-permute-start.25 = (bf16[4,128,256]{2,1,0:T(8,128)(2,1)S(1)}, bf16[4,128,256]{2,1,0:T(8,128)(2,1)S(1)}, u32[]{:S(2)}, u32[]{:S(2)}) collective-permute-start(bf16[4,128,256]{2,1,0:T(8,128)(2,1)S(1)} %get-tuple-element.82.refs_9_), channel_id=1, source_target_pairs={{0,24},{4,28},{8,0},{12,4},{16,8},{20,12},{24,16},{28,20},{32,56},... | collective-permute-start | bytes 786440 | tf_op jit(solution)/shard_map/ppermute | solution.py:601
  65.9 9.5 %collective-permute-start.23 = (bf16[4,128,256]{2,1,0:T(8,128)(2,1)S(1)}, bf16[4,128,256]{2,1,0:T(8,128)(2,1)S(1)}, u32[]{:S(2)}, u32[]{:S(2)}) collective-permute-start(bf16[4,128,256]{2,1,0:T(8,128)(2,1)S(1)} %get-tuple-element.82.refs_9_), channel_id=1, source_target_pairs={{0,8},{4,12},{8,16},{12,20},{16,24},{20,28},{24,0},{28,4},{32,40},... | collective-permute-start | bytes 786440 | tf_op jit(solution)/shard_map/ppermute | solution.py:601
  68.9 7.1 %collective-permute-start.24 = (bf16[4,128,256]{2,1,0:T(8,128)(2,1)S(1)}, bf16[4,128,256]{2,1,0:T(8,128)(2,1)S(1)}, u32[]{:S(2)}, u32[]{:S(2)}) collective-permute-start(bf16[4,128,256]{2,1,0:T(8,128)(2,1)S(1)} %get-tuple-element.81.refs_8_), channel_id=1, source_target_pairs={{0,24},{4,28},{8,0},{12,4},{16,8},{20,12},{24,16},{28,20},{32,56},... | collective-permute-start | bytes 786440 | tf_op jit(solution)/shard_map/ppermute | solution.py:601
  68.9 7.1 %collective-permute-start.16 = (bf16[4,128,256]{2,1,0:T(8,128)(2,1)S(1)}, bf16[4,128,256]{2,1,0:T(8,128)(2,1)S(1)}, u32[]{:S(2)}, u32[]{:S(2)}) collective-permute-start(bf16[4,128,256]{2,1,0:T(8,128)(2,1)S(1)} %collective-permute-done.12.refs_2_), channel_id=1, source_target_pairs={{0,32},{4,36},{8,40},{12,44},{16,48},{20,52},{24,56},{28,60},{32,6... | collective-permute-start | bytes 786440 | tf_op jit(solution)/shard_map/ppermute | solution.py:601
  69.8 6.2 %collective-permute-start.17 = (bf16[4,128,256]{2,1,0:T(8,128)(2,1)S(1)}, bf16[4,128,256]{2,1,0:T(8,128)(2,1)S(1)}, u32[]{:S(2)}, u32[]{:S(2)}) collective-permute-start(bf16[4,128,256]{2,1,0:T(8,128)(2,1)S(1)} %collective-permute-done.15.refs_5_), channel_id=1, source_target_pairs={{0,96},{4,100},{8,104},{12,108},{16,112},{20,116},{24,120},{28,124... | collective-permute-start | bytes 786440 | tf_op jit(solution)/shard_map/ppermute | solution.py:601
  71.6 9.5 %collective-permute-start.26 = (bf16[4,128,256]{2,1,0:T(8,128)(2,1)S(1)}, bf16[4,128,256]{2,1,0:T(8,128)(2,1)S(1)}, u32[]{:S(2)}, u32[]{:S(2)}) collective-permute-start(bf16[4,128,256]{2,1,0:T(8,128)(2,1)S(1)} %collective-permute-done.22.refs_10_), channel_id=1, source_target_pairs={{0,8},{4,12},{8,16},{12,20},{16,24},{20,28},{24,0},{28,4},{32,40},... | collective-permute-start | bytes 786440 | tf_op jit(solution)/shard_map/ppermute | solution.py:601
  75.4 5.7 %collective-permute-start.27 = (bf16[4,128,256]{2,1,0:T(8,128)(2,1)S(1)}, bf16[4,128,256]{2,1,0:T(8,128)(2,1)S(1)}, u32[]{:S(2)}, u32[]{:S(2)}) collective-permute-start(bf16[4,128,256]{2,1,0:T(8,128)(2,1)S(1)} %collective-permute-done.25.refs_13_), channel_id=1, source_target_pairs={{0,24},{4,28},{8,0},{12,4},{16,8},{20,12},{24,16},{28,20},{32,56},... | collective-permute-start | bytes 786440 | tf_op jit(solution)/shard_map/ppermute | solution.py:601
  95.8 12.5 %collective-permute-start.29 = (bf16[16,128,128]{2,1,0:T(8,128)(2,1)S(1)}, bf16[16,128,128]{2,1,0:T(8,128)(2,1)S(1)}, u32[]{:S(2)}, u32[]{:S(2)}) collective-permute-start(bf16[16,128,128]{2,1,0:T(8,128)(2,1)S(1)} %get-tuple-element.87), channel_id=1, source_target_pairs={{0,8},{4,12},{8,16},{12,20},{16,24},{20,28},{24,0},{28,4},{32,40},... | collective-permute-start | bytes 1572872 | tf_op jit(solution)/shard_map/ppermute | solution.py:601
  96.0 10.4 %collective-permute-start.45 = (bf16[128,1280]{1,0:T(8,128)(2,1)}, bf16[128,1280]{1,0:T(8,128)(2,1)S(1)}, u32[]{:S(2)}, u32[]{:S(2)}) collective-permute-start(bf16[128,1280]{1,0:T(8,128)(2,1)} %collective-permute-done.3.bt.refs_1_), channel_id=1, source_target_pairs={{0,4},{4,0},{8,12},{12,8},{16,20},{20,16},{24,28},{28,24},{32,36},... | collective-permute-start | bytes 983048 | tf_op jit(solution)/shard_map/ppermute | solution.py:601
  102.9 25.1 %collective-permute-start.30 = (bf16[16,128,128]{2,1,0:T(8,128)(2,1)S(1)}, bf16[16,128,128]{2,1,0:T(8,128)(2,1)S(1)}, u32[]{:S(2)}, u32[]{:S(2)}) collective-permute-start(bf16[16,128,128]{2,1,0:T(8,128)(2,1)S(1)} %get-tuple-element.88), channel_id=1, source_target_pairs={{0,24},{4,28},{8,0},{12,4},{16,8},{20,12},{24,16},{28,20},{32,56},... | collective-permute-start | bytes 1572872 | tf_op jit(solution)/shard_map/ppermute | solution.py:601
  105.6 23.4 %collective-permute-start.31 = (bf16[16,128,128]{2,1,0:T(8,128)(2,1)S(1)}, bf16[16,128,128]{2,1,0:T(8,128)(2,1)S(1)}, u32[]{:S(2)}, u32[]{:S(2)}) collective-permute-start(bf16[16,128,128]{2,1,0:T(8,128)(2,1)S(1)} %get-tuple-element.89), channel_id=1, source_target_pairs={{0,16},{4,20},{8,24},{12,28},{16,0},{20,4},{24,8},{28,12},{32,48},... | collective-permute-start | bytes 1572872 | tf_op jit(solution)/shard_map/ppermute | solution.py:601
  105.6 23.4 %collective-permute-start.32 = (bf16[16,128,128]{2,1,0:T(8,128)(2,1)S(1)}, bf16[16,128,128]{2,1,0:T(8,128)(2,1)S(1)}, u32[]{:S(2)}, u32[]{:S(2)}) collective-permute-start(bf16[16,128,128]{2,1,0:T(8,128)(2,1)S(1)} %get-tuple-element.91), channel_id=1, source_target_pairs={{0,32},{4,36},{8,40},{12,44},{16,48},{20,52},{24,56},{28,60},{32,6... | collective-permute-start | bytes 1572872 | tf_op jit(solution)/shard_map/ppermute | solution.py:601
  106.4 23.1 %collective-permute-start.33 = (bf16[16,128,128]{2,1,0:T(8,128)(2,1)S(1)}, bf16[16,128,128]{2,1,0:T(8,128)(2,1)S(1)}, u32[]{:S(2)}, u32[]{:S(2)}) collective-permute-start(bf16[16,128,128]{2,1,0:T(8,128)(2,1)S(1)} %get-tuple-element.92), channel_id=1, source_target_pairs={{0,96},{4,100},{8,104},{12,108},{16,112},{20,116},{24,120},{28,124... | collective-permute-start | bytes 1572872 | tf_op jit(solution)/shard_map/ppermute | solution.py:601
  108.3 21.3 %collective-permute-start.34 = (bf16[16,128,128]{2,1,0:T(8,128)(2,1)S(1)}, bf16[16,128,128]{2,1,0:T(8,128)(2,1)S(1)}, u32[]{:S(2)}, u32[]{:S(2)}) collective-permute-start(bf16[16,128,128]{2,1,0:T(8,128)(2,1)S(1)} %get-tuple-element.93), channel_id=1, source_target_pairs={{0,64},{4,68},{8,72},{12,76},{16,80},{20,84},{24,88},{28,92},{32,9... | collective-permute-start | bytes 1572872 | tf_op jit(solution)/shard_map/ppermute | solution.py:601
  128.0 7.4 %collective-permute-start.48 = (bf16[128,1280]{1,0:T(8,128)(2,1)}, bf16[128,1280]{1,0:T(8,128)(2,1)S(1)}, u32[]{:S(2)}, u32[]{:S(2)}) collective-permute-start(bf16[128,1280]{1,0:T(8,128)(2,1)} %collective-permute-done.5.cl.refs_4_), channel_id=1, source_target_pairs={{0,4},{4,0},{8,12},{12,8},{16,20},{20,16},{24,28},{28,24},{32,36},... | collective-permute-start | bytes 983048 | tf_op jit(solution)/shard_map/ppermute | solution.py:601
  129.0 6.5 %collective-permute-start.46 = (bf16[128,1280]{1,0:T(8,128)(2,1)S(1)}, bf16[128,1280]{1,0:T(8,128)(2,1)S(1)}, u32[]{:S(2)}, u32[]{:S(2)}) collective-permute-start(bf16[128,1280]{1,0:T(8,128)(2,1)S(1)} %collective-permute-done.7.bl.refs_2_), channel_id=1, source_target_pairs={{0,4},{4,0},{8,12},{12,8},{16,20},{20,16},{24,28},{28,24},{32,36},... | collective-permute-start | bytes 983048 | tf_op jit(solution)/shard_map/ppermute | solution.py:601
  129.0 9.1 %collective-permute-start.47 = (bf16[128,1280]{1,0:T(8,128)(2,1)S(1)}, bf16[128,1280]{1,0:T(8,128)(2,1)S(1)}, u32[]{:S(2)}, u32[]{:S(2)}) collective-permute-start(bf16[128,1280]{1,0:T(8,128)(2,1)S(1)} %collective-permute-done.8.ct.refs_3_), channel_id=1, source_target_pairs={{0,4},{4,0},{8,12},{12,8},{16,20},{20,16},{24,28},{28,24},{32,36},... | collective-permute-start | bytes 983048 | tf_op jit(solution)/shard_map/ppermute | solution.py:601
  129.5 8.9 %collective-permute-start.49 = (bf16[128,1280]{1,0:T(8,128)(2,1)S(1)}, bf16[128,1280]{1,0:T(8,128)(2,1)S(1)}, u32[]{:S(2)}, u32[]{:S(2)}) collective-permute-start(bf16[128,1280]{1,0:T(8,128)(2,1)S(1)} %collective-permute-done.4.a.refs_5_), channel_id=1, source_target_pairs={{0,4},{4,0},{8,12},{12,8},{16,20},{20,16},{24,28},{28,24},{32,36},... | collective-permute-start | bytes 983048 | tf_op jit(solution)/shard_map/ppermute | solution.py:601
  129.6 8.8 %collective-permute-start.50 = (bf16[128,1280]{1,0:T(8,128)(2,1)S(1)}, bf16[128,1280]{1,0:T(8,128)(2,1)S(1)}, u32[]{:S(2)}, u32[]{:S(2)}) collective-permute-start(bf16[128,1280]{1,0:T(8,128)(2,1)S(1)} %collective-permute-done.6.b.refs_6_), channel_id=1, source_target_pairs={{0,4},{4,0},{8,12},{12,8},{16,20},{20,16},{24,28},{28,24},{32,36},... | collective-permute-start | bytes 983048 | tf_op jit(solution)/shard_map/ppermute | solution.py:601
  135.4 9.1 %collective-permute-start.35 = (f32[4,128,128]{2,1,0:T(8,128)S(1)}, f32[4,128,128]{2,1,0:T(8,128)S(1)}, u32[]{:S(2)}, u32[]{:S(2)}) collective-permute-start(f32[4,128,128]{2,1,0:T(8,128)S(1)} %get-tuple-element.95), channel_id=1, source_target_pairs={{0,32},{4,36},{8,40},{12,44},{16,48},{20,52},{24,56},{28,60},{32,6... | collective-permute-start | bytes 786440 | tf_op jit(solution)/shard_map/ppermute | solution.py:601
  135.5 13.5 %collective-permute-start.36 = (f32[4,128,128]{2,1,0:T(8,128)S(1)}, f32[4,128,128]{2,1,0:T(8,128)S(1)}, u32[]{:S(2)}, u32[]{:S(2)}) collective-permute-start(f32[4,128,128]{2,1,0:T(8,128)S(1)} %get-tuple-element.96), channel_id=1, source_target_pairs={{0,96},{4,100},{8,104},{12,108},{16,112},{20,116},{24,120},{28,124... | collective-permute-start | bytes 786440 | tf_op jit(solution)/shard_map/ppermute | solution.py:601
  138.2 12.2 %collective-permute-start.37 = (f32[4,128,128]{2,1,0:T(8,128)S(1)}, f32[4,128,128]{2,1,0:T(8,128)S(1)}, u32[]{:S(2)}, u32[]{:S(2)}) collective-permute-start(f32[4,128,128]{2,1,0:T(8,128)S(1)} %get-tuple-element.97), channel_id=1, source_target_pairs={{0,64},{4,68},{8,72},{12,76},{16,80},{20,84},{24,88},{28,92},{32,9... | collective-permute-start | bytes 786440 | tf_op jit(solution)/shard_map/ppermute | solution.py:601
  138.4 11.9 %collective-permute-start.38 = (f32[4,128,128]{2,1,0:T(8,128)S(1)}, f32[4,128,128]{2,1,0:T(8,128)S(1)}, u32[]{:S(2)}, u32[]{:S(2)}) collective-permute-start(f32[4,128,128]{2,1,0:T(8,128)S(1)} %get-tuple-element.99), channel_id=1, source_target_pairs={{0,8},{4,12},{8,16},{12,20},{16,24},{20,28},{24,0},{28,4},{32,40},... | collective-permute-start | bytes 786440 | tf_op jit(solution)/shard_map/ppermute | solution.py:601
  138.5 11.9 %collective-permute-start.39 = (f32[4,128,128]{2,1,0:T(8,128)S(1)}, f32[4,128,128]{2,1,0:T(8,128)S(1)}, u32[]{:S(2)}, u32[]{:S(2)}) collective-permute-start(f32[4,128,128]{2,1,0:T(8,128)S(1)} %get-tuple-element.100), channel_id=1, source_target_pairs={{0,24},{4,28},{8,0},{12,4},{16,8},{20,12},{24,16},{28,20},{32,56},... | collective-permute-start | bytes 786440 | tf_op jit(solution)/shard_map/ppermute | solution.py:601
  144.6 8.2 %collective-permute-start.40 = (f32[4,128,128]{2,1,0:T(8,128)S(1)}, f32[4,128,128]{2,1,0:T(8,128)S(1)}, u32[]{:S(2)}, u32[]{:S(2)}) collective-permute-start(f32[4,128,128]{2,1,0:T(8,128)S(1)} %get-tuple-element.101), channel_id=1, source_target_pairs={{0,16},{4,20},{8,24},{12,28},{16,0},{20,4},{24,8},{28,12},{32,48},... | collective-permute-start | bytes 786440 | tf_op jit(solution)/shard_map/ppermute | solution.py:601
  155.5 8.6 %collective-permute-start.51 = (bf16[8,160,128]{2,1,0:T(8,128)(2,1)S(1)}, bf16[8,160,128]{2,1,0:T(8,128)(2,1)S(1)}, u32[]{:S(2)}, u32[]{:S(2)}) collective-permute-start(bf16[8,160,128]{2,1,0:T(8,128)(2,1)S(1)} %get-tuple-element.110), channel_id=1, source_target_pairs={{0,8},{4,12},{8,16},{12,20},{16,24},{20,28},{24,0},{28,4},{32,40},... | collective-permute-start | bytes 983048 | tf_op jit(solution)/shard_map/ppermute | solution.py:601
  156.0 12.2 %collective-permute-start.52 = (bf16[8,160,128]{2,1,0:T(8,128)(2,1)S(1)}, bf16[8,160,128]{2,1,0:T(8,128)(2,1)S(1)}, u32[]{:S(2)}, u32[]{:S(2)}) collective-permute-start(bf16[8,160,128]{2,1,0:T(8,128)(2,1)S(1)} %get-tuple-element.111), channel_id=1, source_target_pairs={{0,24},{4,28},{8,0},{12,4},{16,8},{20,12},{24,16},{28,20},{32,56},... | collective-permute-start | bytes 983048 | tf_op jit(solution)/shard_map/ppermute | solution.py:601
  158.3 13.8 %collective-permute-start.53 = (bf16[8,160,128]{2,1,0:T(8,128)(2,1)S(1)}, bf16[8,160,128]{2,1,0:T(8,128)(2,1)S(1)}, u32[]{:S(2)}, u32[]{:S(2)}) collective-permute-start(bf16[8,160,128]{2,1,0:T(8,128)(2,1)S(1)} %get-tuple-element.112), channel_id=1, source_target_pairs={{0,16},{4,20},{8,24},{12,28},{16,0},{20,4},{24,8},{28,12},{32,48},... | collective-permute-start | bytes 983048 | tf_op jit(solution)/shard_map/ppermute | solution.py:601
  159.0 13.1 %collective-permute-start.54 = (bf16[8,160,128]{2,1,0:T(8,128)(2,1)S(1)}, bf16[8,160,128]{2,1,0:T(8,128)(2,1)S(1)}, u32[]{:S(2)}, u32[]{:S(2)}) collective-permute-start(bf16[8,160,128]{2,1,0:T(8,128)(2,1)S(1)} %get-tuple-element.114), channel_id=1, source_target_pairs={{0,32},{4,36},{8,40},{12,44},{16,48},{20,52},{24,56},{28,60},{32,6... | collective-permute-start | bytes 983048 | tf_op jit(solution)/shard_map/ppermute | solution.py:601
  159.0 13.1 %collective-permute-start.55 = (bf16[8,160,128]{2,1,0:T(8,128)(2,1)S(1)}, bf16[8,160,128]{2,1,0:T(8,128)(2,1)S(1)}, u32[]{:S(2)}, u32[]{:S(2)}) collective-permute-start(bf16[8,160,128]{2,1,0:T(8,128)(2,1)S(1)} %get-tuple-element.115), channel_id=1, source_target_pairs={{0,96},{4,100},{8,104},{12,108},{16,112},{20,116},{24,120},{28,124... | collective-permute-start | bytes 983048 | tf_op jit(solution)/shard_map/ppermute | solution.py:601
  164.1 8.9 %collective-permute-start.56 = (bf16[8,160,128]{2,1,0:T(8,128)(2,1)S(1)}, bf16[8,160,128]{2,1,0:T(8,128)(2,1)S(1)}, u32[]{:S(2)}, u32[]{:S(2)}) collective-permute-start(bf16[8,160,128]{2,1,0:T(8,128)(2,1)S(1)} %get-tuple-element.116), channel_id=1, source_target_pairs={{0,64},{4,68},{8,72},{12,76},{16,80},{20,84},{24,88},{28,92},{32,9... | collective-permute-start | bytes 983048 | tf_op jit(solution)/shard_map/ppermute | solution.py:601
  173.3 20.3 %collective-permute-start.57 = (f32[2,160,128]{2,1,0:T(8,128)S(1)}, f32[2,160,128]{2,1,0:T(8,128)S(1)}, u32[]{:S(2)}, u32[]{:S(2)}) collective-permute-start(f32[2,160,128]{2,1,0:T(8,128)S(1)} %get-tuple-element.118), channel_id=1, source_target_pairs={{0,32},{4,36},{8,40},{12,44},{16,48},{20,52},{24,56},{28,60},{32,6... | collective-permute-start | bytes 491528 | tf_op jit(solution)/shard_map/ppermute | solution.py:601
  174.2 19.5 %collective-permute-start.58 = (f32[2,160,128]{2,1,0:T(8,128)S(1)}, f32[2,160,128]{2,1,0:T(8,128)S(1)}, u32[]{:S(2)}, u32[]{:S(2)}) collective-permute-start(f32[2,160,128]{2,1,0:T(8,128)S(1)} %get-tuple-element.119), channel_id=1, source_target_pairs={{0,96},{4,100},{8,104},{12,108},{16,112},{20,116},{24,120},{28,124... | collective-permute-start | bytes 491528 | tf_op jit(solution)/shard_map/ppermute | solution.py:601
  176.4 19.9 %collective-permute-start.59 = (f32[2,160,128]{2,1,0:T(8,128)S(1)}, f32[2,160,128]{2,1,0:T(8,128)S(1)}, u32[]{:S(2)}, u32[]{:S(2)}) collective-permute-start(f32[2,160,128]{2,1,0:T(8,128)S(1)} %get-tuple-element.120), channel_id=1, source_target_pairs={{0,64},{4,68},{8,72},{12,76},{16,80},{20,84},{24,88},{28,92},{32,9... | collective-permute-start | bytes 491528 | tf_op jit(solution)/shard_map/ppermute | solution.py:601
  177.6 12.6 %collective-permute-start.41 = (bf16[256,256]{1,0:T(8,128)(2,1)S(1)}, bf16[256,256]{1,0:T(8,128)(2,1)S(1)}, u32[]{:S(2)}, u32[]{:S(2)}) collective-permute-start(bf16[256,256]{1,0:T(8,128)(2,1)S(1)} %get-tuple-element.103), channel_id=1, source_target_pairs={{0,4},{4,0},{8,12},{12,8},{16,20},{20,16},{24,28},{28,24},{32,36},... | collective-permute-start | bytes 393224 | tf_op jit(solution)/shard_map/ppermute | solution.py:601
  189.2 7.9 %collective-permute-start.60 = (f32[2,160,128]{2,1,0:T(8,128)S(1)}, f32[2,160,128]{2,1,0:T(8,128)S(1)}, u32[]{:S(2)}, u32[]{:S(2)}) collective-permute-start(f32[2,160,128]{2,1,0:T(8,128)S(1)} %get-tuple-element.122), channel_id=1, source_target_pairs={{0,8},{4,12},{8,16},{12,20},{16,24},{20,28},{24,0},{28,4},{32,40},... | collective-permute-start | bytes 491528 | tf_op jit(solution)/shard_map/ppermute | solution.py:601
  190.2 20.5 %collective-permute-start.28 = (bf16[256,1280]{1,0:T(8,128)(2,1)S(1)}, bf16[256,1280]{1,0:T(8,128)(2,1)S(1)}, u32[]{:S(2)}, u32[]{:S(2)}) collective-permute-start(bf16[256,1280]{1,0:T(8,128)(2,1)S(1)} %slice.3), channel_id=1, source_target_pairs={{0,4},{4,0},{8,12},{12,8},{16,20},{20,16},{24,28},{28,24},{32,36},... | collective-permute-start | bytes 1966088 | tf_op jit(solution)/shard_map/ppermute | solution.py:601
  193.6 20.1 %collective-permute-start.42 = (bf16[256,1280]{1,0:T(8,128)(2,1)S(1)}, bf16[256,1280]{1,0:T(8,128)(2,1)S(1)}, u32[]{:S(2)}, u32[]{:S(2)}) collective-permute-start(bf16[256,1280]{1,0:T(8,128)(2,1)S(1)} %get-tuple-element.105), channel_id=1, source_target_pairs={{0,1},{1,2},{2,3},{3,0},{4,5},{5,6},{6,7},{7,4},{8,9},{9,10},{10,1... | collective-permute-start | bytes 1966088 | tf_op jit(solution)/shard_map/ppermute | solution.py:601
  193.7 30.2 %collective-permute-start.43 = (bf16[256,1280]{1,0:T(8,128)(2,1)S(1)}, bf16[256,1280]{1,0:T(8,128)(2,1)S(1)}, u32[]{:S(2)}, u32[]{:S(2)}) collective-permute-start(bf16[256,1280]{1,0:T(8,128)(2,1)S(1)} %get-tuple-element.106), channel_id=1, source_target_pairs={{0,3},{1,0},{2,1},{3,2},{4,7},{5,4},{6,5},{7,6},{8,11},{9,8},{10,9... | collective-permute-start | bytes 1966088 | tf_op jit(solution)/shard_map/ppermute | solution.py:601
  196.3 29.4 %collective-permute-start.44 = (bf16[256,1280]{1,0:T(8,128)(2,1)S(1)}, bf16[256,1280]{1,0:T(8,128)(2,1)S(1)}, u32[]{:S(2)}, u32[]{:S(2)}) collective-permute-start(bf16[256,1280]{1,0:T(8,128)(2,1)S(1)} %get-tuple-element.107), channel_id=1, source_target_pairs={{0,2},{1,3},{2,0},{3,1},{4,6},{5,7},{6,4},{7,5},{8,10},{9,11},{10,... | collective-permute-start | bytes 1966088 | tf_op jit(solution)/shard_map/ppermute | solution.py:601
  197.1 5.0 %collective-permute-start.61 = (f32[2,160,128]{2,1,0:T(8,128)S(1)}, f32[2,160,128]{2,1,0:T(8,128)S(1)}, u32[]{:S(2)}, u32[]{:S(2)}) collective-permute-start(f32[2,160,128]{2,1,0:T(8,128)S(1)} %get-tuple-element.123), channel_id=1, source_target_pairs={{0,24},{4,28},{8,0},{12,4},{16,8},{20,12},{24,16},{28,20},{32,56},... | collective-permute-start | bytes 491528 | tf_op jit(solution)/shard_map/ppermute | solution.py:601
  202.1 5.7 %collective-permute-start.62 = (f32[2,160,128]{2,1,0:T(8,128)S(1)}, f32[2,160,128]{2,1,0:T(8,128)S(1)}, u32[]{:S(2)}, u32[]{:S(2)}) collective-permute-start(f32[2,160,128]{2,1,0:T(8,128)S(1)} %get-tuple-element.124), channel_id=1, source_target_pairs={{0,16},{4,20},{8,24},{12,28},{16,0},{20,4},{24,8},{28,12},{32,48},... | collective-permute-start | bytes 491528 | tf_op jit(solution)/shard_map/ppermute | solution.py:601
  207.9 4.5 %collective-permute-start.63 = (f32[160,256]{1,0:T(8,128)S(1)}, f32[160,256]{1,0:T(8,128)S(1)}, u32[]{:S(2)}, u32[]{:S(2)}) collective-permute-start(f32[160,256]{1,0:T(8,128)S(1)} %get-tuple-element.126), channel_id=1, source_target_pairs={{0,4},{4,0},{8,12},{12,8},{16,20},{20,16},{24,28},{28,24},{32,36},... | collective-permute-start | bytes 491528 | tf_op jit(solution)/shard_map/ppermute | solution.py:601
  (8 other events, 178.8 us)

commit v6 on v5

--- a/solution.py
+++ b/solution.py
@@ -435,7 +435,7 @@
         ),
         out_shape=[jax.ShapeDtypeStruct((4 * BLOCK, 2 * width), BF)]
         + [jax.ShapeDtypeStruct(s, d) for s, d in grads + grads],
-        compiler_params=pltpu.CompilerParams(vmem_limit_bytes=36 * 1024 * 1024),
+        compiler_params=params(36),
         name="attend",
     )(table, queries, query_peer, upstream, upstream_peer, *pieces)
 
@@ -599,13 +599,6 @@
 
 def mover(axis, pairs):
     return lambda value: lax.ppermute(value, axis, pairs)
-
-
-def spread(value, ahead, behind, across):
-    far = across(value)
-    back = ahead(value)
-    forth = behind(value)
-    return [value, back, forth, far]
 
 
 def ring_gather(first, second, ahead, behind):
@@ -681,8 +674,8 @@
         place, far_top, far_low, key_weight, value_weight, key_sum, value_sum, cosine, sine
     )
     other = swap(send)
-    mine_line = pack(*spread(keep, xn, xb, x2))
-    other_line = pack(*spread(other, yn, yb, y2))
+    mine_line = pack(keep, xn(keep), xb(keep), x2(keep))
+    other_line = pack(other, yn(other), yb(other), y2(other))
     pieces = ring_gather(*mine_line, yn, yb) + ring_gather(*other_line, xn, xb)
 
     near_features = [left_top, left_low, right_top, right_low, far_top, far_low]
@@ -698,6 +691,7 @@
     t_last = send_all(sums[:4], yn, yb, y2) + send_all(sums[4:], xn, xb, x2)
     grads, grads_away = finish_grads(t_last, cosine, sine)
     grads_other = swap(grads_away)
+    grads, grads_other = lax.optimization_barrier((grads, grads_other))
 
     out_other = swap(out[local_rows:])
 

time: 227 us -> 226 us (level)
  waiting for transfers between devices: 88.4 us -> 75.2 us
  starting transfers between devices: 93.6 us -> 106 us
    ppermute x64, waiting for transfers between devices: 88.4 us -> 75.2 us  [mover(): return lambda value: lax.ppermute(value, axis, pairs)]
    ppermute x64, starting transfers between devices: 93.6 us -> 106 us  [mover(): return lambda value: lax.ppermute(value, axis, pairs)]
  transfers between devices with their start and end apart: 64 -> 64, of which waited for: 26 -> 24; matrix products, arithmetic and copies ran while one was open for 1% -> 1% of each run, Pallas kernels for 7% -> 7%
where the time goes in v6:
time: 226 us
  starting transfers between devices  106 us (47%)
  waiting for transfers between devices  75.2 us (33%)
  Pallas kernels  35.4 us (16%)
  local copies, waits for them, and re-layouts  7.15 us (3%)
    ppermute x64, starting transfers between devices, mover(): return lambda value: lax.ppermute(value, axis, pairs)  106 us
    ppermute x64, waiting for transfers between devices, mover(): return lambda value: lax.ppermute(value, axis, pairs)  75.2 us
    pallas_call x1, Pallas kernels, attend(): pl.pallas_call(body, grid_spec=pltpu.PrefetchScalarGridSpec(num_scalar_pr...  14.6 us
  transfers between devices with their start and end apart: 64, of which 24 were waited for; matrix products, arithmetic and copies ran while one was open for 1% of the time, Pallas kernels for 7%

profile of v6, /device:TPU:1, one launch (start us, length us, event | category | flops | bytes accessed | tf_op | source)
XLA Modules:
  0.0 226.0 jit_solution(13752011760263026864)
XLA Ops:
  0.7 1.9 constant_dynamic-slice_fusion.1
  2.5 1.4 collective-permute-start.1
  3.9 1.7 constant_dynamic-slice_fusion
  8.1 1.7 collective-permute-start.3
  9.9 2.1 collective-permute-start.5
  12.7 2.5 %device_tables.1 = (s32[115]{0:T(128)S(1)}, s32[17]{0:T(128)S(1)}, s32[4]{0:T(128)S(1)}) custom-call(s32[64]{0:T(128)S(1)} %copy-done.7, s32[4]{0:T(128)S(1)} %pad_add_fusion.where), custom_call_target="tpu_custom_call" | custom-call | tf_op jit(solution)/shard_map/device_tables/pallas_call | solution.py:89
  15.4 2.7 %collective-permute-start.8 = (bf16[128,1280]{1,0:T(8,128)(2,1)}, bf16[128,1280]{1,0:T(8,128)(2,1)S(1)}, u32[]{:S(2)}, u32[]{:S(2)}) collective-permute-start(bf16[128,1280]{1,0:T(8,128)(2,1)} %get-tuple-element.74), channel_id=1, source_target_pairs={{0,3},{1,0},{2,1},{3,2},{4,7},{5,4},{6,5},{7,6},{8,11},{9,8},{10,9... | collective-permute-start | bytes 983048 | tf_op jit(solution)/shard_map/ppermute | solution.py:601
  18.1 2.3 %collective-permute-done.3.bt.refs_1_ = bf16[128,1280]{1,0:T(8,128)(2,1)} collective-permute-done((bf16[128,1280]{1,0:T(8,128)(2,1)}, bf16[128,1280]{1,0:T(8,128)(2,1)}, u32[]{:S(2)}, u32[]{:S(2)}) %collective-permute-start.3) | collective-permute-done | bytes 327712 | tf_op jit(solution)/shard_map/ppermute | solution.py:601
  20.4 2.7 %collective-permute-start.6 = (bf16[128,1280]{1,0:T(8,128)(2,1)}, bf16[128,1280]{1,0:T(8,128)(2,1)S(1)}, u32[]{:S(2)}, u32[]{:S(2)}) collective-permute-start(bf16[128,1280]{1,0:T(8,128)(2,1)} %collective-permute-done.5.cl.refs_4_), channel_id=1, source_target_pairs={{0,3},{1,0},{2,1},{3,2},{4,7},{5,4},{6,5},{7,6},{8,11},{9,8},{10,9... | collective-permute-start | bytes 983048 | tf_op jit(solution)/shard_map/ppermute | solution.py:601
  24.3 3.0 %collective-permute-done.7.bl.refs_2_ = bf16[128,1280]{1,0:T(8,128)(2,1)S(1)} collective-permute-done((bf16[128,1280]{1,0:T(8,128)(2,1)}, bf16[128,1280]{1,0:T(8,128)(2,1)S(1)}, u32[]{:S(2)}, u32[]{:S(2)}) %collective-permute-start.7) | collective-permute-done | bytes 327712 | tf_op jit(solution)/shard_map/ppermute | solution.py:601
  27.3 1.7 copy-done.1
  29.1 2.8 %project_near.1 = (f32[256,256]{1,0:T(8,128)S(1)}, f32[256,256]{1,0:T(8,128)S(1)}) custom-call(s32[17]{0:T(128)S(1)} %get-tuple-element.70.place_ref.p, bf16[256,1280]{1,0:T(8,128)(2,1)S(1)} %copy-done.4, bf16[128,1280]{1,0:T(8,128)(2,1)} %collective-permute-done.3.bt.refs_1_, bf16[128,1280]{1,0:T(8,128)(2,1)S(1)} %collective-permute-done.7.bl.refs_2_, ...), custom_call_target="tpu_custom_call" | custom-call | tf_op jit(solution)/shard_map/project_near/pallas_call | solution.py:170
  31.9 2.5 %collective-permute-done.4.a.refs_5_ = bf16[128,1280]{1,0:T(8,128)(2,1)S(1)} collective-permute-done((bf16[128,1280]{1,0:T(8,128)(2,1)}, bf16[128,1280]{1,0:T(8,128)(2,1)S(1)}, u32[]{:S(2)}, u32[]{:S(2)}) %collective-permute-start.4) | collective-permute-done | bytes 327712 | tf_op jit(solution)/shard_map/ppermute | solution.py:601
  35.5 2.5 %collective-permute-start.10 = (bf16[256,256]{1,0:T(8,128)(2,1)S(1)}, bf16[256,256]{1,0:T(8,128)(2,1)S(1)}, u32[]{:S(2)}, u32[]{:S(2)}) collective-permute-start(bf16[256,256]{1,0:T(8,128)(2,1)S(1)} %get-tuple-element.79.a), channel_id=1, source_target_pairs={{0,24},{4,28},{8,0},{12,4},{16,8},{20,12},{24,16},{28,20},{32,56},... | collective-permute-start | bytes 393224 | tf_op jit(solution)/shard_map/ppermute | solution.py:601
  39.1 1.4 collective-permute-start.18
  40.9 2.8 %collective-permute-done.11.d = bf16[256,256]{1,0:T(8,128)(2,1)S(1)} collective-permute-done((bf16[256,256]{1,0:T(8,128)(2,1)S(1)}, bf16[256,256]{1,0:T(8,128)(2,1)S(1)}, u32[]{:S(2)}, u32[]{:S(2)}) %collective-permute-start.11) | collective-permute-done | bytes 131104 | tf_op jit(solution)/shard_map/ppermute | solution.py:601
  43.7 4.0 %collective-permute-done.9.b = bf16[256,256]{1,0:T(8,128)(2,1)S(1)} collective-permute-done((bf16[256,256]{1,0:T(8,128)(2,1)S(1)}, bf16[256,256]{1,0:T(8,128)(2,1)S(1)}, u32[]{:S(2)}, u32[]{:S(2)}) %collective-permute-start.9) | collective-permute-done | bytes 131104 | tf_op jit(solution)/shard_map/ppermute | solution.py:601
  47.7 1.4 collective-permute-start.12
  49.1 1.5 collective-permute-start.15
  50.6 2.7 %collective-permute-start.20 = (bf16[256,256]{1,0:T(8,128)(2,1)S(1)}, bf16[256,256]{1,0:T(8,128)(2,1)S(1)}, u32[]{:S(2)}, u32[]{:S(2)}) collective-permute-start(bf16[256,256]{1,0:T(8,128)(2,1)S(1)} %collective-permute-done.18.a), channel_id=1, source_target_pairs={{0,96},{4,100},{8,104},{12,108},{16,112},{20,116},{24,120},{28,124... | collective-permute-start | bytes 393224 | tf_op jit(solution)/shard_map/ppermute | solution.py:601
  53.6 5.6 %collective-permute-done.19.b = bf16[256,256]{1,0:T(8,128)(2,1)S(1)} collective-permute-done((bf16[256,256]{1,0:T(8,128)(2,1)S(1)}, bf16[256,256]{1,0:T(8,128)(2,1)S(1)}, u32[]{:S(2)}, u32[]{:S(2)}) %collective-permute-start.19) | collective-permute-done | bytes 131104 | tf_op jit(solution)/shard_map/ppermute | solution.py:601
  59.2 3.0 %collective-permute-start.14 = (bf16[4,128,256]{2,1,0:T(8,128)(2,1)S(1)}, bf16[4,128,256]{2,1,0:T(8,128)(2,1)S(1)}, u32[]{:S(2)}, u32[]{:S(2)}) collective-permute-start(bf16[4,128,256]{2,1,0:T(8,128)(2,1)S(1)} %get-tuple-element.80.refs_0_), channel_id=1, source_target_pairs={{0,96},{4,100},{8,104},{12,108},{16,112},{20,116},{24,120},{28,124... | collective-permute-start | bytes 786440 | tf_op jit(solution)/shard_map/ppermute | solution.py:601
  63.3 2.7 %collective-permute-start.25 = (bf16[4,128,256]{2,1,0:T(8,128)(2,1)S(1)}, bf16[4,128,256]{2,1,0:T(8,128)(2,1)S(1)}, u32[]{:S(2)}, u32[]{:S(2)}) collective-permute-start(bf16[4,128,256]{2,1,0:T(8,128)(2,1)S(1)} %get-tuple-element.84.refs_9_), channel_id=1, source_target_pairs={{0,24},{4,28},{8,0},{12,4},{16,8},{20,12},{24,16},{28,20},{32,56},... | collective-permute-start | bytes 786440 | tf_op jit(solution)/shard_map/ppermute | solution.py:601
  66.0 2.9 %collective-permute-done.13.refs_3_ = bf16[4,128,256]{2,1,0:T(8,128)(2,1)S(1)} collective-permute-done((bf16[4,128,256]{2,1,0:T(8,128)(2,1)S(1)}, bf16[4,128,256]{2,1,0:T(8,128)(2,1)S(1)}, u32[]{:S(2)}, u32[]{:S(2)}) %collective-permute-start.13) | collective-permute-done | bytes 262176 | tf_op jit(solution)/shard_map/ppermute | solution.py:601
  69.8 1.8 collective-permute-start.17
  71.6 1.5 collective-permute-start.26
  73.0 2.4 %collective-permute-done.23.refs_11_ = bf16[4,128,256]{2,1,0:T(8,128)(2,1)S(1)} collective-permute-done((bf16[4,128,256]{2,1,0:T(8,128)(2,1)S(1)}, bf16[4,128,256]{2,1,0:T(8,128)(2,1)S(1)}, u32[]{:S(2)}, u32[]{:S(2)}) %collective-permute-start.23) | collective-permute-done | bytes 262176 | tf_op jit(solution)/shard_map/ppermute | solution.py:601
  76.0 5.1 %collective-permute-done.26.refs_14_ = bf16[4,128,256]{2,1,0:T(8,128)(2,1)S(1)} collective-permute-done((bf16[4,128,256]{2,1,0:T(8,128)(2,1)S(1)}, bf16[4,128,256]{2,1,0:T(8,128)(2,1)S(1)}, u32[]{:S(2)}, u32[]{:S(2)}) %collective-permute-start.26) | collective-permute-done | bytes 262176 | tf_op jit(solution)/shard_map/ppermute | solution.py:601
  81.1 14.6 %attend.1 = (bf16[512,1280]{1,0:T(8,128)(2,1)S(1)}, f32[16,128,128]{2,1,0:T(8,128)S(1)}, bf16[16,128,128]{2,1,0:T(8,128)(2,1)S(1)}, bf16[16,128,128]{2,1,0:T(8,1...) custom-call(s32[115]{0:T(128)S(1)} %get-tuple-element.71.t, ...), custom_call_target="tpu_custom_call" | custom-call | tf_op jit(solution)/shard_map/attend/pallas_call | solution.py:422
  96.0 2.5 %collective-permute-start.30 = (bf16[16,128,128]{2,1,0:T(8,128)(2,1)S(1)}, bf16[16,128,128]{2,1,0:T(8,128)(2,1)S(1)}, u32[]{:S(2)}, u32[]{:S(2)}) collective-permute-start(bf16[16,128,128]{2,1,0:T(8,128)(2,1)S(1)} %get-tuple-element.90), channel_id=1, source_target_pairs={{0,24},{4,28},{8,0},{12,4},{16,8},{20,12},{24,16},{28,20},{32,56},... | collective-permute-start | bytes 1572872 | tf_op jit(solution)/shard_map/ppermute | solution.py:601
  100.7 1.6 collective-permute-start.33
  102.3 2.8 %collective-permute-done.29.refs_1_ = bf16[16,128,128]{2,1,0:T(8,128)(2,1)S(1)} collective-permute-done((bf16[16,128,128]{2,1,0:T(8,128)(2,1)S(1)}, bf16[16,128,128]{2,1,0:T(8,128)(2,1)S(1)}, u32[]{:S(2)}, u32[]{:S(2)}) %collective-permute-start.29) | collective-permute-done | bytes 524320 | tf_op jit(solution)/shard_map/ppermute | solution.py:601
  107.1 17.9 %collective-permute-start.45 = (bf16[128,1280]{1,0:T(8,128)(2,1)}, bf16[128,1280]{1,0:T(8,128)(2,1)S(1)}, u32[]{:S(2)}, u32[]{:S(2)}) collective-permute-start(bf16[128,1280]{1,0:T(8,128)(2,1)} %collective-permute-done.3.bt.refs_1_), channel_id=1, source_target_pairs={{0,4},{4,0},{8,12},{12,8},{16,20},{20,16},{24,28},{28,24},{32,36},... | collective-permute-start | bytes 983048 | tf_op jit(solution)/shard_map/ppermute | solution.py:601
  125.5 1.4 collective-permute-start.35
  126.9 1.4 collective-permute-start.36
  129.3 2.7 %collective-permute-start.39 = (f32[4,128,128]{2,1,0:T(8,128)S(1)}, f32[4,128,128]{2,1,0:T(8,128)S(1)}, u32[]{:S(2)}, u32[]{:S(2)}) collective-permute-start(f32[4,128,128]{2,1,0:T(8,128)S(1)} %get-tuple-element.102), channel_id=1, source_target_pairs={{0,24},{4,28},{8,0},{12,4},{16,8},{20,12},{24,16},{28,20},{32,56},... | collective-permute-start | bytes 786440 | tf_op jit(solution)/shard_map/ppermute | solution.py:601
  131.9 7.9 %collective-permute-done.35.refs_1_ = f32[4,128,128]{2,1,0:T(8,128)S(1)} collective-permute-done((f32[4,128,128]{2,1,0:T(8,128)S(1)}, f32[4,128,128]{2,1,0:T(8,128)S(1)}, u32[]{:S(2)}, u32[]{:S(2)}) %collective-permute-start.35) | collective-permute-done | bytes 262176 | tf_op jit(solution)/shard_map/ppermute | solution.py:601
  139.9 10.6 %collective-permute-start.48 = (bf16[128,1280]{1,0:T(8,128)(2,1)}, bf16[128,1280]{1,0:T(8,128)(2,1)S(1)}, u32[]{:S(2)}, u32[]{:S(2)}) collective-permute-start(bf16[128,1280]{1,0:T(8,128)(2,1)} %collective-permute-done.5.cl.refs_4_), channel_id=1, source_target_pairs={{0,4},{4,0},{8,12},{12,8},{16,20},{20,16},{24,28},{28,24},{32,36},... | collective-permute-start | bytes 983048 | tf_op jit(solution)/shard_map/ppermute | solution.py:601
  150.5 1.2 collective-permute-start.46
  152.1 1.6 collective-permute-start.49
  153.7 2.3 %collective-permute-start.50 = (bf16[128,1280]{1,0:T(8,128)(2,1)S(1)}, bf16[128,1280]{1,0:T(8,128)(2,1)S(1)}, u32[]{:S(2)}, u32[]{:S(2)}) collective-permute-start(bf16[128,1280]{1,0:T(8,128)(2,1)S(1)} %collective-permute-done.6.b.refs_6_), channel_id=1, source_target_pairs={{0,4},{4,0},{8,12},{12,8},{16,20},{20,16},{24,28},{28,24},{32,36},... | collective-permute-start | bytes 983048 | tf_op jit(solution)/shard_map/ppermute | solution.py:601
  157.3 2.7 %flip.1.ft = bf16[4,1280,512]{2,1,0:T(8,128)(2,1)S(1)} custom-call(bf16[256,1280]{1,0:T(8,128)(2,1)S(1)} %copy-done.4, bf16[128,1280]{1,0:T(8,128)(2,1)} %collective-permute-done.3.bt.refs_1_, bf16[128,1280]{1,0:T(8,128)(2,1)S(1)} %collective-permute-done.7.bl.refs_2_, bf16[128,1280]{1,0:T(8,128)(2,1)S(1)} %collective-permute-done.8.ct.refs_3_, ...), custom_call_target="tpu_custom_call" | custom-call | tf_op jit(solution)/shard_map/flip/pallas_call | solution.py:558
  160.0 2.5 %weight_partials.1 = (f32[8,160,128]{2,1,0:T(8,128)S(1)}, bf16[8,160,128]{2,1,0:T(8,128)(2,1)S(1)}, bf16[8,160,128]{2,1,0:T(8,128)(2,1)S(1)}, bf16[8,160,128]{2,...) custom-call(s32[17]{0:T(128)S(1)} %get-tuple-element.70.place_ref.p,, ...), custom_call_target="tpu_custom_call" | custom-call | tf_op jit(solution)/shard_map/weight_partials/pallas_call | solution.py:588
  162.6 2.7 %collective-permute-start.52 = (bf16[8,160,128]{2,1,0:T(8,128)(2,1)S(1)}, bf16[8,160,128]{2,1,0:T(8,128)(2,1)S(1)}, u32[]{:S(2)}, u32[]{:S(2)}) collective-permute-start(bf16[8,160,128]{2,1,0:T(8,128)(2,1)S(1)} %get-tuple-element.115), channel_id=1, source_target_pairs={{0,24},{4,28},{8,0},{12,4},{16,8},{20,12},{24,16},{28,20},{32,56},... | collective-permute-start | bytes 983048 | tf_op jit(solution)/shard_map/ppermute | solution.py:601
  166.0 2.1 collective-permute-start.55
  168.1 4.6 %collective-permute-done.51.refs_1_ = bf16[8,160,128]{2,1,0:T(8,128)(2,1)S(1)} collective-permute-done((bf16[8,160,128]{2,1,0:T(8,128)(2,1)S(1)}, bf16[8,160,128]{2,1,0:T(8,128)(2,1)S(1)}, u32[]{:S(2)}, u32[]{:S(2)}) %collective-permute-start.51) | collective-permute-done | bytes 327712 | tf_op jit(solution)/shard_map/ppermute | solution.py:601
  172.7 2.2 collective-permute-start.56
  174.9 4.9 %collective-permute-done.53.refs_3_ = bf16[8,160,128]{2,1,0:T(8,128)(2,1)S(1)} collective-permute-done((bf16[8,160,128]{2,1,0:T(8,128)(2,1)S(1)}, bf16[8,160,128]{2,1,0:T(8,128)(2,1)S(1)}, u32[]{:S(2)}, u32[]{:S(2)}) %collective-permute-start.53) | collective-permute-done | bytes 327712 | tf_op jit(solution)/shard_map/ppermute | solution.py:601
  179.9 1.7 collective-permute-done.56.refs_7_
  181.8 2.1 collective-permute-start.57
  183.9 1.2 collective-permute-start.58
  185.1 1.3 collective-permute-start.59
  186.8 3.0 %collective-permute-start.28 = (bf16[256,1280]{1,0:T(8,128)(2,1)S(1)}, bf16[256,1280]{1,0:T(8,128)(2,1)S(1)}, u32[]{:S(2)}, u32[]{:S(2)}) collective-permute-start(bf16[256,1280]{1,0:T(8,128)(2,1)S(1)} %slice.3), channel_id=1, source_target_pairs={{0,4},{4,0},{8,12},{12,8},{16,20},{20,16},{24,28},{28,24},{32,36},... | collective-permute-start | bytes 1966088 | tf_op jit(solution)/shard_map/ppermute | solution.py:601
  189.8 3.0 %input_partials.1 = (bf16[256,1280]{1,0:T(8,128)(2,1)S(1)}, bf16[256,1280]{1,0:T(8,128)(2,1)S(1)}, bf16[256,1280]{1,0:T(8,128)(2,1)S(1)}, bf16[256,1280]{1,0:T(8,128)(2,1)S(1)}) custom-call(s32[17]{0:T(128)S(1)} %get-tuple-element.70.place_ref.p, bf16[512,256]{1,0:T(8,128)(2,1)S(1)} %get-tuple-element.106.a.g, ...), custom_call_target="tpu_custom_call" | custom-call | tf_op jit(solution)/shard_map/input_partials/pallas_call | solution.py:533
  193.0 2.7 %collective-permute-start.43 = (bf16[256,1280]{1,0:T(8,128)(2,1)S(1)}, bf16[256,1280]{1,0:T(8,128)(2,1)S(1)}, u32[]{:S(2)}, u32[]{:S(2)}) collective-permute-start(bf16[256,1280]{1,0:T(8,128)(2,1)S(1)} %get-tuple-element.110), channel_id=1, source_target_pairs={{0,3},{1,0},{2,1},{3,2},{4,7},{5,4},{6,5},{7,6},{8,11},{9,8},{10,9... | collective-permute-start | bytes 1966088 | tf_op jit(solution)/shard_map/ppermute | solution.py:601
  196.1 2.5 %collective-permute-start.61 = (f32[2,160,128]{2,1,0:T(8,128)S(1)}, f32[2,160,128]{2,1,0:T(8,128)S(1)}, u32[]{:S(2)}, u32[]{:S(2)}) collective-permute-start(f32[2,160,128]{2,1,0:T(8,128)S(1)} %get-tuple-element.127), channel_id=1, source_target_pairs={{0,24},{4,28},{8,0},{12,4},{16,8},{20,12},{24,16},{28,20},{32,56},... | collective-permute-start | bytes 491528 | tf_op jit(solution)/shard_map/ppermute | solution.py:601
  198.6 3.1 %collective-permute-done.61.refs_6_ = f32[2,160,128]{2,1,0:T(8,128)S(1)} collective-permute-done((f32[2,160,128]{2,1,0:T(8,128)S(1)}, f32[2,160,128]{2,1,0:T(8,128)S(1)}, u32[]{:S(2)}, u32[]{:S(2)}) %collective-permute-start.61) | collective-permute-done | bytes 163872 | tf_op jit(solution)/shard_map/ppermute | solution.py:601
  201.7 2.2 collective-permute-start.62
  203.9 3.5 %collective-permute-done.62.refs_7_ = f32[2,160,128]{2,1,0:T(8,128)S(1)} collective-permute-done((f32[2,160,128]{2,1,0:T(8,128)S(1)}, f32[2,160,128]{2,1,0:T(8,128)S(1)}, u32[]{:S(2)}, u32[]{:S(2)}) %collective-permute-start.62) | collective-permute-done | bytes 163872 | tf_op jit(solution)/shard_map/ppermute | solution.py:601
  207.5 2.5 %collective-permute-start.63 = (f32[160,256]{1,0:T(8,128)S(1)}, f32[160,256]{1,0:T(8,128)S(1)}, u32[]{:S(2)}, u32[]{:S(2)}) collective-permute-start(f32[160,256]{1,0:T(8,128)S(1)} %get-tuple-element.130), channel_id=1, source_target_pairs={{0,4},{4,0},{8,12},{12,8},{16,20},{20,16},{24,28},{28,24},{32,36},... | collective-permute-start | bytes 491528 | tf_op jit(solution)/shard_map/ppermute | solution.py:601
  210.0 1.7 join_rows.1
  211.7 1.3 join_weights.1
  213.0 10.3 %collective-permute-done.43.c = bf16[256,1280]{1,0:T(8,128)(2,1)S(1)} collective-permute-done((bf16[256,1280]{1,0:T(8,128)(2,1)S(1)}, bf16[256,1280]{1,0:T(8,128)(2,1)S(1)}, u32[]{:S(2)}, u32[]{:S(2)}) %collective-permute-start.43) | collective-permute-done | bytes 655392 | tf_op jit(solution)/shard_map/ppermute | solution.py:601
  223.3 1.5 collective-permute-done.44.d
  (106 shorter events, 21.0 us)
Async XLA Ops:
  2.5 12.8 %collective-permute-start.1 = (bf16[256,640]{1,0:T(8,128)(2,1)}, bf16[256,640]{1,0:T(8,128)(2,1)}, u32[]{:S(2)}, u32[]{:S(2)}) collective-permute-start(bf16[256,640]{1,0:T(8,128)(2,1)} %constant_dynamic-slice_fusion.1), channel_id=1, source_target_pairs={{0,4},{4,0},{8,12},{12,8},{16,20},{20,16},{24,28},{28,24},{32,36},... | collective-permute-start | bytes 983048 | tf_op jit(solution)/shard_map/ppermute | solution.py:601
  5.6 9.7 %collective-permute-start.2 = (bf16[256,640]{1,0:T(8,128)(2,1)}, bf16[256,640]{1,0:T(8,128)(2,1)}, u32[]{:S(2)}, u32[]{:S(2)}) collective-permute-start(bf16[256,640]{1,0:T(8,128)(2,1)} %constant_dynamic-slice_fusion), channel_id=1, source_target_pairs={{0,4},{4,0},{8,12},{12,8},{16,20},{20,16},{24,28},{28,24},{32,36},... | collective-permute-start | bytes 983048 | tf_op jit(solution)/shard_map/ppermute | solution.py:601
  5.7 18.6 %collective-permute-start = (bf16[256,1280]{1,0:T(8,128)(2,1)}, bf16[256,1280]{1,0:T(8,128)(2,1)}, u32[]{:S(2)}, u32[]{:S(2)}) collective-permute-start(bf16[256,1280]{1,0:T(8,128)(2,1)} %refs_0_.1), channel_id=1, source_target_pairs={{0,4},{4,0},{8,12},{12,8},{16,20},{20,16},{24,28},{28,24},{32,36},... | collective-permute-start | bytes 1966088 | tf_op jit(solution)/shard_map/ppermute | solution.py:601
  8.1 12.3 %collective-permute-start.3 = (bf16[128,1280]{1,0:T(8,128)(2,1)}, bf16[128,1280]{1,0:T(8,128)(2,1)}, u32[]{:S(2)}, u32[]{:S(2)}) collective-permute-start(bf16[128,1280]{1,0:T(8,128)(2,1)} %get-tuple-element.74), channel_id=1, source_target_pairs={{0,1},{1,2},{2,3},{3,0},{4,5},{5,6},{6,7},{7,4},{8,9},{9,10},{10,1... | collective-permute-start | bytes 983048 | tf_op jit(solution)/shard_map/ppermute | solution.py:601
  9.9 10.5 %collective-permute-start.5 = (bf16[128,1280]{1,0:T(8,128)(2,1)}, bf16[128,1280]{1,0:T(8,128)(2,1)}, u32[]{:S(2)}, u32[]{:S(2)}) collective-permute-start(bf16[128,1280]{1,0:T(8,128)(2,1)} %get-tuple-element.75), channel_id=1, source_target_pairs={{0,3},{1,0},{2,1},{3,2},{4,7},{5,4},{6,5},{7,6},{8,11},{9,8},{10,9... | collective-permute-start | bytes 983048 | tf_op jit(solution)/shard_map/ppermute | solution.py:601
  15.4 11.9 %collective-permute-start.7 = (bf16[128,1280]{1,0:T(8,128)(2,1)}, bf16[128,1280]{1,0:T(8,128)(2,1)S(1)}, u32[]{:S(2)}, u32[]{:S(2)}) collective-permute-start(bf16[128,1280]{1,0:T(8,128)(2,1)} %get-tuple-element.75), channel_id=1, source_target_pairs={{0,1},{1,2},{2,3},{3,0},{4,5},{5,6},{6,7},{7,4},{8,9},{9,10},{10,1... | collective-permute-start | bytes 983048 | tf_op jit(solution)/shard_map/ppermute | solution.py:601
  15.4 11.9 %collective-permute-start.8 = (bf16[128,1280]{1,0:T(8,128)(2,1)}, bf16[128,1280]{1,0:T(8,128)(2,1)S(1)}, u32[]{:S(2)}, u32[]{:S(2)}) collective-permute-start(bf16[128,1280]{1,0:T(8,128)(2,1)} %get-tuple-element.74), channel_id=1, source_target_pairs={{0,3},{1,0},{2,1},{3,2},{4,7},{5,4},{6,5},{7,6},{8,11},{9,8},{10,9... | collective-permute-start | bytes 983048 | tf_op jit(solution)/shard_map/ppermute | solution.py:601
  20.4 13.9 %collective-permute-start.4 = (bf16[128,1280]{1,0:T(8,128)(2,1)}, bf16[128,1280]{1,0:T(8,128)(2,1)S(1)}, u32[]{:S(2)}, u32[]{:S(2)}) collective-permute-start(bf16[128,1280]{1,0:T(8,128)(2,1)} %collective-permute-done.3.bt.refs_1_), channel_id=1, source_target_pairs={{0,1},{1,2},{2,3},{3,0},{4,5},{5,6},{6,7},{7,4},{8,9},{9,10},{10,1... | collective-permute-start | bytes 983048 | tf_op jit(solution)/shard_map/ppermute | solution.py:601
  20.4 13.9 %collective-permute-start.6 = (bf16[128,1280]{1,0:T(8,128)(2,1)}, bf16[128,1280]{1,0:T(8,128)(2,1)S(1)}, u32[]{:S(2)}, u32[]{:S(2)}) collective-permute-start(bf16[128,1280]{1,0:T(8,128)(2,1)} %collective-permute-done.5.cl.refs_4_), channel_id=1, source_target_pairs={{0,3},{1,0},{2,1},{3,2},{4,7},{5,4},{6,5},{7,6},{8,11},{9,8},{10,9... | collective-permute-start | bytes 983048 | tf_op jit(solution)/shard_map/ppermute | solution.py:601
  35.5 5.4 %collective-permute-start.10 = (bf16[256,256]{1,0:T(8,128)(2,1)S(1)}, bf16[256,256]{1,0:T(8,128)(2,1)S(1)}, u32[]{:S(2)}, u32[]{:S(2)}) collective-permute-start(bf16[256,256]{1,0:T(8,128)(2,1)S(1)} %get-tuple-element.79.a), channel_id=1, source_target_pairs={{0,24},{4,28},{8,0},{12,4},{16,8},{20,12},{24,16},{28,20},{32,56},... | collective-permute-start | bytes 393224 | tf_op jit(solution)/shard_map/ppermute | solution.py:601
  38.0 5.7 %collective-permute-start.11 = (bf16[256,256]{1,0:T(8,128)(2,1)S(1)}, bf16[256,256]{1,0:T(8,128)(2,1)S(1)}, u32[]{:S(2)}, u32[]{:S(2)}) collective-permute-start(bf16[256,256]{1,0:T(8,128)(2,1)S(1)} %get-tuple-element.79.a), channel_id=1, source_target_pairs={{0,16},{4,20},{8,24},{12,28},{16,0},{20,4},{24,8},{28,12},{32,48},... | collective-permute-start | bytes 393224 | tf_op jit(solution)/shard_map/ppermute | solution.py:601
  38.5 9.1 %collective-permute-start.9 = (bf16[256,256]{1,0:T(8,128)(2,1)S(1)}, bf16[256,256]{1,0:T(8,128)(2,1)S(1)}, u32[]{:S(2)}, u32[]{:S(2)}) collective-permute-start(bf16[256,256]{1,0:T(8,128)(2,1)S(1)} %get-tuple-element.79.a), channel_id=1, source_target_pairs={{0,8},{4,12},{8,16},{12,20},{16,24},{20,28},{24,0},{28,4},{32,40},... | collective-permute-start | bytes 393224 | tf_op jit(solution)/shard_map/ppermute | solution.py:601
  39.1 11.5 %collective-permute-start.18 = (bf16[256,256]{1,0:T(8,128)(2,1)S(1)}, bf16[256,256]{1,0:T(8,128)(2,1)S(1)}, u32[]{:S(2)}, u32[]{:S(2)}) collective-permute-start(bf16[256,256]{1,0:T(8,128)(2,1)S(1)} %get-tuple-element.82), channel_id=1, source_target_pairs={{0,4},{4,0},{8,12},{12,8},{16,20},{20,16},{24,28},{28,24},{32,36},... | collective-permute-start | bytes 393224 | tf_op jit(solution)/shard_map/ppermute | solution.py:601
  47.7 15.6 %collective-permute-start.12 = (bf16[4,128,256]{2,1,0:T(8,128)(2,1)S(1)}, bf16[4,128,256]{2,1,0:T(8,128)(2,1)S(1)}, u32[]{:S(2)}, u32[]{:S(2)}) collective-permute-start(bf16[4,128,256]{2,1,0:T(8,128)(2,1)S(1)} %get-tuple-element.80.refs_0_), channel_id=1, source_target_pairs={{0,32},{4,36},{8,40},{12,44},{16,48},{20,52},{24,56},{28,60},{32,6... | collective-permute-start | bytes 786440 | tf_op jit(solution)/shard_map/ppermute | solution.py:601
  49.1 16.9 %collective-permute-start.15 = (bf16[4,128,256]{2,1,0:T(8,128)(2,1)S(1)}, bf16[4,128,256]{2,1,0:T(8,128)(2,1)S(1)}, u32[]{:S(2)}, u32[]{:S(2)}) collective-permute-start(bf16[4,128,256]{2,1,0:T(8,128)(2,1)S(1)} %get-tuple-element.81.refs_1_), channel_id=1, source_target_pairs={{0,96},{4,100},{8,104},{12,108},{16,112},{20,116},{24,120},{28,124... | collective-permute-start | bytes 786440 | tf_op jit(solution)/shard_map/ppermute | solution.py:601
  50.6 8.6 %collective-permute-start.19 = (bf16[256,256]{1,0:T(8,128)(2,1)S(1)}, bf16[256,256]{1,0:T(8,128)(2,1)S(1)}, u32[]{:S(2)}, u32[]{:S(2)}) collective-permute-start(bf16[256,256]{1,0:T(8,128)(2,1)S(1)} %collective-permute-done.18.a), channel_id=1, source_target_pairs={{0,32},{4,36},{8,40},{12,44},{16,48},{20,52},{24,56},{28,60},{32,6... | collective-permute-start | bytes 393224 | tf_op jit(solution)/shard_map/ppermute | solution.py:601
  50.6 8.6 %collective-permute-start.20 = (bf16[256,256]{1,0:T(8,128)(2,1)S(1)}, bf16[256,256]{1,0:T(8,128)(2,1)S(1)}, u32[]{:S(2)}, u32[]{:S(2)}) collective-permute-start(bf16[256,256]{1,0:T(8,128)(2,1)S(1)} %collective-permute-done.18.a), channel_id=1, source_target_pairs={{0,96},{4,100},{8,104},{12,108},{16,112},{20,116},{24,120},{28,124... | collective-permute-start | bytes 393224 | tf_op jit(solution)/shard_map/ppermute | solution.py:601
  53.3 9.9 %collective-permute-start.21 = (bf16[256,256]{1,0:T(8,128)(2,1)S(1)}, bf16[256,256]{1,0:T(8,128)(2,1)S(1)}, u32[]{:S(2)}, u32[]{:S(2)}) collective-permute-start(bf16[256,256]{1,0:T(8,128)(2,1)S(1)} %collective-permute-done.18.a), channel_id=1, source_target_pairs={{0,64},{4,68},{8,72},{12,76},{16,80},{20,84},{24,88},{28,92},{32,9... | collective-permute-start | bytes 393224 | tf_op jit(solution)/shard_map/ppermute | solution.py:601
  59.2 9.7 %collective-permute-start.13 = (bf16[4,128,256]{2,1,0:T(8,128)(2,1)S(1)}, bf16[4,128,256]{2,1,0:T(8,128)(2,1)S(1)}, u32[]{:S(2)}, u32[]{:S(2)}) collective-permute-start(bf16[4,128,256]{2,1,0:T(8,128)(2,1)S(1)} %get-tuple-element.81.refs_1_), channel_id=1, source_target_pairs={{0,32},{4,36},{8,40},{12,44},{16,48},{20,52},{24,56},{28,60},{32,6... | collective-permute-start | bytes 786440 | tf_op jit(solution)/shard_map/ppermute | solution.py:601
  59.2 9.7 %collective-permute-start.14 = (bf16[4,128,256]{2,1,0:T(8,128)(2,1)S(1)}, bf16[4,128,256]{2,1,0:T(8,128)(2,1)S(1)}, u32[]{:S(2)}, u32[]{:S(2)}) collective-permute-start(bf16[4,128,256]{2,1,0:T(8,128)(2,1)S(1)} %get-tuple-element.80.refs_0_), channel_id=1, source_target_pairs={{0,96},{4,100},{8,104},{12,108},{16,112},{20,116},{24,120},{28,124... | collective-permute-start | bytes 786440 | tf_op jit(solution)/shard_map/ppermute | solution.py:601
  63.2 6.6 %collective-permute-start.22 = (bf16[4,128,256]{2,1,0:T(8,128)(2,1)S(1)}, bf16[4,128,256]{2,1,0:T(8,128)(2,1)S(1)}, u32[]{:S(2)}, u32[]{:S(2)}) collective-permute-start(bf16[4,128,256]{2,1,0:T(8,128)(2,1)S(1)} %get-tuple-element.83.refs_8_), channel_id=1, source_target_pairs={{0,8},{4,12},{8,16},{12,20},{16,24},{20,28},{24,0},{28,4},{32,40},... | collective-permute-start | bytes 786440 | tf_op jit(solution)/shard_map/ppermute | solution.py:601
  63.3 8.3 %collective-permute-start.25 = (bf16[4,128,256]{2,1,0:T(8,128)(2,1)S(1)}, bf16[4,128,256]{2,1,0:T(8,128)(2,1)S(1)}, u32[]{:S(2)}, u32[]{:S(2)}) collective-permute-start(bf16[4,128,256]{2,1,0:T(8,128)(2,1)S(1)} %get-tuple-element.84.refs_9_), channel_id=1, source_target_pairs={{0,24},{4,28},{8,0},{12,4},{16,8},{20,12},{24,16},{28,20},{32,56},... | collective-permute-start | bytes 786440 | tf_op jit(solution)/shard_map/ppermute | solution.py:601
  65.9 9.5 %collective-permute-start.23 = (bf16[4,128,256]{2,1,0:T(8,128)(2,1)S(1)}, bf16[4,128,256]{2,1,0:T(8,128)(2,1)S(1)}, u32[]{:S(2)}, u32[]{:S(2)}) collective-permute-start(bf16[4,128,256]{2,1,0:T(8,128)(2,1)S(1)} %get-tuple-element.84.refs_9_), channel_id=1, source_target_pairs={{0,8},{4,12},{8,16},{12,20},{16,24},{20,28},{24,0},{28,4},{32,40},... | collective-permute-start | bytes 786440 | tf_op jit(solution)/shard_map/ppermute | solution.py:601
  68.9 7.1 %collective-permute-start.24 = (bf16[4,128,256]{2,1,0:T(8,128)(2,1)S(1)}, bf16[4,128,256]{2,1,0:T(8,128)(2,1)S(1)}, u32[]{:S(2)}, u32[]{:S(2)}) collective-permute-start(bf16[4,128,256]{2,1,0:T(8,128)(2,1)S(1)} %get-tuple-element.83.refs_8_), channel_id=1, source_target_pairs={{0,24},{4,28},{8,0},{12,4},{16,8},{20,12},{24,16},{28,20},{32,56},... | collective-permute-start | bytes 786440 | tf_op jit(solution)/shard_map/ppermute | solution.py:601
  68.9 7.1 %collective-permute-start.16 = (bf16[4,128,256]{2,1,0:T(8,128)(2,1)S(1)}, bf16[4,128,256]{2,1,0:T(8,128)(2,1)S(1)}, u32[]{:S(2)}, u32[]{:S(2)}) collective-permute-start(bf16[4,128,256]{2,1,0:T(8,128)(2,1)S(1)} %collective-permute-done.12.refs_2_), channel_id=1, source_target_pairs={{0,32},{4,36},{8,40},{12,44},{16,48},{20,52},{24,56},{28,60},{32,6... | collective-permute-start | bytes 786440 | tf_op jit(solution)/shard_map/ppermute | solution.py:601
  69.8 6.2 %collective-permute-start.17 = (bf16[4,128,256]{2,1,0:T(8,128)(2,1)S(1)}, bf16[4,128,256]{2,1,0:T(8,128)(2,1)S(1)}, u32[]{:S(2)}, u32[]{:S(2)}) collective-permute-start(bf16[4,128,256]{2,1,0:T(8,128)(2,1)S(1)} %collective-permute-done.15.refs_5_), channel_id=1, source_target_pairs={{0,96},{4,100},{8,104},{12,108},{16,112},{20,116},{24,120},{28,124... | collective-permute-start | bytes 786440 | tf_op jit(solution)/shard_map/ppermute | solution.py:601
  71.6 9.5 %collective-permute-start.26 = (bf16[4,128,256]{2,1,0:T(8,128)(2,1)S(1)}, bf16[4,128,256]{2,1,0:T(8,128)(2,1)S(1)}, u32[]{:S(2)}, u32[]{:S(2)}) collective-permute-start(bf16[4,128,256]{2,1,0:T(8,128)(2,1)S(1)} %collective-permute-done.22.refs_10_), channel_id=1, source_target_pairs={{0,8},{4,12},{8,16},{12,20},{16,24},{20,28},{24,0},{28,4},{32,40},... | collective-permute-start | bytes 786440 | tf_op jit(solution)/shard_map/ppermute | solution.py:601
  75.4 5.7 %collective-permute-start.27 = (bf16[4,128,256]{2,1,0:T(8,128)(2,1)S(1)}, bf16[4,128,256]{2,1,0:T(8,128)(2,1)S(1)}, u32[]{:S(2)}, u32[]{:S(2)}) collective-permute-start(bf16[4,128,256]{2,1,0:T(8,128)(2,1)S(1)} %collective-permute-done.25.refs_13_), channel_id=1, source_target_pairs={{0,24},{4,28},{8,0},{12,4},{16,8},{20,12},{24,16},{28,20},{32,56},... | collective-permute-start | bytes 786440 | tf_op jit(solution)/shard_map/ppermute | solution.py:601
  95.8 9.3 %collective-permute-start.29 = (bf16[16,128,128]{2,1,0:T(8,128)(2,1)S(1)}, bf16[16,128,128]{2,1,0:T(8,128)(2,1)S(1)}, u32[]{:S(2)}, u32[]{:S(2)}) collective-permute-start(bf16[16,128,128]{2,1,0:T(8,128)(2,1)S(1)} %get-tuple-element.89), channel_id=1, source_target_pairs={{0,8},{4,12},{8,16},{12,20},{16,24},{20,28},{24,0},{28,4},{32,40},... | collective-permute-start | bytes 1572872 | tf_op jit(solution)/shard_map/ppermute | solution.py:601
  96.0 11.1 %collective-permute-start.30 = (bf16[16,128,128]{2,1,0:T(8,128)(2,1)S(1)}, bf16[16,128,128]{2,1,0:T(8,128)(2,1)S(1)}, u32[]{:S(2)}, u32[]{:S(2)}) collective-permute-start(bf16[16,128,128]{2,1,0:T(8,128)(2,1)S(1)} %get-tuple-element.90), channel_id=1, source_target_pairs={{0,24},{4,28},{8,0},{12,4},{16,8},{20,12},{24,16},{28,20},{32,56},... | collective-permute-start | bytes 1572872 | tf_op jit(solution)/shard_map/ppermute | solution.py:601
  98.5 26.5 %collective-permute-start.31 = (bf16[16,128,128]{2,1,0:T(8,128)(2,1)S(1)}, bf16[16,128,128]{2,1,0:T(8,128)(2,1)S(1)}, u32[]{:S(2)}, u32[]{:S(2)}) collective-permute-start(bf16[16,128,128]{2,1,0:T(8,128)(2,1)S(1)} %get-tuple-element.91), channel_id=1, source_target_pairs={{0,16},{4,20},{8,24},{12,28},{16,0},{20,4},{24,8},{28,12},{32,48},... | collective-permute-start | bytes 1572872 | tf_op jit(solution)/shard_map/ppermute | solution.py:601
  99.6 25.4 %collective-permute-start.32 = (bf16[16,128,128]{2,1,0:T(8,128)(2,1)S(1)}, bf16[16,128,128]{2,1,0:T(8,128)(2,1)S(1)}, u32[]{:S(2)}, u32[]{:S(2)}) collective-permute-start(bf16[16,128,128]{2,1,0:T(8,128)(2,1)S(1)} %get-tuple-element.93), channel_id=1, source_target_pairs={{0,32},{4,36},{8,40},{12,44},{16,48},{20,52},{24,56},{28,60},{32,6... | collective-permute-start | bytes 1572872 | tf_op jit(solution)/shard_map/ppermute | solution.py:601
  100.7 24.3 %collective-permute-start.33 = (bf16[16,128,128]{2,1,0:T(8,128)(2,1)S(1)}, bf16[16,128,128]{2,1,0:T(8,128)(2,1)S(1)}, u32[]{:S(2)}, u32[]{:S(2)}) collective-permute-start(bf16[16,128,128]{2,1,0:T(8,128)(2,1)S(1)} %get-tuple-element.94), channel_id=1, source_target_pairs={{0,96},{4,100},{8,104},{12,108},{16,112},{20,116},{24,120},{28,124... | collective-permute-start | bytes 1572872 | tf_op jit(solution)/shard_map/ppermute | solution.py:601
  105.1 20.0 %collective-permute-start.34 = (bf16[16,128,128]{2,1,0:T(8,128)(2,1)S(1)}, bf16[16,128,128]{2,1,0:T(8,128)(2,1)S(1)}, u32[]{:S(2)}, u32[]{:S(2)}) collective-permute-start(bf16[16,128,128]{2,1,0:T(8,128)(2,1)S(1)} %get-tuple-element.95), channel_id=1, source_target_pairs={{0,64},{4,68},{8,72},{12,76},{16,80},{20,84},{24,88},{28,92},{32,9... | collective-permute-start | bytes 1572872 | tf_op jit(solution)/shard_map/ppermute | solution.py:601
  107.1 22.1 %collective-permute-start.45 = (bf16[128,1280]{1,0:T(8,128)(2,1)}, bf16[128,1280]{1,0:T(8,128)(2,1)S(1)}, u32[]{:S(2)}, u32[]{:S(2)}) collective-permute-start(bf16[128,1280]{1,0:T(8,128)(2,1)} %collective-permute-done.3.bt.refs_1_), channel_id=1, source_target_pairs={{0,4},{4,0},{8,12},{12,8},{16,20},{20,16},{24,28},{28,24},{32,36},... | collective-permute-start | bytes 983048 | tf_op jit(solution)/shard_map/ppermute | solution.py:601
  125.5 14.4 %collective-permute-start.35 = (f32[4,128,128]{2,1,0:T(8,128)S(1)}, f32[4,128,128]{2,1,0:T(8,128)S(1)}, u32[]{:S(2)}, u32[]{:S(2)}) collective-permute-start(f32[4,128,128]{2,1,0:T(8,128)S(1)} %get-tuple-element.97), channel_id=1, source_target_pairs={{0,32},{4,36},{8,40},{12,44},{16,48},{20,52},{24,56},{28,60},{32,6... | collective-permute-start | bytes 786440 | tf_op jit(solution)/shard_map/ppermute | solution.py:601
  126.9 13.0 %collective-permute-start.36 = (f32[4,128,128]{2,1,0:T(8,128)S(1)}, f32[4,128,128]{2,1,0:T(8,128)S(1)}, u32[]{:S(2)}, u32[]{:S(2)}) collective-permute-start(f32[4,128,128]{2,1,0:T(8,128)S(1)} %get-tuple-element.98), channel_id=1, source_target_pairs={{0,96},{4,100},{8,104},{12,108},{16,112},{20,116},{24,120},{28,124... | collective-permute-start | bytes 786440 | tf_op jit(solution)/shard_map/ppermute | solution.py:601
  128.3 22.3 %collective-permute-start.37 = (f32[4,128,128]{2,1,0:T(8,128)S(1)}, f32[4,128,128]{2,1,0:T(8,128)S(1)}, u32[]{:S(2)}, u32[]{:S(2)}) collective-permute-start(f32[4,128,128]{2,1,0:T(8,128)S(1)} %get-tuple-element.99), channel_id=1, source_target_pairs={{0,64},{4,68},{8,72},{12,76},{16,80},{20,84},{24,88},{28,92},{32,9... | collective-permute-start | bytes 786440 | tf_op jit(solution)/shard_map/ppermute | solution.py:601
  129.3 22.4 %collective-permute-start.38 = (f32[4,128,128]{2,1,0:T(8,128)S(1)}, f32[4,128,128]{2,1,0:T(8,128)S(1)}, u32[]{:S(2)}, u32[]{:S(2)}) collective-permute-start(f32[4,128,128]{2,1,0:T(8,128)S(1)} %get-tuple-element.101), channel_id=1, source_target_pairs={{0,8},{4,12},{8,16},{12,20},{16,24},{20,28},{24,0},{28,4},{32,40},... | collective-permute-start | bytes 786440 | tf_op jit(solution)/shard_map/ppermute | solution.py:601
  129.3 22.9 %collective-permute-start.39 = (f32[4,128,128]{2,1,0:T(8,128)S(1)}, f32[4,128,128]{2,1,0:T(8,128)S(1)}, u32[]{:S(2)}, u32[]{:S(2)}) collective-permute-start(f32[4,128,128]{2,1,0:T(8,128)S(1)} %get-tuple-element.102), channel_id=1, source_target_pairs={{0,24},{4,28},{8,0},{12,4},{16,8},{20,12},{24,16},{28,20},{32,56},... | collective-permute-start | bytes 786440 | tf_op jit(solution)/shard_map/ppermute | solution.py:601
  139.9 13.9 %collective-permute-start.40 = (f32[4,128,128]{2,1,0:T(8,128)S(1)}, f32[4,128,128]{2,1,0:T(8,128)S(1)}, u32[]{:S(2)}, u32[]{:S(2)}) collective-permute-start(f32[4,128,128]{2,1,0:T(8,128)S(1)} %get-tuple-element.103), channel_id=1, source_target_pairs={{0,16},{4,20},{8,24},{12,28},{16,0},{20,4},{24,8},{28,12},{32,48},... | collective-permute-start | bytes 786440 | tf_op jit(solution)/shard_map/ppermute | solution.py:601
  139.9 16.3 %collective-permute-start.48 = (bf16[128,1280]{1,0:T(8,128)(2,1)}, bf16[128,1280]{1,0:T(8,128)(2,1)S(1)}, u32[]{:S(2)}, u32[]{:S(2)}) collective-permute-start(bf16[128,1280]{1,0:T(8,128)(2,1)} %collective-permute-done.5.cl.refs_4_), channel_id=1, source_target_pairs={{0,4},{4,0},{8,12},{12,8},{16,20},{20,16},{24,28},{28,24},{32,36},... | collective-permute-start | bytes 983048 | tf_op jit(solution)/shard_map/ppermute | solution.py:601
  150.5 6.0 %collective-permute-start.46 = (bf16[128,1280]{1,0:T(8,128)(2,1)S(1)}, bf16[128,1280]{1,0:T(8,128)(2,1)S(1)}, u32[]{:S(2)}, u32[]{:S(2)}) collective-permute-start(bf16[128,1280]{1,0:T(8,128)(2,1)S(1)} %collective-permute-done.7.bl.refs_2_), channel_id=1, source_target_pairs={{0,4},{4,0},{8,12},{12,8},{16,20},{20,16},{24,28},{28,24},{32,36},... | collective-permute-start | bytes 983048 | tf_op jit(solution)/shard_map/ppermute | solution.py:601
  151.7 4.9 %collective-permute-start.47 = (bf16[128,1280]{1,0:T(8,128)(2,1)S(1)}, bf16[128,1280]{1,0:T(8,128)(2,1)S(1)}, u32[]{:S(2)}, u32[]{:S(2)}) collective-permute-start(bf16[128,1280]{1,0:T(8,128)(2,1)S(1)} %collective-permute-done.8.ct.refs_3_), channel_id=1, source_target_pairs={{0,4},{4,0},{8,12},{12,8},{16,20},{20,16},{24,28},{28,24},{32,36},... | collective-permute-start | bytes 983048 | tf_op jit(solution)/shard_map/ppermute | solution.py:601
  152.1 4.4 %collective-permute-start.49 = (bf16[128,1280]{1,0:T(8,128)(2,1)S(1)}, bf16[128,1280]{1,0:T(8,128)(2,1)S(1)}, u32[]{:S(2)}, u32[]{:S(2)}) collective-permute-start(bf16[128,1280]{1,0:T(8,128)(2,1)S(1)} %collective-permute-done.4.a.refs_5_), channel_id=1, source_target_pairs={{0,4},{4,0},{8,12},{12,8},{16,20},{20,16},{24,28},{28,24},{32,36},... | collective-permute-start | bytes 983048 | tf_op jit(solution)/shard_map/ppermute | solution.py:601
  153.7 3.5 %collective-permute-start.50 = (bf16[128,1280]{1,0:T(8,128)(2,1)S(1)}, bf16[128,1280]{1,0:T(8,128)(2,1)S(1)}, u32[]{:S(2)}, u32[]{:S(2)}) collective-permute-start(bf16[128,1280]{1,0:T(8,128)(2,1)S(1)} %collective-permute-done.6.b.refs_6_), channel_id=1, source_target_pairs={{0,4},{4,0},{8,12},{12,8},{16,20},{20,16},{24,28},{28,24},{32,36},... | collective-permute-start | bytes 983048 | tf_op jit(solution)/shard_map/ppermute | solution.py:601
  156.2 3.8 %collective-permute-start.41 = (bf16[256,256]{1,0:T(8,128)(2,1)S(1)}, bf16[256,256]{1,0:T(8,128)(2,1)S(1)}, u32[]{:S(2)}, u32[]{:S(2)}) collective-permute-start(bf16[256,256]{1,0:T(8,128)(2,1)S(1)} %get-tuple-element.105), channel_id=1, source_target_pairs={{0,4},{4,0},{8,12},{12,8},{16,20},{20,16},{24,28},{28,24},{32,36},... | collective-permute-start | bytes 393224 | tf_op jit(solution)/shard_map/ppermute | solution.py:601
  162.5 10.2 %collective-permute-start.51 = (bf16[8,160,128]{2,1,0:T(8,128)(2,1)S(1)}, bf16[8,160,128]{2,1,0:T(8,128)(2,1)S(1)}, u32[]{:S(2)}, u32[]{:S(2)}) collective-permute-start(bf16[8,160,128]{2,1,0:T(8,128)(2,1)S(1)} %get-tuple-element.114), channel_id=1, source_target_pairs={{0,8},{4,12},{8,16},{12,20},{16,24},{20,28},{24,0},{28,4},{32,40},... | collective-permute-start | bytes 983048 | tf_op jit(solution)/shard_map/ppermute | solution.py:601
  162.6 12.3 %collective-permute-start.52 = (bf16[8,160,128]{2,1,0:T(8,128)(2,1)S(1)}, bf16[8,160,128]{2,1,0:T(8,128)(2,1)S(1)}, u32[]{:S(2)}, u32[]{:S(2)}) collective-permute-start(bf16[8,160,128]{2,1,0:T(8,128)(2,1)S(1)} %get-tuple-element.115), channel_id=1, source_target_pairs={{0,24},{4,28},{8,0},{12,4},{16,8},{20,12},{24,16},{28,20},{32,56},... | collective-permute-start | bytes 983048 | tf_op jit(solution)/shard_map/ppermute | solution.py:601
  165.3 14.6 %collective-permute-start.53 = (bf16[8,160,128]{2,1,0:T(8,128)(2,1)S(1)}, bf16[8,160,128]{2,1,0:T(8,128)(2,1)S(1)}, u32[]{:S(2)}, u32[]{:S(2)}) collective-permute-start(bf16[8,160,128]{2,1,0:T(8,128)(2,1)S(1)} %get-tuple-element.116), channel_id=1, source_target_pairs={{0,16},{4,20},{8,24},{12,28},{16,0},{20,4},{24,8},{28,12},{32,48},... | collective-permute-start | bytes 983048 | tf_op jit(solution)/shard_map/ppermute | solution.py:601
  165.4 14.5 %collective-permute-start.54 = (bf16[8,160,128]{2,1,0:T(8,128)(2,1)S(1)}, bf16[8,160,128]{2,1,0:T(8,128)(2,1)S(1)}, u32[]{:S(2)}, u32[]{:S(2)}) collective-permute-start(bf16[8,160,128]{2,1,0:T(8,128)(2,1)S(1)} %get-tuple-element.118), channel_id=1, source_target_pairs={{0,32},{4,36},{8,40},{12,44},{16,48},{20,52},{24,56},{28,60},{32,6... | collective-permute-start | bytes 983048 | tf_op jit(solution)/shard_map/ppermute | solution.py:601
  166.0 13.9 %collective-permute-start.55 = (bf16[8,160,128]{2,1,0:T(8,128)(2,1)S(1)}, bf16[8,160,128]{2,1,0:T(8,128)(2,1)S(1)}, u32[]{:S(2)}, u32[]{:S(2)}) collective-permute-start(bf16[8,160,128]{2,1,0:T(8,128)(2,1)S(1)} %get-tuple-element.119), channel_id=1, source_target_pairs={{0,96},{4,100},{8,104},{12,108},{16,112},{20,116},{24,120},{28,124... | collective-permute-start | bytes 983048 | tf_op jit(solution)/shard_map/ppermute | solution.py:601
  172.7 8.8 %collective-permute-start.56 = (bf16[8,160,128]{2,1,0:T(8,128)(2,1)S(1)}, bf16[8,160,128]{2,1,0:T(8,128)(2,1)S(1)}, u32[]{:S(2)}, u32[]{:S(2)}) collective-permute-start(bf16[8,160,128]{2,1,0:T(8,128)(2,1)S(1)} %get-tuple-element.120), channel_id=1, source_target_pairs={{0,64},{4,68},{8,72},{12,76},{16,80},{20,84},{24,88},{28,92},{32,9... | collective-permute-start | bytes 983048 | tf_op jit(solution)/shard_map/ppermute | solution.py:601
  181.8 11.0 %collective-permute-start.57 = (f32[2,160,128]{2,1,0:T(8,128)S(1)}, f32[2,160,128]{2,1,0:T(8,128)S(1)}, u32[]{:S(2)}, u32[]{:S(2)}) collective-permute-start(f32[2,160,128]{2,1,0:T(8,128)S(1)} %get-tuple-element.122), channel_id=1, source_target_pairs={{0,32},{4,36},{8,40},{12,44},{16,48},{20,52},{24,56},{28,60},{32,6... | collective-permute-start | bytes 491528 | tf_op jit(solution)/shard_map/ppermute | solution.py:601
  183.9 9.1 %collective-permute-start.58 = (f32[2,160,128]{2,1,0:T(8,128)S(1)}, f32[2,160,128]{2,1,0:T(8,128)S(1)}, u32[]{:S(2)}, u32[]{:S(2)}) collective-permute-start(f32[2,160,128]{2,1,0:T(8,128)S(1)} %get-tuple-element.123), channel_id=1, source_target_pairs={{0,96},{4,100},{8,104},{12,108},{16,112},{20,116},{24,120},{28,124... | collective-permute-start | bytes 491528 | tf_op jit(solution)/shard_map/ppermute | solution.py:601
  185.1 10.6 %collective-permute-start.59 = (f32[2,160,128]{2,1,0:T(8,128)S(1)}, f32[2,160,128]{2,1,0:T(8,128)S(1)}, u32[]{:S(2)}, u32[]{:S(2)}) collective-permute-start(f32[2,160,128]{2,1,0:T(8,128)S(1)} %get-tuple-element.124), channel_id=1, source_target_pairs={{0,64},{4,68},{8,72},{12,76},{16,80},{20,84},{24,88},{28,92},{32,9... | collective-permute-start | bytes 491528 | tf_op jit(solution)/shard_map/ppermute | solution.py:601
  186.3 9.8 %collective-permute-start.60 = (f32[2,160,128]{2,1,0:T(8,128)S(1)}, f32[2,160,128]{2,1,0:T(8,128)S(1)}, u32[]{:S(2)}, u32[]{:S(2)}) collective-permute-start(f32[2,160,128]{2,1,0:T(8,128)S(1)} %get-tuple-element.126), channel_id=1, source_target_pairs={{0,8},{4,12},{8,16},{12,20},{16,24},{20,28},{24,0},{28,4},{32,40},... | collective-permute-start | bytes 491528 | tf_op jit(solution)/shard_map/ppermute | solution.py:601
  186.8 23.2 %collective-permute-start.28 = (bf16[256,1280]{1,0:T(8,128)(2,1)S(1)}, bf16[256,1280]{1,0:T(8,128)(2,1)S(1)}, u32[]{:S(2)}, u32[]{:S(2)}) collective-permute-start(bf16[256,1280]{1,0:T(8,128)(2,1)S(1)} %slice.3), channel_id=1, source_target_pairs={{0,4},{4,0},{8,12},{12,8},{16,20},{20,16},{24,28},{28,24},{32,36},... | collective-permute-start | bytes 1966088 | tf_op jit(solution)/shard_map/ppermute | solution.py:601
  192.9 20.1 %collective-permute-start.42 = (bf16[256,1280]{1,0:T(8,128)(2,1)S(1)}, bf16[256,1280]{1,0:T(8,128)(2,1)S(1)}, u32[]{:S(2)}, u32[]{:S(2)}) collective-permute-start(bf16[256,1280]{1,0:T(8,128)(2,1)S(1)} %get-tuple-element.109), channel_id=1, source_target_pairs={{0,1},{1,2},{2,3},{3,0},{4,5},{5,6},{6,7},{7,4},{8,9},{9,10},{10,1... | collective-permute-start | bytes 1966088 | tf_op jit(solution)/shard_map/ppermute | solution.py:601
  193.0 30.3 %collective-permute-start.43 = (bf16[256,1280]{1,0:T(8,128)(2,1)S(1)}, bf16[256,1280]{1,0:T(8,128)(2,1)S(1)}, u32[]{:S(2)}, u32[]{:S(2)}) collective-permute-start(bf16[256,1280]{1,0:T(8,128)(2,1)S(1)} %get-tuple-element.110), channel_id=1, source_target_pairs={{0,3},{1,0},{2,1},{3,2},{4,7},{5,4},{6,5},{7,6},{8,11},{9,8},{10,9... | collective-permute-start | bytes 1966088 | tf_op jit(solution)/shard_map/ppermute | solution.py:601
  195.6 29.2 %collective-permute-start.44 = (bf16[256,1280]{1,0:T(8,128)(2,1)S(1)}, bf16[256,1280]{1,0:T(8,128)(2,1)S(1)}, u32[]{:S(2)}, u32[]{:S(2)}) collective-permute-start(bf16[256,1280]{1,0:T(8,128)(2,1)S(1)} %get-tuple-element.111), channel_id=1, source_target_pairs={{0,2},{1,3},{2,0},{3,1},{4,6},{5,7},{6,4},{7,5},{8,10},{9,11},{10,... | collective-permute-start | bytes 1966088 | tf_op jit(solution)/shard_map/ppermute | solution.py:601
  196.1 5.6 %collective-permute-start.61 = (f32[2,160,128]{2,1,0:T(8,128)S(1)}, f32[2,160,128]{2,1,0:T(8,128)S(1)}, u32[]{:S(2)}, u32[]{:S(2)}) collective-permute-start(f32[2,160,128]{2,1,0:T(8,128)S(1)} %get-tuple-element.127), channel_id=1, source_target_pairs={{0,24},{4,28},{8,0},{12,4},{16,8},{20,12},{24,16},{28,20},{32,56},... | collective-permute-start | bytes 491528 | tf_op jit(solution)/shard_map/ppermute | solution.py:601
  201.7 5.7 %collective-permute-start.62 = (f32[2,160,128]{2,1,0:T(8,128)S(1)}, f32[2,160,128]{2,1,0:T(8,128)S(1)}, u32[]{:S(2)}, u32[]{:S(2)}) collective-permute-start(f32[2,160,128]{2,1,0:T(8,128)S(1)} %get-tuple-element.128), channel_id=1, source_target_pairs={{0,16},{4,20},{8,24},{12,28},{16,0},{20,4},{24,8},{28,12},{32,48},... | collective-permute-start | bytes 491528 | tf_op jit(solution)/shard_map/ppermute | solution.py:601
  207.5 4.2 %collective-permute-start.63 = (f32[160,256]{1,0:T(8,128)S(1)}, f32[160,256]{1,0:T(8,128)S(1)}, u32[]{:S(2)}, u32[]{:S(2)}) collective-permute-start(f32[160,256]{1,0:T(8,128)S(1)} %get-tuple-element.130), channel_id=1, source_target_pairs={{0,4},{4,0},{8,12},{12,8},{16,20},{20,16},{24,28},{28,24},{32,36},... | collective-permute-start | bytes 491528 | tf_op jit(solution)/shard_map/ppermute | solution.py:601
  (8 other events, 171.1 us)
